TPU v7x, 32 devices: a whole 2x2x4 slice. The times are simulated.
32 devices in a mesh: dp: 8 (over z, x), mp: 4 (over y, core).
Axes of the slice: x: 2, y: 2, z: 4, core: 2. Of those that a mesh axis runs over, the one named last changes fastest.
Arguments:
- tokens: bfloat16 [4, 7680, 768], P(None, ('dp', 'mp')), may hold values from -6 to 6
- cotangent: float32 [4, 7680, 768], P(None, ('dp', 'mp')), may hold values from -6 to 6
- text_lengths: int32 [4, 32], P(None, 'dp'), may hold values from 1 to 40, as said below
- modality: int32 [4, 7680], P(None, 'dp'), may hold values from 0 to 1, as said below
- masked_positions: int32 [4, 32, 6], P(None, 'dp'), may hold values from 0 to 39, as said below
- joint_weight: float32 [3, 768, 768], P(None, 'dp', 'mp'), may hold values from -0.21875 to 0.21875
- joint_first: float32 [3, 768, 768], P(None, 'dp', 'mp')
- joint_second: float32 [3, 768, 768], P(None, 'dp', 'mp'), as said below
- output_weight: float32 [768, 768], P('mp', 'dp'), may hold values from -0.625 to 0.625
- output_first: float32 [768, 768], P('mp', 'dp')
- output_second: float32 [768, 768], P('mp', 'dp'), as said below
- lift_weight: float32 [2, 768, 3072], P(None, 'dp', 'mp'), may hold values from -0.21875 to 0.21875
- lift_first: float32 [2, 768, 3072], P(None, 'dp', 'mp')
- lift_second: float32 [2, 768, 3072], P(None, 'dp', 'mp'), as said below
- drop_weight: float32 [2, 3072, 768], P(None, 'mp', 'dp'), may hold values from -0.109375 to 0.109375
- drop_first: float32 [2, 3072, 768], P(None, 'mp', 'dp')
- drop_second: float32 [2, 3072, 768], P(None, 'mp', 'dp'), as said below
- norm_params: float32 [4, 768], replicated, may hold values from -0.5 to 1.3
- norm_first: float32 [4, 768], replicated
- norm_second: float32 [4, 768], replicated, as said below
- extra_params: float32 [3, 768], replicated, may hold values from -3 to 3
- extra_first: float32 [3, 768], replicated
- extra_second: float32 [3, 768], replicated, as said below
Outputs:
- block_output: float32 [4, 7680, 768], P(None, ('dp', 'mp'))
- input_grad: float32 [4, 7680, 768], P(None, ('dp', 'mp'))
- rms_values: float32 [3], replicated
- joint_weight_new: float32 [3, 768, 768], P(None, 'dp', 'mp')
- joint_first_new: float32 [3, 768, 768], P(None, 'dp', 'mp')
- joint_second_new: float32 [3, 768, 768], P(None, 'dp', 'mp')
- joint_copy: bfloat16 [3, 768, 768], P(None, 'dp', 'mp')
- output_weight_new: float32 [768, 768], P('mp', 'dp')
- output_first_new: float32 [768, 768], P('mp', 'dp')
- output_second_new: float32 [768, 768], P('mp', 'dp')
- output_copy: bfloat16 [768, 768], P('mp', 'dp')
- lift_weight_new: float32 [2, 768, 3072], P(None, 'dp', 'mp')
- lift_first_new: float32 [2, 768, 3072], P(None, 'dp', 'mp')
- lift_second_new: float32 [2, 768, 3072], P(None, 'dp', 'mp')
- lift_copy: bfloat16 [2, 768, 3072], P(None, 'dp', 'mp')
- drop_weight_new: float32 [2, 3072, 768], P(None, 'mp', 'dp')
- drop_first_new: float32 [2, 3072, 768], P(None, 'mp', 'dp')
- drop_second_new: float32 [2, 3072, 768], P(None, 'mp', 'dp')
- drop_copy: bfloat16 [2, 3072, 768], P(None, 'mp', 'dp')
- norm_params_new: float32 [4, 768], replicated
- norm_first_new: float32 [4, 768], replicated
- norm_second_new: float32 [4, 768], replicated
- norm_copy: bfloat16 [4, 768], replicated
- extra_params_new: float32 [3, 768], replicated
- extra_first_new: float32 [3, 768], replicated
- extra_second_new: float32 [3, 768], replicated
- extra_copy: bfloat16 [3, 768], replicated
Inputs may be any that keep to these rules, and one draw needn't show every extreme that they name: `text_lengths`: among the 4 items of one index of dp in a micro-batch, one has exactly 40 text tokens. `modality`: follows text_lengths: in each block of 960 rows, the items' patch rows are 0, their text rows and the rows after the last item are 1, so a block holds exactly 788 zeros. `masked_positions`: each position is below its item's text length; repeats may occur. `joint_second`: Positive. `output_second`: Positive. `lift_second`: Positive. `drop_second`: Positive. `norm_second`: Positive. `extra_second`: Positive.
All inputs are finite; a program needn't handle non-finite values.
Results may differ from a plain program's by a relative error of at most 0.015.
Values may be sent and summed in bfloat16 or wider, within the bound.
No kernel may reach another device: no remote copies, remote signals or barrier semaphores. Data moves between devices by JAX's collectives and lax.ppermute only.
A program may use at most 256 MiB of HBM per device.

v0:
```python
import jax
import jax.numpy as jnp
from jax import lax
from jax.sharding import PartitionSpec as P

HEAD_DIM = 64
PATCHES = 197
STEP = 7


norm_epsilon = 1e-06
masked_score = -1000000000.0
first_decay = 0.9
second_decay = 0.98
adam_epsilon = 1e-06
matrix_rate = 0.04
vector_rate = 0.5
weight_decay = 0.01


def layer_norm(values, gain_row, shift_row):
    centred = values - jnp.mean(values, axis=-1, keepdims=True)
    spread = jnp.mean(centred * centred, axis=-1, keepdims=True)
    return centred * lax.rsqrt(spread + norm_epsilon) * gain_row + shift_row


def gelu_exact(values):
    return jax.nn.gelu(values, approximate=False)


def block_layout(lengths, masked, total_rows):
    item_sizes = PATCHES + lengths
    item_ends = jnp.cumsum(item_sizes, dtype=jnp.int32)
    item_starts = item_ends - item_sizes
    row_ids = jnp.arange(total_rows, dtype=jnp.int32)
    segment = jnp.sum(
        (row_ids[:, None] >= item_ends[None, :]).astype(jnp.int32), axis=1, dtype=jnp.int32
    )
    valid_rows = segment < lengths.shape[0]
    targets = (item_starts[:, None] + PATCHES + masked).reshape(-1)
    hidden = jnp.any(row_ids[:, None] == targets[None, :], axis=1)
    return (segment, valid_rows, hidden)


def adamw(weight, first_state, second_state, gradient, step_rate, decay_rate):
    first_new = first_decay * first_state + (1.0 - first_decay) * gradient
    second_new = second_decay * second_state + (1.0 - second_decay) * gradient * gradient
    first_hat = first_new / (1.0 - first_decay**STEP)
    second_hat = second_new / (1.0 - second_decay**STEP)
    weight_new = weight - step_rate * (
        first_hat / (jnp.sqrt(second_hat) + adam_epsilon) + decay_rate * weight
    )
    return (weight_new, first_new, second_new, weight_new.astype(jnp.bfloat16))


def body(
    tokens,
    cotangent,
    text_lengths,
    modality,
    masked_positions,
    joint_weight,
    joint_first,
    joint_second,
    output_weight,
    output_first,
    output_second,
    lift_weight,
    lift_first,
    lift_second,
    drop_weight,
    drop_first,
    drop_second,
    norm_params,
    norm_first,
    norm_second,
    extra_params,
    extra_first,
    extra_second,
):
    micro_count, shard_rows, model_width = tokens.shape
    block_rows = modality.shape[1]
    item_count = text_lengths.shape[1]
    vision_rows = item_count * PATCHES
    offset = lax.axis_index("mp") * shard_rows
    score_scale = HEAD_DIM ** (-0.5)
    joint_all, output_all, lift_all, drop_all = (
        lax.all_gather(joint_weight.astype(jnp.bfloat16), "dp", axis=1, tiled=True),
        lax.all_gather(output_weight.astype(jnp.bfloat16), "dp", axis=1, tiled=True),
        lax.all_gather(lift_weight.astype(jnp.bfloat16), "dp", axis=1, tiled=True),
        lax.all_gather(drop_weight.astype(jnp.bfloat16), "dp", axis=2, tiled=True),
    )
    head_width = joint_all.shape[2]
    head_count = head_width // HEAD_DIM
    shard_sums = (
        jnp.zeros(joint_weight.shape, jnp.float32),
        jnp.zeros(output_weight.shape, jnp.float32),
        jnp.zeros(lift_weight.shape, jnp.float32),
        jnp.zeros(drop_weight.shape, jnp.float32),
    )
    grad_norm = jnp.zeros((4, model_width), jnp.float32)
    grad_extra = jnp.zeros((3, model_width), jnp.float32)
    squares = jnp.zeros((3,), jnp.float32)
    valid_count = jnp.zeros((), jnp.float32)
    output_list = []
    gradient_list = []
    for micro_index in range(micro_count):
        lengths = text_lengths[micro_index]
        masked = masked_positions[micro_index]
        row_kinds = modality[micro_index]
        segment, valid_rows, hidden = block_layout(lengths, masked, block_rows)
        own_valid = lax.dynamic_slice_in_dim(valid_rows, offset, shard_rows).astype(jnp.float32)[
            :, None
        ]
        own_hidden = lax.dynamic_slice_in_dim(hidden, offset, shard_rows)[:, None]
        own_vision = (lax.dynamic_slice_in_dim(row_kinds, offset, shard_rows) == 0)[:, None]
        input_rows = tokens[micro_index].astype(jnp.float32)
        block_input = jnp.where(own_hidden, extra_params[2][None, :], input_rows)
        normed, norm_back = jax.vjp(layer_norm, block_input, norm_params[0], norm_params[1])
        normed_all = lax.all_gather(normed.astype(jnp.bfloat16), "mp", axis=0, tiled=True)
        joint_rows = jnp.einsum(
            "td,kdc->ktc", normed_all, joint_all, preferred_element_type=jnp.float32
        ).astype(jnp.bfloat16)
        head_rows = joint_rows.reshape(3, block_rows, head_count, HEAD_DIM)
        same_item = segment[:, None] == segment[None, :]
        raw_scores = jnp.einsum(
            "qhe,khe->hqk", head_rows[0], head_rows[1], preferred_element_type=jnp.float32
        )
        scores = jnp.where(same_item[None], raw_scores * score_scale, masked_score)
        row_top = jnp.max(scores, axis=-1, keepdims=True)
        exp_scores = jnp.exp(scores - row_top)
        row_total = jnp.sum(exp_scores, axis=-1, keepdims=True)
        softmax_half = (exp_scores / row_total).astype(jnp.bfloat16)
        log_total = row_top + jnp.log(row_total)
        mixed_rows = jnp.einsum(
            "hqk,khe->qhe", softmax_half, head_rows[2], preferred_element_type=jnp.float32
        )
        mixed_rows = mixed_rows.reshape(block_rows, head_width).astype(jnp.bfloat16)
        attended = lax.psum_scatter(
            jnp.dot(mixed_rows, output_all, preferred_element_type=jnp.float32).astype(
                jnp.bfloat16
            ),
            "mp",
            scatter_dimension=0,
            tiled=True,
        ).astype(jnp.float32)
        residual = block_input + attended
        feed_input, feed_norm_back = jax.vjp(layer_norm, residual, norm_params[2], norm_params[3])
        feed_all = lax.all_gather(feed_input.astype(jnp.bfloat16), "mp", axis=0, tiled=True)
        vision_int = (row_kinds == 0).astype(jnp.int32)
        rank_vision = jnp.cumsum(vision_int, dtype=jnp.int32) - 1
        rank_text = jnp.cumsum(1 - vision_int, dtype=jnp.int32) - 1
        sorted_place = jnp.where(vision_int == 1, rank_vision, vision_rows + rank_text)
        sorted_order = (
            jnp.zeros((block_rows,), jnp.int32)
            .at[sorted_place]
            .set(jnp.arange(block_rows, dtype=jnp.int32))
        )
        grouped = feed_all[sorted_order]
        vision_input = grouped[:vision_rows]
        text_input = grouped[vision_rows:]
        lift_vision = jnp.dot(vision_input, lift_all[0], preferred_element_type=jnp.float32)
        lift_text = jnp.dot(text_input, lift_all[1], preferred_element_type=jnp.float32)
        acted_vision, gelu_back_vision = jax.vjp(gelu_exact, lift_vision)
        acted_text, gelu_back_text = jax.vjp(gelu_exact, lift_text)
        acted_vision = acted_vision.astype(jnp.bfloat16)
        acted_text = acted_text.astype(jnp.bfloat16)
        dropped = jnp.concatenate(
            [
                jnp.dot(acted_vision, drop_all[0], preferred_element_type=jnp.float32),
                jnp.dot(acted_text, drop_all[1], preferred_element_type=jnp.float32),
            ],
            axis=0,
        )
        feed_sum = lax.psum_scatter(
            dropped[sorted_place].astype(jnp.bfloat16), "mp", scatter_dimension=0, tiled=True
        ).astype(jnp.float32)
        feed_out = feed_sum + jnp.where(
            own_vision, extra_params[0][None, :], extra_params[1][None, :]
        )
        block_rows_out = residual + feed_out
        output_list.append(block_rows_out)
        grad_out = cotangent[micro_index] * own_valid
        grad_feed_all = lax.all_gather(grad_out.astype(jnp.bfloat16), "mp", axis=0, tiled=True)
        grad_grouped = grad_feed_all[sorted_order]
        grad_vision = grad_grouped[:vision_rows]
        grad_text = grad_grouped[vision_rows:]
        grad_drop = jnp.stack(
            [
                jnp.einsum(
                    "tf,td->fd", acted_vision, grad_vision, preferred_element_type=jnp.float32
                ),
                jnp.einsum("tf,td->fd", acted_text, grad_text, preferred_element_type=jnp.float32),
            ]
        )
        grad_acted_vision = jnp.einsum(
            "td,fd->tf", grad_vision, drop_all[0], preferred_element_type=jnp.float32
        )
        grad_acted_text = jnp.einsum(
            "td,fd->tf", grad_text, drop_all[1], preferred_element_type=jnp.float32
        )
        grad_lift_vision = gelu_back_vision(grad_acted_vision)[0].astype(jnp.bfloat16)
        grad_lift_text = gelu_back_text(grad_acted_text)[0].astype(jnp.bfloat16)
        grad_lift = jnp.stack(
            [
                jnp.einsum(
                    "td,tf->df", vision_input, grad_lift_vision, preferred_element_type=jnp.float32
                ),
                jnp.einsum(
                    "td,tf->df", text_input, grad_lift_text, preferred_element_type=jnp.float32
                ),
            ]
        )
        grad_feed_sorted = jnp.concatenate(
            [
                jnp.einsum(
                    "tf,df->td", grad_lift_vision, lift_all[0], preferred_element_type=jnp.float32
                ),
                jnp.einsum(
                    "tf,df->td", grad_lift_text, lift_all[1], preferred_element_type=jnp.float32
                ),
            ],
            axis=0,
        )
        grad_feed_input = lax.psum_scatter(
            grad_feed_sorted[sorted_place].astype(jnp.bfloat16),
            "mp",
            scatter_dimension=0,
            tiled=True,
        ).astype(jnp.float32)
        grad_residual, grad_gain_second, grad_shift_second = feed_norm_back(grad_feed_input)
        grad_residual = grad_residual + grad_out
        grad_bias_vision = jnp.sum(jnp.where(own_vision, grad_out, 0.0), axis=0)
        grad_bias_text = jnp.sum(jnp.where(own_vision, 0.0, grad_out), axis=0)
        grad_attended_all = lax.all_gather(
            grad_residual.astype(jnp.bfloat16), "mp", axis=0, tiled=True
        )
        grad_output = jnp.einsum(
            "tc,td->cd", mixed_rows, grad_attended_all, preferred_element_type=jnp.float32
        )
        grad_mixed = jnp.einsum(
            "td,cd->tc", grad_attended_all, output_all, preferred_element_type=jnp.float32
        )
        grad_mixed = grad_mixed.astype(jnp.bfloat16).reshape(block_rows, head_count, HEAD_DIM)
        raw_again = jnp.einsum(
            "qhe,khe->hqk", head_rows[0], head_rows[1], preferred_element_type=jnp.float32
        )
        scores_again = jnp.where(same_item[None], raw_again * score_scale, masked_score)
        softmax_rows = jnp.exp(scores_again - log_total)
        softmax_again = softmax_rows.astype(jnp.bfloat16)
        grad_value = jnp.einsum(
            "hqk,qhe->khe", softmax_again, grad_mixed, preferred_element_type=jnp.float32
        )
        grad_probs = jnp.einsum(
            "qhe,khe->hqk", grad_mixed, head_rows[2], preferred_element_type=jnp.float32
        )
        grad_scores = softmax_rows * (
            grad_probs - jnp.sum(softmax_rows * grad_probs, axis=-1, keepdims=True)
        )
        grad_raw = (grad_scores * score_scale).astype(jnp.bfloat16)
        grad_query = jnp.einsum(
            "hqk,khe->qhe", grad_raw, head_rows[1], preferred_element_type=jnp.float32
        )
        grad_key = jnp.einsum(
            "hqk,qhe->khe", grad_raw, head_rows[0], preferred_element_type=jnp.float32
        )
        grad_joint_rows = (
            jnp.stack([grad_query, grad_key, grad_value])
            .reshape(3, block_rows, head_width)
            .astype(jnp.bfloat16)
        )
        grad_joint = jnp.einsum(
            "td,ktc->kdc", normed_all, grad_joint_rows, preferred_element_type=jnp.float32
        )
        grad_normed = lax.psum_scatter(
            jnp.einsum(
                "ktc,kdc->td", grad_joint_rows, joint_all, preferred_element_type=jnp.float32
            ).astype(jnp.bfloat16),
            "mp",
            scatter_dimension=0,
            tiled=True,
        ).astype(jnp.float32)
        grad_block_input, grad_gain_first, grad_shift_first = norm_back(grad_normed)
        grad_block_input = grad_block_input + grad_residual
        grad_mask = jnp.sum(jnp.where(own_hidden, grad_block_input, 0.0), axis=0)
        gradient_list.append(jnp.where(own_hidden, 0.0, grad_block_input))
        grad_norm = grad_norm + jnp.stack(
            [grad_gain_first, grad_shift_first, grad_gain_second, grad_shift_second]
        )
        grad_extra = grad_extra + jnp.stack([grad_bias_vision, grad_bias_text, grad_mask])
        squares = squares + jnp.stack(
            [
                jnp.sum(own_valid * block_rows_out * block_rows_out),
                jnp.sum(own_valid * attended * attended),
                jnp.sum(own_valid * feed_out * feed_out),
            ]
        )
        valid_count = valid_count + jnp.sum(own_valid)
        micro_grads = (grad_joint, grad_output, grad_lift, grad_drop)
        reduced = (
            lax.psum_scatter(micro_grads[0], "dp", scatter_dimension=1, tiled=True),
            lax.psum_scatter(micro_grads[1], "dp", scatter_dimension=1, tiled=True),
            lax.psum_scatter(micro_grads[2], "dp", scatter_dimension=1, tiled=True),
            lax.psum_scatter(micro_grads[3], "dp", scatter_dimension=2, tiled=True),
        )
        shard_sums = tuple((summed + addend for summed, addend in zip(shard_sums, reduced)))
    norm_total, extra_total, squares_total, count_total = lax.psum(
        (grad_norm, grad_extra, squares, valid_count), ("dp", "mp")
    )
    rms_values = jnp.sqrt(squares_total / (count_total * model_width))
    joint_new = adamw(
        joint_weight, joint_first, joint_second, shard_sums[0], matrix_rate, weight_decay
    )
    output_new = adamw(
        output_weight, output_first, output_second, shard_sums[1], matrix_rate, weight_decay
    )
    lift_new = adamw(lift_weight, lift_first, lift_second, shard_sums[2], matrix_rate, weight_decay)
    drop_new = adamw(drop_weight, drop_first, drop_second, shard_sums[3], matrix_rate, weight_decay)
    norm_new = adamw(norm_params, norm_first, norm_second, norm_total, vector_rate, 0.0)
    extra_new = adamw(extra_params, extra_first, extra_second, extra_total, vector_rate, 0.0)
    block_output = jnp.stack(output_list)
    input_grad = jnp.stack(gradient_list)
    return (
        block_output,
        input_grad,
        rms_values,
        joint_new[0],
        joint_new[1],
        joint_new[2],
        joint_new[3],
        output_new[0],
        output_new[1],
        output_new[2],
        output_new[3],
        lift_new[0],
        lift_new[1],
        lift_new[2],
        lift_new[3],
        drop_new[0],
        drop_new[1],
        drop_new[2],
        drop_new[3],
        norm_new[0],
        norm_new[1],
        norm_new[2],
        norm_new[3],
        extra_new[0],
        extra_new[1],
        extra_new[2],
        extra_new[3],
    )


def solution(mesh):
    return jax.shard_map(
        body,
        mesh=mesh,
        in_specs=(
            P(None, ("dp", "mp"), None),
            P(None, ("dp", "mp"), None),
            P(None, "dp"),
            P(None, "dp"),
            P(None, "dp", None),
            P(None, "dp", "mp"),
            P(None, "dp", "mp"),
            P(None, "dp", "mp"),
            P("mp", "dp"),
            P("mp", "dp"),
            P("mp", "dp"),
            P(None, "dp", "mp"),
            P(None, "dp", "mp"),
            P(None, "dp", "mp"),
            P(None, "mp", "dp"),
            P(None, "mp", "dp"),
            P(None, "mp", "dp"),
            P(),
            P(),
            P(),
            P(),
            P(),
            P(),
        ),
        out_specs=(
            P(None, ("dp", "mp"), None),
            P(None, ("dp", "mp"), None),
            P(),
            P(None, "dp", "mp"),
            P(None, "dp", "mp"),
            P(None, "dp", "mp"),
            P(None, "dp", "mp"),
            P("mp", "dp"),
            P("mp", "dp"),
            P("mp", "dp"),
            P("mp", "dp"),
            P(None, "dp", "mp"),
            P(None, "dp", "mp"),
            P(None, "dp", "mp"),
            P(None, "dp", "mp"),
            P(None, "mp", "dp"),
            P(None, "mp", "dp"),
            P(None, "mp", "dp"),
            P(None, "mp", "dp"),
            P(),
            P(),
            P(),
            P(),
            P(),
            P(),
            P(),
            P(),
        ),
        check_vma=False,
    )
```

profile of v0, /device:TPU:0, one launch (start us, length us, event | category | flops | bytes accessed | tf_op | source)
XLA Modules:
  0.0 1466.3 jit_solution(10561530150028786182)
XLA Ops:
  18.3 39.1 %all_gather.61 = bf16[3,768,192]{2,0,1:T(4,128)(2,1)S(1)} all-gather(bf16[3,96,192]{2,0,1:T(4,128)(2,1)S(1)} %copy.210), channel_id=1, replica_groups=mesh['dp'=8,'mp'=4] {'dp'}, dimensions={1}, use_global_device_ids=true | all-gather | bytes 995328 | tf_op jit(solution)/shard_map/all_gather | solution.py:88
  58.5 31.2 %all_gather.62 = bf16[192,768]{0,1:T(8,128)(2,1)S(1)} all-gather(bf16[192,96]{0,1:T(8,128)(2,1)S(1)} %copy.213), channel_id=1, replica_groups=mesh['dp'=8,'mp'=4] {'dp'}, dimensions={1}, use_global_device_ids=true | all-gather | bytes 331776 | tf_op jit(solution)/shard_map/all_gather | solution.py:89
  107.8 25.8 %reduce-scatter.24.cloned.1.call-done = bf16[240,768]{1,0:T(8,128)(2,1)} async-done(((bf16[960,768]{1,0:T(8,128)(2,1)}), bf16[240,768]{1,0:T(8,128)(2,1)}) %reduce-scatter.24.cloned.1.call-update) | async-done | bytes 368656 | tf_op jit(solution)/shard_map/reduce_scatter | solution.py:139
  140.6 16.3 %all-gather.31.cloned.1.call-done = bf16[960,768]{1,0:T(8,128)(2,1)} async-done(((bf16[240,768]{1,0:T(8,128)(2,1)}), bf16[960,768]{1,0:T(8,128)(2,1)}) %all-gather.31.cloned.1.call-update) | async-done | bytes 1474576 | tf_op jit(solution)/shard_map/all_gather | solution.py:120
  165.9 7.2 fusion.10
  173.1 6.8 fusion.180
  192.4 7.0 fusion.11
  213.5 27.3 %reduce-scatter.36.cloned.1.call-done = bf16[240,768]{1,0:T(8,128)(2,1)} async-done(((bf16[960,768]{1,0:T(8,128)(2,1)}), bf16[240,768]{1,0:T(8,128)(2,1)}) %reduce-scatter.36.cloned.1.call-update) | async-done | bytes 368656 | tf_op jit(solution)/shard_map/reduce_scatter | solution.py:139
  254.3 7.9 all-gather.51.cloned.1.call-done
  262.2 7.1 gather_fusion.14
  269.3 14.3 all-gather.37.cloned.1.call-done
  289.8 48.8 %all-gather.23.cloned.1.call-done = bf16[2,768,768]{2,1,0:T(8,128)(2,1)} async-done(((bf16[2,96,768]{2,1,0:T(8,128)(2,1)}), bf16[2,768,768]{2,1,0:T(8,128)(2,1)}) %all-gather.23.cloned.1.call-update) | async-done | bytes 2359312 | tf_op jit(solution)/shard_map/all_gather | solution.py:90
  342.4 8.0 multiply_convert_fusion.4
  350.4 41.8 %all-gather.25.cloned.1.call-done = bf16[2,768,768]{1,2,0:T(8,128)(2,1)} async-done(((bf16[2,768,96]{1,2,0:T(8,128)(2,1)}), bf16[2,768,768]{1,2,0:T(8,128)(2,1)}) %all-gather.25.cloned.1.call-update) | async-done | bytes 2359312 | tf_op jit(solution)/shard_map/all_gather | solution.py:91
  417.1 15.5 %reduce-scatter.52.cloned.1.call-done = bf16[240,768]{1,0:T(8,128)(2,1)} async-done(((bf16[960,768]{1,0:T(8,128)(2,1)}), bf16[240,768]{1,0:T(8,128)(2,1)}) %reduce-scatter.52.cloned.1.call-update) | async-done | bytes 368656 | tf_op jit(solution)/shard_map/reduce_scatter | solution.py:225
  434.8 28.3 %reduce-scatter.38.cloned.1.call-done = bf16[240,768]{1,0:T(8,128)(2,1)} async-done(((bf16[960,768]{1,0:T(8,128)(2,1)}), bf16[240,768]{1,0:T(8,128)(2,1)}) %reduce-scatter.38.cloned.1.call-update) | async-done | bytes 368656 | tf_op jit(solution)/shard_map/reduce_scatter | solution.py:175
  469.7 17.6 %all-gather.27.cloned.1.call-done = bf16[960,768]{1,0:T(8,128)(2,1)} async-done(((bf16[240,768]{1,0:T(8,128)(2,1)}), bf16[960,768]{1,0:T(8,128)(2,1)}) %all-gather.27.cloned.1.call-update) | async-done | bytes 1474576 | tf_op jit(solution)/shard_map/all_gather | solution.py:120
  497.0 7.0 fusion.9
  504.0 6.8 fusion.181
  515.4 25.6 %reduce-scatter.28.cloned.1.call-done = bf16[240,768]{1,0:T(8,128)(2,1)} async-done(((bf16[960,768]{1,0:T(8,128)(2,1)}), bf16[240,768]{1,0:T(8,128)(2,1)}) %reduce-scatter.28.cloned.1.call-update) | async-done | bytes 368656 | tf_op jit(solution)/shard_map/reduce_scatter | solution.py:139
  572.7 9.5 all-gather.39.cloned.1.call-done
  582.2 7.1 gather_fusion.8
  589.3 13.5 all-gather.43.cloned.1.call-done
  602.7 7.1 gather_fusion.10
  610.1 13.8 all-gather.33.cloned.1.call-done
  663.1 6.8 multiply_convert_fusion.7
  735.7 20.5 %reduce-scatter.44.cloned.1.call-done = bf16[240,768]{1,0:T(8,128)(2,1)} async-done(((bf16[960,768]{1,0:T(8,128)(2,1)}), bf16[240,768]{1,0:T(8,128)(2,1)}) %reduce-scatter.44.cloned.1.call-update) | async-done | bytes 368656 | tf_op jit(solution)/shard_map/reduce_scatter | solution.py:225
  759.3 27.1 %reduce-scatter.26.cloned.1.call-done = bf16[240,768]{1,0:T(8,128)(2,1)} async-done(((bf16[960,768]{1,0:T(8,128)(2,1)}), bf16[240,768]{1,0:T(8,128)(2,1)}) %reduce-scatter.26.cloned.1.call-update) | async-done | bytes 368656 | tf_op jit(solution)/shard_map/reduce_scatter | solution.py:175
  792.6 24.0 %reduce-scatter.30.cloned.1.call-done = bf16[240,768]{1,0:T(8,128)(2,1)} async-done(((bf16[960,768]{1,0:T(8,128)(2,1)}), bf16[240,768]{1,0:T(8,128)(2,1)}) %reduce-scatter.30.cloned.1.call-update) | async-done | bytes 368656 | tf_op jit(solution)/shard_map/reduce_scatter | solution.py:175
  822.7 24.1 %reduce-scatter.34.cloned.1.call-done = bf16[240,768]{1,0:T(8,128)(2,1)} async-done(((bf16[960,768]{1,0:T(8,128)(2,1)}), bf16[240,768]{1,0:T(8,128)(2,1)}) %reduce-scatter.34.cloned.1.call-update) | async-done | bytes 368656 | tf_op jit(solution)/shard_map/reduce_scatter | solution.py:175
  867.3 8.2 copy.240
  885.5 18.4 %fusion.186 = bf16[3,64,960]{2,1,0:T(8,128)(2,1)} fusion(bf16[960,3,64]{0,2,1:T(8,128)(2,1)S(1)} %bitcast.594, f32[3,960,960]{1,2,0:T(8,128)} %fusion.564, f32[3,960,960]{1,2,0:T(8,128)} %get-tuple-element.356, f32[3,960]{1,0:T(4,128)S(1)} %log_add_fusion, pred[960,960]{0,1:T(8,128)(4,1)S(1)} %copy-done.19), kind=kOutput, calls=%fused_computation.252 | convolution fusion | flops 384495360 | bytes 23788800 | tf_op jit(solution)/shard_map/hqk,qhe->khe/dot_general | solution.py:264
  903.9 19.8 %fusion.183 = bf16[3,64,960]{2,1,0:T(8,128)(2,1)} fusion(bf16[960,3,64]{0,2,1:T(8,128)(2,1)S(1)} %bitcast.592, f32[3,960,960]{1,2,0:T(8,128)} %fusion.564, f32[3,960,960]{1,2,0:T(8,128)} %get-tuple-element.356, f32[3,960]{1,0:T(4,128)S(1)} %log_add_fusion, pred[960,960]{0,1:T(8,128)(4,1)S(1)} %copy-done.19), kind=kOutput, calls=%fused_computation.251 | convolution fusion | flops 384495360 | bytes 23788800 | tf_op jit(solution)/shard_map/hqk,khe->qhe/dot_general | solution.py:261
  933.7 7.7 fusion.176
  952.5 17.5 %fusion.198 = bf16[3,64,960]{2,1,0:T(8,128)(2,1)S(1)} fusion(bf16[960,3,64]{0,2,1:T(8,128)(2,1)S(1)} %bitcast.598, f32[3,960,960]{1,2,0:T(8,128)} %fusion.562, f32[3,960,960]{1,2,0:T(8,128)} %get-tuple-element.360, f32[3,960]{1,0:T(4,128)S(1)} %log_add_fusion.2, pred[960,960]{0,1:T(8,128)(4,1)S(1)} %copy-done.21), kind=kOutput, calls=%fused_computation.256 | convolution fusion | flops 384495360 | bytes 23788800 | tf_op jit(solution)/shard_map/hqk,qhe->khe/dot_general | solution.py:264
  970.0 19.0 %fusion.195 = bf16[3,64,960]{2,1,0:T(8,128)(2,1)S(1)} fusion(bf16[960,3,64]{0,2,1:T(8,128)(2,1)S(1)} %bitcast.596, f32[3,960,960]{1,2,0:T(8,128)} %fusion.562, f32[3,960,960]{1,2,0:T(8,128)} %get-tuple-element.360, f32[3,960]{1,0:T(4,128)S(1)} %log_add_fusion.2, pred[960,960]{0,1:T(8,128)(4,1)S(1)} %copy-done.21), kind=kOutput, calls=%fused_computation.255 | convolution fusion | flops 384495360 | bytes 23788800 | tf_op jit(solution)/shard_map/hqk,khe->qhe/dot_general | solution.py:261
  1005.7 17.5 %fusion.204 = bf16[3,64,960]{2,1,0:T(8,128)(2,1)S(1)} fusion(bf16[960,3,64]{0,2,1:T(8,128)(2,1)S(1)} %bitcast.586, f32[3,960,960]{1,2,0:T(8,128)} %fusion.561, f32[3,960,960]{1,2,0:T(8,128)} %copy-done.3, f32[3,960]{1,0:T(4,128)S(1)} %log_add_fusion.3, pred[960,960]{0,1:T(8,128)(4,1)S(1)} %copy-done.15), kind=kOutput, calls=%fused_computation.258 | convolution fusion | flops 384495360 | bytes 23788800 | tf_op jit(solution)/shard_map/hqk,qhe->khe/dot_general | solution.py:264
  1023.2 20.1 %fusion.201 = bf16[3,64,960]{2,1,0:T(8,128)(2,1)} fusion(bf16[960,3,64]{0,2,1:T(8,128)(2,1)S(1)} %bitcast.584, f32[3,960,960]{1,2,0:T(8,128)} %fusion.561, f32[3,960,960]{1,2,0:T(8,128)} %copy-done.3, f32[3,960]{1,0:T(4,128)S(1)} %log_add_fusion.3, pred[960,960]{0,1:T(8,128)(4,1)S(1)} %copy-done.15), kind=kOutput, calls=%fused_computation.257 | convolution fusion | flops 384495360 | bytes 23788800 | tf_op jit(solution)/shard_map/hqk,khe->qhe/dot_general | solution.py:261
  1060.3 17.4 %fusion.192 = bf16[3,64,960]{2,1,0:T(8,128)(2,1)S(1)} fusion(bf16[960,3,64]{0,2,1:T(8,128)(2,1)S(1)} %bitcast.590, f32[3,960,960]{1,2,0:T(8,128)} %fusion.563, f32[3,960,960]{1,2,0:T(8,128)} %get-tuple-element.354, f32[3,960]{1,0:T(4,128)S(1)} %log_add_fusion.1, pred[960,960]{0,1:T(8,128)(4,1)S(1)} %copy-done.17), kind=kOutput, calls=%fused_computation.254 | convolution fusion | flops 384495360 | bytes 23788800 | tf_op jit(solution)/shard_map/hqk,qhe->khe/dot_general | solution.py:264
  1077.7 18.9 %fusion.189 = bf16[3,64,960]{2,1,0:T(8,128)(2,1)S(1)} fusion(bf16[960,3,64]{0,2,1:T(8,128)(2,1)S(1)} %bitcast.588, f32[3,960,960]{1,2,0:T(8,128)} %fusion.563, f32[3,960,960]{1,2,0:T(8,128)} %get-tuple-element.354, f32[3,960]{1,0:T(4,128)S(1)} %log_add_fusion.1, pred[960,960]{0,1:T(8,128)(4,1)S(1)} %copy-done.17), kind=kOutput, calls=%fused_computation.253 | convolution fusion | flops 384495360 | bytes 23788800 | tf_op jit(solution)/shard_map/hqk,khe->qhe/dot_general | solution.py:261
  1162.9 8.4 fusion.450
  1178.4 18.7 %reduce-scatter.54.cloned.1.call-done = bf16[240,768]{1,0:T(8,128)(2,1)} async-done(((bf16[960,768]{1,0:T(8,128)(2,1)}), bf16[240,768]{1,0:T(8,128)(2,1)}) %reduce-scatter.54.cloned.1.call-update) | async-done | bytes 368656 | tf_op jit(solution)/shard_map/reduce_scatter | solution.py:275
  1197.2 30.2 %reduce-scatter.46.cloned.1.call-done = bf16[240,768]{1,0:T(8,128)(2,1)} async-done(((bf16[960,768]{1,0:T(8,128)(2,1)}), bf16[240,768]{1,0:T(8,128)(2,1)}) %reduce-scatter.46.cloned.1.call-update) | async-done | bytes 368656 | tf_op jit(solution)/shard_map/reduce_scatter | solution.py:275
  1227.4 30.3 %reduce-scatter.42.cloned.1.call-done = bf16[240,768]{1,0:T(8,128)(2,1)} async-done(((bf16[960,768]{1,0:T(8,128)(2,1)}), bf16[240,768]{1,0:T(8,128)(2,1)}) %reduce-scatter.42.cloned.1.call-update) | async-done | bytes 368656 | tf_op jit(solution)/shard_map/reduce_scatter | solution.py:275
  1257.7 30.0 %reduce-scatter.50.cloned.1.call-done = bf16[240,768]{1,0:T(8,128)(2,1)} async-done(((bf16[960,768]{1,0:T(8,128)(2,1)}), bf16[240,768]{1,0:T(8,128)(2,1)}) %reduce-scatter.50.cloned.1.call-update) | async-done | bytes 368656 | tf_op jit(solution)/shard_map/reduce_scatter | solution.py:275
  1296.5 40.3 %all-reduce.9 = (f32[3]{0:T(128)S(1)}, f32[]{:T(128)}, f32[4,768]{1,0:T(4,128)S(1)}, f32[3,768]{1,0:T(4,128)S(1)}) all-reduce(f32[3]{0:T(128)} %fusion.450, f32[]{:T(128)S(6)} %add.813, f32[4,768]{1,0:T(4,128)S(1)} %fusion.422, f32[3,768]{1,0:T(4,128)S(1)} %fusion.424), channel_id=1, replica_groups=mesh['dp'=8,'mp'=4] {'dp','mp'}, use_global_device_ids=true, to_apply=%region_104.105 | all-reduce | flops 5380 | bytes 43040 | tf_op jit(solution)/shard_map/psum | solution.py:307
  1341.7 16.8 %reduce-scatter.58.cloned.1.call-done = f32[96,576]{1,0:T(8,128)} async-done(((f32[768,576]{1,0:T(8,128)}), f32[96,576]{1,0:T(8,128)}) %reduce-scatter.58.cloned.1.call-update) | async-done | bytes 221200
  1363.6 93.2 %reduce-scatter.56.cloned.1.call-done = f32[2,96,768]{2,1,0:T(8,128)} async-done(((f32[2,768,768]{2,1,0:T(8,128)}), f32[2,96,768]{2,1,0:T(8,128)}) %reduce-scatter.56.cloned.1.call-update) | async-done | bytes 589840 | tf_op jit(solution)/shard_map/reduce_scatter | solution.py:303
  (1052 shorter events, 467.9 us)
Async XLA Ops:
  7.2 83.1 %all-gather.19.cloned.1.call-start = ((), (), s32[]{:S(2)}) async-start(), calls=%async_computation.19 | async-start | bytes 1843200 | tf_op jit(solution)/shard_map/all_gather | solution.py:120
  8.1 458.9 %copy-start.117 = (f32[768]{0:T(1024)}, f32[768]{0:T(1024)S(1)}, u32[]{:S(2)}) copy-start(f32[768]{0:T(1024)S(1)} %get-tuple-element.236) | copy-start | bytes 9220
  8.2 537.1 %copy-start.106 = (f32[768]{0:T(1024)}, f32[768]{0:T(1024)S(1)}, u32[]{:S(2)}) copy-start(f32[768]{0:T(1024)S(1)} %get-tuple-element.234) | copy-start | bytes 9220
  9.0 454.1 %copy-start.143 = (f32[768]{0:T(1024)}, f32[768]{0:T(1024)S(1)}, u32[]{:S(2)}) copy-start(f32[768]{0:T(1024)S(1)} %get-tuple-element.239) | copy-start | bytes 9220
  9.0 454.1 %copy-start.145 = (f32[768]{0:T(1024)}, f32[768]{0:T(1024)S(1)}, u32[]{:S(2)}) copy-start(f32[768]{0:T(1024)S(1)} %get-tuple-element.240) | copy-start | bytes 9220
  9.0 536.2 %copy-start.26 = (f32[768]{0:T(1024)}, f32[768]{0:T(1024)S(1)}, u32[]{:S(2)}) copy-start(f32[768]{0:T(1024)S(1)} %get-tuple-element.238) | copy-start | bytes 9220
  12.6 532.7 %copy-start.154 = (pred[240]{0:T(512)(128)(4,1)}, pred[240]{0:T(512)(128)(4,1)S(1)}, u32[]{:S(2)}) copy-start(pred[240]{0:T(512)(128)(4,1)S(1)} %dynamic_slice.36) | copy-start | bytes 724
  17.1 116.5 %reduce-scatter.24.cloned.1.call-start = ((), (), s32[]{:S(2)}) async-start(), calls=%async_computation.20 | async-start | bytes 1843200 | tf_op jit(solution)/shard_map/reduce_scatter | solution.py:139
  89.7 421.2 %copy-start.4 = (bf16[192,768]{0,1:T(8,128)(2,1)}, bf16[192,768]{0,1:T(8,128)(2,1)S(1)}, u32[]{:S(2)}) copy-start(bf16[192,768]{0,1:T(8,128)(2,1)S(1)} %all_gather.62) | copy-start | bytes 884740
  106.9 50.0 %all-gather.31.cloned.1.call-start = ((), (), s32[]{:S(2)}) async-start(), calls=%async_computation.29 | async-start | bytes 1843200 | tf_op jit(solution)/shard_map/all_gather | solution.py:120
  107.4 437.9 %copy-start.151 = (pred[240]{0:T(512)(128)(4,1)}, pred[240]{0:T(512)(128)(4,1)S(1)}, u32[]{:S(2)}) copy-start(pred[240]{0:T(512)(128)(4,1)S(1)} %dynamic_slice.40) | copy-start | bytes 724
  107.8 434.6 %copy-start.149 = (pred[240]{0:T(512)(128)(4,1)}, pred[240]{0:T(512)(128)(4,1)S(1)}, u32[]{:S(2)}) copy-start(pred[240]{0:T(512)(128)(4,1)S(1)} %dynamic_slice.42) | copy-start | bytes 724
  137.6 45.1 %all-gather.35.cloned.1.call-start = ((), (), s32[]{:S(2)}) async-start(), calls=%async_computation.33 | async-start | bytes 1843200 | tf_op jit(solution)/shard_map/all_gather | solution.py:120
  140.5 73.0 %reduce-scatter.32.cloned.1.call-start = ((), (), s32[]{:S(2)}) async-start(), calls=%async_computation.30 | async-start | bytes 1843200 | tf_op jit(solution)/shard_map/reduce_scatter | solution.py:139
  182.5 58.3 %reduce-scatter.36.cloned.1.call-start = ((), (), s32[]{:S(2)}) async-start(), calls=%async_computation.34 | async-start | bytes 1843200 | tf_op jit(solution)/shard_map/reduce_scatter | solution.py:139
  208.8 53.4 %all-gather.51.cloned.1.call-start = ((), (), s32[]{:S(2)}) async-start(), calls=%async_computation.49 | async-start | bytes 1843200 | tf_op jit(solution)/shard_map/all_gather | solution.py:184
  213.5 70.2 %all-gather.37.cloned.1.call-start = ((), (), s32[]{:S(2)}) async-start(), calls=%async_computation.35 | async-start | bytes 1843200 | tf_op jit(solution)/shard_map/all_gather | solution.py:149
  244.9 93.7 %all-gather.23.cloned.1.call-start = ((), (), s32[]{:S(2)}) async-start(), calls=%async_computation.22 | async-start | bytes 2654208 | tf_op jit(solution)/shard_map/all_gather | solution.py:90
  246.8 145.4 %all-gather.25.cloned.1.call-start = ((), (), s32[]{:S(2)}) async-start(), calls=%async_computation.23 | async-start | bytes 2654208 | tf_op jit(solution)/shard_map/all_gather | solution.py:91
  247.6 185.0 %reduce-scatter.52.cloned.1.call-start = ((), (), s32[]{:S(2)}) async-start(), calls=%async_computation.50 | async-start | bytes 1843200 | tf_op jit(solution)/shard_map/reduce_scatter | solution.py:225
  406.3 56.8 %reduce-scatter.38.cloned.1.call-start = ((), (), s32[]{:S(2)}) async-start(), calls=%async_computation.36 | async-start | bytes 1843200 | tf_op jit(solution)/shard_map/reduce_scatter | solution.py:175
  416.2 71.1 %all-gather.27.cloned.1.call-start = ((), (), s32[]{:S(2)}) async-start(), calls=%async_computation.25 | async-start | bytes 1843200 | tf_op jit(solution)/shard_map/all_gather | solution.py:120
  417.0 128.3 %copy-start.178 = (f32[240]{0:T(256)}, f32[240]{0:T(256)S(1)}, u32[]{:S(2)}) copy-start(f32[240]{0:T(256)S(1)} %broadcast_multiply_fusion.2) | copy-start | bytes 2884
  468.0 73.0 %reduce-scatter.28.cloned.1.call-start = ((), (), s32[]{:S(2)}) async-start(), calls=%async_computation.26 | async-start | bytes 1843200 | tf_op jit(solution)/shard_map/reduce_scatter | solution.py:139
  513.4 53.1 %all-gather.47.cloned.1.call-start = ((), (), s32[]{:S(2)}) async-start(), calls=%async_computation.45 | async-start | bytes 1843200 | tf_op jit(solution)/shard_map/all_gather | solution.py:184
  513.9 68.2 %all-gather.39.cloned.1.call-start = ((), (), s32[]{:S(2)}) async-start(), calls=%async_computation.37 | async-start | bytes 1843200 | tf_op jit(solution)/shard_map/all_gather | solution.py:184
  514.5 88.2 %all-gather.43.cloned.1.call-start = ((), (), s32[]{:S(2)}) async-start(), calls=%async_computation.41 | async-start | bytes 1843200 | tf_op jit(solution)/shard_map/all_gather | solution.py:184
  515.1 108.7 %all-gather.33.cloned.1.call-start = ((), (), s32[]{:S(2)}) async-start(), calls=%async_computation.31 | async-start | bytes 1843200 | tf_op jit(solution)/shard_map/all_gather | solution.py:149
  547.1 104.1 %all-gather.21.cloned.1.call-start = ((), (), s32[]{:S(2)}) async-start(), calls=%async_computation.21 | async-start | bytes 1843200 | tf_op jit(solution)/shard_map/all_gather | solution.py:149
  555.4 122.9 %all-gather.29.cloned.1.call-start = ((), (), s32[]{:S(2)}) async-start(), calls=%async_computation.27 | async-start | bytes 1843200 | tf_op jit(solution)/shard_map/all_gather | solution.py:149
  609.8 125.9 %reduce-scatter.48.cloned.1.call-start = ((), (), s32[]{:S(2)}) async-start(), calls=%async_computation.46 | async-start | bytes 1843200 | tf_op jit(solution)/shard_map/reduce_scatter | solution.py:225
  650.7 85.0 %reduce-scatter.40.cloned.1.call-start = ((), (), s32[]{:S(2)}) async-start(), calls=%async_computation.38 | async-start | bytes 1843200 | tf_op jit(solution)/shard_map/reduce_scatter | solution.py:225
  678.1 78.2 %reduce-scatter.44.cloned.1.call-start = ((), (), s32[]{:S(2)}) async-start(), calls=%async_computation.42 | async-start | bytes 1843200 | tf_op jit(solution)/shard_map/reduce_scatter | solution.py:225
  705.2 81.3 %reduce-scatter.26.cloned.1.call-start = ((), (), s32[]{:S(2)}) async-start(), calls=%async_computation.24 | async-start | bytes 1843200 | tf_op jit(solution)/shard_map/reduce_scatter | solution.py:175
  715.3 101.3 %reduce-scatter.30.cloned.1.call-start = ((), (), s32[]{:S(2)}) async-start(), calls=%async_computation.28 | async-start | bytes 1843200 | tf_op jit(solution)/shard_map/reduce_scatter | solution.py:175
  725.0 121.7 %reduce-scatter.34.cloned.1.call-start = ((), (), s32[]{:S(2)}) async-start(), calls=%async_computation.32 | async-start | bytes 1843200 | tf_op jit(solution)/shard_map/reduce_scatter | solution.py:175
  735.0 141.3 %all-gather.53.cloned.1.call-start = ((), (), s32[]{:S(2)}) async-start(), calls=%async_computation.51 | async-start | bytes 1843200 | tf_op jit(solution)/shard_map/all_gather | solution.py:235
  735.6 188.1 %all-gather.41.cloned.1.call-start = ((), (), s32[]{:S(2)}) async-start(), calls=%async_computation.39 | async-start | bytes 1843200 | tf_op jit(solution)/shard_map/all_gather | solution.py:235
  792.5 133.9 %all-gather.45.cloned.1.call-start = ((), (), s32[]{:S(2)}) async-start(), calls=%async_computation.43 | async-start | bytes 1843200 | tf_op jit(solution)/shard_map/all_gather | solution.py:235
  822.6 107.2 %all-gather.49.cloned.1.call-start = ((), (), s32[]{:S(2)}) async-start(), calls=%async_computation.47 | async-start | bytes 1843200 | tf_op jit(solution)/shard_map/all_gather | solution.py:235
  852.8 320.3 %all-reduce.12.cloned.1.call-start = ((), (), s32[]{:S(2)}) async-start(), calls=%async_computation.56 | async-start | bytes 9437184
  875.6 301.9 %reduce-scatter.60.cloned.1.call-start = ((), (), s32[]{:S(2)}) async-start(), calls=%async_computation.55 | async-start | bytes 884736
  933.6 263.6 %reduce-scatter.54.cloned.1.call-start = ((), (), s32[]{:S(2)}) async-start(), calls=%async_computation.52 | async-start | bytes 1843200 | tf_op jit(solution)/shard_map/reduce_scatter | solution.py:275
  944.6 282.7 %reduce-scatter.46.cloned.1.call-start = ((), (), s32[]{:S(2)}) async-start(), calls=%async_computation.44 | async-start | bytes 1843200 | tf_op jit(solution)/shard_map/reduce_scatter | solution.py:275
  998.7 259.0 %reduce-scatter.42.cloned.1.call-start = ((), (), s32[]{:S(2)}) async-start(), calls=%async_computation.40 | async-start | bytes 1843200 | tf_op jit(solution)/shard_map/reduce_scatter | solution.py:275
  1053.1 234.6 %reduce-scatter.50.cloned.1.call-start = ((), (), s32[]{:S(2)}) async-start(), calls=%async_computation.48 | async-start | bytes 1843200 | tf_op jit(solution)/shard_map/reduce_scatter | solution.py:275
  1105.5 253.1 %reduce-scatter.58.cloned.1.call-start = ((), (), s32[]{:S(2)}) async-start(), calls=%async_computation.54 | async-start | bytes 2211840
  1120.5 336.3 %reduce-scatter.56.cloned.1.call-start = ((), (), s32[]{:S(2)}) async-start(), calls=%async_computation.53 | async-start | bytes 5308416 | tf_op jit(solution)/shard_map/reduce_scatter | solution.py:303
  (285 other events, 6474.7 us)
Sparse Core Ops, SparseCore 0:
  17.2 21.7 all-gather.18
  107.0 26.5 reduce-scatter.23
  137.7 19.1 all-gather.30
  159.0 19.1 all-gather.34
  182.6 27.5 reduce-scatter.31
  213.3 27.5 reduce-scatter.35
  243.1 19.1 all-gather.50
  264.4 19.1 all-gather.36
  286.6 51.9 all-gather.22
  341.4 50.6 all-gather.24
  406.5 26.0 reduce-scatter.51
  435.6 27.5 reduce-scatter.37
  468.1 19.0 all-gather.26
  513.5 27.5 reduce-scatter.27
  542.5 19.1 all-gather.46
  563.0 19.1 all-gather.38
  583.6 19.0 all-gather.42
  604.7 19.0 all-gather.32
  625.4 19.0 all-gather.20
  645.9 19.0 all-gather.28
  668.2 27.5 reduce-scatter.47
  698.6 27.5 reduce-scatter.39
  728.7 27.5 reduce-scatter.43
  758.9 27.5 reduce-scatter.25
  789.0 27.5 reduce-scatter.29
  819.2 27.5 reduce-scatter.33
  848.7 19.1 all-gather.52
  869.4 19.0 all-gather.40
  890.1 19.1 all-gather.44
  910.7 19.0 all-gather.48
  933.5 169.6 all-reduce.11
  1106.5 61.5 reduce-scatter.59
  1170.7 26.4 reduce-scatter.53
  1199.8 27.5 reduce-scatter.45
  1230.1 27.5 reduce-scatter.41
  1260.1 27.5 reduce-scatter.49
  1291.5 67.0 reduce-scatter.57
  1362.2 94.5 reduce-scatter.55
where the time goes:
time: 1480 us; the launch traced here: 1470 us
  waiting for transfers between devices  625 us (42%)
  matrix products  389 us (26%)
  local copies, waits for them, and re-layouts  186 us (13%)
  other arithmetic  126 us (9%)
  blocking collectives  111 us (8%)
  between operations  23 us (2%)
    reduce_scatter x4, waiting for transfers between devices, body(): lax.psum_scatter(jnp.einsum('ktc,kdc->td', grad_joint_rows, joint_all, pr...  109 us
    reduce_scatter x4, waiting for transfers between devices, body(): lax.psum_scatter(dropped[sorted_place].astype(jnp.bfloat16), 'mp', scatte...  104 us
    reduce_scatter x1, waiting for transfers between devices, body(): lax.psum_scatter(micro_grads[2], 'dp', scatter_dimension=1, tiled=True)  93.2 us
    reduce_scatter x4, waiting for transfers between devices, body(): lax.psum_scatter(jnp.dot(mixed_rows, output_all, preferred_element_type=j...  78.7 us
    dot_general x4, matrix products, body(): jnp.einsum('hqk,khe->qhe', grad_raw, head_rows[1], preferred_element_type...  77.8 us
    dot_general x4, matrix products, body(): jnp.einsum('hqk,qhe->khe', grad_raw, head_rows[0], preferred_element_type...  70.8 us
    all_gather x1, waiting for transfers between devices, body(): lax.all_gather(lift_weight.astype(jnp.bfloat16), 'dp', axis=1, tiled=True)  48.8 us
    all_gather x1, waiting for transfers between devices, body(): lax.all_gather(drop_weight.astype(jnp.bfloat16), 'dp', axis=2, tiled=True)  41.8 us
  transfers between devices with their start and end apart: 38, of which 25 were waited for; matrix products, arithmetic and copies ran while one was open for 42% of the time, Pallas kernels for 0%

commit v1 on v0

v1 whole, which is shorter than its diff:
```python
import functools

import jax
import jax.numpy as jnp
from jax import lax
from jax.experimental import pallas as pl
from jax.experimental.pallas import tpu as pltpu
from jax.sharding import PartitionSpec as P

HEAD_DIM = 64
PATCHES = 197
TEXT_MAX = 40
STEP = 7

norm_epsilon = 1e-06
masked_score = -1000000000.0
first_decay = 0.9
second_decay = 0.98
adam_epsilon = 1e-06
matrix_rate = 0.04
vector_rate = 0.5
weight_decay = 0.01

PATCH_STRIDE = 208
TEXT_STRIDE = 48
ITEM_ROWS = PATCH_STRIDE + TEXT_STRIDE

bf16 = jnp.bfloat16
f32 = jnp.float32
VMEM_LIMIT = 58 * 1024 * 1024


def adamw(weight, first_state, second_state, gradient, step_rate, decay_rate):
    first_new = first_decay * first_state + (1.0 - first_decay) * gradient
    second_new = second_decay * second_state + (1.0 - second_decay) * gradient * gradient
    first_hat = first_new / (1.0 - first_decay**STEP)
    second_hat = second_new / (1.0 - second_decay**STEP)
    weight_new = weight - step_rate * (
        first_hat / (jnp.sqrt(second_hat) + adam_epsilon) + decay_rate * weight
    )
    return (weight_new, first_new, second_new, weight_new.astype(bf16))


def dot(left, right, left_dim, right_dim):
    return lax.dot_general(
        left,
        right,
        (((left_dim,), (right_dim,)), ((), ())),
        preferred_element_type=f32,
    )


def loop(count, body):
    lax.fori_loop(0, count, lambda i, c: (body(i), c)[1], 0)


def rows_at(index, size):
    return pl.ds(pl.multiple_of(index * size, 16), size)


def norm_forward(values, gain, shift):
    centred = values - jnp.mean(values, axis=-1, keepdims=True)
    spread = jnp.mean(centred * centred, axis=-1, keepdims=True)
    return centred * lax.rsqrt(spread + norm_epsilon) * gain + shift


def norm_backward(values, gain, grad):
    centred = values - jnp.mean(values, axis=-1, keepdims=True)
    spread = jnp.mean(centred * centred, axis=-1, keepdims=True)
    scale = lax.rsqrt(spread + norm_epsilon)
    hat = centred * scale
    grad_hat = grad * gain
    grad_values = scale * (
        grad_hat
        - jnp.mean(grad_hat, axis=-1, keepdims=True)
        - hat * jnp.mean(grad_hat * hat, axis=-1, keepdims=True)
    )
    grad_gain = jnp.sum(grad * hat, axis=0, keepdims=True)
    grad_shift = jnp.sum(grad, axis=0, keepdims=True)
    return grad_values, grad_gain, grad_shift


def one_hot(row_place, first_row, count):
    place = lax.broadcasted_iota(jnp.int32, (count, row_place.shape[1]), 0) + first_row
    return (place == row_place).astype(bf16)


def attend(query, key, value, allowed):
    scores = dot(query, key, 1, 1)
    scores = jnp.where(allowed, scores, masked_score)
    top = jnp.max(scores, axis=-1, keepdims=True)
    weights = jnp.exp(scores - top)
    total = jnp.sum(weights, axis=-1, keepdims=True)
    weights = (weights * (1.0 / total)).astype(bf16)
    return weights, dot(weights, value, 1, 0)


def attention_kernel(
    meta_ref,
    raw_ref,
    place_ref,
    hidden_ref,
    valid_ref,
    norm_ref,
    extra_ref,
    weight_ref,
    block_ref,
    normed_ref,
    joint_ref,
    mixed_ref,
    probs_ref,
    residual_ref,
    feed_ref,
    square_ref,
    *,
    items,
    heads,
    main_rows,
    all_rows,
):
    step = pl.program_id(0)
    width = heads * HEAD_DIM
    tail_rows = all_rows - main_rows

    @pl.when(step == 0)
    def _():
        def chunk(first, size):
            rows = pl.ds(first, size)
            picked = dot(one_hot(place_ref[...], first, size), raw_ref[...], 1, 0)
            picked = jnp.where(hidden_ref[rows, :] > 0, extra_ref[2:3, :], picked)
            block_ref[rows, :] = picked
            residual_ref[rows, :] = picked
            normed_ref[rows, :] = norm_forward(picked, norm_ref[0:1, :], norm_ref[1:2, :]).astype(bf16)

        loop(items, lambda i: chunk(pl.multiple_of(i * ITEM_ROWS, 16), ITEM_ROWS))
        chunk(main_rows, tail_rows)

    def project(rows):
        joint = dot(normed_ref[rows, :], weight_ref[0, :, : 3 * width], 1, 0)
        joint_ref[0, rows, :width] = (joint[:, :width].astype(bf16).astype(f32) * HEAD_DIM**-0.5).astype(bf16)
        joint_ref[0, rows, width:] = joint[:, width:].astype(bf16)

    loop(items, lambda i: project(rows_at(i, ITEM_ROWS)))
    project(pl.ds(main_rows, tail_rows))

    column = lax.broadcasted_iota(jnp.int32, (1, ITEM_ROWS), 1)

    def one_item(i):
        patch_rows = rows_at(i, PATCH_STRIDE)
        text_rows = pl.ds(pl.multiple_of(items * PATCH_STRIDE + i * TEXT_STRIDE, 16), TEXT_STRIDE)
        joint = jnp.concatenate([joint_ref[0, patch_rows, :], joint_ref[0, text_rows, :]], axis=0)
        allowed = (column < PATCHES) | (
            (column >= PATCH_STRIDE) & (column < PATCH_STRIDE + meta_ref[i])
        )
        outs = []
        for h in range(heads):
            part = lambda k: joint[:, k * width + h * HEAD_DIM : k * width + (h + 1) * HEAD_DIM]
            weights, out = attend(part(0), part(1), part(2), allowed)
            probs_ref[0, i, h] = weights
            outs.append(out.astype(bf16))
        mixed = jnp.concatenate(outs, axis=1)
        mixed_ref[0, patch_rows, :] = mixed[:PATCH_STRIDE]
        mixed_ref[0, text_rows, :] = mixed[PATCH_STRIDE:]

    loop(items, one_item)

    joint = joint_ref[0, main_rows:, :]
    allowed = lax.broadcasted_iota(jnp.int32, (1, tail_rows), 1) < meta_ref[items]
    outs = []
    for h in range(heads):
        part = lambda k: joint[:, k * width + h * HEAD_DIM : k * width + (h + 1) * HEAD_DIM]
        outs.append(attend(part(0), part(1), part(2), allowed)[1].astype(bf16))
    mixed_ref[0, main_rows:, :] = jnp.concatenate(outs, axis=1)

    def add_output(rows):
        residual_ref[rows, :] += dot(mixed_ref[0, rows, :], weight_ref[0, :, 3 * width :], 1, 1)

    loop(items, lambda i: add_output(rows_at(i, ITEM_ROWS)))
    add_output(pl.ds(main_rows, tail_rows))

    @pl.when(step == pl.num_programs(0) - 1)
    def _():
        square_ref[...] = jnp.zeros_like(square_ref)

        def chunk(rows):
            residual = residual_ref[rows, :]
            feed_ref[rows, :] = norm_forward(residual, norm_ref[2:3, :], norm_ref[3:4, :]).astype(bf16)
            attended = (residual - block_ref[rows, :]) * valid_ref[rows, :]
            square_ref[...] += jnp.sum(attended * attended, axis=0, keepdims=True)

        loop(items, lambda i: chunk(rows_at(i, ITEM_ROWS)))
        chunk(pl.ds(main_rows, tail_rows))


def attention_back_kernel(
    grad_attended_ref,
    grad_residual_ref,
    joint_ref,
    mixed_ref,
    probs_ref,
    normed_ref,
    block_ref,
    hidden_ref,
    place_ref,
    norm_ref,
    weight_ref,
    grad_weight_ref,
    grad_raw_ref,
    grad_norm_ref,
    grad_mask_ref,
    grad_normed_ref,
    grad_mixed_ref,
    grad_joint_ref,
    *,
    items,
    heads,
    main_rows,
):
    step = pl.program_id(0)
    width = heads * HEAD_DIM
    half = HEAD_DIM**-0.5

    @pl.when(step == 0)
    def _():
        grad_normed_ref[...] = jnp.zeros_like(grad_normed_ref)

    def mixed_grad(i):
        rows = rows_at(i, ITEM_ROWS)
        grad_mixed_ref[rows, :] = dot(
            grad_attended_ref[rows, :], weight_ref[0, :, 3 * width :], 1, 0
        ).astype(bf16)

    loop(items, mixed_grad)

    def one_item(i):
        patch_rows = rows_at(i, PATCH_STRIDE)
        text_rows = pl.ds(pl.multiple_of(items * PATCH_STRIDE + i * TEXT_STRIDE, 16), TEXT_STRIDE)
        joint = jnp.concatenate([joint_ref[0, patch_rows, :], joint_ref[0, text_rows, :]], axis=0)
        mixed = jnp.concatenate([mixed_ref[0, patch_rows, :], mixed_ref[0, text_rows, :]], axis=0)
        grad_mixed = jnp.concatenate([grad_mixed_ref[patch_rows, :], grad_mixed_ref[text_rows, :]], axis=0)
        grads = [[], [], []]
        for h in range(heads):
            part = lambda k: joint[:, k * width + h * HEAD_DIM : k * width + (h + 1) * HEAD_DIM]
            span = slice(h * HEAD_DIM, (h + 1) * HEAD_DIM)
            grad_out = grad_mixed[:, span]
            weights = probs_ref[0, i, h]
            grad_probs = dot(grad_out, part(2), 1, 1)
            mean_grad = jnp.sum(
                grad_out.astype(f32) * mixed[:, span].astype(f32), axis=-1, keepdims=True
            )
            grad_scores = (weights.astype(f32) * (grad_probs - mean_grad)).astype(bf16)
            grads[0].append((dot(grad_scores, part(1), 1, 0) * half).astype(bf16))
            grads[1].append(dot(grad_scores, part(0), 0, 0).astype(bf16))
            grads[2].append(dot(weights, grad_out, 0, 0).astype(bf16))
        grad_joint = jnp.concatenate(grads[0] + grads[1] + grads[2], axis=1)
        grad_joint_ref[patch_rows, :] = grad_joint[:PATCH_STRIDE]
        grad_joint_ref[text_rows, :] = grad_joint[PATCH_STRIDE:]

    loop(items, one_item)

    model_width = weight_ref.shape[1]
    for first in range(0, model_width, 256):
        cols = slice(first, first + 256)
        grad_weight_ref[0, cols, : 3 * width] = dot(
            normed_ref[:, cols], grad_joint_ref[...], 0, 0
        ).astype(bf16)
        grad_weight_ref[0, cols, 3 * width :] = dot(
            grad_attended_ref[:, cols], mixed_ref[0], 0, 0
        ).astype(bf16)

    def normed_grad(i):
        rows = rows_at(i, ITEM_ROWS)
        grad_normed_ref[rows, :] += dot(grad_joint_ref[rows, :], weight_ref[0, :, : 3 * width], 1, 1)

    loop(items, normed_grad)

    @pl.when(step == pl.num_programs(0) - 1)
    def _():
        grad_norm_ref[...] = jnp.zeros_like(grad_norm_ref)
        grad_mask_ref[...] = jnp.zeros_like(grad_mask_ref)

        def chunk(i):
            rows = rows_at(i, ITEM_ROWS)
            grad, gain, shift = norm_backward(block_ref[rows, :], norm_ref[0:1, :], grad_normed_ref[rows, :])
            grad_norm_ref[0:1, :] += gain
            grad_norm_ref[1:2, :] += shift
            grad = grad + grad_residual_ref[rows, :]
            hidden = hidden_ref[rows, :] > 0
            grad_mask_ref[...] += jnp.sum(jnp.where(hidden, grad, 0.0), axis=0, keepdims=True)
            grad_normed_ref[rows, :] = jnp.where(hidden, 0.0, grad)

        loop(items, chunk)
        unplace(place_ref, grad_normed_ref, grad_raw_ref, main_rows)


def unplace(place_ref, source_ref, raw_ref, source_rows):
    source = source_ref[...].astype(bf16)
    raw_rows = raw_ref.shape[0]
    size = 240 if raw_rows % 240 == 0 else raw_rows

    def chunk(i):
        rows = rows_at(i, size)
        place = lax.broadcasted_iota(jnp.int32, (size, source_rows), 1)
        pick = (place == place_ref[rows, :]).astype(bf16)
        raw_ref[rows, :] = dot(pick, source, 1, 0).astype(bf16)

    loop(raw_rows // size, chunk)


def lift_kernel(feed_ref, weight_ref, acted_ref, slope_ref, *, vision_rows, all_rows):
    def piece(rows, expert):
        lifted = dot(feed_ref[rows, :], weight_ref[expert, 0], 1, 0)
        cumulative = 0.5 * (1.0 + lax.erf(lifted * (0.5**0.5)))
        density = jnp.exp(-0.5 * lifted * lifted) * ((2.0 * jnp.pi) ** -0.5)
        acted_ref[0, rows, :] = (lifted * cumulative).astype(bf16)
        slope_ref[0, rows, :] = (cumulative + lifted * density).astype(bf16)

    loop(vision_rows // PATCH_STRIDE, lambda i: piece(rows_at(i, PATCH_STRIDE), 0))
    text = all_rows - vision_rows
    loop(3, lambda i: piece(pl.ds(pl.multiple_of(vision_rows + i * (text // 3), 16), text // 3), 1))


def drop_weight_kernel(
    raw_ref, place_ref, acted_ref, grad_ref, grad_bias_ref, grad_weight_ref, *, vision_rows, main_rows
):
    @pl.when(pl.program_id(0) == 0)
    def _():
        def chunk(i):
            rows = rows_at(i, ITEM_ROWS)
            grad_ref[rows, :] = dot(
                one_hot(place_ref[...], i * ITEM_ROWS, ITEM_ROWS), raw_ref[...], 1, 0
            ).astype(bf16)

        loop(main_rows // ITEM_ROWS, chunk)
        grad_bias_ref[0:1, :] = jnp.sum(
            grad_ref[:vision_rows, :].astype(f32), axis=0, keepdims=True
        )
        grad_bias_ref[1:2, :] = jnp.sum(
            grad_ref[vision_rows:, :].astype(f32), axis=0, keepdims=True
        )

    for expert, rows in ((0, slice(0, vision_rows)), (1, slice(vision_rows, main_rows))):
        for first in range(0, grad_ref.shape[1], 256):
            cols = slice(first, first + 256)
            grad_weight_ref[expert, 0, cols, :] = dot(
                grad_ref[rows, cols], acted_ref[0, rows, :], 0, 0
            ).astype(bf16)


def drop_kernel(
    acted_ref,
    residual_ref,
    valid_ref,
    place_ref,
    extra_ref,
    weight_ref,
    raw_ref,
    square_ref,
    total_ref,
    *,
    vision_rows,
    all_rows,
):
    step = pl.program_id(0)
    text = all_rows - vision_rows

    @pl.when(step == 0)
    def _():
        total_ref[:vision_rows, :] = jnp.broadcast_to(extra_ref[0:1, :], (vision_rows, total_ref.shape[1]))
        total_ref[vision_rows:, :] = jnp.broadcast_to(extra_ref[1:2, :], (text, total_ref.shape[1]))

    def piece(rows, expert):
        total_ref[rows, :] += dot(acted_ref[0, rows, :], weight_ref[expert, 0], 1, 1)

    def everything(body):
        loop(vision_rows // PATCH_STRIDE, lambda i: body(rows_at(i, PATCH_STRIDE), 0))
        loop(3, lambda i: body(pl.ds(pl.multiple_of(vision_rows + i * (text // 3), 16), text // 3), 1))

    everything(piece)

    @pl.when(step == pl.num_programs(0) - 1)
    def _():
        square_ref[...] = jnp.zeros_like(square_ref)

        def finish(rows, expert):
            fed = total_ref[rows, :]
            out = residual_ref[rows, :] + fed
            valid = valid_ref[rows, :]
            square_ref[0:1, :] += jnp.sum(valid * out * out, axis=0, keepdims=True)
            square_ref[1:2, :] += jnp.sum(valid * fed * fed, axis=0, keepdims=True)
            total_ref[rows, :] = out

        everything(finish)
        unplace(place_ref, total_ref, raw_ref, all_rows)


def expert_back_kernel(
    grad_ref,
    slope_ref,
    feed_ref,
    residual_ref,
    norm_ref,
    drop_ref,
    lift_ref,
    grad_weight_ref,
    grad_residual_ref,
    grad_attended_ref,
    grad_norm_ref,
    grad_lifted_ref,
    *,
    vision_rows,
    main_rows,
):
    step = pl.program_id(0)

    @pl.when(step == 0)
    def _():
        grad_residual_ref[...] = jnp.zeros_like(grad_residual_ref)

    def piece(rows, expert):
        grad_acted = dot(grad_ref[rows, :], drop_ref[expert, 0], 1, 0)
        grad_lifted = (grad_acted * slope_ref[0, rows, :].astype(f32)).astype(bf16)
        grad_lifted_ref[rows, :] = grad_lifted
        grad_residual_ref[rows, :] += dot(grad_lifted, lift_ref[expert, 0], 1, 1)

    loop(vision_rows // PATCH_STRIDE, lambda i: piece(rows_at(i, PATCH_STRIDE), 0))
    piece(pl.ds(vision_rows, main_rows - vision_rows), 1)

    for expert, rows in ((0, slice(0, vision_rows)), (1, slice(vision_rows, main_rows))):
        for first in range(0, feed_ref.shape[1], 256):
            cols = slice(first, first + 256)
            grad_weight_ref[expert, 0, cols, :] = dot(
                feed_ref[rows, cols], grad_lifted_ref[rows, :], 0, 0
            ).astype(bf16)

    @pl.when(step == pl.num_programs(0) - 1)
    def _():
        grad_norm_ref[...] = jnp.zeros_like(grad_norm_ref)

        def chunk(i):
            rows = rows_at(i, ITEM_ROWS)
            grad, gain, shift = norm_backward(
                residual_ref[rows, :], norm_ref[2:3, :], grad_residual_ref[rows, :]
            )
            grad_norm_ref[0:1, :] += gain
            grad_norm_ref[1:2, :] += shift
            grad = grad + grad_ref[rows, :].astype(f32)
            grad_residual_ref[rows, :] = grad
            grad_attended_ref[rows, :] = grad.astype(bf16)

        loop(main_rows // ITEM_ROWS, chunk)


def whole(*shape):
    return pl.BlockSpec(shape, lambda *_: (0,) * len(shape))


def stepped(*shape):
    return pl.BlockSpec(shape, lambda i, *_: (i,) + (0,) * (len(shape) - 1))


def stepped_pair(*shape):
    return pl.BlockSpec(shape, lambda i, *_: (0, i) + (0,) * (len(shape) - 2))


def call(kernel, name, steps, in_specs, out_specs, out_shapes, scratch, flops, moved, args, scalars=0):
    return pl.pallas_call(
        kernel,
        name=name,
        grid_spec=pltpu.PrefetchScalarGridSpec(
            num_scalar_prefetch=scalars,
            grid=(steps,),
            in_specs=in_specs,
            out_specs=out_specs,
            scratch_shapes=scratch,
        ),
        out_shape=[jax.ShapeDtypeStruct(s, d) for s, d in out_shapes],
        compiler_params=pltpu.CompilerParams(
            dimension_semantics=("arbitrary",), vmem_limit_bytes=VMEM_LIMIT
        ),
        cost_estimate=pl.CostEstimate(flops=flops, bytes_accessed=moved, transcendentals=0),
    )(*args)


def body(
    tokens,
    cotangent,
    text_lengths,
    modality,
    masked_positions,
    joint_weight,
    joint_first,
    joint_second,
    output_weight,
    output_first,
    output_second,
    lift_weight,
    lift_first,
    lift_second,
    drop_weight,
    drop_first,
    drop_second,
    norm_params,
    norm_first,
    norm_second,
    extra_params,
    extra_first,
    extra_second,
):
    micro_count, shard_rows, model_width = tokens.shape
    block_rows = modality.shape[1]
    parts = block_rows // shard_rows
    assert micro_count == parts
    items = text_lengths.shape[1]
    width = joint_weight.shape[2]
    heads = width // HEAD_DIM
    hidden_width = lift_weight.shape[2]
    shard = joint_weight.shape[1]
    vision_rows = items * PATCH_STRIDE
    main_rows = items * ITEM_ROWS
    tail = block_rows - items * PATCHES - TEXT_MAX - (items - 1)
    tail = (tail + 47) // 48 * 48
    all_rows = main_rows + tail
    assert 4 * width == model_width and hidden_width == model_width

    shard_attend = jnp.concatenate(
        [joint_weight[0], joint_weight[1], joint_weight[2], output_weight.T], axis=1
    ).astype(bf16)
    shard_lift = lift_weight.astype(bf16)
    shard_drop = jnp.swapaxes(drop_weight, 1, 2).astype(bf16)

    def gather(values, axis):
        return lax.all_gather(values, ("mp", "dp"), axis=axis, tiled=True)

    def scatter(values, axis):
        return lax.psum_scatter(values, ("mp", "dp"), scatter_dimension=axis, tiled=True)

    def exchange(values):
        return lax.all_to_all(values, "mp", split_axis=0, concat_axis=1, tiled=True)[0]

    def give_back(values):
        return lax.all_to_all(
            values.reshape(parts, shard_rows, model_width), "mp", split_axis=0, concat_axis=0, tiled=True
        )

    raw_tokens = exchange(tokens)
    attend_all = gather(shard_attend, 0).reshape(parts, model_width, model_width)
    raw_grad = exchange(cotangent.astype(bf16))
    lift_all = gather(shard_lift, 1).reshape(2, parts, model_width, hidden_width)
    drop_all = gather(shard_drop, 1).reshape(2, parts, model_width, hidden_width)

    micro = lax.axis_index("mp")
    lengths = lax.dynamic_index_in_dim(text_lengths, micro, 0, keepdims=False)
    masked = lax.dynamic_index_in_dim(masked_positions, micro, 0, keepdims=False)
    item_ids = jnp.arange(items, dtype=jnp.int32)
    sizes = PATCHES + lengths
    ends = jnp.sum(jnp.where(item_ids[:, None] <= item_ids[None, :], sizes[:, None], 0), axis=0)
    used = jnp.sum(sizes)

    def place_of(row):
        segment = jnp.sum((row[..., None] >= ends).astype(jnp.int32), axis=-1)
        start = jnp.sum(jnp.where(row[..., None] >= ends, sizes, 0), axis=-1)
        inside = row - start
        return jnp.where(
            segment == items,
            main_rows + inside,
            jnp.where(
                inside < PATCHES,
                PATCH_STRIDE * segment + inside,
                vision_rows + TEXT_STRIDE * segment + inside - PATCHES,
            ),
        )

    place_row = place_of(jnp.arange(block_rows, dtype=jnp.int32))[None, :]
    place_column = place_of(jnp.arange(block_rows, dtype=jnp.int32))[:, None]
    targets = (vision_rows + TEXT_STRIDE * item_ids[:, None] + masked).reshape(-1)
    spots = jnp.arange(all_rows, dtype=jnp.int32)
    hidden = jnp.any(spots[:, None] == targets[None, :], axis=1).astype(jnp.int32)[:, None]
    text_spot = spots - vision_rows
    text_item = text_spot // TEXT_STRIDE
    text_end = jnp.sum(jnp.where(text_item[:, None] == item_ids, lengths, 0), axis=1)
    valid = jnp.where(
        text_spot < 0, spots % PATCH_STRIDE < PATCHES, text_spot - text_item * TEXT_STRIDE < text_end
    )
    valid = valid.astype(f32)[:, None]
    meta = jnp.concatenate([lengths, (block_rows - used)[None]])

    square = model_width * model_width
    block_input, normed, joint_rows, mixed, probs, residual, feed_input, attended_square = call(
        functools.partial(
            attention_kernel, items=items, heads=heads, main_rows=main_rows, all_rows=all_rows
        ),
        "attention",
        parts,
        [
            whole(block_rows, model_width),
            whole(1, block_rows),
            whole(all_rows, 1),
            whole(all_rows, 1),
            whole(4, model_width),
            whole(3, model_width),
            stepped(1, model_width, model_width),
        ],
        [
            whole(all_rows, model_width),
            whole(all_rows, model_width),
            stepped(1, all_rows, 3 * width),
            stepped(1, all_rows, width),
            stepped(1, items, heads, ITEM_ROWS, ITEM_ROWS),
            whole(all_rows, model_width),
            whole(all_rows, model_width),
            whole(1, model_width),
        ],
        [
            ((all_rows, model_width), f32),
            ((all_rows, model_width), bf16),
            ((parts, all_rows, 3 * width), bf16),
            ((parts, all_rows, width), bf16),
            ((parts, items, heads, ITEM_ROWS, ITEM_ROWS), bf16),
            ((all_rows, model_width), f32),
            ((all_rows, model_width), bf16),
            ((1, model_width), f32),
        ],
        [],
        2 * all_rows * square * parts + 2 * block_rows * all_rows * model_width,
        40 << 20,
        (meta, raw_tokens, place_row, hidden, valid, norm_params, extra_params, attend_all),
        scalars=1,
    )
    acted, slope = call(
        functools.partial(lift_kernel, vision_rows=vision_rows, all_rows=all_rows),
        "lift",
        parts,
        [whole(all_rows, model_width), stepped_pair(2, 1, model_width, hidden_width)],
        [stepped(1, all_rows, hidden_width)] * 2,
        [((parts, all_rows, hidden_width), bf16)] * 2,
        [],
        2 * all_rows * square * parts,
        30 << 20,
        (feed_input, lift_all),
    )
    grad_rows, grad_bias, grad_drop = call(
        functools.partial(drop_weight_kernel, vision_rows=vision_rows, main_rows=main_rows),
        "drop_weight_grad",
        parts,
        [
            whole(block_rows, model_width),
            whole(1, block_rows),
            stepped(1, main_rows, hidden_width),
        ],
        [
            whole(main_rows, model_width),
            whole(2, model_width),
            stepped_pair(2, 1, model_width, hidden_width),
        ],
        [
            ((main_rows, model_width), bf16),
            ((2, model_width), f32),
            ((2, parts, model_width, hidden_width), bf16),
        ],
        [],
        2 * main_rows * square * parts,
        20 << 20,
        (raw_grad, place_row, acted),
    )
    drop_sum = scatter(grad_drop.reshape(2, parts * model_width, hidden_width), 1)

    grad_lift, grad_residual, grad_attended, grad_norm_second = call(
        functools.partial(expert_back_kernel, vision_rows=vision_rows, main_rows=main_rows),
        "expert_back",
        parts,
        [
            whole(main_rows, model_width),
            stepped(1, main_rows, hidden_width),
            whole(main_rows, model_width),
            whole(main_rows, model_width),
            whole(4, model_width),
            stepped_pair(2, 1, model_width, hidden_width),
            stepped_pair(2, 1, model_width, hidden_width),
        ],
        [
            stepped_pair(2, 1, model_width, hidden_width),
            whole(main_rows, model_width),
            whole(main_rows, model_width),
            whole(2, model_width),
        ],
        [
            ((2, parts, model_width, hidden_width), bf16),
            ((main_rows, model_width), f32),
            ((main_rows, model_width), bf16),
            ((2, model_width), f32),
        ],
        [pltpu.VMEM((main_rows, hidden_width), bf16)],
        6 * main_rows * square * parts,
        45 << 20,
        (grad_rows, slope, feed_input, residual, norm_params, drop_all, lift_all),
    )
    lift_sum = scatter(grad_lift.reshape(2, parts * model_width, hidden_width), 1)

    grad_attend, grad_raw, grad_norm_first, grad_mask = call(
        functools.partial(attention_back_kernel, items=items, heads=heads, main_rows=main_rows),
        "attention_back",
        parts,
        [
            whole(main_rows, model_width),
            whole(main_rows, model_width),
            stepped(1, main_rows, 3 * width),
            stepped(1, main_rows, width),
            stepped(1, items, heads, ITEM_ROWS, ITEM_ROWS),
            whole(main_rows, model_width),
            whole(main_rows, model_width),
            whole(all_rows, 1),
            whole(block_rows, 1),
            whole(4, model_width),
            stepped(1, model_width, model_width),
        ],
        [
            stepped(1, model_width, model_width),
            whole(block_rows, model_width),
            whole(2, model_width),
            whole(1, model_width),
        ],
        [
            ((parts, model_width, model_width), bf16),
            ((block_rows, model_width), bf16),
            ((2, model_width), f32),
            ((1, model_width), f32),
        ],
        [
            pltpu.VMEM((main_rows, model_width), f32),
            pltpu.VMEM((main_rows, width), bf16),
            pltpu.VMEM((main_rows, 3 * width), bf16),
        ],
        4 * main_rows * square * parts,
        40 << 20,
        (
            grad_attended,
            grad_residual,
            joint_rows,
            mixed,
            probs,
            normed,
            block_input,
            hidden,
            place_column,
            norm_params,
            attend_all,
        ),
    )
    attend_sum = scatter(grad_attend.reshape(parts * model_width, model_width), 0)
    input_grad = give_back(grad_raw).astype(f32)

    raw_out, feed_square = call(
        functools.partial(drop_kernel, vision_rows=vision_rows, all_rows=all_rows),
        "drop",
        parts,
        [
            stepped(1, all_rows, hidden_width),
            whole(all_rows, model_width),
            whole(all_rows, 1),
            whole(block_rows, 1),
            whole(3, model_width),
            stepped_pair(2, 1, model_width, hidden_width),
        ],
        [whole(block_rows, model_width), whole(2, model_width)],
        [((block_rows, model_width), bf16), ((2, model_width), f32)],
        [pltpu.VMEM((all_rows, model_width), f32)],
        2 * all_rows * square * parts,
        25 << 20,
        (acted, residual, valid, place_column, extra_params, drop_all),
    )
    block_output = give_back(raw_out).astype(f32)

    squares = jnp.stack(
        [jnp.sum(feed_square[0]), jnp.sum(attended_square), jnp.sum(feed_square[1]), used.astype(f32)]
    )
    small = jnp.concatenate(
        [
            grad_norm_first,
            grad_norm_second,
            grad_bias,
            grad_mask,
            jnp.pad(squares, (0, model_width - 4))[None],
        ],
        axis=0,
    )
    small = lax.psum(small, ("dp", "mp"))
    norm_total, extra_total = small[:4], small[4:7]
    rms_values = jnp.sqrt(small[7, :3] / (small[7, 3] * model_width))

    attend_sum = attend_sum.astype(f32)
    joint_grad = jnp.stack([attend_sum[:, k * width : (k + 1) * width] for k in range(3)])
    output_grad = attend_sum[:, 3 * width :].T
    lift_grad = lift_sum.astype(f32)
    drop_grad = jnp.swapaxes(drop_sum, 1, 2).astype(f32)
    results = [block_output, input_grad, rms_values]
    results += adamw(joint_weight, joint_first, joint_second, joint_grad, matrix_rate, weight_decay)
    results += adamw(output_weight, output_first, output_second, output_grad, matrix_rate, weight_decay)
    results += adamw(lift_weight, lift_first, lift_second, lift_grad, matrix_rate, weight_decay)
    results += adamw(drop_weight, drop_first, drop_second, drop_grad, matrix_rate, weight_decay)
    results += adamw(norm_params, norm_first, norm_second, norm_total, vector_rate, 0.0)
    results += adamw(extra_params, extra_first, extra_second, extra_total, vector_rate, 0.0)
    return tuple(results)


def solution(mesh):
    rows = P(None, ("dp", "mp"), None)
    joint, output, lift, drop = (
        P(None, "dp", "mp"),
        P("mp", "dp"),
        P(None, "dp", "mp"),
        P(None, "mp", "dp"),
    )
    return jax.shard_map(
        body,
        mesh=mesh,
        in_specs=(rows, rows, P(None, "dp"), P(None, "dp"), P(None, "dp", None))
        + (joint,) * 3
        + (output,) * 3
        + (lift,) * 3
        + (drop,) * 3
        + (P(),) * 6,
        out_specs=(rows, rows, P())
        + (joint,) * 4
        + (output,) * 4
        + (lift,) * 4
        + (drop,) * 4
        + (P(),) * 8,
        check_vma=False,
    )
```

time: 1480 us -> 761 us (0.51)
  matrix products: 389 us -> 0 us
  Pallas kernels: 0 us -> 194 us
  waiting for transfers between devices: 625 us -> 443 us
  local copies, waits for them, and re-layouts: 186 us -> 14.4 us
  other arithmetic: 126 us -> 29.9 us
  blocking collectives: 111 us -> 45.9 us
    dot_general x92 -> x0, matrix products: 379 us -> none  [the longest x4 77.8 us: body(): jnp.einsum('hqk,khe->qhe', grad_raw, head_rows[1], preferred_element_type...]
    pallas_call x0 -> x6, Pallas kernels: none -> 194 us  [call(): pl.pallas_call(kernel, name=name, grid_spec=pltpu.PrefetchScalarGridSpec(...]
    reduce_scatter x17 -> x2, waiting for transfers between devices: 421 us -> 268 us  [scatter(): lax.psum_scatter(values, ('mp', 'dp'), scatter_dimension=axis, tiled=True)]
    gather x16 -> x0, local copies, waits for them, and re-layouts: 93.4 us -> none  [the longest x4 27.4 us: body(): grad_grouped = grad_feed_all[sorted_order]]
    all_gather x2 -> x0, blocking collectives: 70.3 us -> none  [the longest x1 39.1 us: body(): lax.all_gather(joint_weight.astype(jnp.bfloat16), 'dp', axis=1, tiled=True)]
    reduce_sum x30 -> x6, other arithmetic: 65.1 us -> 2.8 us  [the longest x1 1.3 us: body(): jnp.sum(attended_square)]
    all_gather x18 -> x3, waiting for transfers between devices: 185 us -> 151 us  [gather(): return lax.all_gather(values, ('mp', 'dp'), axis=axis, tiled=True)]
    unnamed x606 -> x35, local copies, waits for them, and re-layouts: 38.3 us -> 9.79 us
  transfers between devices with their start and end apart: 38 -> 10, of which waited for: 25 -> 7; matrix products, arithmetic and copies ran while one was open for 42% -> 5% of each run, Pallas kernels for 0% -> 12%
where the time goes in v1:
time: 761 us; the launch traced here: 760 us
  waiting for transfers between devices  443 us (58%)
  Pallas kernels  194 us (25%)
  blocking collectives  45.9 us (6%)
  other arithmetic  29.9 us (4%)
  between operations  16.4 us (2%)
  starting transfers between devices  15.7 us (2%)
  local copies, waits for them, and re-layouts  14.4 us (2%)
    reduce_scatter x2, waiting for transfers between devices, scatter(): lax.psum_scatter(values, ('mp', 'dp'), scatter_dimension=axis, tiled=True)  268 us
    pallas_call x6, Pallas kernels, call(): pl.pallas_call(kernel, name=name, grid_spec=pltpu.PrefetchScalarGridSpec(...  194 us
    all_gather x3, waiting for transfers between devices, gather(): return lax.all_gather(values, ('mp', 'dp'), axis=axis, tiled=True)  151 us
    psum x1, blocking collectives, body(): small = lax.psum(small, ('dp', 'mp'))  45.9 us
  transfers between devices with their start and end apart: 10, of which 7 were waited for; matrix products, arithmetic and copies ran while one was open for 5% of the time, Pallas kernels for 12%

profile of v1, /device:TPU:0, one launch (start us, length us, event | category | flops | bytes accessed | tf_op | source)
XLA Modules:
  0.0 759.9 jit_solution(18401450858675094286)
XLA Ops:
  7.3 1.0 copy.96
  8.3 1.1 convert.17
  9.4 0.8 pad_maximum_fusion.1
  10.3 1.8 convert_element_type.85
  12.1 4.3 all-to-all-start
  16.8 1.1 reshape.326.hidden_ref
  17.9 1.3 convert_element_type.89
  19.2 0.7 broadcast_add_fusion
  19.9 0.6 fusion.23
  22.7 1.9 fusion.8.valid_ref
  24.6 12.6 %all-to-all-done = bf16[4,240,768]{2,1,0:T(8,128)(2,1)} async-done(((bf16[4,240,768]{2,1,0:T(8,128)(2,1)}), bf16[4,240,768]{2,1,0:T(8,128)(2,1)}, u32[]{:S(2)}, u32[]{:S(2)}) %all-to-all-start) | async-done | bytes 1474592 | tf_op jit(solution)/shard_map/all_to_all | solution.py:539
  37.2 3.6 all-to-all-start.2
  40.9 37.5 %all-gather.4.cloned.1.call-done = bf16[3072,768]{1,0:T(8,128)(2,1)} async-done(((bf16[96,768]{1,0:T(8,128)(2,1)}), bf16[3072,768]{1,0:T(8,128)(2,1)}) %all-gather.4.cloned.1.call-update) | async-done | bytes 4718608 | tf_op jit(solution)/shard_map/all_gather | solution.py:533
  78.3 52.1 %attention.1 = (f32[1168,768]{1,0:T(8,128)}, bf16[1168,768]{1,0:T(8,128)(2,1)}, bf16[4,1168,576]{2,1,0:T(8,128)(2,1)}, bf16[4,1168,192]{2,1,0:T(8,128)(2,1)}, bf...) custom-call(s32[5]{0:T(128)} %pad_add_fusion.meta_ref, ...), custom_call_target="tpu_custom_call" | custom-call | flops 7233601536 | bytes 41943040 | tf_op jit(solution)/shard_map/attention/pallas_call | solution.py:467
  130.5 32.9 %all-gather.6.cloned.1.call-done = bf16[2,3072,768]{2,1,0:T(8,128)(2,1)} async-done(((bf16[2,96,768]{2,1,0:T(8,128)(2,1)}), bf16[2,3072,768]{2,1,0:T(8,128)(2,1)}) %all-gather.6.cloned.1.call-update) | async-done | bytes 9437200 | tf_op jit(solution)/shard_map/all_gather | solution.py:533
  163.3 17.4 %lift.1 = (bf16[4,1168,768]{2,1,0:T(8,128)(2,1)}, bf16[4,1168,768]{2,1,0:T(8,128)(2,1)}) custom-call(bf16[1168,768]{1,0:T(8,128)(2,1)} %get-tuple-element.50.feed_ref, bf16[2,4,768,768]{3,2,1,0:T(8,128)(2,1)} %bitcast.74), custom_call_target="tpu_custom_call" | custom-call | flops 5511315456 | bytes 31457280 | tf_op jit(solution)/shard_map/lift/pallas_call | solution.py:467
  180.7 1.1 copy-done.4
  181.9 13.6 %drop_weight_grad.1 = (bf16[1024,768]{1,0:T(8,128)(2,1)}, f32[2,768]{1,0:T(2,128)}, bf16[2,4,768,768]{3,2,1,0:T(8,128)(2,1)}) custom-call(bf16[960,768]{1,0:T(8,128)(2,1)} %bitcast.66, s32[1,960]{1,0:T(1,128)} %reshape_select_fusion.place_ref, bf16[4,1168,768]{2,1,0:T(8,128)(2,1)} %get-tuple-element.51.acted_ref), custom_call_target="tpu_custom_call" | custom-call | flops 4831838208 | bytes 20971520 | tf_op jit(solution)/shard_map/drop_weight_grad/pallas_call | solution.py:467
  195.6 134.4 %reduce-scatter.8.cloned.1.call-done = bf16[2,96,768]{2,1,0:T(8,128)(2,1)} async-done(((bf16[2,3072,768]{2,1,0:T(8,128)(2,1)}), bf16[2,96,768]{2,1,0:T(8,128)(2,1)}) %reduce-scatter.8.cloned.1.call-update) | async-done | bytes 294928 | tf_op jit(solution)/shard_map/reduce_scatter | solution.py:536
  330.0 2.7 fusion.28
  333.6 1.0 select_select_fusion.place_ref
  334.6 80.5 %all-gather.8.cloned.1.call-done = bf16[2,3072,768]{2,1,0:T(8,128)(2,1)} async-done(((bf16[2,96,768]{2,1,0:T(8,128)(2,1)}), bf16[2,3072,768]{2,1,0:T(8,128)(2,1)}) %all-gather.8.cloned.1.call-update) | async-done | bytes 9437200 | tf_op jit(solution)/shard_map/all_gather | solution.py:533
  415.1 33.0 %expert_back.1 = (bf16[2,4,768,768]{3,2,1,0:T(8,128)(2,1)}, f32[1024,768]{1,0:T(8,128)}, bf16[1024,768]{1,0:T(8,128)(2,1)}, f32[2,768]{1,0:T(2,128)}) custom-call(bf16[1024,768]{1,0:T(8,128)(2,1)} %get-tuple-element.54.grad_ref, bf16[4,1168,768]{2,1,0:T(8,128)(2,1)} %get-tuple-element.55.slope_ref, bf16[1168,768]{1,0:T(8,128)(2,1)} %get-tuple-element.50.feed_ref, ...), custom_call_target="tpu_custom_call" | custom-call | flops 14495514624 | bytes 47185920 | tf_op jit(solution)/shard_map/expert_back/pallas_call | solution.py:467
  448.0 53.1 %attention_back.1 = (bf16[4,768,768]{2,1,0:T(8,128)(2,1)}, bf16[960,768]{1,0:T(8,128)(2,1)}, f32[2,768]{1,0:T(2,128)}, f32[1,768]{1,0:T(1,128)}) custom-call(bf16[1024,768]{1,0:T(8,128)(2,1)} %get-tuple-element.56.grad_attended_ref, f32[1024,768]{1,0:T(8,128)} %get-tuple-element.57.grad_residual_ref, bf16[4,1168,576]{2,1,0:T(8,128)(2,1)} %get-tuple-element.58.joint_ref, ...), custom_call_target="tpu_custom_call" | custom-call | flops 9663676416 | bytes 41943040 | tf_op jit(solution)/shard_map/attention_back/pallas_call | solution.py:467
  501.8 3.6 all-to-all-start.3
  505.3 25.0 %drop.1 = (bf16[960,768]{1,0:T(8,128)(2,1)}, f32[2,768]{1,0:T(2,128)}) custom-call(bf16[4,1168,768]{2,1,0:T(8,128)(2,1)} %get-tuple-element.51.acted_ref, f32[1168,768]{1,0:T(8,128)} %get-tuple-element.52.residual_ref, f32[1168,1]{1,0:T(8,128)} %fusion.8.valid_ref, s32[960,1]{1,0:T(8,128)} %select_select_fusion.place_ref, f32[3,768]{1,0:T(4,128)} %extra_ref.3, ...), custom_call_target="tpu_custom_call" | custom-call | flops 5511315456 | bytes 26214400 | tf_op jit(solution)/shard_map/drop/pallas_call | solution.py:467
  530.4 3.7 all-to-all-start.1
  534.9 1.1 copy.103
  536.0 1.8 copy.105
  537.8 1.3 reduce_sum.95
  539.7 2.0 select_maximum_fusion
  541.8 1.3 concatenate.12
  543.1 45.9 %psum.7 = f32[8,768]{1,0:T(8,128)} all-reduce(f32[8,768]{1,0:T(8,128)} %concatenate.12), channel_id=1, replica_groups=mesh['dp'=8,'mp'=4] {'dp','mp'}, use_global_device_ids=true, to_apply=%region_9.10 | all-reduce | flops 6144 | bytes 49152 | tf_op jit(solution)/shard_map/psum | solution.py:787
  589.0 1.3 slice.59
  590.9 1.2 fusion.22
  592.2 1.4 fusion.24
  593.6 1.4 fusion.26
  594.9 1.8 convert_element_type.90
  596.8 1.8 convert_element_type.88
  598.6 11.3 %reduce-scatter.10.cloned.1.call-done = bf16[96,768]{1,0:T(8,128)(2,1)} async-done(((bf16[3072,768]{1,0:T(8,128)(2,1)}), bf16[96,768]{1,0:T(8,128)(2,1)}) %reduce-scatter.10.cloned.1.call-update) | async-done | bytes 147472
  609.9 1.1 copy.113
  611.3 0.8 copy.111
  612.1 0.9 copy.108
  613.0 0.9 copy.109
  613.9 0.9 copy.110
  614.8 1.8 fusion.34
  616.5 133.8 %reduce-scatter.6.cloned.1.call-done = bf16[2,96,768]{2,1,0:T(8,128)(2,1)} async-done(((bf16[2,3072,768]{2,1,0:T(8,128)(2,1)}), bf16[2,96,768]{2,1,0:T(8,128)(2,1)}) %reduce-scatter.6.cloned.1.call-update) | async-done | bytes 294928 | tf_op jit(solution)/shard_map/reduce_scatter | solution.py:536
  750.3 2.8 fusion.31
  (66 shorter events, 4.7 us)
Async XLA Ops:
  7.2 9.3 %copy-start = (s32[4,4,6]{2,1,0:T(4,128)S(1)}, s32[4,4,6]{2,1,0:T(4,128)}, u32[]{:S(2)}) copy-start(s32[4,4,6]{2,1,0:T(4,128)} %param.26) | copy-start | bytes 1156
  7.2 71.1 %all-gather.4.cloned.1.call-start = ((), (), s32[]{:S(2)}) async-start(), calls=%async_computation.7 | async-start | bytes 4866048 | tf_op jit(solution)/shard_map/all_gather | solution.py:533
  8.3 9.7 %copy-start.2 = (f32[4,240,768]{2,1,0:T(8,128)S(1)}, f32[4,240,768]{2,1,0:T(8,128)}, u32[]{:S(2)}) copy-start(f32[4,240,768]{2,1,0:T(8,128)} %param.24) | copy-start | bytes 8847364
  10.2 153.1 %all-gather.6.cloned.1.call-start = ((), (), s32[]{:S(2)}) async-start(), calls=%async_computation.8 | async-start | bytes 9732096 | tf_op jit(solution)/shard_map/all_gather | solution.py:533
  12.1 25.1 %all-to-all-start = ((bf16[4,240,768]{2,1,0:T(8,128)(2,1)}), bf16[4,240,768]{2,1,0:T(8,128)(2,1)}, u32[]{:S(2)}, u32[]{:S(2)}) async-start(bf16[4,240,768]{2,1,0:T(8,128)(2,1)} %param.23), calls=%async_computation | async-start | bytes 2949120 | tf_op jit(solution)/shard_map/all_to_all | solution.py:539
  37.2 143.5 %all-to-all-start.2 = ((bf16[4,240,768]{2,1,0:T(8,128)(2,1)}), bf16[4,240,768]{2,1,0:T(8,128)(2,1)S(1)}, u32[]{:S(2)}, u32[]{:S(2)}) async-start(bf16[4,240,768]{2,1,0:T(8,128)(2,1)} %convert_element_type.89), calls=%async_computation.2 | async-start | bytes 2949120 | tf_op jit(solution)/shard_map/all_to_all | solution.py:539
  40.8 289.1 %reduce-scatter.8.cloned.1.call-start = ((), (), s32[]{:S(2)}) async-start(), calls=%async_computation.11 | async-start | bytes 9732096 | tf_op jit(solution)/shard_map/reduce_scatter | solution.py:536
  180.7 1.2 copy-start.4
  195.5 134.5 %copy-start.7 = (f32[2,768,96]{1,2,0:T(8,128)S(1)}, f32[2,768,96]{1,2,0:T(8,128)}, u32[]{:S(2)}) copy-start(f32[2,768,96]{1,2,0:T(8,128)} %param.36) | copy-start | bytes 1769476
  195.5 134.5 %copy-start.8 = (f32[2,768,96]{1,2,0:T(8,128)S(1)}, f32[2,768,96]{1,2,0:T(8,128)}, u32[]{:S(2)}) copy-start(f32[2,768,96]{1,2,0:T(8,128)} %param.37) | copy-start | bytes 1769476
  195.5 134.5 %copy-start.9 = (f32[2,768,96]{1,2,0:T(8,128)S(1)}, f32[2,768,96]{1,2,0:T(8,128)}, u32[]{:S(2)}) copy-start(f32[2,768,96]{1,2,0:T(8,128)} %param.38) | copy-start | bytes 1769476
  195.5 219.5 %all-gather.8.cloned.1.call-start = ((), (), s32[]{:S(2)}) async-start(), calls=%async_computation.9 | async-start | bytes 9732096 | tf_op jit(solution)/shard_map/all_gather | solution.py:533
  332.7 277.2 %reduce-scatter.10.cloned.1.call-start = ((), (), s32[]{:S(2)}) async-start(), calls=%async_computation.12 | async-start | bytes 4866048
  501.2 249.1 %reduce-scatter.6.cloned.1.call-start = ((), (), s32[]{:S(2)}) async-start(), calls=%async_computation.10 | async-start | bytes 9732096 | tf_op jit(solution)/shard_map/reduce_scatter | solution.py:536
  501.8 28.6 %all-to-all-start.3 = ((bf16[4,240,768]{2,1,0:T(8,128)(2,1)}), bf16[4,240,768]{2,1,0:T(8,128)(2,1)S(1)}, u32[]{:S(2)}, u32[]{:S(2)}) async-start(bf16[4,240,768]{2,1,0:T(8,128)(2,1)} %bitcast.20), calls=%async_computation.3 | async-start | bytes 2949120 | tf_op jit(solution)/shard_map/all_to_all | solution.py:542
  530.3 4.4 copy-start.6
  530.3 8.8 %copy-start.12 = (f32[2,768]{1,0:T(2,128)S(1)}, f32[2,768]{1,0:T(2,128)}, u32[]{:S(2)}) copy-start(f32[2,768]{1,0:T(2,128)} %get-tuple-element.68) | copy-start | bytes 18436
  530.3 11.4 %copy-start.11 = (f32[2,768]{1,0:T(2,128)S(1)}, f32[2,768]{1,0:T(2,128)}, u32[]{:S(2)}) copy-start(f32[2,768]{1,0:T(2,128)} %get-tuple-element.66) | copy-start | bytes 18436
  530.4 66.4 %all-to-all-start.1 = ((bf16[4,240,768]{2,1,0:T(8,128)(2,1)}), bf16[4,240,768]{2,1,0:T(8,128)(2,1)S(1)}, u32[]{:S(2)}, u32[]{:S(2)}) async-start(bf16[4,240,768]{2,1,0:T(8,128)(2,1)} %bitcast.65), calls=%async_computation.1 | async-start | bytes 2949120 | tf_op jit(solution)/shard_map/all_to_all | solution.py:542
  596.8 14.3 %copy-start.5 = (f32[3,96,192]{1,2,0:T(8,128)S(1)}, f32[3,96,192]{1,2,0:T(8,128)}, u32[]{:S(2)}) copy-start(f32[3,96,192]{1,2,0:T(8,128)} %copy.105) | copy-start | bytes 663556
  611.0 139.3 %copy-start.3 = (f32[2,96,768]{2,1,0:T(8,128)S(1)}, f32[2,96,768]{2,1,0:T(8,128)}, u32[]{:S(2)}) copy-start(f32[2,96,768]{2,1,0:T(8,128)} %param.33) | copy-start | bytes 1769476
  611.0 139.3 %copy-start.10 = (f32[2,96,768]{2,1,0:T(8,128)S(1)}, f32[2,96,768]{2,1,0:T(8,128)}, u32[]{:S(2)}) copy-start(f32[2,96,768]{2,1,0:T(8,128)} %param.34) | copy-start | bytes 1769476
  613.0 140.0 %copy-start.1 = (s32[4,4,6]{2,1,0:T(4,128)S(1)}, s32[4,4,6]{2,1,0:T(4,128)}, u32[]{:S(2)}) copy-start(s32[4,4,6]{2,1,0:T(4,128)} %param.26) | copy-start | bytes 1156
Sparse Core Ops, SparseCore 0:
  11.6 66.6 all-gather.3
  82.0 81.3 all-gather.5
  195.7 134.2 reduce-scatter.7
  333.9 81.0 all-gather.7
  501.3 108.5 reduce-scatter.9
  615.6 134.5 reduce-scatter.5

commit v2 on v1

v2 whole, which is shorter than its diff:
```python
import functools

import jax
import jax.numpy as jnp
from jax import lax
from jax.experimental import pallas as pl
from jax.experimental.pallas import tpu as pltpu
from jax.sharding import PartitionSpec as P

HEAD_DIM = 64
PATCHES = 197
TEXT_MAX = 40
STEP = 7

norm_epsilon = 1e-06
masked_score = -1000000000.0
first_decay = 0.9
second_decay = 0.98
adam_epsilon = 1e-06
matrix_rate = 0.04
vector_rate = 0.5
weight_decay = 0.01

PATCH_STRIDE = 208
TEXT_STRIDE = 48
ITEM_ROWS = PATCH_STRIDE + TEXT_STRIDE

bf16 = jnp.bfloat16
f32 = jnp.float32
VMEM_LIMIT = 58 * 1024 * 1024
ATTENTION_US = 26
LIFT_US = 17
DROP_WEIGHT_US = 8
EXPERT_BACK_US = 18
ATTENTION_BACK_US = 27
DROP_US = 24


def adamw(weight, first_state, second_state, gradient, step_rate, decay_rate):
    first_new = first_decay * first_state + (1.0 - first_decay) * gradient
    second_new = second_decay * second_state + (1.0 - second_decay) * gradient * gradient
    first_hat = first_new / (1.0 - first_decay**STEP)
    second_hat = second_new / (1.0 - second_decay**STEP)
    weight_new = weight - step_rate * (
        first_hat / (jnp.sqrt(second_hat) + adam_epsilon) + decay_rate * weight
    )
    return (weight_new, first_new, second_new, weight_new.astype(bf16))


def dot(left, right, left_dim, right_dim):
    return lax.dot_general(
        left,
        right,
        (((left_dim,), (right_dim,)), ((), ())),
        preferred_element_type=f32,
    )


def loop(count, body):
    lax.fori_loop(0, count, lambda i, c: (body(i), c)[1], 0)


def rows_at(index, size):
    return pl.ds(pl.multiple_of(index * size, 16), size)


def norm_forward(values, gain, shift):
    centred = values - jnp.mean(values, axis=-1, keepdims=True)
    spread = jnp.mean(centred * centred, axis=-1, keepdims=True)
    return centred * lax.rsqrt(spread + norm_epsilon) * gain + shift


def norm_backward(values, gain, grad):
    centred = values - jnp.mean(values, axis=-1, keepdims=True)
    spread = jnp.mean(centred * centred, axis=-1, keepdims=True)
    scale = lax.rsqrt(spread + norm_epsilon)
    hat = centred * scale
    grad_hat = grad * gain
    grad_values = scale * (
        grad_hat
        - jnp.mean(grad_hat, axis=-1, keepdims=True)
        - hat * jnp.mean(grad_hat * hat, axis=-1, keepdims=True)
    )
    grad_gain = jnp.sum(grad * hat, axis=0, keepdims=True)
    grad_shift = jnp.sum(grad, axis=0, keepdims=True)
    return grad_values, grad_gain, grad_shift


def one_hot(row_place, first_row, count):
    place = lax.broadcasted_iota(jnp.int32, (count, row_place.shape[1]), 0) + first_row
    return (place == row_place).astype(bf16)


def relative_block(mine, block):
    other = jnp.bitwise_xor(mine, block)
    return jnp.bitwise_and(other, 1) * 4 + jnp.right_shift(other, 1)


def store_grad(grad_ref, mine, index, first, rows, value):
    value = value.astype(bf16)
    size = grad_ref.shape[-2]
    for part in range(rows // size):
        place = relative_block(mine, first // size + part)
        grad_ref[0, place, index] = value[part * size : (part + 1) * size]


def attend(query, key, value, allowed):
    scores = dot(query, key, 1, 1)
    scores = jnp.where(allowed, scores, masked_score)
    top = jnp.max(scores, axis=-1, keepdims=True)
    weights = jnp.exp(scores - top)
    total = jnp.sum(weights, axis=-1, keepdims=True)
    weights = (weights * (1.0 / total)).astype(bf16)
    return weights, dot(weights, value, 1, 0)


def attention_kernel(
    meta_ref,
    raw_ref,
    place_ref,
    hidden_ref,
    norm_ref,
    extra_ref,
    weight_ref,
    block_ref,
    normed_ref,
    residual_ref,
    joint_ref,
    mixed_ref,
    probs_ref,
    **sizes,
):
    main_rows, all_rows = sizes["main_rows"], sizes["all_rows"]

    @pl.when(pl.program_id(0) == 0)
    def _():
        def chunk(first, size):
            rows = pl.ds(first, size)
            picked = dot(one_hot(place_ref[...], first, size), raw_ref[...], 1, 0)
            picked = jnp.where(hidden_ref[rows, :] > 0, extra_ref[2:3, :], picked)
            block_ref[rows, :] = picked
            residual_ref[rows, :] = picked
            normed_ref[rows, :] = norm_forward(picked, norm_ref[0:1, :], norm_ref[1:2, :]).astype(bf16)

        loop(sizes["items"], lambda i: chunk(pl.multiple_of(i * ITEM_ROWS, 16), ITEM_ROWS))
        chunk(main_rows, all_rows - main_rows)

    attend_heads(meta_ref, weight_ref, normed_ref, residual_ref, joint_ref, mixed_ref, probs_ref, **sizes)


def attention_end_kernel(
    meta_ref,
    normed_ref,
    block_ref,
    before_ref,
    valid_ref,
    norm_ref,
    weight_ref,
    residual_ref,
    joint_ref,
    mixed_ref,
    probs_ref,
    feed_ref,
    square_ref,
    **sizes,
):
    items, main_rows = sizes["items"], sizes["main_rows"]

    @pl.when(pl.program_id(0) == 0)
    def _():
        residual_ref[...] = before_ref[...]

    attend_heads(meta_ref, weight_ref, normed_ref, residual_ref, joint_ref, mixed_ref, probs_ref, **sizes)

    @pl.when(pl.program_id(0) == pl.num_programs(0) - 1)
    def _():
        square_ref[...] = jnp.zeros_like(square_ref)

        def chunk(rows):
            residual = residual_ref[rows, :]
            feed_ref[rows, :] = norm_forward(residual, norm_ref[2:3, :], norm_ref[3:4, :]).astype(bf16)
            attended = (residual - block_ref[rows, :]) * valid_ref[rows, :]
            square_ref[...] += jnp.sum(attended * attended, axis=0, keepdims=True)

        loop(items, lambda i: chunk(rows_at(i, ITEM_ROWS)))
        chunk(pl.ds(main_rows, sizes["all_rows"] - main_rows))


def attend_heads(
    meta_ref,
    weight_ref,
    normed_ref,
    residual_ref,
    joint_ref,
    mixed_ref,
    probs_ref,
    *,
    items,
    heads,
    main_rows,
    all_rows,
):
    width = heads * HEAD_DIM
    tail_rows = all_rows - main_rows

    def project(rows):
        joint = dot(normed_ref[rows, :], weight_ref[0, :, : 3 * width], 1, 0)
        joint_ref[0, rows, :width] = (joint[:, :width].astype(bf16).astype(f32) * HEAD_DIM**-0.5).astype(bf16)
        joint_ref[0, rows, width:] = joint[:, width:].astype(bf16)

    loop(items, lambda i: project(rows_at(i, ITEM_ROWS)))
    project(pl.ds(main_rows, tail_rows))

    column = lax.broadcasted_iota(jnp.int32, (1, ITEM_ROWS), 1)

    def one_item(i):
        patch_rows = rows_at(i, PATCH_STRIDE)
        text_rows = pl.ds(pl.multiple_of(items * PATCH_STRIDE + i * TEXT_STRIDE, 16), TEXT_STRIDE)
        joint = jnp.concatenate([joint_ref[0, patch_rows, :], joint_ref[0, text_rows, :]], axis=0)
        allowed = (column < PATCHES) | (
            (column >= PATCH_STRIDE) & (column < PATCH_STRIDE + meta_ref[i])
        )
        outs = []
        for h in range(heads):
            part = lambda k: joint[:, k * width + h * HEAD_DIM : k * width + (h + 1) * HEAD_DIM]
            weights, out = attend(part(0), part(1), part(2), allowed)
            probs_ref[0, i, h] = weights
            outs.append(out.astype(bf16))
        mixed = jnp.concatenate(outs, axis=1)
        mixed_ref[0, patch_rows, :] = mixed[:PATCH_STRIDE]
        mixed_ref[0, text_rows, :] = mixed[PATCH_STRIDE:]

    loop(items, one_item)

    joint = joint_ref[0, main_rows:, :]
    allowed = lax.broadcasted_iota(jnp.int32, (1, tail_rows), 1) < meta_ref[items]
    outs = []
    for h in range(heads):
        part = lambda k: joint[:, k * width + h * HEAD_DIM : k * width + (h + 1) * HEAD_DIM]
        outs.append(attend(part(0), part(1), part(2), allowed)[1].astype(bf16))
    mixed_ref[0, main_rows:, :] = jnp.concatenate(outs, axis=1)

    def add_output(rows):
        residual_ref[rows, :] += dot(mixed_ref[0, rows, :], weight_ref[0, :, 3 * width :], 1, 1)

    loop(items, lambda i: add_output(rows_at(i, ITEM_ROWS)))
    add_output(pl.ds(main_rows, tail_rows))


def attention_back_kernel(
    mine_ref,
    grad_attended_ref,
    joint_ref,
    mixed_ref,
    probs_ref,
    normed_ref,
    weight_ref,
    grad_weight_ref,
    grad_normed_ref,
    grad_mixed_ref,
    grad_joint_ref,
    **sizes,
):
    @pl.when(pl.program_id(0) == 0)
    def _():
        grad_normed_ref[...] = jnp.zeros_like(grad_normed_ref)

    heads_back(
        mine_ref,
        grad_attended_ref,
        joint_ref,
        mixed_ref,
        probs_ref,
        normed_ref,
        weight_ref,
        grad_weight_ref,
        grad_normed_ref,
        grad_mixed_ref,
        grad_joint_ref,
        **sizes,
    )


def attention_back_end_kernel(
    mine_ref,
    grad_attended_ref,
    joint_ref,
    mixed_ref,
    probs_ref,
    normed_ref,
    weight_ref,
    before_ref,
    grad_residual_ref,
    block_ref,
    hidden_ref,
    place_ref,
    norm_ref,
    grad_weight_ref,
    grad_raw_ref,
    grad_norm_ref,
    grad_mask_ref,
    grad_normed_ref,
    grad_mixed_ref,
    grad_joint_ref,
    **sizes,
):
    @pl.when(pl.program_id(0) == 0)
    def _():
        grad_normed_ref[...] = before_ref[...]

    heads_back(
        mine_ref,
        grad_attended_ref,
        joint_ref,
        mixed_ref,
        probs_ref,
        normed_ref,
        weight_ref,
        grad_weight_ref,
        grad_normed_ref,
        grad_mixed_ref,
        grad_joint_ref,
        **sizes,
    )

    @pl.when(pl.program_id(0) == pl.num_programs(0) - 1)
    def _():
        grad_norm_ref[...] = jnp.zeros_like(grad_norm_ref)
        grad_mask_ref[...] = jnp.zeros_like(grad_mask_ref)

        def chunk(i):
            rows = rows_at(i, ITEM_ROWS)
            grad, gain, shift = norm_backward(block_ref[rows, :], norm_ref[0:1, :], grad_normed_ref[rows, :])
            grad_norm_ref[0:1, :] += gain
            grad_norm_ref[1:2, :] += shift
            grad = grad + grad_residual_ref[rows, :]
            hidden = hidden_ref[rows, :] > 0
            grad_mask_ref[...] += jnp.sum(jnp.where(hidden, grad, 0.0), axis=0, keepdims=True)
            grad_normed_ref[rows, :] = jnp.where(hidden, 0.0, grad)

        loop(sizes["items"], chunk)
        unplace(place_ref, grad_normed_ref, grad_raw_ref, grad_normed_ref.shape[0])


def heads_back(
    mine_ref,
    grad_attended_ref,
    joint_ref,
    mixed_ref,
    probs_ref,
    normed_ref,
    weight_ref,
    grad_weight_ref,
    grad_normed_ref,
    grad_mixed_ref,
    grad_joint_ref,
    *,
    items,
    heads,
):
    width = heads * HEAD_DIM
    half = HEAD_DIM**-0.5

    def mixed_grad(i):
        rows = rows_at(i, ITEM_ROWS)
        grad_mixed_ref[rows, :] = dot(
            grad_attended_ref[rows, :], weight_ref[0, :, 3 * width :], 1, 0
        ).astype(bf16)

    loop(items, mixed_grad)

    def one_item(i):
        patch_rows = rows_at(i, PATCH_STRIDE)
        text_rows = pl.ds(pl.multiple_of(items * PATCH_STRIDE + i * TEXT_STRIDE, 16), TEXT_STRIDE)
        joint = jnp.concatenate([joint_ref[0, patch_rows, :], joint_ref[0, text_rows, :]], axis=0)
        mixed = jnp.concatenate([mixed_ref[0, patch_rows, :], mixed_ref[0, text_rows, :]], axis=0)
        grad_mixed = jnp.concatenate([grad_mixed_ref[patch_rows, :], grad_mixed_ref[text_rows, :]], axis=0)
        grads = [[], [], []]
        for h in range(heads):
            part = lambda k: joint[:, k * width + h * HEAD_DIM : k * width + (h + 1) * HEAD_DIM]
            span = slice(h * HEAD_DIM, (h + 1) * HEAD_DIM)
            grad_out = grad_mixed[:, span]
            weights = probs_ref[0, i, h]
            grad_probs = dot(grad_out, part(2), 1, 1)
            mean_grad = jnp.sum(
                grad_out.astype(f32) * mixed[:, span].astype(f32), axis=-1, keepdims=True
            )
            grad_scores = (weights.astype(f32) * (grad_probs - mean_grad)).astype(bf16)
            grads[0].append((dot(grad_scores, part(1), 1, 0) * half).astype(bf16))
            grads[1].append(dot(grad_scores, part(0), 0, 0).astype(bf16))
            grads[2].append(dot(weights, grad_out, 0, 0).astype(bf16))
        grad_joint = jnp.concatenate(grads[0] + grads[1] + grads[2], axis=1)
        grad_joint_ref[patch_rows, :] = grad_joint[:PATCH_STRIDE]
        grad_joint_ref[text_rows, :] = grad_joint[PATCH_STRIDE:]

    loop(items, one_item)

    model_width = weight_ref.shape[1]
    for first in range(0, model_width, 384):
        cols = slice(first, first + 384)
        grad_weight = jnp.concatenate(
            [
                dot(normed_ref[:, cols], grad_joint_ref[...], 0, 0),
                dot(grad_attended_ref[:, cols], mixed_ref[0], 0, 0),
            ],
            axis=1,
        )
        store_grad(grad_weight_ref, mine_ref[0], 0, first, 384, grad_weight)

    def normed_grad(i):
        rows = rows_at(i, ITEM_ROWS)
        grad_normed_ref[rows, :] += dot(grad_joint_ref[rows, :], weight_ref[0, :, : 3 * width], 1, 1)

    loop(items, normed_grad)


def unplace(place_ref, source_ref, raw_ref, source_rows):
    source = source_ref[...].astype(bf16)
    raw_rows = raw_ref.shape[0]
    size = 240 if raw_rows % 240 == 0 else raw_rows

    def chunk(i):
        rows = rows_at(i, size)
        place = lax.broadcasted_iota(jnp.int32, (size, source_rows), 1)
        pick = (place == place_ref[rows, :]).astype(bf16)
        raw_ref[rows, :] = dot(pick, source, 1, 0).astype(bf16)

    loop(raw_rows // size, chunk)


def lift_kernel(feed_ref, weight_ref, acted_ref, slope_ref, *, vision_rows, all_rows):
    def piece(rows, expert):
        lifted = dot(feed_ref[rows, :], weight_ref[expert, 0], 1, 0)
        cumulative = 0.5 * (1.0 + lax.erf(lifted * (0.5**0.5)))
        density = jnp.exp(-0.5 * lifted * lifted) * ((2.0 * jnp.pi) ** -0.5)
        acted_ref[0, rows, :] = (lifted * cumulative).astype(bf16)
        slope_ref[0, rows, :] = (cumulative + lifted * density).astype(bf16)

    loop(vision_rows // PATCH_STRIDE, lambda i: piece(rows_at(i, PATCH_STRIDE), 0))
    text = all_rows - vision_rows
    loop(3, lambda i: piece(pl.ds(pl.multiple_of(vision_rows + i * (text // 3), 16), text // 3), 1))


def place_grad_kernel(raw_ref, place_ref, grad_ref, grad_bias_ref, *, vision_rows):
    def chunk(i):
        rows = rows_at(i, ITEM_ROWS)
        pick = one_hot(place_ref[...], i * ITEM_ROWS, ITEM_ROWS)
        grad_ref[rows, :] = dot(pick, raw_ref[...], 1, 0).astype(bf16)

    loop(grad_ref.shape[0] // ITEM_ROWS, chunk)
    grad_bias_ref[0:1, :] = jnp.sum(grad_ref[:vision_rows, :].astype(f32), axis=0, keepdims=True)
    grad_bias_ref[1:2, :] = jnp.sum(grad_ref[vision_rows:, :].astype(f32), axis=0, keepdims=True)


def expert_weight_grad(grad_weight_ref, mine, left_ref, right, vision_rows):
    rows_total, width = left_ref.shape
    for expert, rows in ((0, slice(0, vision_rows)), (1, slice(vision_rows, rows_total))):
        for first in range(0, width, 384):
            grad_weight = dot(left_ref[rows, first : first + 384], right(rows), 0, 0)
            store_grad(grad_weight_ref, mine, expert, first, 384, grad_weight)


def drop_weight_kernel(mine_ref, grad_ref, acted_ref, grad_weight_ref, *, vision_rows):
    expert_weight_grad(
        grad_weight_ref, mine_ref[0], grad_ref, lambda rows: acted_ref[0, rows, :], vision_rows
    )


def drop_kernel(
    acted_ref,
    residual_ref,
    valid_ref,
    place_ref,
    extra_ref,
    weight_ref,
    raw_ref,
    square_ref,
    total_ref,
    *,
    vision_rows,
    all_rows,
):
    step = pl.program_id(0)
    text = all_rows - vision_rows

    @pl.when(step == 0)
    def _():
        total_ref[:vision_rows, :] = jnp.broadcast_to(extra_ref[0:1, :], (vision_rows, total_ref.shape[1]))
        total_ref[vision_rows:, :] = jnp.broadcast_to(extra_ref[1:2, :], (text, total_ref.shape[1]))

    def piece(rows, expert):
        total_ref[rows, :] += dot(acted_ref[0, rows, :], weight_ref[expert, 0], 1, 1)

    def everything(body):
        loop(vision_rows // PATCH_STRIDE, lambda i: body(rows_at(i, PATCH_STRIDE), 0))
        loop(3, lambda i: body(pl.ds(pl.multiple_of(vision_rows + i * (text // 3), 16), text // 3), 1))

    everything(piece)

    @pl.when(step == pl.num_programs(0) - 1)
    def _():
        square_ref[...] = jnp.zeros_like(square_ref)

        def finish(rows, expert):
            fed = total_ref[rows, :]
            out = residual_ref[rows, :] + fed
            valid = valid_ref[rows, :]
            square_ref[0:1, :] += jnp.sum(valid * out * out, axis=0, keepdims=True)
            square_ref[1:2, :] += jnp.sum(valid * fed * fed, axis=0, keepdims=True)
            total_ref[rows, :] = out

        everything(finish)
        unplace(place_ref, total_ref, raw_ref, all_rows)


def expert_back_step(
    mine_ref, grad_ref, slope_ref, feed_ref, drop_ref, lift_ref, grad_weight_ref, total_ref, lifted_ref, vision_rows
):
    def piece(rows, expert):
        grad_acted = dot(grad_ref[rows, :], drop_ref[expert, 0], 1, 0)
        grad_lifted = (grad_acted * slope_ref[0, rows, :].astype(f32)).astype(bf16)
        lifted_ref[rows, :] = grad_lifted
        total_ref[rows, :] += dot(grad_lifted, lift_ref[expert, 0], 1, 1)

    loop(vision_rows // PATCH_STRIDE, lambda i: piece(rows_at(i, PATCH_STRIDE), 0))
    piece(pl.ds(vision_rows, grad_ref.shape[0] - vision_rows), 1)
    expert_weight_grad(
        grad_weight_ref, mine_ref[0], feed_ref, lambda rows: lifted_ref[rows, :], vision_rows
    )


def expert_back_kernel(
    mine_ref,
    grad_ref,
    slope_ref,
    feed_ref,
    drop_ref,
    lift_ref,
    grad_weight_ref,
    total_ref,
    lifted_ref,
    *,
    vision_rows,
):
    @pl.when(pl.program_id(0) == 0)
    def _():
        total_ref[...] = jnp.zeros_like(total_ref)

    expert_back_step(
        mine_ref, grad_ref, slope_ref, feed_ref, drop_ref, lift_ref, grad_weight_ref, total_ref, lifted_ref, vision_rows
    )


def expert_back_end_kernel(
    mine_ref,
    grad_ref,
    slope_ref,
    feed_ref,
    drop_ref,
    lift_ref,
    before_ref,
    residual_ref,
    norm_ref,
    grad_weight_ref,
    grad_residual_ref,
    grad_attended_ref,
    grad_norm_ref,
    lifted_ref,
    *,
    vision_rows,
):
    @pl.when(pl.program_id(0) == 0)
    def _():
        grad_residual_ref[...] = before_ref[...]

    expert_back_step(
        mine_ref,
        grad_ref,
        slope_ref,
        feed_ref,
        drop_ref,
        lift_ref,
        grad_weight_ref,
        grad_residual_ref,
        lifted_ref,
        vision_rows,
    )

    @pl.when(pl.program_id(0) == pl.num_programs(0) - 1)
    def _():
        grad_norm_ref[...] = jnp.zeros_like(grad_norm_ref)

        def chunk(i):
            rows = rows_at(i, ITEM_ROWS)
            grad, gain, shift = norm_backward(
                residual_ref[rows, :], norm_ref[2:3, :], grad_residual_ref[rows, :]
            )
            grad_norm_ref[0:1, :] += gain
            grad_norm_ref[1:2, :] += shift
            grad = grad + grad_ref[rows, :].astype(f32)
            grad_residual_ref[rows, :] = grad
            grad_attended_ref[rows, :] = grad.astype(bf16)

        loop(grad_ref.shape[0] // ITEM_ROWS, chunk)


def whole(*shape):
    return pl.BlockSpec(shape, lambda *_: (0,) * len(shape))


def stepped(*shape, first=0):
    return pl.BlockSpec(shape, lambda i, *_: (i + first,) + (0,) * (len(shape) - 1))


def stepped_pair(*shape, first=0):
    return pl.BlockSpec(shape, lambda i, *_: (0, i + first) + (0,) * (len(shape) - 2))


def call(kernel, name, steps, ins, outs, scratch, microseconds, scalars=(), aliases=None):
    return pl.pallas_call(
        kernel,
        name=name,
        grid_spec=pltpu.PrefetchScalarGridSpec(
            num_scalar_prefetch=len(scalars),
            grid=(steps,),
            in_specs=[block for _, block in ins],
            out_specs=[block for _, _, block in outs],
            scratch_shapes=scratch,
        ),
        out_shape=[jax.ShapeDtypeStruct(shape, kind) for shape, kind, _ in outs],
        compiler_params=pltpu.CompilerParams(
            dimension_semantics=("arbitrary",), vmem_limit_bytes=VMEM_LIMIT
        ),
        cost_estimate=pl.CostEstimate(
            flops=int(microseconds * 1e9), bytes_accessed=int(microseconds * 1e6), transcendentals=0
        ),
    )(*scalars, *[array for array, _ in ins])


def assemble_kernel(mine_ref, *refs):
    count = len(refs) - 2
    pieces, whole_ref, sems = refs[:count], refs[count], refs[count + 1]
    size = pieces[0].shape[2]
    for step in range(4):

        @pl.when(pl.program_id(0) == step)
        def _():
            core, y = 1 - step // 2, step % 2
            copies = []
            for kind, ref in enumerate(pieces[5 * core : 5 * core + 5]):
                x, from_y = ((0, 0), (1, 0), (0, 1), (1, 1), (1, 1))[kind]
                if from_y != y:
                    continue
                for i in range(ref.shape[0]):
                    z = i + 2 * (kind == 4)
                    group = jnp.bitwise_xor(mine_ref[0], 2 * z + x)
                    rows = pl.ds(pl.multiple_of(group * size, 16), size)
                    copies.append(
                        pltpu.make_async_copy(
                            ref.at[i], whole_ref.at[:, 0, rows, :], sems.at[len(copies)]
                        )
                    )
            for copy in copies:
                copy.start()
            for copy in copies:
                copy.wait()


def assemble(mine, pieces, parts, rows):
    count, _, columns = pieces[0].shape[1:]
    return pl.pallas_call(
        assemble_kernel,
        name="assemble",
        grid_spec=pltpu.PrefetchScalarGridSpec(
            num_scalar_prefetch=1,
            grid=(parts,),
            in_specs=[pl.BlockSpec(memory_space=pl.ANY)] * len(pieces),
            out_specs=pl.BlockSpec((count, 1, rows, columns), lambda i, mine: (0, i, 0, 0)),
            scratch_shapes=[pltpu.SemaphoreType.DMA((8,))],
        ),
        out_shape=jax.ShapeDtypeStruct((count, parts, rows, columns), bf16),
        compiler_params=pltpu.CompilerParams(
            dimension_semantics=("arbitrary",), vmem_limit_bytes=20 << 20
        ),
        cost_estimate=pl.CostEstimate(
            flops=0, bytes_accessed=4 * count * parts * rows * columns, transcendentals=0
        ),
    )(mine, *pieces)


def body(
    tokens,
    cotangent,
    text_lengths,
    modality,
    masked_positions,
    joint_weight,
    joint_first,
    joint_second,
    output_weight,
    output_first,
    output_second,
    lift_weight,
    lift_first,
    lift_second,
    drop_weight,
    drop_first,
    drop_second,
    norm_params,
    norm_first,
    norm_second,
    extra_params,
    extra_first,
    extra_second,
):
    micro_count, shard_rows, model_width = tokens.shape
    block_rows = modality.shape[1]
    parts = block_rows // shard_rows
    assert micro_count == parts
    items = text_lengths.shape[1]
    width = joint_weight.shape[2]
    heads = width // HEAD_DIM
    hidden_width = lift_weight.shape[2]
    shard = joint_weight.shape[1]
    vision_rows = items * PATCH_STRIDE
    main_rows = items * ITEM_ROWS
    tail = block_rows - items * PATCHES - TEXT_MAX - (items - 1)
    tail = (tail + 47) // 48 * 48
    all_rows = main_rows + tail
    assert 4 * width == model_width and hidden_width == model_width

    shard_attend = jnp.concatenate(
        [joint_weight[0], joint_weight[1], joint_weight[2], output_weight.T], axis=1
    ).astype(bf16)[None]
    shard_lift = lift_weight.astype(bf16)
    shard_drop = jnp.swapaxes(drop_weight, 1, 2).astype(bf16)

    groups = lax.axis_size("dp")
    cube = groups == 8
    piece = model_width // 8
    order = [1, 3, 0, 2]
    if cube:
        mine = jnp.stack([lax.axis_index("dp"), lax.axis_index("mp")]).astype(jnp.int32)
    else:
        mine = jnp.zeros((2,), jnp.int32)

    def after(values, *others):
        return lax.optimization_barrier((values, others))[0]

    def swap(values, axis, bit):
        size = lax.axis_size(axis)
        return lax.ppermute(values, axis, [(i, i ^ bit) for i in range(size)])

    def exchange(values):
        return lax.all_to_all(values, "mp", split_axis=0, concat_axis=1, tiled=True)[0]

    def give_back(values):
        return lax.all_to_all(
            values.reshape(parts, shard_rows, model_width), "mp", split_axis=0, concat_axis=0, tiled=True
        )

    def gather(values):
        whole_values = lax.all_gather(values, ("mp", "dp"), axis=1, tiled=True)
        shape = (-1, parts, model_width, values.shape[2])
        return jnp.stack([whole_values.reshape(shape)[:, i] for i in order], axis=1)

    def gather_line(values):
        return jnp.stack([values] + [swap(values, "dp", bit) for bit in (2, 4, 6)])

    def gather_plane(line):
        return swap(line, "dp", 1), swap(line, "mp", 2)

    def gather_corner(along_x, along_y):
        return swap(along_x[:2], "mp", 2), swap(along_y[2:], "dp", 1)

    def gather_cores(line, along, corner):
        own = (line,) + along + corner
        return assemble(
            mine, own + tuple(swap(part, "mp", 1) for part in own), parts, model_width
        )

    def add(*terms):
        total = terms[0].astype(f32)
        for term in terms[1:]:
            total = total + term.astype(f32)
        return total

    def scatter(keep, send):
        shape = (2, 2, 4) + keep.shape[2:]
        both = jnp.stack([keep.reshape(shape), send.reshape(shape)], axis=1)
        both = jnp.transpose(both, (4, 0, 1, 3, 2, 5, 6))
        both = both.reshape(both.shape[0], parts * model_width, shape[-1])
        both = lax.psum_scatter(both, ("mp", "dp"), scatter_dimension=1, tiled=True)
        return both.astype(f32)

    def scatter_corner(keep, received):
        shape = (2, 2, 4) + keep.shape[2:]
        keep, received = keep.reshape(shape), received.reshape(shape)
        return add(keep[1, 1], received[1, 1]).astype(bf16)

    def scatter_plane(keep, received, from_x, from_y):
        shape = (2, 2, 4) + keep.shape[2:]
        keep, received = keep.reshape(shape), received.reshape(shape)
        part_x = add(keep[0, 1], received[0, 1])
        part_y = add(keep[1, 0], received[1, 0])
        part_x = jnp.concatenate([part_x[:2], add(part_x[2:], from_y)]).astype(bf16)
        part_y = jnp.concatenate([add(part_y[:2], from_x), part_y[2:]]).astype(bf16)
        return part_x, part_y

    def scatter_line(keep, received, from_x, from_y):
        shape = (2, 2, 4) + keep.shape[2:]
        keep, received = keep.reshape(shape), received.reshape(shape)
        return add(keep[0, 0], received[0, 0], from_x, from_y).astype(bf16)

    def send_corner(corner):
        return swap(corner[:2], "dp", 1), swap(corner[2:], "mp", 2)

    def send_plane(part_x, part_y):
        return swap(part_x, "dp", 1), swap(part_y, "mp", 2)

    def send_line(line):
        return tuple(swap(line[i], "dp", 2 * i) for i in (1, 2, 3))

    micro = lax.axis_index("mp")
    lengths = lax.dynamic_index_in_dim(text_lengths, micro, 0, keepdims=False)
    masked = lax.dynamic_index_in_dim(masked_positions, micro, 0, keepdims=False)
    item_ids = jnp.arange(items, dtype=jnp.int32)
    sizes = PATCHES + lengths
    ends = jnp.sum(jnp.where(item_ids[:, None] <= item_ids[None, :], sizes[:, None], 0), axis=0)
    used = jnp.sum(sizes)

    def place_of(row):
        segment = jnp.sum((row[..., None] >= ends).astype(jnp.int32), axis=-1)
        start = jnp.sum(jnp.where(row[..., None] >= ends, sizes, 0), axis=-1)
        inside = row - start
        return jnp.where(
            segment == items,
            main_rows + inside,
            jnp.where(
                inside < PATCHES,
                PATCH_STRIDE * segment + inside,
                vision_rows + TEXT_STRIDE * segment + inside - PATCHES,
            ),
        )

    place_row = place_of(jnp.arange(block_rows, dtype=jnp.int32))[None, :]
    place_column = place_of(jnp.arange(block_rows, dtype=jnp.int32))[:, None]
    targets = (vision_rows + TEXT_STRIDE * item_ids[:, None] + masked).reshape(-1)
    spots = jnp.arange(all_rows, dtype=jnp.int32)
    hidden = jnp.any(spots[:, None] == targets[None, :], axis=1).astype(jnp.int32)[:, None]
    text_spot = spots - vision_rows
    text_item = text_spot // TEXT_STRIDE
    text_end = jnp.sum(jnp.where(text_item[:, None] == item_ids, lengths, 0), axis=1)
    valid = jnp.where(
        text_spot < 0, spots % PATCH_STRIDE < PATCHES, text_spot - text_item * TEXT_STRIDE < text_end
    )
    valid = valid.astype(f32)[:, None]
    meta = jnp.concatenate([lengths, (block_rows - used)[None]])

    def rows_of(count, kind):
        return ((count, model_width), kind, whole(count, model_width))

    def plain(values):
        return (values, whole(*values.shape))

    def heads_out():
        return [
            ((2, all_rows, 3 * width), bf16, stepped(1, all_rows, 3 * width)),
            ((2, all_rows, width), bf16, stepped(1, all_rows, width)),
            (
                (2, items, heads, ITEM_ROWS, ITEM_ROWS),
                bf16,
                stepped(1, items, heads, ITEM_ROWS, ITEM_ROWS),
            ),
        ]

    def part_weight(values, first, count=2):
        return (values, stepped_pair(count, 1, *values.shape[2:], first=first))

    def grad_out(count):
        shape = (2, 8, count, piece, model_width)
        return (shape, bf16, stepped(1, *shape[1:]))

    head_sizes = dict(items=items, heads=heads)
    row_sizes = dict(main_rows=main_rows, all_rows=all_rows)

    def attention(raw, weights):
        return call(
            functools.partial(attention_kernel, **head_sizes, **row_sizes),
            "attention",
            2,
            [plain(raw), plain(place_row), plain(hidden), plain(norm_params), plain(extra_params)]
            + [(weights, stepped(1, model_width, model_width))],
            [rows_of(all_rows, f32), rows_of(all_rows, bf16), rows_of(all_rows, f32)] + heads_out(),
            [],
            ATTENTION_US,
            (meta,),
        )

    def attention_end(normed, block_input, residual, weights):
        return call(
            functools.partial(attention_end_kernel, **head_sizes, **row_sizes),
            "attention_end",
            2,
            [plain(normed), plain(block_input), plain(residual), plain(valid), plain(norm_params)]
            + [(weights, stepped(1, model_width, model_width, first=2))],
            [rows_of(all_rows, f32)] + heads_out() + [rows_of(all_rows, bf16), rows_of(1, f32)],
            [],
            ATTENTION_US,
            (meta,),
        )

    def lift(feed_input, weights):
        shape = (parts, all_rows, hidden_width)
        return call(
            functools.partial(lift_kernel, vision_rows=vision_rows, all_rows=all_rows),
            "lift",
            parts,
            [plain(feed_input), part_weight(weights, 0)],
            [(shape, bf16, stepped(1, *shape[1:]))] * 2,
            [],
            LIFT_US,
        )

    def place_grad(raw):
        return call(
            functools.partial(place_grad_kernel, vision_rows=vision_rows),
            "place_grad",
            1,
            [plain(raw), plain(place_row)],
            [rows_of(main_rows, bf16), rows_of(2, f32)],
            [],
            5,
        )

    def drop_weight_grad(grad_rows, acted, first):
        return call(
            functools.partial(drop_weight_kernel, vision_rows=vision_rows),
            "drop_weight_grad",
            2,
            [plain(grad_rows), (acted, stepped(1, main_rows, hidden_width, first=first))],
            [grad_out(2)],
            [],
            DROP_WEIGHT_US,
            (mine,),
        )[0]

    def expert_ins(grad_rows, slope, feed_input, drop_weights, lift_weights, first):
        return [
            plain(grad_rows),
            (slope, stepped(1, main_rows, hidden_width, first=first)),
            (feed_input, whole(main_rows, model_width)),
            part_weight(drop_weights, first),
            part_weight(lift_weights, first),
        ]

    def expert_back(*args):
        return call(
            functools.partial(expert_back_kernel, vision_rows=vision_rows),
            "expert_back",
            2,
            expert_ins(*args, 0),
            [grad_out(2), rows_of(main_rows, f32)],
            [pltpu.VMEM((main_rows, hidden_width), bf16)],
            EXPERT_BACK_US,
            (mine,),
        )

    def expert_back_end(before, residual, *args):
        return call(
            functools.partial(expert_back_end_kernel, vision_rows=vision_rows),
            "expert_back_end",
            2,
            expert_ins(*args, 2)
            + [plain(before), (residual, whole(main_rows, model_width)), plain(norm_params)],
            [grad_out(2), rows_of(main_rows, f32), rows_of(main_rows, bf16), rows_of(2, f32)],
            [pltpu.VMEM((main_rows, hidden_width), bf16)],
            EXPERT_BACK_US,
            (mine,),
        )

    def heads_ins(grad_attended, joint_rows, mixed, probs, normed, weights, first):
        return [
            plain(grad_attended),
            (joint_rows, stepped(1, main_rows, 3 * width)),
            (mixed, stepped(1, main_rows, width)),
            (probs, stepped(1, *probs.shape[1:])),
            (normed, whole(main_rows, model_width)),
            (weights, stepped(1, model_width, model_width, first=first)),
        ]

    heads_scratch = [
        pltpu.VMEM((main_rows, width), bf16),
        pltpu.VMEM((main_rows, 3 * width), bf16),
    ]

    def attention_back(*args):
        return call(
            functools.partial(attention_back_kernel, **head_sizes),
            "attention_back",
            2,
            heads_ins(*args, 0),
            [grad_out(1), rows_of(main_rows, f32)],
            heads_scratch,
            ATTENTION_BACK_US,
            (mine,),
        )

    def attention_back_end(before, grad_residual, block_input, *args):
        return call(
            functools.partial(attention_back_end_kernel, **head_sizes),
            "attention_back_end",
            2,
            heads_ins(*args, 2)
            + [
                plain(before),
                plain(grad_residual),
                (block_input, whole(main_rows, model_width)),
                (hidden, whole(main_rows, 1)),
                plain(place_column),
                plain(norm_params),
            ],
            [grad_out(1), rows_of(block_rows, bf16), rows_of(2, f32), rows_of(1, f32)],
            [pltpu.VMEM((main_rows, model_width), f32)] + heads_scratch,
            ATTENTION_BACK_US,
            (mine,),
        )

    def drop(acted, residual, weights):
        return call(
            functools.partial(drop_kernel, vision_rows=vision_rows, all_rows=all_rows),
            "drop",
            parts,
            [(acted, stepped(1, all_rows, hidden_width)), plain(residual), plain(valid)]
            + [plain(place_column), plain(extra_params), part_weight(weights, 0)],
            [rows_of(block_rows, bf16), rows_of(2, f32)],
            [pltpu.VMEM((all_rows, model_width), f32)],
            DROP_US,
        )

    raw_tokens = exchange(tokens)
    if cube:
        line_attend = gather_line(shard_attend)
        plane_attend = gather_plane(line_attend)
        line_lift = gather_line(after(shard_lift, line_attend))
        corner_attend = gather_corner(*plane_attend)
        line_drop = gather_line(after(shard_drop, line_lift))
        attend_all = gather_cores(line_attend, plane_attend, corner_attend)[0]
        plane_lift = gather_plane(after(line_lift, corner_attend))
    else:
        attend_all = gather(shard_attend)[0]

    block_input, normed, residual, *heads_first = attention(raw_tokens, attend_all)
    if cube:
        plane_lift, residual = after((plane_lift, residual))
        corner_lift = gather_corner(*plane_lift)
        raw_grad = exchange(after(cotangent.astype(bf16), plane_lift))
    else:
        raw_grad = exchange(cotangent.astype(bf16))
    residual, *heads_second, feed_input, attended_square = attention_end(
        normed, block_input, residual, attend_all
    )
    if cube:
        corner_lift, feed_input = after((corner_lift, feed_input))
        plane_drop = gather_plane(after(line_drop, corner_lift))
        lift_all = gather_cores(line_lift, plane_lift, corner_lift)
    else:
        lift_all = gather(shard_lift)
    acted, slope = lift(feed_input, lift_all)
    if cube:
        plane_drop, acted, slope, raw_grad = after((plane_drop, acted, slope, raw_grad))
        corner_drop = gather_corner(*plane_drop)
    grad_rows, grad_bias = place_grad(raw_grad)
    drop_send = drop_weight_grad(grad_rows, acted, 0)
    if cube:
        drop_received = swap(drop_send, "mp", 1)
    drop_keep = drop_weight_grad(grad_rows, after(acted, drop_send), 2)
    if cube:
        corner_drop, drop_keep = after((corner_drop, drop_keep))
        drop_all = gather_cores(line_drop, plane_drop, corner_drop)
        drop_all, drop_received = after((drop_all, drop_received))
        corner = scatter_corner(drop_keep, drop_received)
        corner, grad_rows = after((corner, grad_rows))
        from_corner = send_corner(corner)
    else:
        drop_all = gather(shard_drop)
        drop_grad = scatter(drop_keep, drop_send)

    lift_send, grad_feed = expert_back(grad_rows, slope, feed_input, drop_all, lift_all)
    if cube:
        lift_received = swap(lift_send, "mp", 1)
        from_corner, grad_feed = after((from_corner, grad_feed))
        plane = scatter_plane(drop_keep, drop_received, *from_corner)
        plane, grad_feed = after((plane, grad_feed))
        from_plane = send_plane(*plane)
    lift_keep, grad_residual, grad_attended, grad_norm_second = expert_back_end(
        grad_feed, residual, grad_rows, slope, feed_input, drop_all, lift_all
    )
    if cube:
        lift_received, from_plane, grad_attended = after((lift_received, from_plane, grad_attended))
        line = scatter_line(drop_keep, drop_received, *from_plane)
        lift_corner = scatter_corner(lift_keep, lift_received)
        line, lift_corner, grad_attended = after((line, lift_corner, grad_attended))
        from_line = send_line(line)
        from_corner = send_corner(lift_corner)
    else:
        lift_grad = scatter(lift_keep, lift_send)

    attend_send, grad_normed = attention_back(grad_attended, *heads_first, normed, attend_all)
    if cube:
        attend_received = swap(attend_send, "mp", 1)
        from_line, from_corner, grad_normed = after((from_line, from_corner, grad_normed))
        drop_grad = add(line[0], *from_line)
        plane = scatter_plane(lift_keep, lift_received, *from_corner)
        plane, grad_normed = after((plane, grad_normed))
        from_plane = send_plane(*plane)
    attend_keep, grad_raw, grad_norm_first, grad_mask = attention_back_end(
        grad_normed, grad_residual, block_input, grad_attended, *heads_second, normed, attend_all
    )
    if cube:
        attend_received, from_plane, attend_keep = after((attend_received, from_plane, attend_keep))
        line = scatter_line(lift_keep, lift_received, *from_plane)
        attend_corner = scatter_corner(attend_keep, attend_received)
        line, attend_corner, acted = after((line, attend_corner, acted))
        from_line = send_line(line)
        from_corner = send_corner(attend_corner)
    input_grad = give_back(grad_raw).astype(f32)
    raw_out, feed_square = drop(acted, residual, drop_all)
    block_output = give_back(raw_out).astype(f32)
    if cube:
        from_line, from_corner, raw_out = after((from_line, from_corner, raw_out))
        lift_grad = add(line[0], *from_line)
        from_plane = send_plane(*scatter_plane(attend_keep, attend_received, *from_corner))
        line = scatter_line(attend_keep, attend_received, *from_plane)
        attend_grad = add(line[0], *send_line(line))[0]
    else:
        attend_grad = scatter(attend_keep, attend_send)[0]

    squares = jnp.stack(
        [jnp.sum(feed_square[0]), jnp.sum(attended_square), jnp.sum(feed_square[1]), used.astype(f32)]
    )
    small = jnp.concatenate(
        [
            grad_norm_first,
            grad_norm_second,
            grad_bias,
            grad_mask,
            jnp.pad(squares, (0, model_width - 4))[None],
        ],
        axis=0,
    )
    if cube:
        for axis, bit in (("mp", 1), ("mp", 2), ("dp", 1), ("dp", 2), ("dp", 4)):
            small = small + swap(small, axis, bit)
    else:
        small = lax.psum(small, ("dp", "mp"))
    norm_total, extra_total = small[:4], small[4:7]
    rms_values = jnp.sqrt(small[7, :3] / (small[7, 3] * model_width))

    joint_grad = jnp.stack([attend_grad[:, k * width : (k + 1) * width] for k in range(3)])
    output_grad = attend_grad[:, 3 * width :].T
    drop_grad = jnp.swapaxes(drop_grad, 1, 2)
    results = [block_output, input_grad, rms_values]
    results += adamw(joint_weight, joint_first, joint_second, joint_grad, matrix_rate, weight_decay)
    results += adamw(output_weight, output_first, output_second, output_grad, matrix_rate, weight_decay)
    results += adamw(lift_weight, lift_first, lift_second, lift_grad, matrix_rate, weight_decay)
    results += adamw(drop_weight, drop_first, drop_second, drop_grad, matrix_rate, weight_decay)
    results += adamw(norm_params, norm_first, norm_second, norm_total, vector_rate, 0.0)
    results += adamw(extra_params, extra_first, extra_second, extra_total, vector_rate, 0.0)
    return tuple(results)


def solution(mesh):
    rows = P(None, ("dp", "mp"), None)
    joint, output, lift, drop = (
        P(None, "dp", "mp"),
        P("mp", "dp"),
        P(None, "dp", "mp"),
        P(None, "mp", "dp"),
    )
    return jax.shard_map(
        body,
        mesh=mesh,
        in_specs=(rows, rows, P(None, "dp"), P(None, "dp"), P(None, "dp", None))
        + (joint,) * 3
        + (output,) * 3
        + (lift,) * 3
        + (drop,) * 3
        + (P(),) * 6,
        out_specs=(rows, rows, P())
        + (joint,) * 4
        + (output,) * 4
        + (lift,) * 4
        + (drop,) * 4
        + (P(),) * 8,
        check_vma=False,
    )
```

time: 761 us -> 552 us (0.73); the launches traced: 760 us -> 542 us
  waiting for transfers between devices: 443 us -> 130 us
  starting transfers between devices: 15.7 us -> 86.1 us
  Pallas kernels: 194 us -> 243 us
  blocking collectives: 45.9 us -> 0 us
  other arithmetic: 29.9 us -> 50.5 us
  local copies, waits for them, and re-layouts: 14.4 us -> 28.6 us
  between operations: 16.4 us -> 3.83 us
    reduce_scatter x2 -> x0, waiting for transfers between devices: 268 us -> none  [scatter(): lax.psum_scatter(values, ('mp', 'dp'), scatter_dimension=axis, tiled=True)]
    all_gather x3 -> x0, waiting for transfers between devices: 151 us -> none  [gather(): return lax.all_gather(values, ('mp', 'dp'), axis=axis, tiled=True)]
    ppermute x0 -> x65, waiting for transfers between devices: none -> 130 us  [swap(): return lax.ppermute(values, axis, [(i, i ^ bit) for i in range(size)])]
    ppermute x0 -> x65, starting transfers between devices: none -> 69.9 us  [swap(): return lax.ppermute(values, axis, [(i, i ^ bit) for i in range(size)])]
    psum x1 -> x0, blocking collectives: 45.9 us -> none  [body(): small = lax.psum(small, ('dp', 'mp'))]
    pallas_call x6 -> x11, Pallas kernels: 194 us -> 225 us  [call(): pl.pallas_call(kernel, name=name, grid_spec=pltpu.PrefetchScalarGridSpec(...]
    pallas_call x0 -> x3, Pallas kernels: none -> 18.1 us  [assemble(): pl.pallas_call(assemble_kernel, name='assemble', grid_spec=pltpu.Prefetch...]
    all_to_all x2, waiting for transfers between devices: 12.6 us -> 0.01 us  [exchange(): lax.all_to_all(values, 'mp', split_axis=0, concat_axis=1, tiled=True)[0]]
  transfers between devices with their start and end apart: 10 -> 69, of which waited for: 7 -> 25; matrix products, arithmetic and copies ran while one was open for 5% -> 10% of each run, Pallas kernels for 12% -> 39%
where the time goes in v2:
time: 552 us; the launch traced here: 542 us
  Pallas kernels  243 us (44%)
  waiting for transfers between devices  130 us (24%)
  starting transfers between devices  86.1 us (16%)
  other arithmetic  50.5 us (9%)
  local copies, waits for them, and re-layouts  28.6 us (5%)
    pallas_call x11, Pallas kernels, call(): pl.pallas_call(kernel, name=name, grid_spec=pltpu.PrefetchScalarGridSpec(...  225 us
    ppermute x65, waiting for transfers between devices, swap(): return lax.ppermute(values, axis, [(i, i ^ bit) for i in range(size)])  130 us
    ppermute x65, starting transfers between devices, swap(): return lax.ppermute(values, axis, [(i, i ^ bit) for i in range(size)])  69.9 us
    pallas_call x3, Pallas kernels, assemble(): pl.pallas_call(assemble_kernel, name='assemble', grid_spec=pltpu.Prefetch...  18.1 us
    unnamed x107, local copies, waits for them, and re-layouts  14.1 us
  transfers between devices with their start and end apart: 69, of which 25 were waited for; matrix products, arithmetic and copies ran while one was open for 10% of the time, Pallas kernels for 39%

profile of v2, /device:TPU:0, one launch (start us, length us, event | category | flops | bytes accessed | tf_op | source)
XLA Modules:
  0.0 541.8 jit_solution(16061643426518184903)
XLA Ops:
  2.9 5.1 collective-permute-start.2
  8.6 4.3 all-to-all-start
  14.2 6.2 %collective-permute-done.1 = bf16[1,96,768]{2,1,0:T(8,128)(2,1)S(1)} collective-permute-done((bf16[1,96,768]{2,1,0:T(8,128)(2,1)S(1)}, bf16[1,96,768]{2,1,0:T(8,128)(2,1)S(1)}, u32[]{:S(2)}, u32[]{:S(2)}) %collective-permute-start.1) | collective-permute-done | bytes 147488 | tf_op jit(solution)/shard_map/ppermute | solution.py:752
  25.1 2.6 collective-permute-start.5
  29.5 5.5 %collective-permute-done.9.refs_1_ = bf16[4,1,96,768]{3,2,1,0:T(8,128)(2,1)S(1)} collective-permute-done((bf16[4,1,96,768]{3,2,1,0:T(8,128)(2,1)S(1)}, bf16[4,1,96,768]{3,2,1,0:T(8,128)(2,1)S(1)}, u32[]{:S(2)}, u32[]{:S(2)}) %collective-permute-start.9) | collective-permute-done | bytes 589856 | tf_op jit(solution)/shard_map/ppermute | solution.py:752
  36.6 8.5 %collective-permute-done.11.refs_2_ = bf16[4,1,96,768]{3,2,1,0:T(8,128)(2,1)} collective-permute-done((bf16[4,1,96,768]{3,2,1,0:T(8,128)(2,1)S(1)}, bf16[4,1,96,768]{3,2,1,0:T(8,128)(2,1)}, u32[]{:S(2)}, u32[]{:S(2)}) %collective-permute-start.11) | collective-permute-done | bytes 589856 | tf_op jit(solution)/shard_map/ppermute | solution.py:752
  48.4 2.1 collective-permute-done.4
  51.7 2.6 collective-permute-done.12.refs_4_
  58.5 6.8 %assemble.3 = bf16[1,4,768,768]{3,2,1,0:T(8,128)(2,1)S(1)} custom-call(s32[2]{0:T(128)S(1)} %pad_add_fusion.mine_ref, bf16[4,1,96,768]{3,2,1,0:T(8,128)(2,1)S(1)} %pad_maximum_fusion.6.refs_0_, bf16[4,1,96,768]{3,2,1,0:T(8,128)(2,1)S(1)} %collective-permute-done.9.refs_1_, bf16[4,1,96,768]{3,2,1,0:T(8,128)(2,1)} %collective-permute-done.11.refs_2_, ...), custom_call_target="tpu_custom_call" | custom-call | bytes 9437184 | tf_op jit(solution)/shard_map/assemble/pallas_call | solution.py:671
  65.3 2.1 copy-done.4
  67.5 29.7 %attention.1 = (f32[1168,768]{1,0:T(8,128)}, bf16[1168,768]{1,0:T(8,128)(2,1)}, f32[1168,768]{1,0:T(8,128)}, bf16[2,1168,576]{2,1,0:T(8,128)(2,1)}, bf16[2,1168,...) custom-call(s32[5]{0:T(128)} %pad_add_fusion.1.meta_ref, bf16[960,768]{1,0:T(8,128)(2,1)} %bitcast.22.raw_ref, ...), custom_call_target="tpu_custom_call" | custom-call | flops 25999998976 | bytes 26000000 | tf_op jit(solution)/shard_map/attention/pallas_call | solution.py:620
  100.4 3.8 collective-permute-start.8
  106.8 5.4 collective-permute-done.8
  112.8 2.2 collective-permute-done.21.refs_4_
  115.0 30.0 %attention_end.1 = (f32[1168,768]{1,0:T(8,128)}, bf16[2,1168,576]{2,1,0:T(8,128)(2,1)}, bf16[2,1168,192]{2,1,0:T(8,128)(2,1)}, bf16[2,4,3,256,256]{4,3,2,1,0:T(8...) custom-call(s32[5]{0:T(128)} %pad_add_fusion.1.meta_ref, bf16[1168,768]{1,0:T(8,128)(2,1)} %get-tuple-element.121.normed_ref, ...), custom_call_target="tpu_custom_call" | custom-call | flops 25999998976 | bytes 26000000 | tf_op jit(solution)/shard_map/attention_end/pallas_call | solution.py:620
  148.1 4.6 all-to-all-start.1
  155.1 6.6 %assemble.4.weight_ref.lift_ref = bf16[2,4,768,768]{3,2,1,0:T(8,128)(2,1)S(1)} custom-call(s32[2]{0:T(128)S(1)} %pad_add_fusion.mine_ref, bf16[4,2,96,768]{3,2,1,0:T(8,128)(2,1)S(1)} %pad_maximum_fusion.refs_0_, bf16[4,2,96,768]{3,2,1,0:T(8,128)(2,1)S(1)} %collective-permute-done.13.refs_1_, bf16[4,2,96,768]{3,2,1,0:T(8,128)(2,1)} %collective-permute-done.14.refs_2_, ...), custom_call_target="tpu_custom_call" | custom-call | bytes 18874368 | tf_op jit(solution)/shard_map/assemble/pallas_call | solution.py:671
  161.7 3.5 copy-done.3
  165.2 17.3 %lift.1 = (bf16[4,1168,768]{2,1,0:T(8,128)(2,1)}, bf16[4,1168,768]{2,1,0:T(8,128)(2,1)}) custom-call(bf16[1168,768]{1,0:T(8,128)(2,1)} %get-tuple-element.128.feed_ref, bf16[2,4,768,768]{3,2,1,0:T(8,128)(2,1)} %copy-done.3), custom_call_target="tpu_custom_call" | custom-call | flops 16999999488 | bytes 17000000 | tf_op jit(solution)/shard_map/lift/pallas_call | solution.py:620
  182.5 14.5 %collective-permute-done.23.refs_2_ = bf16[4,2,96,768]{3,2,1,0:T(8,128)(2,1)} collective-permute-done((bf16[4,2,96,768]{3,2,1,0:T(8,128)(2,1)S(1)}, bf16[4,2,96,768]{3,2,1,0:T(8,128)(2,1)}, u32[]{:S(2)}, u32[]{:S(2)}) %collective-permute-start.23) | collective-permute-done | bytes 1179680 | tf_op jit(solution)/shard_map/ppermute | solution.py:752
  197.0 4.9 place_grad.1
  201.9 7.5 %drop_weight_grad.2 = bf16[2,8,2,96,768]{4,3,2,1,0:T(8,128)(2,1)} custom-call(s32[2]{0:T(128)} %copy-done.5, bf16[1024,768]{1,0:T(8,128)(2,1)} %get-tuple-element.142.grad_ref, bf16[4,1168,768]{2,1,0:T(8,128)(2,1)} %get-tuple-element.184.acted_ref), custom_call_target="tpu_custom_call" | custom-call | flops 8000000000 | bytes 8000000 | tf_op jit(solution)/shard_map/drop_weight_grad/pallas_call | solution.py:620
  213.5 12.7 %collective-permute-done.29.refs_3_ = bf16[2,2,96,768]{3,2,1,0:T(8,128)(2,1)S(1)} collective-permute-done((bf16[2,2,96,768]{3,2,1,0:T(8,128)(2,1)S(1)}, bf16[2,2,96,768]{3,2,1,0:T(8,128)(2,1)S(1)}, u32[]{:S(2)}, u32[]{:S(2)}) %collective-permute-start.29) | collective-permute-done | bytes 589856 | tf_op jit(solution)/shard_map/ppermute | solution.py:752
  226.7 7.5 %drop_weight_grad.3 = bf16[2,8,2,96,768]{4,3,2,1,0:T(8,128)(2,1)} custom-call(s32[2]{0:T(128)} %copy-done.5, bf16[1024,768]{1,0:T(8,128)(2,1)} %get-tuple-element.142.grad_ref, bf16[4,1168,768]{2,1,0:T(8,128)(2,1)} %get-tuple-element.184.acted_ref), custom_call_target="tpu_custom_call" | custom-call | flops 8000000000 | bytes 8000000 | tf_op jit(solution)/shard_map/drop_weight_grad/pallas_call | solution.py:620
  234.1 7.3 %collective-permute-done.30.refs_4_ = bf16[2,2,96,768]{3,2,1,0:T(8,128)(2,1)S(1)} collective-permute-done((bf16[2,2,96,768]{3,2,1,0:T(8,128)(2,1)}, bf16[2,2,96,768]{3,2,1,0:T(8,128)(2,1)S(1)}, u32[]{:S(2)}, u32[]{:S(2)}) %collective-permute-start.30) | collective-permute-done | bytes 589856 | tf_op jit(solution)/shard_map/ppermute | solution.py:752
  244.3 4.7 assemble.5.drop_ref.weight_ref
  249.1 3.7 copy-done.2
  252.8 4.5 convert_add_fusion.2
  257.3 18.2 %expert_back.1 = (bf16[2,8,2,96,768]{4,3,2,1,0:T(8,128)(2,1)}, f32[1024,768]{1,0:T(8,128)}) custom-call(s32[2]{0:T(128)} %copy-done.5, bf16[1024,768]{1,0:T(8,128)(2,1)} %get-tuple-element.142.grad_ref, bf16[4,1168,768]{2,1,0:T(8,128)(2,1)} %get-tuple-element.143.slope_ref, bf16[1168,768]{1,0:T(8,128)(2,1)} %get-tuple-element.128.feed_ref, ...), custom_call_target="tpu_custom_call" | custom-call | flops 17999998976 | bytes 18000000 | tf_op jit(solution)/shard_map/expert_back/pallas_call | solution.py:620
  283.8 8.8 %collective-permute-done.37 = bf16[2,2,96,768]{3,2,1,0:T(8,128)(2,1)} collective-permute-done((bf16[2,2,96,768]{3,2,1,0:T(8,128)(2,1)}, bf16[2,2,96,768]{3,2,1,0:T(8,128)(2,1)}, u32[]{:S(2)}, u32[]{:S(2)}) %collective-permute-start.37) | collective-permute-done | bytes 589856 | tf_op jit(solution)/shard_map/ppermute | solution.py:752
  296.6 23.6 %expert_back_end.1 = (bf16[2,8,2,96,768]{4,3,2,1,0:T(8,128)(2,1)}, f32[1024,768]{1,0:T(8,128)}, bf16[1024,768]{1,0:T(8,128)(2,1)}, f32[2,768]{1,0:T(2,128)}) custom-call(s32[2]{0:T(128)} %copy-done.5, bf16[1024,768]{1,0:T(8,128)(2,1)} %get-tuple-element.142.grad_ref, bf16[4,1168,768]{2,1,0:T(8,128)(2,1)} %get-tuple-element.143.slope_ref, ...), custom_call_target="tpu_custom_call" | custom-call | flops 17999998976 | bytes 18000000 | tf_op jit(solution)/shard_map/expert_back_end/pallas_call | solution.py:620
  323.1 2.6 fusion.1
  326.2 3.1 convert_add_fusion
  330.2 9.8 %collective-permute-start.43 = (bf16[2,96,768]{2,1,0:T(8,128)(2,1)}, bf16[2,96,768]{2,1,0:T(8,128)(2,1)S(1)}, u32[]{:S(2)}, u32[]{:S(2)}) collective-permute-start(bf16[2,96,768]{2,1,0:T(8,128)(2,1)} %get-tuple-element.357), channel_id=1, source_target_pairs={{0,8},{4,12},{8,0},{12,4},{16,24},{20,28},{24,16},{28,20},{1,9},{5... | collective-permute-start | bytes 884744 | tf_op jit(solution)/shard_map/ppermute | solution.py:752
  345.4 26.7 %attention_back.1 = (bf16[2,8,1,96,768]{4,3,2,1,0:T(8,128)(2,1)}, f32[1024,768]{1,0:T(8,128)}) custom-call(s32[2]{0:T(128)} %copy-done.5, bf16[1024,768]{1,0:T(8,128)(2,1)} %get-tuple-element.161.grad_attended_ref, bf16[2,1168,576]{2,1,0:T(8,128)(2,1)} %get-tuple-element.162.joint_ref, bf16[2,1168,192]{2,1,0:T(8,128)(2,1)} %get-tuple-element.163.mixed_ref, ...), custom_call_target="tpu_custom_call" | custom-call | flops 27000000512 | bytes 27000000 | tf_op jit(solution)/shard_map/attention_back/pallas_call | solution.py:620
  377.3 34.8 %attention_back_end.1 = (bf16[2,8,1,96,768]{4,3,2,1,0:T(8,128)(2,1)}, bf16[960,768]{1,0:T(8,128)(2,1)}, f32[2,768]{1,0:T(2,128)}, f32[1,768]{1,0:T(1,128)}) custom-call(s32[2]{0:T(128)} %copy-done.5, bf16[1024,768]{1,0:T(8,128)(2,1)} %get-tuple-element.161.grad_attended_ref, bf16[2,1168,576]{2,1,0:T(8,128)(2,1)} %get-tuple-element.174.joint_ref, ...), custom_call_target="tpu_custom_call" | custom-call | flops 27000000512 | bytes 27000000 | tf_op jit(solution)/shard_map/attention_back_end/pallas_call | solution.py:620
  412.1 3.6 all-to-all-start.3
  415.7 3.1 fusion.3
  418.8 3.2 convert_add_fusion.5
  422.1 24.9 %drop.1 = (bf16[960,768]{1,0:T(8,128)(2,1)}, f32[2,768]{1,0:T(2,128)}) custom-call(bf16[4,1168,768]{2,1,0:T(8,128)(2,1)} %get-tuple-element.184.acted_ref, f32[1168,768]{1,0:T(8,128)} %get-tuple-element.151.residual_ref, f32[1168,1]{1,0:T(8,128)} %fusion.24.valid_ref, s32[960,1]{1,0:T(8,128)} %select_select_fusion.place_ref, f32[3,768]{1,0:T(4,128)} %extra_ref.3, ...), custom_call_target="tpu_custom_call" | custom-call | flops 24000000000 | bytes 24000000 | tf_op jit(solution)/shard_map/drop/pallas_call | solution.py:620
  454.5 2.1 collective-permute-done.51
  458.8 3.3 fusion.61
  463.9 3.8 all-to-all-start.2
  475.1 24.6 %collective-permute-done.54 = f32[8,768]{1,0:T(8,128)S(1)} collective-permute-done((f32[8,768]{1,0:T(8,128)S(1)}, f32[8,768]{1,0:T(8,128)S(1)}, u32[]{:S(2)}, u32[]{:S(2)}) %collective-permute-start.54) | collective-permute-done | bytes 24608 | tf_op jit(solution)/shard_map/ppermute | solution.py:752
  502.8 4.7 collective-permute-done.59
  511.6 9.2 %collective-permute-done.61 = bf16[4,1,96,768]{3,2,1,0:T(8,128)(2,1)S(1)} collective-permute-done((bf16[4,1,96,768]{3,2,1,0:T(8,128)(2,1)S(1)}, bf16[4,1,96,768]{3,2,1,0:T(8,128)(2,1)S(1)}, u32[]{:S(2)}, u32[]{:S(2)}) %collective-permute-start.61) | collective-permute-done | bytes 589856 | tf_op jit(solution)/shard_map/ppermute | solution.py:752
  523.4 2.4 collective-permute-start.64
  530.8 4.5 collective-permute-done.63
  (301 shorter events, 104.9 us)
Async XLA Ops:
  8.0 12.5 %collective-permute-start.1 = (bf16[1,96,768]{2,1,0:T(8,128)(2,1)S(1)}, bf16[1,96,768]{2,1,0:T(8,128)(2,1)S(1)}, u32[]{:S(2)}, u32[]{:S(2)}) collective-permute-start(bf16[1,96,768]{2,1,0:T(8,128)(2,1)S(1)} %pad_maximum_fusion.10), channel_id=1, source_target_pairs={{0,16},{4,20},{8,24},{12,28},{16,0},{20,4},{24,8},{28,12},{1,17},{... | collective-permute-start | bytes 442376 | tf_op jit(solution)/shard_map/ppermute | solution.py:752
  8.6 58.8 %all-to-all-start = ((bf16[4,240,768]{2,1,0:T(8,128)(2,1)}), bf16[4,240,768]{2,1,0:T(8,128)(2,1)}, u32[]{:S(2)}, u32[]{:S(2)}) async-start(bf16[4,240,768]{2,1,0:T(8,128)(2,1)} %param.23), calls=%async_computation | async-start | bytes 2949120 | tf_op jit(solution)/shard_map/all_to_all | solution.py:755
  20.6 14.4 %collective-permute-start.9 = (bf16[4,1,96,768]{3,2,1,0:T(8,128)(2,1)S(1)}, bf16[4,1,96,768]{3,2,1,0:T(8,128)(2,1)S(1)}, u32[]{:S(2)}, u32[]{:S(2)}) collective-permute-start(bf16[4,1,96,768]{3,2,1,0:T(8,128)(2,1)S(1)} %pad_maximum_fusion.6.refs_0_), channel_id=1, source_target_pairs={{0,4},{4,0},{8,12},{12,8},{16,20},{20,16},{24,28},{28,24},{1,5},{5... | collective-permute-start | bytes 1769480 | tf_op jit(solution)/shard_map/ppermute | solution.py:752
  22.1 23.0 %collective-permute-start.11 = (bf16[4,1,96,768]{3,2,1,0:T(8,128)(2,1)S(1)}, bf16[4,1,96,768]{3,2,1,0:T(8,128)(2,1)}, u32[]{:S(2)}, u32[]{:S(2)}) collective-permute-start(bf16[4,1,96,768]{3,2,1,0:T(8,128)(2,1)S(1)} %pad_maximum_fusion.6.refs_0_), channel_id=1, source_target_pairs={{0,2},{1,3},{2,0},{3,1},{4,6},{5,7},{6,4},{7,5},{8,10},{9,11},{10,... | collective-permute-start | bytes 1769480 | tf_op jit(solution)/shard_map/ppermute | solution.py:752
  25.1 23.4 %collective-permute-start.5 = (bf16[2,96,768]{2,1,0:T(8,128)(2,1)S(1)}, bf16[2,96,768]{2,1,0:T(8,128)(2,1)S(1)}, u32[]{:S(2)}, u32[]{:S(2)}) collective-permute-start(bf16[2,96,768]{2,1,0:T(8,128)(2,1)S(1)} %convert_element_type.391), channel_id=1, source_target_pairs={{0,24},{4,28},{8,16},{12,20},{16,8},{20,12},{24,0},{28,4},{1,25},{... | collective-permute-start | bytes 884744 | tf_op jit(solution)/shard_map/ppermute | solution.py:752
  27.6 22.9 %collective-permute-start.4 = (bf16[2,96,768]{2,1,0:T(8,128)(2,1)S(1)}, bf16[2,96,768]{2,1,0:T(8,128)(2,1)S(1)}, u32[]{:S(2)}, u32[]{:S(2)}) collective-permute-start(bf16[2,96,768]{2,1,0:T(8,128)(2,1)S(1)} %convert_element_type.391), channel_id=1, source_target_pairs={{0,16},{4,20},{8,24},{12,28},{16,0},{20,4},{24,8},{28,12},{1,17},{... | collective-permute-start | bytes 884744 | tf_op jit(solution)/shard_map/ppermute | solution.py:752
  27.6 22.9 %collective-permute-start.3 = (bf16[2,96,768]{2,1,0:T(8,128)(2,1)S(1)}, bf16[2,96,768]{2,1,0:T(8,128)(2,1)S(1)}, u32[]{:S(2)}, u32[]{:S(2)}) collective-permute-start(bf16[2,96,768]{2,1,0:T(8,128)(2,1)S(1)} %convert_element_type.391), channel_id=1, source_target_pairs={{0,8},{4,12},{8,0},{12,4},{16,24},{20,28},{24,16},{28,20},{1,9},{5... | collective-permute-start | bytes 884744 | tf_op jit(solution)/shard_map/ppermute | solution.py:752
  35.0 16.6 %collective-permute-start.10 = (bf16[2,1,96,768]{3,2,1,0:T(8,128)(2,1)S(1)}, bf16[2,1,96,768]{3,2,1,0:T(8,128)(2,1)S(1)}, u32[]{:S(2)}, u32[]{:S(2)}) collective-permute-start(bf16[2,1,96,768]{3,2,1,0:T(8,128)(2,1)S(1)} %slice.346), channel_id=1, source_target_pairs={{0,2},{1,3},{2,0},{3,1},{4,6},{5,7},{6,4},{7,5},{8,10},{9,11},{10,... | collective-permute-start | bytes 884744 | tf_op jit(solution)/shard_map/ppermute | solution.py:752
  56.2 41.0 %collective-permute-start.13 = (bf16[4,2,96,768]{3,2,1,0:T(8,128)(2,1)S(1)}, bf16[4,2,96,768]{3,2,1,0:T(8,128)(2,1)S(1)}, u32[]{:S(2)}, u32[]{:S(2)}) collective-permute-start(bf16[4,2,96,768]{3,2,1,0:T(8,128)(2,1)S(1)} %pad_maximum_fusion.refs_0_), channel_id=1, source_target_pairs={{0,4},{4,0},{8,12},{12,8},{16,20},{20,16},{24,28},{28,24},{1,5},{5... | collective-permute-start | bytes 3538952 | tf_op jit(solution)/shard_map/ppermute | solution.py:752
  57.9 39.3 %collective-permute-start.14 = (bf16[4,2,96,768]{3,2,1,0:T(8,128)(2,1)S(1)}, bf16[4,2,96,768]{3,2,1,0:T(8,128)(2,1)}, u32[]{:S(2)}, u32[]{:S(2)}) collective-permute-start(bf16[4,2,96,768]{3,2,1,0:T(8,128)(2,1)S(1)} %pad_maximum_fusion.refs_0_), channel_id=1, source_target_pairs={{0,2},{1,3},{2,0},{3,1},{4,6},{5,7},{6,4},{7,5},{8,10},{9,11},{10,... | collective-permute-start | bytes 3538952 | tf_op jit(solution)/shard_map/ppermute | solution.py:752
  97.3 15.3 %collective-permute-start.20 = (bf16[2,2,96,768]{3,2,1,0:T(8,128)(2,1)S(1)}, bf16[2,2,96,768]{3,2,1,0:T(8,128)(2,1)}, u32[]{:S(2)}, u32[]{:S(2)}) collective-permute-start(bf16[2,2,96,768]{3,2,1,0:T(8,128)(2,1)S(1)} %slice.266), channel_id=1, source_target_pairs={{0,2},{1,3},{2,0},{3,1},{4,6},{5,7},{6,4},{7,5},{8,10},{9,11},{10,... | collective-permute-start | bytes 1769480 | tf_op jit(solution)/shard_map/ppermute | solution.py:752
  99.9 15.1 %collective-permute-start.21 = (bf16[2,2,96,768]{3,2,1,0:T(8,128)(2,1)S(1)}, bf16[2,2,96,768]{3,2,1,0:T(8,128)(2,1)}, u32[]{:S(2)}, u32[]{:S(2)}) collective-permute-start(bf16[2,2,96,768]{3,2,1,0:T(8,128)(2,1)S(1)} %slice.267), channel_id=1, source_target_pairs={{0,4},{4,0},{8,12},{12,8},{16,20},{20,16},{24,28},{28,24},{1,5},{5... | collective-permute-start | bytes 1769480 | tf_op jit(solution)/shard_map/ppermute | solution.py:752
  106.2 38.8 %collective-permute-start.7 = (bf16[2,96,768]{2,1,0:T(8,128)(2,1)S(1)}, bf16[2,96,768]{2,1,0:T(8,128)(2,1)}, u32[]{:S(2)}, u32[]{:S(2)}) collective-permute-start(bf16[2,96,768]{2,1,0:T(8,128)(2,1)S(1)} %convert_bitcast_fusion), channel_id=1, source_target_pairs={{0,16},{4,20},{8,24},{12,28},{16,0},{20,4},{24,8},{28,12},{1,17},{... | collective-permute-start | bytes 884744 | tf_op jit(solution)/shard_map/ppermute | solution.py:752
  106.2 39.3 %collective-permute-start.6 = (bf16[2,96,768]{2,1,0:T(8,128)(2,1)S(1)}, bf16[2,96,768]{2,1,0:T(8,128)(2,1)}, u32[]{:S(2)}, u32[]{:S(2)}) collective-permute-start(bf16[2,96,768]{2,1,0:T(8,128)(2,1)S(1)} %convert_bitcast_fusion), channel_id=1, source_target_pairs={{0,8},{4,12},{8,0},{12,4},{16,24},{20,28},{24,16},{28,20},{1,9},{5... | collective-permute-start | bytes 884744 | tf_op jit(solution)/shard_map/ppermute | solution.py:752
  112.2 40.4 %collective-permute-start.24 = (bf16[4,2,96,768]{3,2,1,0:T(8,128)(2,1)S(1)}, bf16[4,2,96,768]{3,2,1,0:T(8,128)(2,1)}, u32[]{:S(2)}, u32[]{:S(2)}) collective-permute-start(bf16[4,2,96,768]{3,2,1,0:T(8,128)(2,1)S(1)} %pad_maximum_fusion.refs_0_), channel_id=1, source_target_pairs={{0,1},{1,0},{2,3},{3,2},{4,5},{5,4},{6,7},{7,6},{8,9},{9,8},{10,11... | collective-permute-start | bytes 3538952 | tf_op jit(solution)/shard_map/ppermute | solution.py:752
  112.6 40.5 %collective-permute-start.25 = (bf16[4,2,96,768]{3,2,1,0:T(8,128)(2,1)S(1)}, bf16[4,2,96,768]{3,2,1,0:T(8,128)(2,1)}, u32[]{:S(2)}, u32[]{:S(2)}) collective-permute-start(bf16[4,2,96,768]{3,2,1,0:T(8,128)(2,1)S(1)} %collective-permute-done.13.refs_1_), channel_id=1, source_target_pairs={{0,1},{1,0},{2,3},{3,2},{4,5},{5,4},{6,7},{7,6},{8,9},{9,8},{10,11... | collective-permute-start | bytes 3538952 | tf_op jit(solution)/shard_map/ppermute | solution.py:752
  114.9 40.2 %collective-permute-start.26 = (bf16[4,2,96,768]{3,2,1,0:T(8,128)(2,1)}, bf16[4,2,96,768]{3,2,1,0:T(8,128)(2,1)}, u32[]{:S(2)}, u32[]{:S(2)}) collective-permute-start(bf16[4,2,96,768]{3,2,1,0:T(8,128)(2,1)} %collective-permute-done.14.refs_2_), channel_id=1, source_target_pairs={{0,1},{1,0},{2,3},{3,2},{4,5},{5,4},{6,7},{7,6},{8,9},{9,8},{10,11... | collective-permute-start | bytes 3538952 | tf_op jit(solution)/shard_map/ppermute | solution.py:752
  148.1 34.4 %all-to-all-start.1 = ((bf16[4,240,768]{2,1,0:T(8,128)(2,1)}), bf16[4,240,768]{2,1,0:T(8,128)(2,1)}, u32[]{:S(2)}, u32[]{:S(2)}) async-start(bf16[4,240,768]{2,1,0:T(8,128)(2,1)} %convert_element_type.396), calls=%async_computation.1 | async-start | bytes 2949120 | tf_op jit(solution)/shard_map/all_to_all | solution.py:755
  152.7 29.9 %collective-permute-start.22 = (bf16[4,2,96,768]{3,2,1,0:T(8,128)(2,1)S(1)}, bf16[4,2,96,768]{3,2,1,0:T(8,128)(2,1)}, u32[]{:S(2)}, u32[]{:S(2)}) collective-permute-start(bf16[4,2,96,768]{3,2,1,0:T(8,128)(2,1)S(1)} %pad_maximum_fusion.1.refs_0_), channel_id=1, source_target_pairs={{0,4},{4,0},{8,12},{12,8},{16,20},{20,16},{24,28},{28,24},{1,5},{5... | collective-permute-start | bytes 3538952 | tf_op jit(solution)/shard_map/ppermute | solution.py:752
  153.1 43.9 %collective-permute-start.23 = (bf16[4,2,96,768]{3,2,1,0:T(8,128)(2,1)S(1)}, bf16[4,2,96,768]{3,2,1,0:T(8,128)(2,1)}, u32[]{:S(2)}, u32[]{:S(2)}) collective-permute-start(bf16[4,2,96,768]{3,2,1,0:T(8,128)(2,1)S(1)} %pad_maximum_fusion.1.refs_0_), channel_id=1, source_target_pairs={{0,2},{1,3},{2,0},{3,1},{4,6},{5,7},{6,4},{7,5},{8,10},{9,11},{10,... | collective-permute-start | bytes 3538952 | tf_op jit(solution)/shard_map/ppermute | solution.py:752
  209.4 43.4 %collective-permute-start.36 = (bf16[2,8,2,96,768]{4,3,2,1,0:T(8,128)(2,1)}, bf16[2,8,2,96,768]{4,3,2,1,0:T(8,128)(2,1)}, u32[]{:S(2)}, u32[]{:S(2)}) collective-permute-start(bf16[2,8,2,96,768]{4,3,2,1,0:T(8,128)(2,1)} %drop_weight_grad.2), channel_id=1, source_target_pairs={{0,1},{1,0},{2,3},{3,2},{4,5},{5,4},{6,7},{7,6},{8,9},{9,8},{10,11... | collective-permute-start | bytes 14155784 | tf_op jit(solution)/shard_map/ppermute | solution.py:752
  210.5 15.8 %collective-permute-start.29 = (bf16[2,2,96,768]{3,2,1,0:T(8,128)(2,1)S(1)}, bf16[2,2,96,768]{3,2,1,0:T(8,128)(2,1)S(1)}, u32[]{:S(2)}, u32[]{:S(2)}) collective-permute-start(bf16[2,2,96,768]{3,2,1,0:T(8,128)(2,1)S(1)} %slice.268), channel_id=1, source_target_pairs={{0,2},{1,3},{2,0},{3,1},{4,6},{5,7},{6,4},{7,5},{8,10},{9,11},{10,... | collective-permute-start | bytes 1769480 | tf_op jit(solution)/shard_map/ppermute | solution.py:752
  210.9 30.6 %collective-permute-start.31 = (bf16[4,2,96,768]{3,2,1,0:T(8,128)(2,1)S(1)}, bf16[4,2,96,768]{3,2,1,0:T(8,128)(2,1)S(1)}, u32[]{:S(2)}, u32[]{:S(2)}) collective-permute-start(bf16[4,2,96,768]{3,2,1,0:T(8,128)(2,1)S(1)} %pad_maximum_fusion.1.refs_0_), channel_id=1, source_target_pairs={{0,1},{1,0},{2,3},{3,2},{4,5},{5,4},{6,7},{7,6},{8,9},{9,8},{10,11... | collective-permute-start | bytes 3538952 | tf_op jit(solution)/shard_map/ppermute | solution.py:752
  211.1 33.2 %collective-permute-start.32 = (bf16[4,2,96,768]{3,2,1,0:T(8,128)(2,1)}, bf16[4,2,96,768]{3,2,1,0:T(8,128)(2,1)S(1)}, u32[]{:S(2)}, u32[]{:S(2)}) collective-permute-start(bf16[4,2,96,768]{3,2,1,0:T(8,128)(2,1)} %collective-permute-done.22.refs_1_), channel_id=1, source_target_pairs={{0,1},{1,0},{2,3},{3,2},{4,5},{5,4},{6,7},{7,6},{8,9},{9,8},{10,11... | collective-permute-start | bytes 3538952 | tf_op jit(solution)/shard_map/ppermute | solution.py:752
  213.3 31.0 %collective-permute-start.33 = (bf16[4,2,96,768]{3,2,1,0:T(8,128)(2,1)}, bf16[4,2,96,768]{3,2,1,0:T(8,128)(2,1)S(1)}, u32[]{:S(2)}, u32[]{:S(2)}) collective-permute-start(bf16[4,2,96,768]{3,2,1,0:T(8,128)(2,1)} %collective-permute-done.23.refs_2_), channel_id=1, source_target_pairs={{0,1},{1,0},{2,3},{3,2},{4,5},{5,4},{6,7},{7,6},{8,9},{9,8},{10,11... | collective-permute-start | bytes 3538952 | tf_op jit(solution)/shard_map/ppermute | solution.py:752
  226.3 15.2 %collective-permute-start.30 = (bf16[2,2,96,768]{3,2,1,0:T(8,128)(2,1)}, bf16[2,2,96,768]{3,2,1,0:T(8,128)(2,1)S(1)}, u32[]{:S(2)}, u32[]{:S(2)}) collective-permute-start(bf16[2,2,96,768]{3,2,1,0:T(8,128)(2,1)} %slice.269), channel_id=1, source_target_pairs={{0,4},{4,0},{8,12},{12,8},{16,20},{20,16},{24,28},{28,24},{1,5},{5... | collective-permute-start | bytes 1769480 | tf_op jit(solution)/shard_map/ppermute | solution.py:752
  275.5 47.6 %collective-permute-start.39 = (bf16[2,8,2,96,768]{4,3,2,1,0:T(8,128)(2,1)}, bf16[2,8,2,96,768]{4,3,2,1,0:T(8,128)(2,1)}, u32[]{:S(2)}, u32[]{:S(2)}) collective-permute-start(bf16[2,8,2,96,768]{4,3,2,1,0:T(8,128)(2,1)} %get-tuple-element.153), channel_id=1, source_target_pairs={{0,1},{1,0},{2,3},{3,2},{4,5},{5,4},{6,7},{7,6},{8,9},{9,8},{10,11... | collective-permute-start | bytes 14155784 | tf_op jit(solution)/shard_map/ppermute | solution.py:752
  276.7 15.9 %collective-permute-start.37 = (bf16[2,2,96,768]{3,2,1,0:T(8,128)(2,1)}, bf16[2,2,96,768]{3,2,1,0:T(8,128)(2,1)}, u32[]{:S(2)}, u32[]{:S(2)}) collective-permute-start(bf16[2,2,96,768]{3,2,1,0:T(8,128)(2,1)} %get-tuple-element.359), channel_id=1, source_target_pairs={{0,4},{4,0},{8,12},{12,8},{16,20},{20,16},{24,28},{28,24},{1,5},{5... | collective-permute-start | bytes 1769480 | tf_op jit(solution)/shard_map/ppermute | solution.py:752
  277.1 15.6 %collective-permute-start.38 = (bf16[2,2,96,768]{3,2,1,0:T(8,128)(2,1)}, bf16[2,2,96,768]{3,2,1,0:T(8,128)(2,1)}, u32[]{:S(2)}, u32[]{:S(2)}) collective-permute-start(bf16[2,2,96,768]{3,2,1,0:T(8,128)(2,1)} %get-tuple-element.358), channel_id=1, source_target_pairs={{0,2},{1,3},{2,0},{3,1},{4,6},{5,7},{6,4},{7,5},{8,10},{9,11},{10,... | collective-permute-start | bytes 1769480 | tf_op jit(solution)/shard_map/ppermute | solution.py:752
  294.6 27.4 %collective-permute-start.40 = (bf16[4,2,96,768]{3,2,1,0:T(8,128)(2,1)S(1)}, bf16[4,2,96,768]{3,2,1,0:T(8,128)(2,1)S(1)}, u32[]{:S(2)}, u32[]{:S(2)}) collective-permute-start(bf16[4,2,96,768]{3,2,1,0:T(8,128)(2,1)S(1)} %pad_maximum_fusion.2), channel_id=1, source_target_pairs={{0,4},{4,0},{8,12},{12,8},{16,20},{20,16},{24,28},{28,24},{1,5},{5... | collective-permute-start | bytes 3538952 | tf_op jit(solution)/shard_map/ppermute | solution.py:752
  296.3 26.8 %collective-permute-start.41 = (bf16[4,2,96,768]{3,2,1,0:T(8,128)(2,1)S(1)}, bf16[4,2,96,768]{3,2,1,0:T(8,128)(2,1)S(1)}, u32[]{:S(2)}, u32[]{:S(2)}) collective-permute-start(bf16[4,2,96,768]{3,2,1,0:T(8,128)(2,1)S(1)} %pad_maximum_fusion.3), channel_id=1, source_target_pairs={{0,2},{1,3},{2,0},{3,1},{4,6},{5,7},{6,4},{7,5},{8,10},{9,11},{10,... | collective-permute-start | bytes 3538952 | tf_op jit(solution)/shard_map/ppermute | solution.py:752
  330.2 42.0 %collective-permute-start.43 = (bf16[2,96,768]{2,1,0:T(8,128)(2,1)}, bf16[2,96,768]{2,1,0:T(8,128)(2,1)S(1)}, u32[]{:S(2)}, u32[]{:S(2)}) collective-permute-start(bf16[2,96,768]{2,1,0:T(8,128)(2,1)} %get-tuple-element.357), channel_id=1, source_target_pairs={{0,8},{4,12},{8,0},{12,4},{16,24},{20,28},{24,16},{28,20},{1,9},{5... | collective-permute-start | bytes 884744 | tf_op jit(solution)/shard_map/ppermute | solution.py:752
  340.0 32.3 %collective-permute-start.44 = (bf16[2,96,768]{2,1,0:T(8,128)(2,1)}, bf16[2,96,768]{2,1,0:T(8,128)(2,1)}, u32[]{:S(2)}, u32[]{:S(2)}) collective-permute-start(bf16[2,96,768]{2,1,0:T(8,128)(2,1)} %get-tuple-element.356), channel_id=1, source_target_pairs={{0,16},{4,20},{8,24},{12,28},{16,0},{20,4},{24,8},{28,12},{1,17},{... | collective-permute-start | bytes 884744 | tf_op jit(solution)/shard_map/ppermute | solution.py:752
  341.3 31.1 %collective-permute-start.45 = (bf16[2,96,768]{2,1,0:T(8,128)(2,1)}, bf16[2,96,768]{2,1,0:T(8,128)(2,1)}, u32[]{:S(2)}, u32[]{:S(2)}) collective-permute-start(bf16[2,96,768]{2,1,0:T(8,128)(2,1)} %get-tuple-element.355), channel_id=1, source_target_pairs={{0,24},{4,28},{8,16},{12,20},{16,8},{20,12},{24,0},{28,4},{1,25},{... | collective-permute-start | bytes 884744 | tf_op jit(solution)/shard_map/ppermute | solution.py:752
  343.6 28.8 %collective-permute-start.46 = (bf16[2,2,96,768]{3,2,1,0:T(8,128)(2,1)}, bf16[2,2,96,768]{3,2,1,0:T(8,128)(2,1)S(1)}, u32[]{:S(2)}, u32[]{:S(2)}) collective-permute-start(bf16[2,2,96,768]{3,2,1,0:T(8,128)(2,1)} %get-tuple-element.354), channel_id=1, source_target_pairs={{0,4},{4,0},{8,12},{12,8},{16,20},{20,16},{24,28},{28,24},{1,5},{5... | collective-permute-start | bytes 1769480 | tf_op jit(solution)/shard_map/ppermute | solution.py:752
  345.0 27.4 %collective-permute-start.47 = (bf16[2,2,96,768]{3,2,1,0:T(8,128)(2,1)S(1)}, bf16[2,2,96,768]{3,2,1,0:T(8,128)(2,1)}, u32[]{:S(2)}, u32[]{:S(2)}) collective-permute-start(bf16[2,2,96,768]{3,2,1,0:T(8,128)(2,1)S(1)} %get-tuple-element.353), channel_id=1, source_target_pairs={{0,2},{1,3},{2,0},{3,1},{4,6},{5,7},{6,4},{7,5},{8,10},{9,11},{10,... | collective-permute-start | bytes 1769480 | tf_op jit(solution)/shard_map/ppermute | solution.py:752
  372.3 43.4 %collective-permute-start.42 = (bf16[2,8,1,96,768]{4,3,2,1,0:T(8,128)(2,1)}, bf16[2,8,1,96,768]{4,3,2,1,0:T(8,128)(2,1)}, u32[]{:S(2)}, u32[]{:S(2)}) collective-permute-start(bf16[2,8,1,96,768]{4,3,2,1,0:T(8,128)(2,1)} %get-tuple-element.165), channel_id=1, source_target_pairs={{0,1},{1,0},{2,3},{3,2},{4,5},{5,4},{6,7},{7,6},{8,9},{9,8},{10,11... | collective-permute-start | bytes 7077896 | tf_op jit(solution)/shard_map/ppermute | solution.py:752
  375.0 40.6 %collective-permute-start.48 = (bf16[4,2,96,768]{3,2,1,0:T(8,128)(2,1)}, bf16[4,2,96,768]{3,2,1,0:T(8,128)(2,1)}, u32[]{:S(2)}, u32[]{:S(2)}) collective-permute-start(bf16[4,2,96,768]{3,2,1,0:T(8,128)(2,1)} %pad_maximum_fusion.4), channel_id=1, source_target_pairs={{0,4},{4,0},{8,12},{12,8},{16,20},{20,16},{24,28},{28,24},{1,5},{5... | collective-permute-start | bytes 3538952 | tf_op jit(solution)/shard_map/ppermute | solution.py:752
  375.7 40.0 %collective-permute-start.49 = (bf16[4,2,96,768]{3,2,1,0:T(8,128)(2,1)S(1)}, bf16[4,2,96,768]{3,2,1,0:T(8,128)(2,1)}, u32[]{:S(2)}, u32[]{:S(2)}) collective-permute-start(bf16[4,2,96,768]{3,2,1,0:T(8,128)(2,1)S(1)} %pad_maximum_fusion.5), channel_id=1, source_target_pairs={{0,2},{1,3},{2,0},{3,1},{4,6},{5,7},{6,4},{7,5},{8,10},{9,11},{10,... | collective-permute-start | bytes 3538952 | tf_op jit(solution)/shard_map/ppermute | solution.py:752
  412.1 50.0 %all-to-all-start.3 = ((bf16[4,240,768]{2,1,0:T(8,128)(2,1)}), bf16[4,240,768]{2,1,0:T(8,128)(2,1)S(1)}, u32[]{:S(2)}, u32[]{:S(2)}) async-start(bf16[4,240,768]{2,1,0:T(8,128)(2,1)} %bitcast.209), calls=%async_computation.3 | async-start | bytes 2949120 | tf_op jit(solution)/shard_map/all_to_all | solution.py:758
  463.9 75.8 %all-to-all-start.2 = ((bf16[4,240,768]{2,1,0:T(8,128)(2,1)}), bf16[4,240,768]{2,1,0:T(8,128)(2,1)S(1)}, u32[]{:S(2)}, u32[]{:S(2)}) async-start(bf16[4,240,768]{2,1,0:T(8,128)(2,1)} %bitcast.208), calls=%async_computation.2 | async-start | bytes 2949120 | tf_op jit(solution)/shard_map/all_to_all | solution.py:758
  468.7 34.1 %collective-permute-start.55 = (bf16[2,96,768]{2,1,0:T(8,128)(2,1)S(1)}, bf16[2,96,768]{2,1,0:T(8,128)(2,1)S(1)}, u32[]{:S(2)}, u32[]{:S(2)}) collective-permute-start(bf16[2,96,768]{2,1,0:T(8,128)(2,1)S(1)} %get-tuple-element.352), channel_id=1, source_target_pairs={{0,8},{4,12},{8,0},{12,4},{16,24},{20,28},{24,16},{28,20},{1,9},{5... | collective-permute-start | bytes 884744 | tf_op jit(solution)/shard_map/ppermute | solution.py:752
  470.0 32.8 %collective-permute-start.56 = (bf16[2,96,768]{2,1,0:T(8,128)(2,1)S(1)}, bf16[2,96,768]{2,1,0:T(8,128)(2,1)S(1)}, u32[]{:S(2)}, u32[]{:S(2)}) collective-permute-start(bf16[2,96,768]{2,1,0:T(8,128)(2,1)S(1)} %get-tuple-element.351), channel_id=1, source_target_pairs={{0,16},{4,20},{8,24},{12,28},{16,0},{20,4},{24,8},{28,12},{1,17},{... | collective-permute-start | bytes 884744 | tf_op jit(solution)/shard_map/ppermute | solution.py:752
  472.0 30.8 %collective-permute-start.57 = (bf16[2,96,768]{2,1,0:T(8,128)(2,1)S(1)}, bf16[2,96,768]{2,1,0:T(8,128)(2,1)S(1)}, u32[]{:S(2)}, u32[]{:S(2)}) collective-permute-start(bf16[2,96,768]{2,1,0:T(8,128)(2,1)S(1)} %get-tuple-element.350), channel_id=1, source_target_pairs={{0,24},{4,28},{8,16},{12,20},{16,8},{20,12},{24,0},{28,4},{1,25},{... | collective-permute-start | bytes 884744 | tf_op jit(solution)/shard_map/ppermute | solution.py:752
  473.1 26.6 %collective-permute-start.54 = (f32[8,768]{1,0:T(8,128)S(1)}, f32[8,768]{1,0:T(8,128)S(1)}, u32[]{:S(2)}, u32[]{:S(2)}) collective-permute-start(f32[8,768]{1,0:T(8,128)S(1)} %add.463), channel_id=1, source_target_pairs={{0,16},{4,20},{8,24},{12,28},{16,0},{20,4},{24,8},{28,12},{1,17},{... | collective-permute-start | bytes 73736 | tf_op jit(solution)/shard_map/ppermute | solution.py:752
  474.5 28.3 %collective-permute-start.58 = (bf16[2,1,96,768]{3,2,1,0:T(8,128)(2,1)S(1)}, bf16[2,1,96,768]{3,2,1,0:T(8,128)(2,1)S(1)}, u32[]{:S(2)}, u32[]{:S(2)}) collective-permute-start(bf16[2,1,96,768]{3,2,1,0:T(8,128)(2,1)S(1)} %get-tuple-element.364), channel_id=1, source_target_pairs={{0,4},{4,0},{8,12},{12,8},{16,20},{20,16},{24,28},{28,24},{1,5},{5... | collective-permute-start | bytes 884744 | tf_op jit(solution)/shard_map/ppermute | solution.py:752
  507.7 13.2 %collective-permute-start.61 = (bf16[4,1,96,768]{3,2,1,0:T(8,128)(2,1)S(1)}, bf16[4,1,96,768]{3,2,1,0:T(8,128)(2,1)S(1)}, u32[]{:S(2)}, u32[]{:S(2)}) collective-permute-start(bf16[4,1,96,768]{3,2,1,0:T(8,128)(2,1)S(1)} %pad_maximum_fusion.8), channel_id=1, source_target_pairs={{0,2},{1,3},{2,0},{3,1},{4,6},{5,7},{6,4},{7,5},{8,10},{9,11},{10,... | collective-permute-start | bytes 1769480 | tf_op jit(solution)/shard_map/ppermute | solution.py:752
  509.1 12.5 %collective-permute-start.60 = (bf16[4,1,96,768]{3,2,1,0:T(8,128)(2,1)S(1)}, bf16[4,1,96,768]{3,2,1,0:T(8,128)(2,1)S(1)}, u32[]{:S(2)}, u32[]{:S(2)}) collective-permute-start(bf16[4,1,96,768]{3,2,1,0:T(8,128)(2,1)S(1)} %pad_maximum_fusion.7), channel_id=1, source_target_pairs={{0,4},{4,0},{8,12},{12,8},{16,20},{20,16},{24,28},{28,24},{1,5},{5... | collective-permute-start | bytes 1769480 | tf_op jit(solution)/shard_map/ppermute | solution.py:752
  (71 other events, 871.1 us)

commit v3 on v2

--- a/solution.py
+++ b/solution.py
@@ -28,12 +28,12 @@
 bf16 = jnp.bfloat16
 f32 = jnp.float32
 VMEM_LIMIT = 58 * 1024 * 1024
-ATTENTION_US = 26
-LIFT_US = 17
-DROP_WEIGHT_US = 8
-EXPERT_BACK_US = 18
-ATTENTION_BACK_US = 27
-DROP_US = 24
+ATTENTION_US = 38
+LIFT_US = 16
+DROP_WEIGHT_US = 7
+EXPERT_BACK_US = 17
+ATTENTION_BACK_US = 19
+DROP_US = 17
 
 
 def adamw(weight, first_state, second_state, gradient, step_rate, decay_rate):
@@ -96,6 +96,58 @@
     return jnp.bitwise_and(other, 1) * 4 + jnp.right_shift(other, 1)
 
 
+def piece_copies(pieces, mine, place_of, sems):
+    even, *odd = pieces
+    blocks = [(even, i, 2 * i) for i in range(4)]
+    z = 0
+    for ref in odd:
+        for i in range(ref.shape[0]):
+            blocks.append((ref, i, 2 * z + 1))
+            z += 1
+    size = even.shape[2]
+    copies = []
+    for index, (ref, i, block) in enumerate(blocks):
+        first = jnp.bitwise_xor(mine, block) * size
+        rows = pl.ds(pl.multiple_of(first, 16), size)
+        copies.append(pltpu.make_async_copy(ref.at[i], place_of(rows), sems.at[index]))
+    return copies
+
+
+def step_copies(pieces, mine, weight_ref, sems):
+    by_step = []
+    for step in range(4):
+        even, odd, high, front, back = pieces[5 * (1 - step // 2) :][:5]
+        parts = (high, front, back) if step % 2 else (even, odd)
+        place_of = lambda rows, step=step: weight_ref.at[:, step, rows, :]
+        by_step.append(piece_copies(parts, mine, place_of, sems.at[step]))
+    return by_step
+
+
+def start_all(by_step):
+    for copies in by_step:
+        for copy in copies:
+            copy.start()
+
+
+def out_copy(weight_ref, out_ref, out_sems, step):
+    return pltpu.make_async_copy(weight_ref.at[:, step], out_ref.at[:, step], out_sems.at[step])
+
+
+def wait_step(by_step, weight_ref, out_ref, out_sems):
+    for step, copies in enumerate(by_step):
+
+        @pl.when(pl.program_id(0) == step)
+        def _():
+            for copy in copies:
+                copy.wait()
+            out_copy(weight_ref, out_ref, out_sems, step).start()
+
+
+def wait_out(weight_ref, out_ref, out_sems):
+    for step in range(4):
+        out_copy(weight_ref, out_ref, out_sems, step).wait()
+
+
 def store_grad(grad_ref, mine, index, first, rows, value):
     value = value.astype(bf16)
     size = grad_ref.shape[-2]
@@ -104,36 +156,45 @@
         grad_ref[0, place, index] = value[part * size : (part + 1) * size]
 
 
-def attend(query, key, value, allowed):
-    scores = dot(query, key, 1, 1)
-    scores = jnp.where(allowed, scores, masked_score)
-    top = jnp.max(scores, axis=-1, keepdims=True)
-    weights = jnp.exp(scores - top)
-    total = jnp.sum(weights, axis=-1, keepdims=True)
-    weights = (weights * (1.0 / total)).astype(bf16)
-    return weights, dot(weights, value, 1, 0)
+def attend(queries, keys, values, allowed):
+    scores = [dot(key, query, 1, 1) for query, key in zip(queries, keys)]
+    scores = [jnp.where(mask, score, masked_score) for mask, score in zip(allowed, scores)]
+    tops = [jnp.max(score, axis=0, keepdims=True) for score in scores]
+    weights = [jnp.exp(score - top) for score, top in zip(scores, tops)]
+    totals = [jnp.sum(weight, axis=0, keepdims=True) for weight in weights]
+    weights = [(weight * (1.0 / total)).astype(bf16) for weight, total in zip(weights, totals)]
+    return weights, [dot(value, weight, 0, 0) for value, weight in zip(values, weights)]
+
+
+def item_slices(items, i):
+    first = items * PATCH_STRIDE + i * TEXT_STRIDE
+    return slice(i * PATCH_STRIDE, (i + 1) * PATCH_STRIDE), slice(first, first + TEXT_STRIDE)
+
+
+def item_rows(ref, index, items, i):
+    patch_rows, text_rows = item_slices(items, i)
+    return jnp.concatenate([ref[index + (patch_rows,)], ref[index + (text_rows,)]], axis=0)
+
+
+def head_columns(rows, kind, heads, h):
+    first = (kind * heads + h) * HEAD_DIM
+    return rows[:, first : first + HEAD_DIM]
 
 
 def attention_kernel(
-    meta_ref,
-    raw_ref,
-    place_ref,
-    hidden_ref,
-    norm_ref,
-    extra_ref,
-    weight_ref,
-    block_ref,
-    normed_ref,
-    residual_ref,
-    joint_ref,
-    mixed_ref,
-    probs_ref,
-    **sizes,
+    meta_ref, raw_ref, place_ref, hidden_ref, valid_ref, norm_ref, extra_ref, *refs, **sizes
 ):
-    main_rows, all_rows = sizes["main_rows"], sizes["all_rows"]
-
-    @pl.when(pl.program_id(0) == 0)
+    pieces, outs = refs[:10], refs[10:]
+    block_ref, normed_ref, residual_ref, feed_ref, square_ref = outs[:5]
+    out_ref, joint_ref, mixed_ref, probs_ref, weight_ref, sems, out_sems = outs[5:]
+    items, main_rows, all_rows = sizes["items"], sizes["main_rows"], sizes["all_rows"]
+    step = pl.program_id(0)
+    by_step = step_copies(pieces, meta_ref[items + 1], weight_ref, sems)
+
+    @pl.when(step == 0)
     def _():
+        start_all(by_step)
+
         def chunk(first, size):
             rows = pl.ds(first, size)
             picked = dot(one_hot(place_ref[...], first, size), raw_ref[...], 1, 0)
@@ -142,37 +203,15 @@
             residual_ref[rows, :] = picked
             normed_ref[rows, :] = norm_forward(picked, norm_ref[0:1, :], norm_ref[1:2, :]).astype(bf16)
 
-        loop(sizes["items"], lambda i: chunk(pl.multiple_of(i * ITEM_ROWS, 16), ITEM_ROWS))
+        loop(items, lambda i: chunk(pl.multiple_of(i * ITEM_ROWS, 16), ITEM_ROWS))
         chunk(main_rows, all_rows - main_rows)
 
-    attend_heads(meta_ref, weight_ref, normed_ref, residual_ref, joint_ref, mixed_ref, probs_ref, **sizes)
-
-
-def attention_end_kernel(
-    meta_ref,
-    normed_ref,
-    block_ref,
-    before_ref,
-    valid_ref,
-    norm_ref,
-    weight_ref,
-    residual_ref,
-    joint_ref,
-    mixed_ref,
-    probs_ref,
-    feed_ref,
-    square_ref,
-    **sizes,
-):
-    items, main_rows = sizes["items"], sizes["main_rows"]
-
-    @pl.when(pl.program_id(0) == 0)
-    def _():
-        residual_ref[...] = before_ref[...]
-
-    attend_heads(meta_ref, weight_ref, normed_ref, residual_ref, joint_ref, mixed_ref, probs_ref, **sizes)
-
-    @pl.when(pl.program_id(0) == pl.num_programs(0) - 1)
+    wait_step(by_step, weight_ref, out_ref, out_sems)
+    attend_heads(
+        meta_ref, weight_ref.at[0, step], normed_ref, residual_ref, joint_ref, mixed_ref, probs_ref, **sizes
+    )
+
+    @pl.when(step == pl.num_programs(0) - 1)
     def _():
         square_ref[...] = jnp.zeros_like(square_ref)
 
@@ -183,7 +222,8 @@
             square_ref[...] += jnp.sum(attended * attended, axis=0, keepdims=True)
 
         loop(items, lambda i: chunk(rows_at(i, ITEM_ROWS)))
-        chunk(pl.ds(main_rows, sizes["all_rows"] - main_rows))
+        chunk(pl.ds(main_rows, all_rows - main_rows))
+        wait_out(weight_ref, out_ref, out_sems)
 
 
 def attend_heads(
@@ -204,47 +244,42 @@
     tail_rows = all_rows - main_rows
 
     def project(rows):
-        joint = dot(normed_ref[rows, :], weight_ref[0, :, : 3 * width], 1, 0)
+        joint = dot(normed_ref[rows, :], weight_ref[:, : 3 * width], 1, 0)
         joint_ref[0, rows, :width] = (joint[:, :width].astype(bf16).astype(f32) * HEAD_DIM**-0.5).astype(bf16)
         joint_ref[0, rows, width:] = joint[:, width:].astype(bf16)
 
-    loop(items, lambda i: project(rows_at(i, ITEM_ROWS)))
-    project(pl.ds(main_rows, tail_rows))
-
-    column = lax.broadcasted_iota(jnp.int32, (1, ITEM_ROWS), 1)
-
-    def one_item(i):
-        patch_rows = rows_at(i, PATCH_STRIDE)
-        text_rows = pl.ds(pl.multiple_of(items * PATCH_STRIDE + i * TEXT_STRIDE, 16), TEXT_STRIDE)
-        joint = jnp.concatenate([joint_ref[0, patch_rows, :], joint_ref[0, text_rows, :]], axis=0)
-        allowed = (column < PATCHES) | (
-            (column >= PATCH_STRIDE) & (column < PATCH_STRIDE + meta_ref[i])
-        )
-        outs = []
-        for h in range(heads):
-            part = lambda k: joint[:, k * width + h * HEAD_DIM : k * width + (h + 1) * HEAD_DIM]
-            weights, out = attend(part(0), part(1), part(2), allowed)
-            probs_ref[0, i, h] = weights
-            outs.append(out.astype(bf16))
-        mixed = jnp.concatenate(outs, axis=1)
-        mixed_ref[0, patch_rows, :] = mixed[:PATCH_STRIDE]
-        mixed_ref[0, text_rows, :] = mixed[PATCH_STRIDE:]
-
-    loop(items, one_item)
-
-    joint = joint_ref[0, main_rows:, :]
-    allowed = lax.broadcasted_iota(jnp.int32, (1, tail_rows), 1) < meta_ref[items]
-    outs = []
-    for h in range(heads):
-        part = lambda k: joint[:, k * width + h * HEAD_DIM : k * width + (h + 1) * HEAD_DIM]
-        outs.append(attend(part(0), part(1), part(2), allowed)[1].astype(bf16))
-    mixed_ref[0, main_rows:, :] = jnp.concatenate(outs, axis=1)
+    project(pl.ds(0, all_rows))
+
+    key_row = lax.broadcasted_iota(jnp.int32, (ITEM_ROWS, 1), 0)
+    blocks = [item_rows(joint_ref, (0,), items, i) for i in range(items)]
+    masks = [
+        (key_row < PATCHES)
+        | ((key_row >= PATCH_STRIDE) & (key_row < PATCH_STRIDE + meta_ref[i]))
+        for i in range(items)
+    ]
+    blocks.append(joint_ref[0, main_rows:, :])
+    masks.append(lax.broadcasted_iota(jnp.int32, (tail_rows, 1), 0) < meta_ref[items])
+    pairs = [(i, h) for i in range(items + 1) for h in range(heads)]
+    weights, outs = attend(
+        *[[head_columns(blocks[i], kind, heads, h) for i, h in pairs] for kind in range(3)],
+        [masks[i] for i, _ in pairs],
+    )
+    for (i, h), weight in zip(pairs, weights):
+        if i < items:
+            probs_ref[0, i, h] = weight
+    for i in range(items + 1):
+        mixed = jnp.concatenate(outs[i * heads : (i + 1) * heads], axis=0).T.astype(bf16)
+        if i == items:
+            mixed_ref[0, main_rows:, :] = mixed
+        else:
+            patch_rows, text_rows = item_slices(items, i)
+            mixed_ref[0, patch_rows, :] = mixed[:PATCH_STRIDE]
+            mixed_ref[0, text_rows, :] = mixed[PATCH_STRIDE:]
 
     def add_output(rows):
-        residual_ref[rows, :] += dot(mixed_ref[0, rows, :], weight_ref[0, :, 3 * width :], 1, 1)
-
-    loop(items, lambda i: add_output(rows_at(i, ITEM_ROWS)))
-    add_output(pl.ds(main_rows, tail_rows))
+        residual_ref[rows, :] += dot(mixed_ref[0, rows, :], weight_ref[:, 3 * width :], 1, 1)
+
+    add_output(pl.ds(0, all_rows))
 
 
 def attention_back_kernel(
@@ -290,15 +325,7 @@
     normed_ref,
     weight_ref,
     before_ref,
-    grad_residual_ref,
-    block_ref,
-    hidden_ref,
-    place_ref,
-    norm_ref,
     grad_weight_ref,
-    grad_raw_ref,
-    grad_norm_ref,
-    grad_mask_ref,
     grad_normed_ref,
     grad_mixed_ref,
     grad_joint_ref,
@@ -323,23 +350,34 @@
         **sizes,
     )
 
-    @pl.when(pl.program_id(0) == pl.num_programs(0) - 1)
-    def _():
-        grad_norm_ref[...] = jnp.zeros_like(grad_norm_ref)
-        grad_mask_ref[...] = jnp.zeros_like(grad_mask_ref)
-
-        def chunk(i):
-            rows = rows_at(i, ITEM_ROWS)
-            grad, gain, shift = norm_backward(block_ref[rows, :], norm_ref[0:1, :], grad_normed_ref[rows, :])
-            grad_norm_ref[0:1, :] += gain
-            grad_norm_ref[1:2, :] += shift
-            grad = grad + grad_residual_ref[rows, :]
-            hidden = hidden_ref[rows, :] > 0
-            grad_mask_ref[...] += jnp.sum(jnp.where(hidden, grad, 0.0), axis=0, keepdims=True)
-            grad_normed_ref[rows, :] = jnp.where(hidden, 0.0, grad)
-
-        loop(sizes["items"], chunk)
-        unplace(place_ref, grad_normed_ref, grad_raw_ref, grad_normed_ref.shape[0])
+
+def input_grad_kernel(
+    grad_normed_ref,
+    grad_residual_ref,
+    block_ref,
+    hidden_ref,
+    place_ref,
+    norm_ref,
+    grad_raw_ref,
+    grad_norm_ref,
+    grad_mask_ref,
+    grad_block_ref,
+):
+    grad_norm_ref[...] = jnp.zeros_like(grad_norm_ref)
+    grad_mask_ref[...] = jnp.zeros_like(grad_mask_ref)
+
+    def chunk(i):
+        rows = rows_at(i, ITEM_ROWS)
+        grad, gain, shift = norm_backward(block_ref[rows, :], norm_ref[0:1, :], grad_normed_ref[rows, :])
+        grad_norm_ref[0:1, :] += gain
+        grad_norm_ref[1:2, :] += shift
+        grad = grad + grad_residual_ref[rows, :]
+        hidden = hidden_ref[rows, :] > 0
+        grad_mask_ref[...] += jnp.sum(jnp.where(hidden, grad, 0.0), axis=0, keepdims=True)
+        grad_block_ref[rows, :] = jnp.where(hidden, 0.0, grad).astype(bf16)
+
+    loop(grad_normed_ref.shape[0] // ITEM_ROWS, chunk)
+    unplace(place_ref, grad_block_ref, grad_raw_ref, grad_block_ref.shape[0])
 
 
 def heads_back(
@@ -361,39 +399,37 @@
     width = heads * HEAD_DIM
     half = HEAD_DIM**-0.5
 
-    def mixed_grad(i):
-        rows = rows_at(i, ITEM_ROWS)
-        grad_mixed_ref[rows, :] = dot(
-            grad_attended_ref[rows, :], weight_ref[0, :, 3 * width :], 1, 0
-        ).astype(bf16)
-
-    loop(items, mixed_grad)
-
-    def one_item(i):
-        patch_rows = rows_at(i, PATCH_STRIDE)
-        text_rows = pl.ds(pl.multiple_of(items * PATCH_STRIDE + i * TEXT_STRIDE, 16), TEXT_STRIDE)
-        joint = jnp.concatenate([joint_ref[0, patch_rows, :], joint_ref[0, text_rows, :]], axis=0)
-        mixed = jnp.concatenate([mixed_ref[0, patch_rows, :], mixed_ref[0, text_rows, :]], axis=0)
-        grad_mixed = jnp.concatenate([grad_mixed_ref[patch_rows, :], grad_mixed_ref[text_rows, :]], axis=0)
-        grads = [[], [], []]
-        for h in range(heads):
-            part = lambda k: joint[:, k * width + h * HEAD_DIM : k * width + (h + 1) * HEAD_DIM]
-            span = slice(h * HEAD_DIM, (h + 1) * HEAD_DIM)
-            grad_out = grad_mixed[:, span]
-            weights = probs_ref[0, i, h]
-            grad_probs = dot(grad_out, part(2), 1, 1)
-            mean_grad = jnp.sum(
-                grad_out.astype(f32) * mixed[:, span].astype(f32), axis=-1, keepdims=True
-            )
-            grad_scores = (weights.astype(f32) * (grad_probs - mean_grad)).astype(bf16)
-            grads[0].append((dot(grad_scores, part(1), 1, 0) * half).astype(bf16))
-            grads[1].append(dot(grad_scores, part(0), 0, 0).astype(bf16))
-            grads[2].append(dot(weights, grad_out, 0, 0).astype(bf16))
-        grad_joint = jnp.concatenate(grads[0] + grads[1] + grads[2], axis=1)
+    grad_mixed_ref[...] = dot(grad_attended_ref[...], weight_ref[0, :, 3 * width :], 1, 0).astype(bf16)
+
+    blocks = [item_rows(joint_ref, (0,), items, i) for i in range(items)]
+    outs = [item_rows(grad_mixed_ref, (), items, i) for i in range(items)]
+    products = [
+        (outs[i].astype(f32) * item_rows(mixed_ref, (0,), items, i).astype(f32)).T for i in range(items)
+    ]
+    pairs = [(i, h) for i in range(items) for h in range(heads)]
+    queries, keys, values = [
+        [head_columns(blocks[i], kind, heads, h) for i, h in pairs] for kind in range(3)
+    ]
+    grad_outs = [head_columns(outs[i], 0, heads, h) for i, h in pairs]
+    weights = [probs_ref[0, i, h] for i, h in pairs]
+    grad_probs = [dot(value, grad_out, 1, 1) for value, grad_out in zip(values, grad_outs)]
+    means = [
+        jnp.sum(products[i][h * HEAD_DIM : (h + 1) * HEAD_DIM], axis=0, keepdims=True) for i, h in pairs
+    ]
+    grad_scores = [
+        (weight.astype(f32) * (grad - mean)).astype(bf16)
+        for weight, grad, mean in zip(weights, grad_probs, means)
+    ]
+    grad_values = [dot(weight, grad_out, 1, 0).astype(bf16) for weight, grad_out in zip(weights, grad_outs)]
+    grad_keys = [dot(score, query, 1, 0).astype(bf16) for score, query in zip(grad_scores, queries)]
+    grad_queries = [dot(key, score, 0, 0) * half for key, score in zip(keys, grad_scores)]
+    for i in range(items):
+        own = slice(i * heads, (i + 1) * heads)
+        grad_query = jnp.concatenate(grad_queries[own], axis=0).T.astype(bf16)
+        grad_joint = jnp.concatenate([grad_query] + grad_keys[own] + grad_values[own], axis=1)
+        patch_rows, text_rows = item_slices(items, i)
         grad_joint_ref[patch_rows, :] = grad_joint[:PATCH_STRIDE]
         grad_joint_ref[text_rows, :] = grad_joint[PATCH_STRIDE:]
-
-    loop(items, one_item)
 
     model_width = weight_ref.shape[1]
     for first in range(0, model_width, 384):
@@ -407,11 +443,7 @@
         )
         store_grad(grad_weight_ref, mine_ref[0], 0, first, 384, grad_weight)
 
-    def normed_grad(i):
-        rows = rows_at(i, ITEM_ROWS)
-        grad_normed_ref[rows, :] += dot(grad_joint_ref[rows, :], weight_ref[0, :, : 3 * width], 1, 1)
-
-    loop(items, normed_grad)
+    grad_normed_ref[...] += dot(grad_joint_ref[...], weight_ref[0, :, : 3 * width], 1, 1)
 
 
 def unplace(place_ref, source_ref, raw_ref, source_rows):
@@ -428,17 +460,29 @@
     loop(raw_rows // size, chunk)
 
 
-def lift_kernel(feed_ref, weight_ref, acted_ref, slope_ref, *, vision_rows, all_rows):
+def lift_kernel(mine_ref, feed_ref, *refs, vision_rows, all_rows):
+    pieces, (acted_ref, slope_ref, out_ref, weight_ref, sems, out_sems) = refs[:10], refs[10:]
+    by_step = step_copies(pieces, mine_ref[0], weight_ref, sems)
+
+    @pl.when(pl.program_id(0) == 0)
+    def _():
+        start_all(by_step)
+
+    wait_step(by_step, weight_ref, out_ref, out_sems)
+
     def piece(rows, expert):
-        lifted = dot(feed_ref[rows, :], weight_ref[expert, 0], 1, 0)
+        lifted = dot(feed_ref[rows, :], weight_ref[expert, pl.program_id(0)], 1, 0)
         cumulative = 0.5 * (1.0 + lax.erf(lifted * (0.5**0.5)))
         density = jnp.exp(-0.5 * lifted * lifted) * ((2.0 * jnp.pi) ** -0.5)
         acted_ref[0, rows, :] = (lifted * cumulative).astype(bf16)
         slope_ref[0, rows, :] = (cumulative + lifted * density).astype(bf16)
 
-    loop(vision_rows // PATCH_STRIDE, lambda i: piece(rows_at(i, PATCH_STRIDE), 0))
-    text = all_rows - vision_rows
-    loop(3, lambda i: piece(pl.ds(pl.multiple_of(vision_rows + i * (text // 3), 16), text // 3), 1))
+    loop(2, lambda i: piece(rows_at(i, vision_rows // 2), 0))
+    piece(pl.ds(vision_rows, all_rows - vision_rows), 1)
+
+    @pl.when(pl.program_id(0) == pl.num_programs(0) - 1)
+    def _():
+        wait_out(weight_ref, out_ref, out_sems)
 
 
 def place_grad_kernel(raw_ref, place_ref, grad_ref, grad_bias_ref, *, vision_rows):
@@ -467,6 +511,7 @@
 
 
 def drop_kernel(
+    mine_ref,
     acted_ref,
     residual_ref,
     valid_ref,
@@ -491,11 +536,8 @@
     def piece(rows, expert):
         total_ref[rows, :] += dot(acted_ref[0, rows, :], weight_ref[expert, 0], 1, 1)
 
-    def everything(body):
-        loop(vision_rows // PATCH_STRIDE, lambda i: body(rows_at(i, PATCH_STRIDE), 0))
-        loop(3, lambda i: body(pl.ds(pl.multiple_of(vision_rows + i * (text // 3), 16), text // 3), 1))
-
-    everything(piece)
+    piece(pl.ds(0, vision_rows), 0)
+    piece(pl.ds(vision_rows, text), 1)
 
     @pl.when(step == pl.num_programs(0) - 1)
     def _():
@@ -509,7 +551,8 @@
             square_ref[1:2, :] += jnp.sum(valid * fed * fed, axis=0, keepdims=True)
             total_ref[rows, :] = out
 
-        everything(finish)
+        loop(vision_rows // PATCH_STRIDE, lambda i: finish(rows_at(i, PATCH_STRIDE), 0))
+        loop(3, lambda i: finish(pl.ds(pl.multiple_of(vision_rows + i * (text // 3), 16), text // 3), 1))
         unplace(place_ref, total_ref, raw_ref, all_rows)
 
 
@@ -522,7 +565,7 @@
         lifted_ref[rows, :] = grad_lifted
         total_ref[rows, :] += dot(grad_lifted, lift_ref[expert, 0], 1, 1)
 
-    loop(vision_rows // PATCH_STRIDE, lambda i: piece(rows_at(i, PATCH_STRIDE), 0))
+    piece(pl.ds(0, vision_rows), 0)
     piece(pl.ds(vision_rows, grad_ref.shape[0] - vision_rows), 1)
     expert_weight_grad(
         grad_weight_ref, mine_ref[0], feed_ref, lambda rows: lifted_ref[rows, :], vision_rows
@@ -616,6 +659,20 @@
     return pl.BlockSpec(shape, lambda i, *_: (0, i + first) + (0,) * (len(shape) - 2))
 
 
+def part_of(step, mine):
+    return jnp.bitwise_xor(mine[1], (step % 2) * 2 + 1 - step // 2)
+
+
+def part_pair(*shape, first=0):
+    return pl.BlockSpec(
+        shape, lambda i, mine: (0, part_of(i + first, mine)) + (0,) * (len(shape) - 2)
+    )
+
+
+def anywhere(values):
+    return (values, pl.BlockSpec(memory_space=pl.ANY))
+
+
 def call(kernel, name, steps, ins, outs, scratch, microseconds, scalars=(), aliases=None):
     return pl.pallas_call(
         kernel,
@@ -628,6 +685,7 @@
             scratch_shapes=scratch,
         ),
         out_shape=[jax.ShapeDtypeStruct(shape, kind) for shape, kind, _ in outs],
+        input_output_aliases=aliases or {},
         compiler_params=pltpu.CompilerParams(
             dimension_semantics=("arbitrary",), vmem_limit_bytes=VMEM_LIMIT
         ),
@@ -635,57 +693,6 @@
             flops=int(microseconds * 1e9), bytes_accessed=int(microseconds * 1e6), transcendentals=0
         ),
     )(*scalars, *[array for array, _ in ins])
-
-
-def assemble_kernel(mine_ref, *refs):
-    count = len(refs) - 2
-    pieces, whole_ref, sems = refs[:count], refs[count], refs[count + 1]
-    size = pieces[0].shape[2]
-    for step in range(4):
-
-        @pl.when(pl.program_id(0) == step)
-        def _():
-            core, y = 1 - step // 2, step % 2
-            copies = []
-            for kind, ref in enumerate(pieces[5 * core : 5 * core + 5]):
-                x, from_y = ((0, 0), (1, 0), (0, 1), (1, 1), (1, 1))[kind]
-                if from_y != y:
-                    continue
-                for i in range(ref.shape[0]):
-                    z = i + 2 * (kind == 4)
-                    group = jnp.bitwise_xor(mine_ref[0], 2 * z + x)
-                    rows = pl.ds(pl.multiple_of(group * size, 16), size)
-                    copies.append(
-                        pltpu.make_async_copy(
-                            ref.at[i], whole_ref.at[:, 0, rows, :], sems.at[len(copies)]
-                        )
-                    )
-            for copy in copies:
-                copy.start()
-            for copy in copies:
-                copy.wait()
-
-
-def assemble(mine, pieces, parts, rows):
-    count, _, columns = pieces[0].shape[1:]
-    return pl.pallas_call(
-        assemble_kernel,
-        name="assemble",
-        grid_spec=pltpu.PrefetchScalarGridSpec(
-            num_scalar_prefetch=1,
-            grid=(parts,),
-            in_specs=[pl.BlockSpec(memory_space=pl.ANY)] * len(pieces),
-            out_specs=pl.BlockSpec((count, 1, rows, columns), lambda i, mine: (0, i, 0, 0)),
-            scratch_shapes=[pltpu.SemaphoreType.DMA((8,))],
-        ),
-        out_shape=jax.ShapeDtypeStruct((count, parts, rows, columns), bf16),
-        compiler_params=pltpu.CompilerParams(
-            dimension_semantics=("arbitrary",), vmem_limit_bytes=20 << 20
-        ),
-        cost_estimate=pl.CostEstimate(
-            flops=0, bytes_accessed=4 * count * parts * rows * columns, transcendentals=0
-        ),
-    )(mine, *pieces)
 
 
 def body(
@@ -738,7 +745,6 @@
     groups = lax.axis_size("dp")
     cube = groups == 8
     piece = model_width // 8
-    order = [1, 3, 0, 2]
     if cube:
         mine = jnp.stack([lax.axis_index("dp"), lax.axis_index("mp")]).astype(jnp.int32)
     else:
@@ -761,8 +767,15 @@
 
     def gather(values):
         whole_values = lax.all_gather(values, ("mp", "dp"), axis=1, tiled=True)
-        shape = (-1, parts, model_width, values.shape[2])
-        return jnp.stack([whole_values.reshape(shape)[:, i] for i in order], axis=1)
+        return whole_values.reshape(-1, parts, model_width, values.shape[2])
+
+    def gather_pieces(values):
+        whole_values = jnp.swapaxes(gather(values).reshape(-1, parts, 4, 2, piece, model_width), 0, 3)
+        pieces = []
+        for core in range(2):
+            low, high = whole_values[:, core], whole_values[:, 2 + core]
+            pieces += [low[0], low[1], high[0], high[1, :2], high[1, 2:]]
+        return pieces
 
     def gather_line(values):
         return jnp.stack([values] + [swap(values, "dp", bit) for bit in (2, 4, 6)])
@@ -775,9 +788,7 @@
 
     def gather_cores(line, along, corner):
         own = (line,) + along + corner
-        return assemble(
-            mine, own + tuple(swap(part, "mp", 1) for part in own), parts, model_width
-        )
+        return own + tuple(swap(part, "mp", 1) for part in own)
 
     def add(*terms):
         total = terms[0].astype(f32)
@@ -789,9 +800,11 @@
         shape = (2, 2, 4) + keep.shape[2:]
         both = jnp.stack([keep.reshape(shape), send.reshape(shape)], axis=1)
         both = jnp.transpose(both, (4, 0, 1, 3, 2, 5, 6))
-        both = both.reshape(both.shape[0], parts * model_width, shape[-1])
-        both = lax.psum_scatter(both, ("mp", "dp"), scatter_dimension=1, tiled=True)
-        return both.astype(f32)
+        return reduce(both.reshape(both.shape[0], parts * model_width, shape[-1]))
+
+    def reduce(values):
+        values = lax.psum_scatter(values, ("mp", "dp"), scatter_dimension=1, tiled=True)
+        return values.astype(f32)
 
     def scatter_corner(keep, received):
         shape = (2, 2, 4) + keep.shape[2:]
@@ -855,7 +868,7 @@
         text_spot < 0, spots % PATCH_STRIDE < PATCHES, text_spot - text_item * TEXT_STRIDE < text_end
     )
     valid = valid.astype(f32)[:, None]
-    meta = jnp.concatenate([lengths, (block_rows - used)[None]])
+    meta = jnp.concatenate([lengths, (block_rows - used)[None], mine[:1]])
 
     def rows_of(count, kind):
         return ((count, model_width), kind, whole(count, model_width))
@@ -864,14 +877,19 @@
         return (values, whole(*values.shape))
 
     def heads_out():
-        return [
-            ((2, all_rows, 3 * width), bf16, stepped(1, all_rows, 3 * width)),
-            ((2, all_rows, width), bf16, stepped(1, all_rows, width)),
-            (
-                (2, items, heads, ITEM_ROWS, ITEM_ROWS),
-                bf16,
-                stepped(1, items, heads, ITEM_ROWS, ITEM_ROWS),
-            ),
+        shapes = [
+            (parts, all_rows, 3 * width),
+            (parts, all_rows, width),
+            (parts, items, heads, ITEM_ROWS, ITEM_ROWS),
+        ]
+        return [(shape, bf16, stepped(1, *shape[1:])) for shape in shapes]
+
+    def whole_weight(count):
+        shape = (count, parts, model_width, model_width)
+        return (shape, bf16, pl.BlockSpec(memory_space=pl.ANY)), [
+            pltpu.VMEM(shape, bf16),
+            pltpu.SemaphoreType.DMA((parts, 8)),
+            pltpu.SemaphoreType.DMA((parts,)),
         ]
 
     def part_weight(values, first, count=2):
@@ -884,42 +902,36 @@
     head_sizes = dict(items=items, heads=heads)
     row_sizes = dict(main_rows=main_rows, all_rows=all_rows)
 
-    def attention(raw, weights):
-        return call(
+    def attention(raw, pieces):
+        weight_out, scratch = whole_weight(1)
+        block_input, normed, residual, feed_input, squared, weights, *made = call(
             functools.partial(attention_kernel, **head_sizes, **row_sizes),
             "attention",
-            2,
-            [plain(raw), plain(place_row), plain(hidden), plain(norm_params), plain(extra_params)]
-            + [(weights, stepped(1, model_width, model_width))],
-            [rows_of(all_rows, f32), rows_of(all_rows, bf16), rows_of(all_rows, f32)] + heads_out(),
-            [],
+            parts,
+            [plain(raw), plain(place_row), plain(hidden), plain(valid), plain(norm_params)]
+            + [plain(extra_params)]
+            + [anywhere(values) for values in pieces],
+            [rows_of(all_rows, f32), rows_of(all_rows, bf16), rows_of(all_rows, f32)]
+            + [rows_of(all_rows, bf16), rows_of(1, f32), weight_out]
+            + heads_out(),
+            scratch,
             ATTENTION_US,
             (meta,),
         )
-
-    def attention_end(normed, block_input, residual, weights):
-        return call(
-            functools.partial(attention_end_kernel, **head_sizes, **row_sizes),
-            "attention_end",
-            2,
-            [plain(normed), plain(block_input), plain(residual), plain(valid), plain(norm_params)]
-            + [(weights, stepped(1, model_width, model_width, first=2))],
-            [rows_of(all_rows, f32)] + heads_out() + [rows_of(all_rows, bf16), rows_of(1, f32)],
-            [],
-            ATTENTION_US,
-            (meta,),
-        )
-
-    def lift(feed_input, weights):
+        return block_input, normed, residual, feed_input, squared, [weights[0], *made]
+
+    def lift(feed_input, pieces):
         shape = (parts, all_rows, hidden_width)
+        weight_out, scratch = whole_weight(2)
         return call(
             functools.partial(lift_kernel, vision_rows=vision_rows, all_rows=all_rows),
             "lift",
             parts,
-            [plain(feed_input), part_weight(weights, 0)],
-            [(shape, bf16, stepped(1, *shape[1:]))] * 2,
-            [],
+            [plain(feed_input)] + [anywhere(values) for values in pieces],
+            [(shape, bf16, stepped(1, *shape[1:]))] * 2 + [weight_out],
+            scratch,
             LIFT_US,
+            (mine,),
         )
 
     def place_grad(raw):
@@ -950,7 +962,7 @@
             plain(grad_rows),
             (slope, stepped(1, main_rows, hidden_width, first=first)),
             (feed_input, whole(main_rows, model_width)),
-            part_weight(drop_weights, first),
+            (drop_weights, part_pair(2, 1, *drop_weights.shape[2:], first=first)),
             part_weight(lift_weights, first),
         ]
 
@@ -979,12 +991,12 @@
             (mine,),
         )
 
-    def heads_ins(grad_attended, joint_rows, mixed, probs, normed, weights, first):
+    def heads_ins(grad_attended, normed, weights, joint_rows, mixed, probs, first):
         return [
             plain(grad_attended),
-            (joint_rows, stepped(1, main_rows, 3 * width)),
-            (mixed, stepped(1, main_rows, width)),
-            (probs, stepped(1, *probs.shape[1:])),
+            (joint_rows, stepped(1, main_rows, 3 * width, first=first)),
+            (mixed, stepped(1, main_rows, width, first=first)),
+            (probs, stepped(1, *probs.shape[1:], first=first)),
             (normed, whole(main_rows, model_width)),
             (weights, stepped(1, model_width, model_width, first=first)),
         ]
@@ -1006,24 +1018,34 @@
             (mine,),
         )
 
-    def attention_back_end(before, grad_residual, block_input, *args):
+    def attention_back_end(before, *args):
         return call(
             functools.partial(attention_back_end_kernel, **head_sizes),
             "attention_back_end",
             2,
-            heads_ins(*args, 2)
-            + [
-                plain(before),
+            heads_ins(*args, 2) + [plain(before)],
+            [grad_out(1), rows_of(main_rows, f32)],
+            heads_scratch,
+            ATTENTION_BACK_US,
+            (mine,),
+        )
+
+    def finish_input_grad(grad_normed, grad_residual, block_input):
+        return call(
+            input_grad_kernel,
+            "input_grad",
+            1,
+            [
+                plain(grad_normed),
                 plain(grad_residual),
                 (block_input, whole(main_rows, model_width)),
                 (hidden, whole(main_rows, 1)),
                 plain(place_column),
                 plain(norm_params),
             ],
-            [grad_out(1), rows_of(block_rows, bf16), rows_of(2, f32), rows_of(1, f32)],
-            [pltpu.VMEM((main_rows, model_width), f32)] + heads_scratch,
-            ATTENTION_BACK_US,
-            (mine,),
+            [rows_of(block_rows, bf16), rows_of(2, f32), rows_of(1, f32)],
+            [pltpu.VMEM((main_rows, model_width), bf16)],
+            9,
         )
 
     def drop(acted, residual, weights):
@@ -1032,58 +1054,52 @@
             "drop",
             parts,
             [(acted, stepped(1, all_rows, hidden_width)), plain(residual), plain(valid)]
-            + [plain(place_column), plain(extra_params), part_weight(weights, 0)],
+            + [plain(place_column), plain(extra_params)]
+            + [(weights, part_pair(2, 1, *weights.shape[2:]))],
             [rows_of(block_rows, bf16), rows_of(2, f32)],
             [pltpu.VMEM((all_rows, model_width), f32)],
             DROP_US,
+            (mine,),
         )
 
     raw_tokens = exchange(tokens)
     if cube:
-        line_attend = gather_line(shard_attend)
+        line_attend, raw_tokens = after((gather_line(shard_attend), raw_tokens))
+        line_lift = gather_line(after(shard_lift, line_attend))
         plane_attend = gather_plane(line_attend)
-        line_lift = gather_line(after(shard_lift, line_attend))
         corner_attend = gather_corner(*plane_attend)
-        line_drop = gather_line(after(shard_drop, line_lift))
-        attend_all = gather_cores(line_attend, plane_attend, corner_attend)[0]
-        plane_lift = gather_plane(after(line_lift, corner_attend))
+        attend_pieces = gather_cores(line_attend, plane_attend, corner_attend)
+        line_lift, raw_tokens = after((line_lift, raw_tokens))
+        drop_all = gather(after(shard_drop, line_lift, corner_attend))
+        plane_lift = gather_plane(line_lift)
+        raw_grad = exchange(after(cotangent.astype(bf16), line_lift))
     else:
-        attend_all = gather(shard_attend)[0]
-
-    block_input, normed, residual, *heads_first = attention(raw_tokens, attend_all)
+        attend_pieces = gather_pieces(shard_attend)
+        drop_all = gather(shard_drop)
+        raw_grad = exchange(cotangent.astype(bf16))
+
+    block_input, normed, residual, feed_input, attended_square, made = attention(raw_tokens, attend_pieces)
+    raw_grad, feed_input = after((raw_grad, feed_input))
     if cube:
-        plane_lift, residual = after((plane_lift, residual))
+        plane_lift, feed_input = after((plane_lift, feed_input))
         corner_lift = gather_corner(*plane_lift)
-        raw_grad = exchange(after(cotangent.astype(bf16), plane_lift))
+    grad_rows, grad_bias = place_grad(raw_grad)
+    if cube:
+        corner_lift, grad_rows = after((corner_lift, grad_rows))
+        lift_pieces = gather_cores(line_lift, plane_lift, corner_lift)
     else:
-        raw_grad = exchange(cotangent.astype(bf16))
-    residual, *heads_second, feed_input, attended_square = attention_end(
-        normed, block_input, residual, attend_all
-    )
-    if cube:
-        corner_lift, feed_input = after((corner_lift, feed_input))
-        plane_drop = gather_plane(after(line_drop, corner_lift))
-        lift_all = gather_cores(line_lift, plane_lift, corner_lift)
-    else:
-        lift_all = gather(shard_lift)
-    acted, slope = lift(feed_input, lift_all)
-    if cube:
-        plane_drop, acted, slope, raw_grad = after((plane_drop, acted, slope, raw_grad))
-        corner_drop = gather_corner(*plane_drop)
-    grad_rows, grad_bias = place_grad(raw_grad)
+        lift_pieces = gather_pieces(shard_lift)
+    acted, slope, lift_all = lift(feed_input, lift_pieces)
     drop_send = drop_weight_grad(grad_rows, acted, 0)
     if cube:
         drop_received = swap(drop_send, "mp", 1)
     drop_keep = drop_weight_grad(grad_rows, after(acted, drop_send), 2)
     if cube:
-        corner_drop, drop_keep = after((corner_drop, drop_keep))
-        drop_all = gather_cores(line_drop, plane_drop, corner_drop)
-        drop_all, drop_received = after((drop_all, drop_received))
+        drop_received, drop_keep = after((drop_received, drop_keep))
         corner = scatter_corner(drop_keep, drop_received)
         corner, grad_rows = after((corner, grad_rows))
         from_corner = send_corner(corner)
     else:
-        drop_all = gather(shard_drop)
         drop_grad = scatter(drop_keep, drop_send)
 
     lift_send, grad_feed = expert_back(grad_rows, slope, feed_input, drop_all, lift_all)
@@ -1098,43 +1114,48 @@
     )
     if cube:
         lift_received, from_plane, grad_attended = after((lift_received, from_plane, grad_attended))
-        line = scatter_line(drop_keep, drop_received, *from_plane)
         lift_corner = scatter_corner(lift_keep, lift_received)
-        line, lift_corner, grad_attended = after((line, lift_corner, grad_attended))
-        from_line = send_line(line)
+        drop_line = scatter_line(drop_keep, drop_received, *from_plane)
+        lift_corner, drop_line, acted = after((lift_corner, drop_line, acted))
         from_corner = send_corner(lift_corner)
+        from_line = send_line(drop_line)
     else:
         lift_grad = scatter(lift_keep, lift_send)
-
-    attend_send, grad_normed = attention_back(grad_attended, *heads_first, normed, attend_all)
+    raw_out, feed_square = drop(acted, residual, drop_all)
+    if cube:
+        from_corner, raw_out = after((from_corner, raw_out))
+        plane = scatter_plane(lift_keep, lift_received, *from_corner)
+        from_line, plane, grad_attended = after((from_line, plane, grad_attended))
+        drop_grad = add(drop_line[0], *from_line)
+        from_plane = send_plane(*plane)
+
+    attend_send, grad_normed = attention_back(grad_attended, normed, *made)
     if cube:
         attend_received = swap(attend_send, "mp", 1)
-        from_line, from_corner, grad_normed = after((from_line, from_corner, grad_normed))
-        drop_grad = add(line[0], *from_line)
-        plane = scatter_plane(lift_keep, lift_received, *from_corner)
-        plane, grad_normed = after((plane, grad_normed))
+        from_plane, raw_out, grad_normed = after((from_plane, raw_out, grad_normed))
+        lift_line = scatter_line(lift_keep, lift_received, *from_plane)
+        lift_line, grad_normed = after((lift_line, grad_normed))
+        from_line = send_line(lift_line)
+    block_output = give_back(raw_out)
+    attend_keep, grad_normed = attention_back_end(grad_normed, grad_attended, normed, *made)
+    if cube:
+        attend_received, from_line, attend_keep = after((attend_received, from_line, attend_keep))
+        corner = scatter_corner(attend_keep, attend_received)
+        corner, block_output, grad_normed = after((corner, block_output, grad_normed))
+        from_corner = send_corner(corner)
+    block_output = block_output.astype(f32)
+    grad_raw, grad_norm_first, grad_mask = finish_input_grad(grad_normed, grad_residual, block_input)
+    if cube:
+        from_corner, grad_raw = after((from_corner, grad_raw))
+        plane = scatter_plane(attend_keep, attend_received, *from_corner)
         from_plane = send_plane(*plane)
-    attend_keep, grad_raw, grad_norm_first, grad_mask = attention_back_end(
-        grad_normed, grad_residual, block_input, grad_attended, *heads_second, normed, attend_all
-    )
-    if cube:
-        attend_received, from_plane, attend_keep = after((attend_received, from_plane, attend_keep))
-        line = scatter_line(lift_keep, lift_received, *from_plane)
-        attend_corner = scatter_corner(attend_keep, attend_received)
-        line, attend_corner, acted = after((line, attend_corner, acted))
-        from_line = send_line(line)
-        from_corner = send_corner(attend_corner)
-    input_grad = give_back(grad_raw).astype(f32)
-    raw_out, feed_square = drop(acted, residual, drop_all)
-    block_output = give_back(raw_out).astype(f32)
-    if cube:
-        from_line, from_corner, raw_out = after((from_line, from_corner, raw_out))
-        lift_grad = add(line[0], *from_line)
-        from_plane = send_plane(*scatter_plane(attend_keep, attend_received, *from_corner))
+        lift_grad = add(lift_line[0], *from_line)
+        from_plane, grad_raw = after((from_plane, grad_raw))
         line = scatter_line(attend_keep, attend_received, *from_plane)
         attend_grad = add(line[0], *send_line(line))[0]
     else:
         attend_grad = scatter(attend_keep, attend_send)[0]
+    input_grad = give_back(grad_raw).astype(f32)
 
     squares = jnp.stack(
         [jnp.sum(feed_square[0]), jnp.sum(attended_square), jnp.sum(feed_square[1]), used.astype(f32)]
@@ -1150,7 +1171,11 @@
         axis=0,
     )
     if cube:
-        for axis, bit in (("mp", 1), ("mp", 2), ("dp", 1), ("dp", 2), ("dp", 4)):
+        small = after(small, plane)
+        for axis, bit in (("mp", 1), ("dp", 2), ("dp", 4)):
+            small = small + swap(small, axis, bit)
+        small = after(small, line)
+        for axis, bit in (("mp", 2), ("dp", 1)):
             small = small + swap(small, axis, bit)
     else:
         small = lax.psum(small, ("dp", "mp"))

time: 552 us -> 444 us (0.80)
  Pallas kernels: 243 us -> 172 us
  waiting for transfers between devices: 130 us -> 105 us
  starting transfers between devices: 86.1 us -> 62.9 us
  between operations: 3.83 us -> 17.4 us
  other arithmetic: 50.5 us -> 58.9 us
    pallas_call x11, Pallas kernels: 225 us -> 172 us  [call(): pl.pallas_call(kernel, name=name, grid_spec=pltpu.PrefetchScalarGridSpec(...]
    ppermute x65 -> x53, waiting for transfers between devices: 130 us -> 104 us  [swap(): return lax.ppermute(values, axis, [(i, i ^ bit) for i in range(size)])]
    ppermute x65 -> x53, starting transfers between devices: 69.9 us -> 47.1 us  [swap(): return lax.ppermute(values, axis, [(i, i ^ bit) for i in range(size)])]
    pallas_call x3 -> x0, Pallas kernels: 18.1 us -> none  [assemble(): pl.pallas_call(assemble_kernel, name='assemble', grid_spec=pltpu.Prefetch...]
    unnamed x107 -> x127, local copies, waits for them, and re-layouts: 14.1 us -> 9.19 us
  transfers between devices with their start and end apart: 69 -> 58, of which waited for: 25 -> 24; matrix products, arithmetic and copies ran while one was open for 10% -> 14% of each run, Pallas kernels for 39% -> 36%
where the time goes in v3:
time: 444 us; the launch traced here: 439 us
  Pallas kernels  172 us (39%)
  waiting for transfers between devices  105 us (24%)
  starting transfers between devices  62.9 us (14%)
  other arithmetic  58.9 us (13%)
  local copies, waits for them, and re-layouts  23.1 us (5%)
  between operations  17.4 us (4%)
    pallas_call x11, Pallas kernels, call(): pl.pallas_call(kernel, name=name, grid_spec=pltpu.PrefetchScalarGridSpec(...  172 us
    ppermute x53, waiting for transfers between devices, swap(): return lax.ppermute(values, axis, [(i, i ^ bit) for i in range(size)])  104 us
    ppermute x53, starting transfers between devices, swap(): return lax.ppermute(values, axis, [(i, i ^ bit) for i in range(size)])  47.1 us
    add x3, other arithmetic, add(): total = total + term.astype(f32)  13.4 us
    unnamed x127, local copies, waits for them, and re-layouts  9.19 us
  transfers between devices with their start and end apart: 58, of which 24 were waited for; matrix products, arithmetic and copies ran while one was open for 14% of the time, Pallas kernels for 36%

profile of v3, /device:TPU:0, one launch (start us, length us, event | category | flops | bytes accessed | tf_op | source)
XLA Modules:
  0.0 439.3 jit_solution(2004516094217609683)
XLA Ops:
  7.2 4.4 all-to-all-start
  11.9 4.5 %collective-permute-start.2 = (bf16[1,96,768]{2,1,0:T(8,128)(2,1)S(1)}, bf16[1,96,768]{2,1,0:T(8,128)(2,1)S(1)}, u32[]{:S(2)}, u32[]{:S(2)}) collective-permute-start(bf16[1,96,768]{2,1,0:T(8,128)(2,1)S(1)} %pad_maximum_fusion.9), channel_id=1, source_target_pairs={{0,24},{4,28},{8,16},{12,20},{16,8},{20,12},{24,0},{28,4},{1,25},{... | collective-permute-start | bytes 442376 | tf_op jit(solution)/shard_map/ppermute | solution.py:758
  17.0 4.2 collective-permute-done.2
  21.2 8.3 %collective-permute-done.1 = bf16[1,96,768]{2,1,0:T(8,128)(2,1)S(1)} collective-permute-done((bf16[1,96,768]{2,1,0:T(8,128)(2,1)S(1)}, bf16[1,96,768]{2,1,0:T(8,128)(2,1)S(1)}, u32[]{:S(2)}, u32[]{:S(2)}) %collective-permute-start.1) | collective-permute-done | bytes 147488 | tf_op jit(solution)/shard_map/ppermute | solution.py:758
  30.7 2.2 collective-permute-start.8
  34.0 3.6 collective-permute-start.5
  38.4 7.6 %collective-permute-done.8.refs_1_ = bf16[4,1,96,768]{3,2,1,0:T(8,128)(2,1)S(1)} collective-permute-done((bf16[4,1,96,768]{3,2,1,0:T(8,128)(2,1)S(1)}, bf16[4,1,96,768]{3,2,1,0:T(8,128)(2,1)S(1)}, u32[]{:S(2)}, u32[]{:S(2)}) %collective-permute-start.8) | collective-permute-done | bytes 589856 | tf_op jit(solution)/shard_map/ppermute | solution.py:758
  50.7 11.8 %collective-permute-done.4 = bf16[2,96,768]{2,1,0:T(8,128)(2,1)} collective-permute-done((bf16[2,96,768]{2,1,0:T(8,128)(2,1)}, bf16[2,96,768]{2,1,0:T(8,128)(2,1)}, u32[]{:S(2)}, u32[]{:S(2)}) %collective-permute-start.4) | collective-permute-done | bytes 294944 | tf_op jit(solution)/shard_map/ppermute | solution.py:758
  62.5 2.4 pad_maximum_fusion.refs_0_
  74.2 1.9 fusion.24.valid_ref
  76.1 4.2 all-to-all-start.1
  80.9 2.0 collective-permute-start.7
  82.9 31.5 %attention.1 = (f32[1168,768]{1,0:T(8,128)}, bf16[1168,768]{1,0:T(8,128)(2,1)}, f32[1168,768]{1,0:T(8,128)}, bf16[1168,768]{1,0:T(8,128)(2,1)}, f32[1,768]{1,0:T...) custom-call(s32[6]{0:T(128)} %pad_add_fusion.1.meta_ref, ...), custom_call_target="tpu_custom_call" | custom-call | flops 38000001024 | bytes 38000000 | tf_op jit(solution)/shard_map/attention/pallas_call | solution.py:677
  114.4 2.9 collective-permute-done.6.refs_1_
  117.2 16.2 %collective-permute-done.7.refs_2_ = bf16[4,2,96,768]{3,2,1,0:T(8,128)(2,1)} collective-permute-done((bf16[4,2,96,768]{3,2,1,0:T(8,128)(2,1)S(1)}, bf16[4,2,96,768]{3,2,1,0:T(8,128)(2,1)}, u32[]{:S(2)}, u32[]{:S(2)}) %collective-permute-start.7) | collective-permute-done | bytes 1179680 | tf_op jit(solution)/shard_map/ppermute | solution.py:758
  136.6 4.9 %place_grad.1 = (bf16[1024,768]{1,0:T(8,128)(2,1)}, f32[2,768]{1,0:T(2,128)}) custom-call(bf16[960,768]{1,0:T(8,128)(2,1)} %bitcast.206, s32[1,960]{1,0:T(1,128)} %reshape_select_fusion.place_ref), custom_call_target="tpu_custom_call" | custom-call | flops 5000000000 | bytes 5000000 | tf_op jit(solution)/shard_map/place_grad/pallas_call | solution.py:677
  141.5 16.8 %collective-permute-done.17.refs_3_ = bf16[2,2,96,768]{3,2,1,0:T(8,128)(2,1)S(1)} collective-permute-done((bf16[2,2,96,768]{3,2,1,0:T(8,128)(2,1)S(1)}, bf16[2,2,96,768]{3,2,1,0:T(8,128)(2,1)S(1)}, u32[]{:S(2)}, u32[]{:S(2)}) %collective-permute-start.17) | collective-permute-done | bytes 589856 | tf_op jit(solution)/shard_map/ppermute | solution.py:758
  162.8 17.0 %lift.1 = (bf16[4,1168,768]{2,1,0:T(8,128)(2,1)}, bf16[4,1168,768]{2,1,0:T(8,128)(2,1)}, bf16[2,4,768,768]{3,2,1,0:T(8,128)(2,1)}) custom-call(s32[2]{0:T(128)} %pad_add_fusion.mine_ref, bf16[1168,768]{1,0:T(8,128)(2,1)} %get-tuple-element.133.feed_ref, bf16[4,2,96,768]{3,2,1,0:T(8,128)(2,1)} %pad_maximum_fusion.refs_0_, ...), custom_call_target="tpu_custom_call" | custom-call | flops 16000000000 | bytes 16000000 | tf_op jit(solution)/shard_map/lift/pallas_call | solution.py:677
  179.9 7.4 %drop_weight_grad.2 = bf16[2,8,2,96,768]{4,3,2,1,0:T(8,128)(2,1)} custom-call(s32[2]{0:T(128)} %pad_add_fusion.mine_ref, bf16[1024,768]{1,0:T(8,128)(2,1)} %get-tuple-element.140.grad_ref, bf16[4,1168,768]{2,1,0:T(8,128)(2,1)} %get-tuple-element.161.acted_ref), custom_call_target="tpu_custom_call" | custom-call | flops 7000000000 | bytes 7000000 | tf_op jit(solution)/shard_map/drop_weight_grad/pallas_call | solution.py:677
  187.3 7.6 %drop_weight_grad.3 = bf16[2,8,2,96,768]{4,3,2,1,0:T(8,128)(2,1)} custom-call(s32[2]{0:T(128)} %pad_add_fusion.mine_ref, bf16[1024,768]{1,0:T(8,128)(2,1)} %get-tuple-element.140.grad_ref, bf16[4,1168,768]{2,1,0:T(8,128)(2,1)} %get-tuple-element.161.acted_ref), custom_call_target="tpu_custom_call" | custom-call | flops 7000000000 | bytes 7000000 | tf_op jit(solution)/shard_map/drop_weight_grad/pallas_call | solution.py:677
  195.5 2.1 copy-done.3
  197.6 5.5 %convert_add_fusion.2 = (f32[1,1,4,2,96,768]{5,4,3,2,1,0:T(8,128)S(1)}, f32[1,1,4,2,96,768]{5,4,3,2,1,0:T(8,128)}, bf16[4,2,96,768]{3,2,1,0:T(8,128)(2,1)S(1)}) fusion(bf16[2,2,4,2,96,768]{5,4,3,2,1,0:T(8,128)(2,1)} %bitcast.197, bf16[2,2,4,2,96,768]{5,4,3,2,1,0:T(8,128)(2,1)} %bitcast.199), kind=kLoop, calls=%fused_computation.9 | loop fusion | flops 5898240 | bytes 12976128 | tf_op jit(solution)/shard_map/add | solution.py:796
  203.1 15.6 %expert_back.1 = (bf16[2,8,2,96,768]{4,3,2,1,0:T(8,128)(2,1)}, f32[1024,768]{1,0:T(8,128)}) custom-call(s32[2]{0:T(128)} %pad_add_fusion.mine_ref, bf16[1024,768]{1,0:T(8,128)(2,1)} %get-tuple-element.140.grad_ref, bf16[4,1168,768]{2,1,0:T(8,128)(2,1)} %get-tuple-element.141.slope_ref, bf16[1168,768]{1,0:T(8,128)(2,1)} %get-tuple-element.133.feed_ref, ...), custom_call_target="tpu_custom_call" | custom-call | flops 16999999488 | bytes 17000000 | tf_op jit(solution)/shard_map/expert_back/pallas_call | solution.py:677
  222.8 2.0 select_select_fusion.place_ref
  227.0 8.8 %collective-permute-done.25 = bf16[2,2,96,768]{3,2,1,0:T(8,128)(2,1)} collective-permute-done((bf16[2,2,96,768]{3,2,1,0:T(8,128)(2,1)}, bf16[2,2,96,768]{3,2,1,0:T(8,128)(2,1)}, u32[]{:S(2)}, u32[]{:S(2)}) %collective-permute-start.25) | collective-permute-done | bytes 589856 | tf_op jit(solution)/shard_map/ppermute | solution.py:758
  239.8 21.0 %expert_back_end.1 = (bf16[2,8,2,96,768]{4,3,2,1,0:T(8,128)(2,1)}, f32[1024,768]{1,0:T(8,128)}, bf16[1024,768]{1,0:T(8,128)(2,1)}, f32[2,768]{1,0:T(2,128)}) custom-call(s32[2]{0:T(128)} %pad_add_fusion.mine_ref, bf16[1024,768]{1,0:T(8,128)(2,1)} %get-tuple-element.140.grad_ref, bf16[4,1168,768]{2,1,0:T(8,128)(2,1)} %get-tuple-element.141.slope_ref, ...), custom_call_target="tpu_custom_call" | custom-call | flops 16999999488 | bytes 17000000 | tf_op jit(solution)/shard_map/expert_back_end/pallas_call | solution.py:677
  260.8 4.4 %collective-permute-done.28 = bf16[4,2,96,768]{3,2,1,0:T(8,128)(2,1)S(1)} collective-permute-done((bf16[4,2,96,768]{3,2,1,0:T(8,128)(2,1)S(1)}, bf16[4,2,96,768]{3,2,1,0:T(8,128)(2,1)S(1)}, u32[]{:S(2)}, u32[]{:S(2)}) %collective-permute-start.28) | collective-permute-done | bytes 1179680 | tf_op jit(solution)/shard_map/ppermute | solution.py:758
  267.4 4.2 convert_add_fusion
  271.5 2.7 fusion.3
  275.2 2.2 collective-permute-start.31
  277.4 2.2 collective-permute-start.32
  281.6 17.8 %drop.1 = (bf16[960,768]{1,0:T(8,128)(2,1)}, f32[2,768]{1,0:T(2,128)}) custom-call(s32[2]{0:T(128)} %pad_add_fusion.mine_ref, bf16[4,1168,768]{2,1,0:T(8,128)(2,1)} %get-tuple-element.161.acted_ref, f32[1168,768]{1,0:T(8,128)} %get-tuple-element.150.residual_ref, f32[1168,1]{1,0:T(8,128)} %fusion.24.valid_ref, s32[960,1]{1,0:T(8,128)} %select_select_fusion.place_ref, ...), custom_call_target="tpu_custom_call" | custom-call | flops 16999999488 | bytes 17000000 | tf_op jit(solution)/shard_map/drop/pallas_call | solution.py:677
  305.2 18.8 %attention_back.1 = (bf16[2,8,1,96,768]{4,3,2,1,0:T(8,128)(2,1)}, f32[1024,768]{1,0:T(8,128)}) custom-call(s32[2]{0:T(128)} %pad_add_fusion.mine_ref, bf16[1024,768]{1,0:T(8,128)(2,1)} %get-tuple-element.166.grad_attended_ref, bf16[4,1168,576]{2,1,0:T(8,128)(2,1)} %get-tuple-element.167.joint_ref, bf16[4,1168,192]{2,1,0:T(8,128)(2,1)} %get-tuple-element.168.mixed_ref, ...), custom_call_target="tpu_custom_call" | custom-call | flops 19000000512 | bytes 19000000 | tf_op jit(solution)/shard_map/attention_back/pallas_call | solution.py:677
  324.1 2.7 collective-permute-done.36
  327.8 2.4 fusion.1
  336.6 3.6 all-to-all-start.2
  340.1 19.5 %attention_back_end.1 = (bf16[2,8,1,96,768]{4,3,2,1,0:T(8,128)(2,1)}, f32[1024,768]{1,0:T(8,128)}) custom-call(s32[2]{0:T(128)} %pad_add_fusion.mine_ref, bf16[1024,768]{1,0:T(8,128)(2,1)} %get-tuple-element.166.grad_attended_ref, bf16[4,1168,576]{2,1,0:T(8,128)(2,1)} %get-tuple-element.167.joint_ref, bf16[4,1168,192]{2,1,0:T(8,128)(2,1)} %get-tuple-element.168.mixed_ref, ...), custom_call_target="tpu_custom_call" | custom-call | flops 19000000512 | bytes 19000000 | tf_op jit(solution)/shard_map/attention_back_end/pallas_call | solution.py:677
  360.4 3.7 convert_add_fusion.4
  365.9 2.0 collective-permute-start.42
  367.9 10.7 %input_grad.1 = (bf16[960,768]{1,0:T(8,128)(2,1)}, f32[2,768]{1,0:T(2,128)}, f32[1,768]{1,0:T(1,128)}) custom-call(f32[1024,768]{1,0:T(8,128)} %get-tuple-element.189.grad_normed_ref, f32[1024,768]{1,0:T(8,128)} %get-tuple-element.190.grad_residual_ref, f32[1168,768]{1,0:T(8,128)} %get-tuple-element.191.block_ref, s32[1168,1]{1,0:T(8,128)} %reshape.702.hidden_ref, ...), custom_call_target="tpu_custom_call" | custom-call | flops 8999999488 | bytes 9000000 | tf_op jit(solution)/shard_map/input_grad/pallas_call | solution.py:677
  382.3 2.0 select_maximum_fusion
  386.7 3.8 collective-permute-done.46
  391.7 3.2 fusion.61
  396.5 2.1 fusion.15
  400.1 2.7 fusion.63
  405.8 3.7 all-to-all-start.3
  409.5 2.1 collective-permute-start.52
  418.2 7.5 %collective-permute-done.51 = bf16[1,96,768]{2,1,0:T(8,128)(2,1)S(1)} collective-permute-done((bf16[1,96,768]{2,1,0:T(8,128)(2,1)S(1)}, bf16[1,96,768]{2,1,0:T(8,128)(2,1)S(1)}, u32[]{:S(2)}, u32[]{:S(2)}) %collective-permute-start.51) | collective-permute-done | bytes 147488 | tf_op jit(solution)/shard_map/ppermute | solution.py:758
  (294 shorter events, 81.7 us)
Async XLA Ops:
  7.2 23.4 %all-to-all-start = ((bf16[4,240,768]{2,1,0:T(8,128)(2,1)}), bf16[4,240,768]{2,1,0:T(8,128)(2,1)S(1)}, u32[]{:S(2)}, u32[]{:S(2)}) async-start(bf16[4,240,768]{2,1,0:T(8,128)(2,1)} %param.23), calls=%async_computation | async-start | bytes 2949120 | tf_op jit(solution)/shard_map/all_to_all | solution.py:761
  11.6 191.5 %all-gather.2.cloned.1.call-start = ((), (), s32[]{:S(2)}) async-start(), calls=%async_computation.4 | async-start | bytes 9732096 | tf_op jit(solution)/shard_map/all_gather | solution.py:769
  16.4 13.1 %collective-permute-start.1 = (bf16[1,96,768]{2,1,0:T(8,128)(2,1)S(1)}, bf16[1,96,768]{2,1,0:T(8,128)(2,1)S(1)}, u32[]{:S(2)}, u32[]{:S(2)}) collective-permute-start(bf16[1,96,768]{2,1,0:T(8,128)(2,1)S(1)} %pad_maximum_fusion.9), channel_id=1, source_target_pairs={{0,16},{4,20},{8,24},{12,28},{16,0},{20,4},{24,8},{28,12},{1,17},{... | collective-permute-start | bytes 442376 | tf_op jit(solution)/shard_map/ppermute | solution.py:758
  16.4 13.1 %collective-permute-start = (bf16[1,96,768]{2,1,0:T(8,128)(2,1)S(1)}, bf16[1,96,768]{2,1,0:T(8,128)(2,1)S(1)}, u32[]{:S(2)}, u32[]{:S(2)}) collective-permute-start(bf16[1,96,768]{2,1,0:T(8,128)(2,1)S(1)} %pad_maximum_fusion.9), channel_id=1, source_target_pairs={{0,8},{4,12},{8,0},{12,4},{16,24},{20,28},{24,16},{28,20},{1,9},{5... | collective-permute-start | bytes 442376 | tf_op jit(solution)/shard_map/ppermute | solution.py:758
  30.7 15.4 %collective-permute-start.8 = (bf16[4,1,96,768]{3,2,1,0:T(8,128)(2,1)S(1)}, bf16[4,1,96,768]{3,2,1,0:T(8,128)(2,1)S(1)}, u32[]{:S(2)}, u32[]{:S(2)}) collective-permute-start(bf16[4,1,96,768]{3,2,1,0:T(8,128)(2,1)S(1)} %pad_maximum_fusion.5.refs_0_), channel_id=1, source_target_pairs={{0,4},{4,0},{8,12},{12,8},{16,20},{20,16},{24,28},{28,24},{1,5},{5... | collective-permute-start | bytes 1769480 | tf_op jit(solution)/shard_map/ppermute | solution.py:758
  32.9 14.6 %collective-permute-start.9 = (bf16[4,1,96,768]{3,2,1,0:T(8,128)(2,1)S(1)}, bf16[4,1,96,768]{3,2,1,0:T(8,128)(2,1)S(1)}, u32[]{:S(2)}, u32[]{:S(2)}) collective-permute-start(bf16[4,1,96,768]{3,2,1,0:T(8,128)(2,1)S(1)} %pad_maximum_fusion.5.refs_0_), channel_id=1, source_target_pairs={{0,2},{1,3},{2,0},{3,1},{4,6},{5,7},{6,4},{7,5},{8,10},{9,11},{10,... | collective-permute-start | bytes 1769480 | tf_op jit(solution)/shard_map/ppermute | solution.py:758
  34.0 16.7 %collective-permute-start.5 = (bf16[2,96,768]{2,1,0:T(8,128)(2,1)}, bf16[2,96,768]{2,1,0:T(8,128)(2,1)}, u32[]{:S(2)}, u32[]{:S(2)}) collective-permute-start(bf16[2,96,768]{2,1,0:T(8,128)(2,1)} %convert_element_type.389), channel_id=1, source_target_pairs={{0,24},{4,28},{8,16},{12,20},{16,8},{20,12},{24,0},{28,4},{1,25},{... | collective-permute-start | bytes 884744 | tf_op jit(solution)/shard_map/ppermute | solution.py:758
  37.6 24.9 %collective-permute-start.4 = (bf16[2,96,768]{2,1,0:T(8,128)(2,1)}, bf16[2,96,768]{2,1,0:T(8,128)(2,1)}, u32[]{:S(2)}, u32[]{:S(2)}) collective-permute-start(bf16[2,96,768]{2,1,0:T(8,128)(2,1)} %convert_element_type.389), channel_id=1, source_target_pairs={{0,16},{4,20},{8,24},{12,28},{16,0},{20,4},{24,8},{28,12},{1,17},{... | collective-permute-start | bytes 884744 | tf_op jit(solution)/shard_map/ppermute | solution.py:758
  37.6 24.9 %collective-permute-start.3 = (bf16[2,96,768]{2,1,0:T(8,128)(2,1)}, bf16[2,96,768]{2,1,0:T(8,128)(2,1)}, u32[]{:S(2)}, u32[]{:S(2)}) collective-permute-start(bf16[2,96,768]{2,1,0:T(8,128)(2,1)} %convert_element_type.389), channel_id=1, source_target_pairs={{0,8},{4,12},{8,0},{12,4},{16,24},{20,28},{24,16},{28,20},{1,9},{5... | collective-permute-start | bytes 884744 | tf_op jit(solution)/shard_map/ppermute | solution.py:758
  46.8 18.2 %collective-permute-start.10 = (bf16[2,1,96,768]{3,2,1,0:T(8,128)(2,1)}, bf16[2,1,96,768]{3,2,1,0:T(8,128)(2,1)}, u32[]{:S(2)}, u32[]{:S(2)}) collective-permute-start(bf16[2,1,96,768]{3,2,1,0:T(8,128)(2,1)} %slice.338), channel_id=1, source_target_pairs={{0,2},{1,3},{2,0},{3,1},{4,6},{5,7},{6,4},{7,5},{8,10},{9,11},{10,... | collective-permute-start | bytes 884744 | tf_op jit(solution)/shard_map/ppermute | solution.py:758
  48.3 16.7 %collective-permute-start.11 = (bf16[2,1,96,768]{3,2,1,0:T(8,128)(2,1)}, bf16[2,1,96,768]{3,2,1,0:T(8,128)(2,1)}, u32[]{:S(2)}, u32[]{:S(2)}) collective-permute-start(bf16[2,1,96,768]{3,2,1,0:T(8,128)(2,1)} %slice.339), channel_id=1, source_target_pairs={{0,4},{4,0},{8,12},{12,8},{16,20},{20,16},{24,28},{28,24},{1,5},{5... | collective-permute-start | bytes 884744 | tf_op jit(solution)/shard_map/ppermute | solution.py:758
  67.6 12.7 %collective-permute-start.12 = (bf16[4,1,96,768]{3,2,1,0:T(8,128)(2,1)S(1)}, bf16[4,1,96,768]{3,2,1,0:T(8,128)(2,1)}, u32[]{:S(2)}, u32[]{:S(2)}) collective-permute-start(bf16[4,1,96,768]{3,2,1,0:T(8,128)(2,1)S(1)} %copy-done.25), channel_id=1, source_target_pairs={{0,1},{1,0},{2,3},{3,2},{4,5},{5,4},{6,7},{7,6},{8,9},{9,8},{10,11... | collective-permute-start | bytes 1769480 | tf_op jit(solution)/shard_map/ppermute | solution.py:758
  67.7 15.2 %collective-permute-start.13 = (bf16[4,1,96,768]{3,2,1,0:T(8,128)(2,1)}, bf16[4,1,96,768]{3,2,1,0:T(8,128)(2,1)}, u32[]{:S(2)}, u32[]{:S(2)}) collective-permute-start(bf16[4,1,96,768]{3,2,1,0:T(8,128)(2,1)} %copy-done.35), channel_id=1, source_target_pairs={{0,1},{1,0},{2,3},{3,2},{4,5},{5,4},{6,7},{7,6},{8,9},{9,8},{10,11... | collective-permute-start | bytes 1769480 | tf_op jit(solution)/shard_map/ppermute | solution.py:758
  68.2 14.8 %collective-permute-start.14 = (bf16[4,1,96,768]{3,2,1,0:T(8,128)(2,1)}, bf16[4,1,96,768]{3,2,1,0:T(8,128)(2,1)}, u32[]{:S(2)}, u32[]{:S(2)}) collective-permute-start(bf16[4,1,96,768]{3,2,1,0:T(8,128)(2,1)} %copy-done.36), channel_id=1, source_target_pairs={{0,1},{1,0},{2,3},{3,2},{4,5},{5,4},{6,7},{7,6},{8,9},{9,8},{10,11... | collective-permute-start | bytes 1769480 | tf_op jit(solution)/shard_map/ppermute | solution.py:758
  70.1 10.8 %collective-permute-start.15 = (bf16[2,1,96,768]{3,2,1,0:T(8,128)(2,1)}, bf16[2,1,96,768]{3,2,1,0:T(8,128)(2,1)}, u32[]{:S(2)}, u32[]{:S(2)}) collective-permute-start(bf16[2,1,96,768]{3,2,1,0:T(8,128)(2,1)} %collective-permute-done.10.refs_3_), channel_id=1, source_target_pairs={{0,1},{1,0},{2,3},{3,2},{4,5},{5,4},{6,7},{7,6},{8,9},{9,8},{10,11... | collective-permute-start | bytes 884744 | tf_op jit(solution)/shard_map/ppermute | solution.py:758
  70.6 12.3 %collective-permute-start.16 = (bf16[2,1,96,768]{3,2,1,0:T(8,128)(2,1)}, bf16[2,1,96,768]{3,2,1,0:T(8,128)(2,1)}, u32[]{:S(2)}, u32[]{:S(2)}) collective-permute-start(bf16[2,1,96,768]{3,2,1,0:T(8,128)(2,1)} %collective-permute-done.11.refs_4_), channel_id=1, source_target_pairs={{0,1},{1,0},{2,3},{3,2},{4,5},{5,4},{6,7},{7,6},{8,9},{9,8},{10,11... | collective-permute-start | bytes 884744 | tf_op jit(solution)/shard_map/ppermute | solution.py:758
  76.1 38.3 %all-to-all-start.1 = ((bf16[4,240,768]{2,1,0:T(8,128)(2,1)}), bf16[4,240,768]{2,1,0:T(8,128)(2,1)S(1)}, u32[]{:S(2)}, u32[]{:S(2)}) async-start(bf16[4,240,768]{2,1,0:T(8,128)(2,1)} %convert_element_type.390), calls=%async_computation.1 | async-start | bytes 2949120 | tf_op jit(solution)/shard_map/all_to_all | solution.py:761
  80.3 36.9 %collective-permute-start.6 = (bf16[4,2,96,768]{3,2,1,0:T(8,128)(2,1)S(1)}, bf16[4,2,96,768]{3,2,1,0:T(8,128)(2,1)}, u32[]{:S(2)}, u32[]{:S(2)}) collective-permute-start(bf16[4,2,96,768]{3,2,1,0:T(8,128)(2,1)S(1)} %copy-done.14), channel_id=1, source_target_pairs={{0,4},{4,0},{8,12},{12,8},{16,20},{20,16},{24,28},{28,24},{1,5},{5... | collective-permute-start | bytes 3538952 | tf_op jit(solution)/shard_map/ppermute | solution.py:758
  80.9 52.5 %collective-permute-start.7 = (bf16[4,2,96,768]{3,2,1,0:T(8,128)(2,1)S(1)}, bf16[4,2,96,768]{3,2,1,0:T(8,128)(2,1)}, u32[]{:S(2)}, u32[]{:S(2)}) collective-permute-start(bf16[4,2,96,768]{3,2,1,0:T(8,128)(2,1)S(1)} %copy-done.14), channel_id=1, source_target_pairs={{0,2},{1,3},{2,0},{3,1},{4,6},{5,7},{6,4},{7,5},{8,10},{9,11},{10,... | collective-permute-start | bytes 3538952 | tf_op jit(solution)/shard_map/ppermute | solution.py:758
  134.6 23.7 %collective-permute-start.17 = (bf16[2,2,96,768]{3,2,1,0:T(8,128)(2,1)S(1)}, bf16[2,2,96,768]{3,2,1,0:T(8,128)(2,1)S(1)}, u32[]{:S(2)}, u32[]{:S(2)}) collective-permute-start(bf16[2,2,96,768]{3,2,1,0:T(8,128)(2,1)S(1)} %slice.260), channel_id=1, source_target_pairs={{0,2},{1,3},{2,0},{3,1},{4,6},{5,7},{6,4},{7,5},{8,10},{9,11},{10,... | collective-permute-start | bytes 1769480 | tf_op jit(solution)/shard_map/ppermute | solution.py:758
  135.9 22.4 %collective-permute-start.18 = (bf16[2,2,96,768]{3,2,1,0:T(8,128)(2,1)S(1)}, bf16[2,2,96,768]{3,2,1,0:T(8,128)(2,1)}, u32[]{:S(2)}, u32[]{:S(2)}) collective-permute-start(bf16[2,2,96,768]{3,2,1,0:T(8,128)(2,1)S(1)} %slice.261), channel_id=1, source_target_pairs={{0,4},{4,0},{8,12},{12,8},{16,20},{20,16},{24,28},{28,24},{1,5},{5... | collective-permute-start | bytes 1769480 | tf_op jit(solution)/shard_map/ppermute | solution.py:758
  136.0 23.4 %collective-permute-start.19 = (bf16[4,2,96,768]{3,2,1,0:T(8,128)(2,1)S(1)}, bf16[4,2,96,768]{3,2,1,0:T(8,128)(2,1)S(1)}, u32[]{:S(2)}, u32[]{:S(2)}) collective-permute-start(bf16[4,2,96,768]{3,2,1,0:T(8,128)(2,1)S(1)} %copy-done.14), channel_id=1, source_target_pairs={{0,1},{1,0},{2,3},{3,2},{4,5},{5,4},{6,7},{7,6},{8,9},{9,8},{10,11... | collective-permute-start | bytes 3538952 | tf_op jit(solution)/shard_map/ppermute | solution.py:758
  136.0 23.3 %collective-permute-start.20 = (bf16[4,2,96,768]{3,2,1,0:T(8,128)(2,1)}, bf16[4,2,96,768]{3,2,1,0:T(8,128)(2,1)S(1)}, u32[]{:S(2)}, u32[]{:S(2)}) collective-permute-start(bf16[4,2,96,768]{3,2,1,0:T(8,128)(2,1)} %collective-permute-done.6.refs_1_), channel_id=1, source_target_pairs={{0,1},{1,0},{2,3},{3,2},{4,5},{5,4},{6,7},{7,6},{8,9},{9,8},{10,11... | collective-permute-start | bytes 3538952 | tf_op jit(solution)/shard_map/ppermute | solution.py:758
  136.5 22.8 %collective-permute-start.21 = (bf16[4,2,96,768]{3,2,1,0:T(8,128)(2,1)}, bf16[4,2,96,768]{3,2,1,0:T(8,128)(2,1)}, u32[]{:S(2)}, u32[]{:S(2)}) collective-permute-start(bf16[4,2,96,768]{3,2,1,0:T(8,128)(2,1)} %collective-permute-done.7.refs_2_), channel_id=1, source_target_pairs={{0,1},{1,0},{2,3},{3,2},{4,5},{5,4},{6,7},{7,6},{8,9},{9,8},{10,11... | collective-permute-start | bytes 3538952 | tf_op jit(solution)/shard_map/ppermute | solution.py:758
  218.7 47.6 %collective-permute-start.27 = (bf16[2,8,2,96,768]{4,3,2,1,0:T(8,128)(2,1)}, bf16[2,8,2,96,768]{4,3,2,1,0:T(8,128)(2,1)}, u32[]{:S(2)}, u32[]{:S(2)}) collective-permute-start(bf16[2,8,2,96,768]{4,3,2,1,0:T(8,128)(2,1)} %get-tuple-element.152), channel_id=1, source_target_pairs={{0,1},{1,0},{2,3},{3,2},{4,5},{5,4},{6,7},{7,6},{8,9},{9,8},{10,11... | collective-permute-start | bytes 14155784 | tf_op jit(solution)/shard_map/ppermute | solution.py:758
  219.9 15.9 %collective-permute-start.25 = (bf16[2,2,96,768]{3,2,1,0:T(8,128)(2,1)}, bf16[2,2,96,768]{3,2,1,0:T(8,128)(2,1)}, u32[]{:S(2)}, u32[]{:S(2)}) collective-permute-start(bf16[2,2,96,768]{3,2,1,0:T(8,128)(2,1)} %get-tuple-element.369), channel_id=1, source_target_pairs={{0,4},{4,0},{8,12},{12,8},{16,20},{20,16},{24,28},{28,24},{1,5},{5... | collective-permute-start | bytes 1769480 | tf_op jit(solution)/shard_map/ppermute | solution.py:758
  220.4 15.6 %collective-permute-start.26 = (bf16[2,2,96,768]{3,2,1,0:T(8,128)(2,1)}, bf16[2,2,96,768]{3,2,1,0:T(8,128)(2,1)}, u32[]{:S(2)}, u32[]{:S(2)}) collective-permute-start(bf16[2,2,96,768]{3,2,1,0:T(8,128)(2,1)} %get-tuple-element.368), channel_id=1, source_target_pairs={{0,2},{1,3},{2,0},{3,1},{4,6},{5,7},{6,4},{7,5},{8,10},{9,11},{10,... | collective-permute-start | bytes 1769480 | tf_op jit(solution)/shard_map/ppermute | solution.py:758
  237.8 27.4 %collective-permute-start.28 = (bf16[4,2,96,768]{3,2,1,0:T(8,128)(2,1)S(1)}, bf16[4,2,96,768]{3,2,1,0:T(8,128)(2,1)S(1)}, u32[]{:S(2)}, u32[]{:S(2)}) collective-permute-start(bf16[4,2,96,768]{3,2,1,0:T(8,128)(2,1)S(1)} %pad_maximum_fusion.1), channel_id=1, source_target_pairs={{0,4},{4,0},{8,12},{12,8},{16,20},{20,16},{24,28},{28,24},{1,5},{5... | collective-permute-start | bytes 3538952 | tf_op jit(solution)/shard_map/ppermute | solution.py:758
  239.5 26.8 %collective-permute-start.29 = (bf16[4,2,96,768]{3,2,1,0:T(8,128)(2,1)S(1)}, bf16[4,2,96,768]{3,2,1,0:T(8,128)(2,1)S(1)}, u32[]{:S(2)}, u32[]{:S(2)}) collective-permute-start(bf16[4,2,96,768]{3,2,1,0:T(8,128)(2,1)S(1)} %pad_maximum_fusion.2), channel_id=1, source_target_pairs={{0,2},{1,3},{2,0},{3,1},{4,6},{5,7},{6,4},{7,5},{8,10},{9,11},{10,... | collective-permute-start | bytes 3538952 | tf_op jit(solution)/shard_map/ppermute | solution.py:758
  275.2 27.0 %collective-permute-start.30 = (bf16[2,96,768]{2,1,0:T(8,128)(2,1)}, bf16[2,96,768]{2,1,0:T(8,128)(2,1)S(1)}, u32[]{:S(2)}, u32[]{:S(2)}) collective-permute-start(bf16[2,96,768]{2,1,0:T(8,128)(2,1)} %get-tuple-element.367), channel_id=1, source_target_pairs={{0,8},{4,12},{8,0},{12,4},{16,24},{20,28},{24,16},{28,20},{1,9},{5... | collective-permute-start | bytes 884744 | tf_op jit(solution)/shard_map/ppermute | solution.py:758
  275.2 27.1 %collective-permute-start.31 = (bf16[2,96,768]{2,1,0:T(8,128)(2,1)}, bf16[2,96,768]{2,1,0:T(8,128)(2,1)}, u32[]{:S(2)}, u32[]{:S(2)}) collective-permute-start(bf16[2,96,768]{2,1,0:T(8,128)(2,1)} %get-tuple-element.366), channel_id=1, source_target_pairs={{0,16},{4,20},{8,24},{12,28},{16,0},{20,4},{24,8},{28,12},{1,17},{... | collective-permute-start | bytes 884744 | tf_op jit(solution)/shard_map/ppermute | solution.py:758
  277.4 24.9 %collective-permute-start.32 = (bf16[2,96,768]{2,1,0:T(8,128)(2,1)}, bf16[2,96,768]{2,1,0:T(8,128)(2,1)}, u32[]{:S(2)}, u32[]{:S(2)}) collective-permute-start(bf16[2,96,768]{2,1,0:T(8,128)(2,1)} %get-tuple-element.365), channel_id=1, source_target_pairs={{0,24},{4,28},{8,16},{12,20},{16,8},{20,12},{24,0},{28,4},{1,25},{... | collective-permute-start | bytes 884744 | tf_op jit(solution)/shard_map/ppermute | solution.py:758
  280.6 18.9 %collective-permute-start.33 = (bf16[2,2,96,768]{3,2,1,0:T(8,128)(2,1)}, bf16[2,2,96,768]{3,2,1,0:T(8,128)(2,1)}, u32[]{:S(2)}, u32[]{:S(2)}) collective-permute-start(bf16[2,2,96,768]{3,2,1,0:T(8,128)(2,1)} %get-tuple-element.364), channel_id=1, source_target_pairs={{0,4},{4,0},{8,12},{12,8},{16,20},{20,16},{24,28},{28,24},{1,5},{5... | collective-permute-start | bytes 1769480 | tf_op jit(solution)/shard_map/ppermute | solution.py:758
  281.3 18.2 %collective-permute-start.34 = (bf16[2,2,96,768]{3,2,1,0:T(8,128)(2,1)}, bf16[2,2,96,768]{3,2,1,0:T(8,128)(2,1)}, u32[]{:S(2)}, u32[]{:S(2)}) collective-permute-start(bf16[2,2,96,768]{3,2,1,0:T(8,128)(2,1)} %get-tuple-element.363), channel_id=1, source_target_pairs={{0,2},{1,3},{2,0},{3,1},{4,6},{5,7},{6,4},{7,5},{8,10},{9,11},{10,... | collective-permute-start | bytes 1769480 | tf_op jit(solution)/shard_map/ppermute | solution.py:758
  302.2 24.6 %collective-permute-start.36 = (bf16[4,2,96,768]{3,2,1,0:T(8,128)(2,1)S(1)}, bf16[4,2,96,768]{3,2,1,0:T(8,128)(2,1)S(1)}, u32[]{:S(2)}, u32[]{:S(2)}) collective-permute-start(bf16[4,2,96,768]{3,2,1,0:T(8,128)(2,1)S(1)} %pad_maximum_fusion.3), channel_id=1, source_target_pairs={{0,4},{4,0},{8,12},{12,8},{16,20},{20,16},{24,28},{28,24},{1,5},{5... | collective-permute-start | bytes 3538952 | tf_op jit(solution)/shard_map/ppermute | solution.py:758
  303.7 24.1 %collective-permute-start.37 = (bf16[4,2,96,768]{3,2,1,0:T(8,128)(2,1)S(1)}, bf16[4,2,96,768]{3,2,1,0:T(8,128)(2,1)S(1)}, u32[]{:S(2)}, u32[]{:S(2)}) collective-permute-start(bf16[4,2,96,768]{3,2,1,0:T(8,128)(2,1)S(1)} %pad_maximum_fusion.4), channel_id=1, source_target_pairs={{0,2},{1,3},{2,0},{3,1},{4,6},{5,7},{6,4},{7,5},{8,10},{9,11},{10,... | collective-permute-start | bytes 3538952 | tf_op jit(solution)/shard_map/ppermute | solution.py:758
  324.0 35.7 %collective-permute-start.35 = (bf16[2,8,1,96,768]{4,3,2,1,0:T(8,128)(2,1)}, bf16[2,8,1,96,768]{4,3,2,1,0:T(8,128)(2,1)}, u32[]{:S(2)}, u32[]{:S(2)}) collective-permute-start(bf16[2,8,1,96,768]{4,3,2,1,0:T(8,128)(2,1)} %get-tuple-element.172), channel_id=1, source_target_pairs={{0,1},{1,0},{2,3},{3,2},{4,5},{5,4},{6,7},{7,6},{8,9},{9,8},{10,11... | collective-permute-start | bytes 7077896 | tf_op jit(solution)/shard_map/ppermute | solution.py:758
  332.2 27.4 %collective-permute-start.38 = (bf16[2,96,768]{2,1,0:T(8,128)(2,1)}, bf16[2,96,768]{2,1,0:T(8,128)(2,1)S(1)}, u32[]{:S(2)}, u32[]{:S(2)}) collective-permute-start(bf16[2,96,768]{2,1,0:T(8,128)(2,1)} %get-tuple-element.362), channel_id=1, source_target_pairs={{0,8},{4,12},{8,0},{12,4},{16,24},{20,28},{24,16},{28,20},{1,9},{5... | collective-permute-start | bytes 884744 | tf_op jit(solution)/shard_map/ppermute | solution.py:758
  333.3 26.4 %collective-permute-start.39 = (bf16[2,96,768]{2,1,0:T(8,128)(2,1)}, bf16[2,96,768]{2,1,0:T(8,128)(2,1)S(1)}, u32[]{:S(2)}, u32[]{:S(2)}) collective-permute-start(bf16[2,96,768]{2,1,0:T(8,128)(2,1)} %get-tuple-element.361), channel_id=1, source_target_pairs={{0,16},{4,20},{8,24},{12,28},{16,0},{20,4},{24,8},{28,12},{1,17},{... | collective-permute-start | bytes 884744 | tf_op jit(solution)/shard_map/ppermute | solution.py:758
  334.7 24.9 %collective-permute-start.40 = (bf16[2,96,768]{2,1,0:T(8,128)(2,1)}, bf16[2,96,768]{2,1,0:T(8,128)(2,1)S(1)}, u32[]{:S(2)}, u32[]{:S(2)}) collective-permute-start(bf16[2,96,768]{2,1,0:T(8,128)(2,1)} %get-tuple-element.360), channel_id=1, source_target_pairs={{0,24},{4,28},{8,16},{12,20},{16,8},{20,12},{24,0},{28,4},{1,25},{... | collective-permute-start | bytes 884744 | tf_op jit(solution)/shard_map/ppermute | solution.py:758
  336.6 27.6 %all-to-all-start.2 = ((bf16[4,240,768]{2,1,0:T(8,128)(2,1)}), bf16[4,240,768]{2,1,0:T(8,128)(2,1)S(1)}, u32[]{:S(2)}, u32[]{:S(2)}) async-start(bf16[4,240,768]{2,1,0:T(8,128)(2,1)} %bitcast.205), calls=%async_computation.2 | async-start | bytes 2949120 | tf_op jit(solution)/shard_map/all_to_all | solution.py:764
  364.9 13.7 %collective-permute-start.41 = (bf16[2,1,96,768]{3,2,1,0:T(8,128)(2,1)}, bf16[2,1,96,768]{3,2,1,0:T(8,128)(2,1)S(1)}, u32[]{:S(2)}, u32[]{:S(2)}) collective-permute-start(bf16[2,1,96,768]{3,2,1,0:T(8,128)(2,1)} %get-tuple-element.374), channel_id=1, source_target_pairs={{0,4},{4,0},{8,12},{12,8},{16,20},{20,16},{24,28},{28,24},{1,5},{5... | collective-permute-start | bytes 884744 | tf_op jit(solution)/shard_map/ppermute | solution.py:758
  365.9 12.7 %collective-permute-start.42 = (bf16[2,1,96,768]{3,2,1,0:T(8,128)(2,1)S(1)}, bf16[2,1,96,768]{3,2,1,0:T(8,128)(2,1)S(1)}, u32[]{:S(2)}, u32[]{:S(2)}) collective-permute-start(bf16[2,1,96,768]{3,2,1,0:T(8,128)(2,1)S(1)} %get-tuple-element.373), channel_id=1, source_target_pairs={{0,2},{1,3},{2,0},{3,1},{4,6},{5,7},{6,4},{7,5},{8,10},{9,11},{10,... | collective-permute-start | bytes 884744 | tf_op jit(solution)/shard_map/ppermute | solution.py:758
  379.6 16.4 %collective-permute-start.43 = (bf16[4,1,96,768]{3,2,1,0:T(8,128)(2,1)}, bf16[4,1,96,768]{3,2,1,0:T(8,128)(2,1)}, u32[]{:S(2)}, u32[]{:S(2)}) collective-permute-start(bf16[4,1,96,768]{3,2,1,0:T(8,128)(2,1)} %pad_maximum_fusion.6), channel_id=1, source_target_pairs={{0,4},{4,0},{8,12},{12,8},{16,20},{20,16},{24,28},{28,24},{1,5},{5... | collective-permute-start | bytes 1769480 | tf_op jit(solution)/shard_map/ppermute | solution.py:758
  381.7 14.9 %collective-permute-start.44 = (bf16[4,1,96,768]{3,2,1,0:T(8,128)(2,1)}, bf16[4,1,96,768]{3,2,1,0:T(8,128)(2,1)}, u32[]{:S(2)}, u32[]{:S(2)}) collective-permute-start(bf16[4,1,96,768]{3,2,1,0:T(8,128)(2,1)} %pad_maximum_fusion.7), channel_id=1, source_target_pairs={{0,2},{1,3},{2,0},{3,1},{4,6},{5,7},{6,4},{7,5},{8,10},{9,11},{10,... | collective-permute-start | bytes 1769480 | tf_op jit(solution)/shard_map/ppermute | solution.py:758
  405.8 24.4 %all-to-all-start.3 = ((bf16[4,240,768]{2,1,0:T(8,128)(2,1)}), bf16[4,240,768]{2,1,0:T(8,128)(2,1)S(1)}, u32[]{:S(2)}, u32[]{:S(2)}) async-start(bf16[4,240,768]{2,1,0:T(8,128)(2,1)} %bitcast.204), calls=%async_computation.3 | async-start | bytes 2949120 | tf_op jit(solution)/shard_map/all_to_all | solution.py:764
  411.6 14.1 %collective-permute-start.51 = (bf16[1,96,768]{2,1,0:T(8,128)(2,1)S(1)}, bf16[1,96,768]{2,1,0:T(8,128)(2,1)S(1)}, u32[]{:S(2)}, u32[]{:S(2)}) collective-permute-start(bf16[1,96,768]{2,1,0:T(8,128)(2,1)S(1)} %get-tuple-element.372), channel_id=1, source_target_pairs={{0,16},{4,20},{8,24},{12,28},{16,0},{20,4},{24,8},{28,12},{1,17},{... | collective-permute-start | bytes 442376 | tf_op jit(solution)/shard_map/ppermute | solution.py:758
  412.1 13.6 %collective-permute-start.50 = (bf16[1,96,768]{2,1,0:T(8,128)(2,1)S(1)}, bf16[1,96,768]{2,1,0:T(8,128)(2,1)S(1)}, u32[]{:S(2)}, u32[]{:S(2)}) collective-permute-start(bf16[1,96,768]{2,1,0:T(8,128)(2,1)S(1)} %get-tuple-element.370), channel_id=1, source_target_pairs={{0,8},{4,12},{8,0},{12,4},{16,24},{20,28},{24,16},{28,20},{1,9},{5... | collective-permute-start | bytes 442376 | tf_op jit(solution)/shard_map/ppermute | solution.py:758
  (70 other events, 533.9 us)
Sparse Core Ops, SparseCore 0:
  65.1 103.6 all-gather.1

commit v4 on v3

--- a/solution.py
+++ b/solution.py
@@ -28,7 +28,7 @@
 bf16 = jnp.bfloat16
 f32 = jnp.float32
 VMEM_LIMIT = 58 * 1024 * 1024
-ATTENTION_US = 38
+ATTENTION_US = 18
 LIFT_US = 16
 DROP_WEIGHT_US = 7
 EXPERT_BACK_US = 17
@@ -113,13 +113,19 @@
     return copies
 
 
-def step_copies(pieces, mine, weight_ref, sems):
+def step_parts(pieces):
+    parts = []
+    for step in range(2 * len(pieces) // 5):
+        even, odd, high, front, back = pieces[len(pieces) - 5 - 5 * (step // 2) :][:5]
+        parts.append((high, front, back) if step % 2 else (even, odd))
+    return parts
+
+
+def step_copies(parts, mine, weight_ref, sems):
     by_step = []
-    for step in range(4):
-        even, odd, high, front, back = pieces[5 * (1 - step // 2) :][:5]
-        parts = (high, front, back) if step % 2 else (even, odd)
+    for step, pieces in enumerate(parts):
         place_of = lambda rows, step=step: weight_ref.at[:, step, rows, :]
-        by_step.append(piece_copies(parts, mine, place_of, sems.at[step]))
+        by_step.append(piece_copies(pieces, mine, place_of, sems.at[step]))
     return by_step
 
 
@@ -129,23 +135,25 @@
             copy.start()
 
 
-def out_copy(weight_ref, out_ref, out_sems, step):
-    return pltpu.make_async_copy(weight_ref.at[:, step], out_ref.at[:, step], out_sems.at[step])
-
-
-def wait_step(by_step, weight_ref, out_ref, out_sems):
+def out_copy(weight_ref, out_ref, out_sems, step, places):
+    return pltpu.make_async_copy(
+        weight_ref.at[:, step], out_ref.at[:, places[step]], out_sems.at[step]
+    )
+
+
+def wait_step(by_step, weight_ref, out_ref, out_sems, places):
     for step, copies in enumerate(by_step):
 
         @pl.when(pl.program_id(0) == step)
         def _():
             for copy in copies:
                 copy.wait()
-            out_copy(weight_ref, out_ref, out_sems, step).start()
-
-
-def wait_out(weight_ref, out_ref, out_sems):
-    for step in range(4):
-        out_copy(weight_ref, out_ref, out_sems, step).wait()
+            out_copy(weight_ref, out_ref, out_sems, step, places).start()
+
+
+def wait_out(weight_ref, out_ref, out_sems, places):
+    for step in range(weight_ref.shape[1]):
+        out_copy(weight_ref, out_ref, out_sems, step, places).wait()
 
 
 def store_grad(grad_ref, mine, index, first, rows, value):
@@ -181,15 +189,13 @@
     return rows[:, first : first + HEAD_DIM]
 
 
-def attention_kernel(
-    meta_ref, raw_ref, place_ref, hidden_ref, valid_ref, norm_ref, extra_ref, *refs, **sizes
-):
-    pieces, outs = refs[:10], refs[10:]
-    block_ref, normed_ref, residual_ref, feed_ref, square_ref = outs[:5]
-    out_ref, joint_ref, mixed_ref, probs_ref, weight_ref, sems, out_sems = outs[5:]
+def attention_kernel(meta_ref, raw_ref, place_ref, hidden_ref, norm_ref, extra_ref, *refs, **sizes):
+    parts, outs = (refs[:2], refs[2:4]), refs[4:]
+    block_ref, normed_ref, residual_ref, out_ref, joint_ref, mixed_ref, probs_ref = outs[:7]
+    weight_ref, sems, out_sems = outs[7:]
     items, main_rows, all_rows = sizes["items"], sizes["main_rows"], sizes["all_rows"]
     step = pl.program_id(0)
-    by_step = step_copies(pieces, meta_ref[items + 1], weight_ref, sems)
+    by_step = step_copies(parts, meta_ref[items + 1], weight_ref, sems)
 
     @pl.when(step == 0)
     def _():
@@ -206,7 +212,30 @@
         loop(items, lambda i: chunk(pl.multiple_of(i * ITEM_ROWS, 16), ITEM_ROWS))
         chunk(main_rows, all_rows - main_rows)
 
-    wait_step(by_step, weight_ref, out_ref, out_sems)
+    wait_step(by_step, weight_ref, out_ref, out_sems, (0, 2))
+    attend_heads(
+        meta_ref, weight_ref.at[0, step], normed_ref, residual_ref, joint_ref, mixed_ref, probs_ref, **sizes
+    )
+
+    @pl.when(step == pl.num_programs(0) - 1)
+    def _():
+        wait_out(weight_ref, out_ref, out_sems, (0, 2))
+
+
+def attention_end_kernel(meta_ref, normed_ref, block_ref, before_ref, valid_ref, norm_ref, *refs, **sizes):
+    parts, outs = (refs[:3], refs[3:6]), refs[10:]
+    residual_ref, feed_ref, square_ref, out_ref, joint_ref, mixed_ref, probs_ref = outs[:7]
+    weight_ref, sems, out_sems = outs[7:]
+    items, main_rows, all_rows = sizes["items"], sizes["main_rows"], sizes["all_rows"]
+    step = pl.program_id(0)
+    by_step = step_copies(parts, meta_ref[items + 1], weight_ref, sems)
+
+    @pl.when(step == 0)
+    def _():
+        start_all(by_step)
+        residual_ref[...] = before_ref[...]
+
+    wait_step(by_step, weight_ref, out_ref, out_sems, (1, 3))
     attend_heads(
         meta_ref, weight_ref.at[0, step], normed_ref, residual_ref, joint_ref, mixed_ref, probs_ref, **sizes
     )
@@ -223,7 +252,7 @@
 
         loop(items, lambda i: chunk(rows_at(i, ITEM_ROWS)))
         chunk(pl.ds(main_rows, all_rows - main_rows))
-        wait_out(weight_ref, out_ref, out_sems)
+        wait_out(weight_ref, out_ref, out_sems, (1, 3))
 
 
 def attend_heads(
@@ -462,13 +491,13 @@
 
 def lift_kernel(mine_ref, feed_ref, *refs, vision_rows, all_rows):
     pieces, (acted_ref, slope_ref, out_ref, weight_ref, sems, out_sems) = refs[:10], refs[10:]
-    by_step = step_copies(pieces, mine_ref[0], weight_ref, sems)
+    by_step = step_copies(step_parts(pieces), mine_ref[0], weight_ref, sems)
 
     @pl.when(pl.program_id(0) == 0)
     def _():
         start_all(by_step)
 
-    wait_step(by_step, weight_ref, out_ref, out_sems)
+    wait_step(by_step, weight_ref, out_ref, out_sems, (0, 1, 2, 3))
 
     def piece(rows, expert):
         lifted = dot(feed_ref[rows, :], weight_ref[expert, pl.program_id(0)], 1, 0)
@@ -482,7 +511,7 @@
 
     @pl.when(pl.program_id(0) == pl.num_programs(0) - 1)
     def _():
-        wait_out(weight_ref, out_ref, out_sems)
+        wait_out(weight_ref, out_ref, out_sems, (0, 1, 2, 3))
 
 
 def place_grad_kernel(raw_ref, place_ref, grad_ref, grad_bias_ref, *, vision_rows):
@@ -511,7 +540,6 @@
 
 
 def drop_kernel(
-    mine_ref,
     acted_ref,
     residual_ref,
     valid_ref,
@@ -557,10 +585,12 @@
 
 
 def expert_back_step(
-    mine_ref, grad_ref, slope_ref, feed_ref, drop_ref, lift_ref, grad_weight_ref, total_ref, lifted_ref, vision_rows
+    mine_ref, grad_ref, slope_ref, feed_ref, lift_ref, drop_ref, grad_weight_ref, total_ref, lifted_ref, vision_rows
 ):
+    step = pl.program_id(0)
+
     def piece(rows, expert):
-        grad_acted = dot(grad_ref[rows, :], drop_ref[expert, 0], 1, 0)
+        grad_acted = dot(grad_ref[rows, :], drop_ref[expert, step], 1, 0)
         grad_lifted = (grad_acted * slope_ref[0, rows, :].astype(f32)).astype(bf16)
         lifted_ref[rows, :] = grad_lifted
         total_ref[rows, :] += dot(grad_lifted, lift_ref[expert, 0], 1, 1)
@@ -572,57 +602,45 @@
     )
 
 
-def expert_back_kernel(
-    mine_ref,
-    grad_ref,
-    slope_ref,
-    feed_ref,
-    drop_ref,
-    lift_ref,
-    grad_weight_ref,
-    total_ref,
-    lifted_ref,
-    *,
-    vision_rows,
-):
+def expert_back_kernel(mine_ref, grad_ref, slope_ref, feed_ref, lift_ref, *refs, vision_rows):
+    pieces, (grad_weight_ref, out_ref, total_ref) = refs[:5], refs[5:8]
+    lifted_ref, drop_ref, sems, out_sems = refs[8:]
+    by_step = step_copies(step_parts(pieces), mine_ref[0], drop_ref, sems)
+
     @pl.when(pl.program_id(0) == 0)
     def _():
+        start_all(by_step)
         total_ref[...] = jnp.zeros_like(total_ref)
 
+    wait_step(by_step, drop_ref, out_ref, out_sems, (0, 1))
     expert_back_step(
-        mine_ref, grad_ref, slope_ref, feed_ref, drop_ref, lift_ref, grad_weight_ref, total_ref, lifted_ref, vision_rows
-    )
-
-
-def expert_back_end_kernel(
-    mine_ref,
-    grad_ref,
-    slope_ref,
-    feed_ref,
-    drop_ref,
-    lift_ref,
-    before_ref,
-    residual_ref,
-    norm_ref,
-    grad_weight_ref,
-    grad_residual_ref,
-    grad_attended_ref,
-    grad_norm_ref,
-    lifted_ref,
-    *,
-    vision_rows,
-):
+        mine_ref, grad_ref, slope_ref, feed_ref, lift_ref, drop_ref, grad_weight_ref, total_ref, lifted_ref, vision_rows
+    )
+
+    @pl.when(pl.program_id(0) == pl.num_programs(0) - 1)
+    def _():
+        wait_out(drop_ref, out_ref, out_sems, (0, 1))
+
+
+def expert_back_end_kernel(mine_ref, grad_ref, slope_ref, feed_ref, lift_ref, *refs, vision_rows):
+    pieces, (_, before_ref, residual_ref, norm_ref) = refs[:5], refs[5:9]
+    grad_weight_ref, out_ref, grad_residual_ref, grad_attended_ref, grad_norm_ref = refs[9:14]
+    lifted_ref, drop_ref, sems, out_sems = refs[14:]
+    by_step = step_copies(step_parts(pieces), mine_ref[0], drop_ref, sems)
+
     @pl.when(pl.program_id(0) == 0)
     def _():
+        start_all(by_step)
         grad_residual_ref[...] = before_ref[...]
 
+    wait_step(by_step, drop_ref, out_ref, out_sems, (2, 3))
     expert_back_step(
         mine_ref,
         grad_ref,
         slope_ref,
         feed_ref,
+        lift_ref,
         drop_ref,
-        lift_ref,
         grad_weight_ref,
         grad_residual_ref,
         lifted_ref,
@@ -645,6 +663,7 @@
             grad_attended_ref[rows, :] = grad.astype(bf16)
 
         loop(grad_ref.shape[0] // ITEM_ROWS, chunk)
+        wait_out(drop_ref, out_ref, out_sems, (2, 3))
 
 
 def whole(*shape):
@@ -659,14 +678,8 @@
     return pl.BlockSpec(shape, lambda i, *_: (0, i + first) + (0,) * (len(shape) - 2))
 
 
-def part_of(step, mine):
-    return jnp.bitwise_xor(mine[1], (step % 2) * 2 + 1 - step // 2)
-
-
-def part_pair(*shape, first=0):
-    return pl.BlockSpec(
-        shape, lambda i, mine: (0, part_of(i + first, mine)) + (0,) * (len(shape) - 2)
-    )
+def every_other(*shape, first=0):
+    return pl.BlockSpec(shape, lambda i, *_: (2 * i + first,) + (0,) * (len(shape) - 1))
 
 
 def anywhere(values):
@@ -750,8 +763,8 @@
     else:
         mine = jnp.zeros((2,), jnp.int32)
 
-    def after(values, *others):
-        return lax.optimization_barrier((values, others))[0]
+    def together(*values):
+        return lax.optimization_barrier(values)
 
     def swap(values, axis, bit):
         size = lax.axis_size(axis)
@@ -777,8 +790,11 @@
             pieces += [low[0], low[1], high[0], high[1, :2], high[1, 2:]]
         return pieces
 
+    def line_parts(values):
+        return (values,) + tuple(swap(values, "dp", bit) for bit in (2, 4, 6))
+
     def gather_line(values):
-        return jnp.stack([values] + [swap(values, "dp", bit) for bit in (2, 4, 6)])
+        return jnp.stack(line_parts(values))
 
     def gather_plane(line):
         return swap(line, "dp", 1), swap(line, "mp", 2)
@@ -786,9 +802,8 @@
     def gather_corner(along_x, along_y):
         return swap(along_x[:2], "mp", 2), swap(along_y[2:], "dp", 1)
 
-    def gather_cores(line, along, corner):
-        own = (line,) + along + corner
-        return own + tuple(swap(part, "mp", 1) for part in own)
+    def over_cores(*pieces):
+        return tuple(swap(part, "mp", 1) for part in pieces)
 
     def add(*terms):
         total = terms[0].astype(f32)
@@ -806,24 +821,26 @@
         values = lax.psum_scatter(values, ("mp", "dp"), scatter_dimension=1, tiled=True)
         return values.astype(f32)
 
-    def scatter_corner(keep, received):
+    def quarters(keep, received, *others):
+        keep, received, others = together(keep, received, others)
         shape = (2, 2, 4) + keep.shape[2:]
         keep, received = keep.reshape(shape), received.reshape(shape)
-        return add(keep[1, 1], received[1, 1]).astype(bf16)
+        return (lambda y, x: add(keep[y, x], received[y, x])), others
+
+    def scatter_corner(keep, received):
+        quarter, _ = quarters(keep, received)
+        return quarter(1, 1).astype(bf16)
 
     def scatter_plane(keep, received, from_x, from_y):
-        shape = (2, 2, 4) + keep.shape[2:]
-        keep, received = keep.reshape(shape), received.reshape(shape)
-        part_x = add(keep[0, 1], received[0, 1])
-        part_y = add(keep[1, 0], received[1, 0])
+        quarter, (from_x, from_y) = quarters(keep, received, from_x, from_y)
+        part_x, part_y = quarter(0, 1), quarter(1, 0)
         part_x = jnp.concatenate([part_x[:2], add(part_x[2:], from_y)]).astype(bf16)
         part_y = jnp.concatenate([add(part_y[:2], from_x), part_y[2:]]).astype(bf16)
         return part_x, part_y
 
     def scatter_line(keep, received, from_x, from_y):
-        shape = (2, 2, 4) + keep.shape[2:]
-        keep, received = keep.reshape(shape), received.reshape(shape)
-        return add(keep[0, 0], received[0, 0], from_x, from_y).astype(bf16)
+        quarter, (from_x, from_y) = quarters(keep, received, from_x, from_y)
+        return add(quarter(0, 0), from_x, from_y).astype(bf16)
 
     def send_corner(corner):
         return swap(corner[:2], "dp", 1), swap(corner[2:], "mp", 2)
@@ -876,20 +893,22 @@
     def plain(values):
         return (values, whole(*values.shape))
 
-    def heads_out():
+    def heads_out(first):
         shapes = [
             (parts, all_rows, 3 * width),
             (parts, all_rows, width),
             (parts, items, heads, ITEM_ROWS, ITEM_ROWS),
         ]
-        return [(shape, bf16, stepped(1, *shape[1:])) for shape in shapes]
+        return [(shape, bf16, every_other(1, *shape[1:], first=first)) for shape in shapes]
 
     def whole_weight(count):
-        shape = (count, parts, model_width, model_width)
-        return (shape, bf16, pl.BlockSpec(memory_space=pl.ANY)), [
-            pltpu.VMEM(shape, bf16),
-            pltpu.SemaphoreType.DMA((parts, 8)),
-            pltpu.SemaphoreType.DMA((parts,)),
+        return ((count, parts, model_width, model_width), bf16, pl.BlockSpec(memory_space=pl.ANY))
+
+    def weight_scratch(count, steps):
+        return [
+            pltpu.VMEM((count, steps, model_width, model_width), bf16),
+            pltpu.SemaphoreType.DMA((steps, 8)),
+            pltpu.SemaphoreType.DMA((steps,)),
         ]
 
     def part_weight(values, first, count=2):
@@ -903,33 +922,44 @@
     row_sizes = dict(main_rows=main_rows, all_rows=all_rows)
 
     def attention(raw, pieces):
-        weight_out, scratch = whole_weight(1)
-        block_input, normed, residual, feed_input, squared, weights, *made = call(
+        return call(
             functools.partial(attention_kernel, **head_sizes, **row_sizes),
             "attention",
-            parts,
-            [plain(raw), plain(place_row), plain(hidden), plain(valid), plain(norm_params)]
-            + [plain(extra_params)]
+            2,
+            [plain(raw), plain(place_row), plain(hidden), plain(norm_params), plain(extra_params)]
             + [anywhere(values) for values in pieces],
-            [rows_of(all_rows, f32), rows_of(all_rows, bf16), rows_of(all_rows, f32)]
-            + [rows_of(all_rows, bf16), rows_of(1, f32), weight_out]
-            + heads_out(),
-            scratch,
+            [rows_of(all_rows, f32), rows_of(all_rows, bf16), rows_of(all_rows, f32), whole_weight(1)]
+            + heads_out(0),
+            weight_scratch(1, 2),
             ATTENTION_US,
             (meta,),
         )
-        return block_input, normed, residual, feed_input, squared, [weights[0], *made]
+
+    def attention_end(normed, block_input, residual, pieces, made):
+        return call(
+            functools.partial(attention_end_kernel, **head_sizes, **row_sizes),
+            "attention_end",
+            2,
+            [plain(normed), plain(block_input), plain(residual), plain(valid), plain(norm_params)]
+            + [anywhere(values) for values in pieces]
+            + [anywhere(values) for values in made],
+            [rows_of(all_rows, f32), rows_of(all_rows, bf16), rows_of(1, f32), whole_weight(1)]
+            + heads_out(1),
+            weight_scratch(1, 2),
+            ATTENTION_US,
+            (meta,),
+            {12 + i: 3 + i for i in range(4)},
+        )
 
     def lift(feed_input, pieces):
         shape = (parts, all_rows, hidden_width)
-        weight_out, scratch = whole_weight(2)
         return call(
             functools.partial(lift_kernel, vision_rows=vision_rows, all_rows=all_rows),
             "lift",
             parts,
             [plain(feed_input)] + [anywhere(values) for values in pieces],
-            [(shape, bf16, stepped(1, *shape[1:]))] * 2 + [weight_out],
-            scratch,
+            [(shape, bf16, stepped(1, *shape[1:]))] * 2 + [whole_weight(2)],
+            weight_scratch(2, parts),
             LIFT_US,
             (mine,),
         )
@@ -957,38 +987,43 @@
             (mine,),
         )[0]
 
-    def expert_ins(grad_rows, slope, feed_input, drop_weights, lift_weights, first):
+    def expert_ins(grad_rows, slope, feed_input, lift_weights, pieces, first):
         return [
             plain(grad_rows),
             (slope, stepped(1, main_rows, hidden_width, first=first)),
             (feed_input, whole(main_rows, model_width)),
-            (drop_weights, part_pair(2, 1, *drop_weights.shape[2:], first=first)),
             part_weight(lift_weights, first),
-        ]
-
-    def expert_back(*args):
+        ] + [anywhere(values) for values in pieces]
+
+    drop_out = whole_weight(2)
+    expert_scratch = [pltpu.VMEM((main_rows, hidden_width), bf16)] + weight_scratch(2, 2)
+
+    def expert_back(pieces, *args):
         return call(
             functools.partial(expert_back_kernel, vision_rows=vision_rows),
             "expert_back",
             2,
-            expert_ins(*args, 0),
-            [grad_out(2), rows_of(main_rows, f32)],
-            [pltpu.VMEM((main_rows, hidden_width), bf16)],
+            expert_ins(*args, pieces[5:], 0),
+            [grad_out(2), drop_out, rows_of(main_rows, f32)],
+            expert_scratch,
             EXPERT_BACK_US,
             (mine,),
         )
 
-    def expert_back_end(before, residual, *args):
+    def expert_back_end(made, before, residual, pieces, *args):
         return call(
             functools.partial(expert_back_end_kernel, vision_rows=vision_rows),
             "expert_back_end",
             2,
-            expert_ins(*args, 2)
-            + [plain(before), (residual, whole(main_rows, model_width)), plain(norm_params)],
-            [grad_out(2), rows_of(main_rows, f32), rows_of(main_rows, bf16), rows_of(2, f32)],
-            [pltpu.VMEM((main_rows, hidden_width), bf16)],
+            expert_ins(*args, pieces[:5], 2)
+            + [anywhere(made), plain(before), (residual, whole(main_rows, model_width))]
+            + [plain(norm_params)],
+            [grad_out(2), drop_out, rows_of(main_rows, f32), rows_of(main_rows, bf16)]
+            + [rows_of(2, f32)],
+            expert_scratch,
             EXPERT_BACK_US,
             (mine,),
+            {10: 1},
         )
 
     def heads_ins(grad_attended, normed, weights, joint_rows, mixed, probs, first):
@@ -1055,127 +1090,141 @@
             parts,
             [(acted, stepped(1, all_rows, hidden_width)), plain(residual), plain(valid)]
             + [plain(place_column), plain(extra_params)]
-            + [(weights, part_pair(2, 1, *weights.shape[2:]))],
+            + [part_weight(weights, 0)],
             [rows_of(block_rows, bf16), rows_of(2, f32)],
             [pltpu.VMEM((all_rows, model_width), f32)],
             DROP_US,
-            (mine,),
-        )
-
+        )
+
+    tables = (place_row, place_column, hidden, valid, meta)
     raw_tokens = exchange(tokens)
     if cube:
-        line_attend, raw_tokens = after((gather_line(shard_attend), raw_tokens))
-        line_lift = gather_line(after(shard_lift, line_attend))
-        plane_attend = gather_plane(line_attend)
-        corner_attend = gather_corner(*plane_attend)
-        attend_pieces = gather_cores(line_attend, plane_attend, corner_attend)
-        line_lift, raw_tokens = after((line_lift, raw_tokens))
-        drop_all = gather(after(shard_drop, line_lift, corner_attend))
+        line, tables = together(gather_line(shard_attend), tables)
+        place_row, place_column, hidden, valid, meta = tables
+        even, high = gather_plane(line)
+        even, high, raw_tokens, shard_lift, cotangent = together(
+            even, high, raw_tokens, shard_lift, cotangent
+        )
+        corner = gather_corner(even, high)
+        line_lift = line_parts(shard_lift)
+        raw_grad = exchange(cotangent.astype(bf16))
+        early = over_cores(line, even) + (line, even)
+    else:
+        pieces = gather_pieces(shard_attend)
+        early = [pieces[i] for i in (5, 6, 0, 1)]
+        late = [pieces[i] for i in (7, 8, 9, 2, 3, 4)]
+        raw_grad = exchange(cotangent.astype(bf16))
+
+    block_input, normed, residual, *made = attention(raw_tokens, early)
+    if cube:
+        corner, line_lift, raw_grad, residual = together(corner, line_lift, raw_grad, residual)
+        late = (high,) + corner
+        late = over_cores(*late) + late
+        line_lift, shard_drop = together(jnp.stack(line_lift), shard_drop)
         plane_lift = gather_plane(line_lift)
-        raw_grad = exchange(after(cotangent.astype(bf16), line_lift))
-    else:
-        attend_pieces = gather_pieces(shard_attend)
-        drop_all = gather(shard_drop)
-        raw_grad = exchange(cotangent.astype(bf16))
-
-    block_input, normed, residual, feed_input, attended_square, made = attention(raw_tokens, attend_pieces)
-    raw_grad, feed_input = after((raw_grad, feed_input))
-    if cube:
-        plane_lift, feed_input = after((plane_lift, feed_input))
+        line_drop = line_parts(shard_drop)
+    residual, feed_input, attended_square, *made = attention_end(normed, block_input, residual, late, made)
+    made[0] = made[0][0]
+    if cube:
+        plane_lift, line_drop, raw_grad, feed_input = together(plane_lift, line_drop, raw_grad, feed_input)
         corner_lift = gather_corner(*plane_lift)
+        lift_others = over_cores(line_lift, *plane_lift)
     grad_rows, grad_bias = place_grad(raw_grad)
     if cube:
-        corner_lift, grad_rows = after((corner_lift, grad_rows))
-        lift_pieces = gather_cores(line_lift, plane_lift, corner_lift)
+        corner_lift, lift_others, line_drop, grad_rows = together(
+            corner_lift, lift_others, line_drop, grad_rows
+        )
+        lift_pieces = (line_lift,) + plane_lift + corner_lift
+        lift_pieces += lift_others + over_cores(*corner_lift)
+        line_drop = jnp.stack(line_drop)
+        plane_drop = gather_plane(line_drop)
     else:
         lift_pieces = gather_pieces(shard_lift)
     acted, slope, lift_all = lift(feed_input, lift_pieces)
+    if cube:
+        plane_drop, acted = together(plane_drop, acted)
+        corner_drop = gather_corner(*plane_drop)
+        drop_others = over_cores(line_drop, *plane_drop)
     drop_send = drop_weight_grad(grad_rows, acted, 0)
     if cube:
+        corner_drop, drop_others, drop_send, acted = together(corner_drop, drop_others, drop_send, acted)
         drop_received = swap(drop_send, "mp", 1)
-    drop_keep = drop_weight_grad(grad_rows, after(acted, drop_send), 2)
-    if cube:
-        drop_received, drop_keep = after((drop_received, drop_keep))
-        corner = scatter_corner(drop_keep, drop_received)
-        corner, grad_rows = after((corner, grad_rows))
+        drop_pieces = (line_drop,) + plane_drop + corner_drop
+        drop_pieces += drop_others + over_cores(*corner_drop)
+    drop_keep = drop_weight_grad(grad_rows, acted, 2)
+    if cube:
+        drop_pieces, drop_received, drop_keep = together(drop_pieces, drop_received, drop_keep)
+        corner, grad_rows = together(scatter_corner(drop_keep, drop_received), grad_rows)
         from_corner = send_corner(corner)
     else:
+        drop_pieces = gather_pieces(shard_drop)
         drop_grad = scatter(drop_keep, drop_send)
 
-    lift_send, grad_feed = expert_back(grad_rows, slope, feed_input, drop_all, lift_all)
-    if cube:
+    lift_send, drop_all, grad_feed = expert_back(drop_pieces, grad_rows, slope, feed_input, lift_all)
+    if cube:
+        from_corner, grad_feed = together(from_corner, grad_feed)
+        plane = scatter_plane(drop_keep, drop_received, *from_corner)
+        plane, lift_send, grad_feed = together(plane, lift_send, grad_feed)
+        from_plane = send_plane(*plane)
         lift_received = swap(lift_send, "mp", 1)
-        from_corner, grad_feed = after((from_corner, grad_feed))
-        plane = scatter_plane(drop_keep, drop_received, *from_corner)
-        plane, grad_feed = after((plane, grad_feed))
-        from_plane = send_plane(*plane)
-    lift_keep, grad_residual, grad_attended, grad_norm_second = expert_back_end(
-        grad_feed, residual, grad_rows, slope, feed_input, drop_all, lift_all
-    )
-    if cube:
-        lift_received, from_plane, grad_attended = after((lift_received, from_plane, grad_attended))
+    lift_keep, drop_all, grad_residual, grad_attended, grad_norm_second = expert_back_end(
+        drop_all, grad_feed, residual, drop_pieces, grad_rows, slope, feed_input, lift_all
+    )
+    if cube:
+        lift_received, from_plane, grad_attended = together(lift_received, from_plane, grad_attended)
         lift_corner = scatter_corner(lift_keep, lift_received)
         drop_line = scatter_line(drop_keep, drop_received, *from_plane)
-        lift_corner, drop_line, acted = after((lift_corner, drop_line, acted))
+        lift_corner, drop_line, acted = together(lift_corner, drop_line, acted)
         from_corner = send_corner(lift_corner)
-        from_line = send_line(drop_line)
+        from_drop_line = send_line(drop_line)
     else:
         lift_grad = scatter(lift_keep, lift_send)
     raw_out, feed_square = drop(acted, residual, drop_all)
     if cube:
-        from_corner, raw_out = after((from_corner, raw_out))
+        from_corner, raw_out = together(from_corner, raw_out)
         plane = scatter_plane(lift_keep, lift_received, *from_corner)
-        from_line, plane, grad_attended = after((from_line, plane, grad_attended))
-        drop_grad = add(drop_line[0], *from_line)
+        from_drop_line, plane, grad_attended = together(from_drop_line, plane, grad_attended)
         from_plane = send_plane(*plane)
 
     attend_send, grad_normed = attention_back(grad_attended, normed, *made)
     if cube:
         attend_received = swap(attend_send, "mp", 1)
-        from_plane, raw_out, grad_normed = after((from_plane, raw_out, grad_normed))
+        from_plane, raw_out, grad_normed = together(from_plane, raw_out, grad_normed)
         lift_line = scatter_line(lift_keep, lift_received, *from_plane)
-        lift_line, grad_normed = after((lift_line, grad_normed))
-        from_line = send_line(lift_line)
+        lift_line, grad_normed = together(lift_line, grad_normed)
+        from_lift_line = send_line(lift_line)
     block_output = give_back(raw_out)
     attend_keep, grad_normed = attention_back_end(grad_normed, grad_attended, normed, *made)
-    if cube:
-        attend_received, from_line, attend_keep = after((attend_received, from_line, attend_keep))
+    squares = jnp.stack(
+        [jnp.sum(feed_square[0]), jnp.sum(attended_square), jnp.sum(feed_square[1]), used.astype(f32)]
+    )
+    squares = jnp.pad(squares, (0, model_width - 4))[None]
+    if cube:
+        attend_received, from_lift_line, squares, attend_keep = together(
+            attend_received, from_lift_line, squares, attend_keep
+        )
         corner = scatter_corner(attend_keep, attend_received)
-        corner, block_output, grad_normed = after((corner, block_output, grad_normed))
+        corner, block_output, grad_normed = together(corner, block_output, grad_normed)
         from_corner = send_corner(corner)
     block_output = block_output.astype(f32)
     grad_raw, grad_norm_first, grad_mask = finish_input_grad(grad_normed, grad_residual, block_input)
-    if cube:
-        from_corner, grad_raw = after((from_corner, grad_raw))
+    small = (grad_norm_first, grad_norm_second, grad_bias, grad_mask, squares)
+    if cube:
+        from_corner, small, grad_raw = together(from_corner, small, grad_raw)
         plane = scatter_plane(attend_keep, attend_received, *from_corner)
-        from_plane = send_plane(*plane)
-        lift_grad = add(lift_line[0], *from_line)
-        from_plane, grad_raw = after((from_plane, grad_raw))
-        line = scatter_line(attend_keep, attend_received, *from_plane)
+        plane, small, grad_raw, block_output = together(plane, small, grad_raw, block_output)
+        line = scatter_line(attend_keep, attend_received, *send_plane(*plane))
+        line, small, grad_raw, drop_line, lift_line = together(line, small, grad_raw, drop_line, lift_line)
         attend_grad = add(line[0], *send_line(line))[0]
+        drop_grad = add(drop_line[0], *from_drop_line)
+        lift_grad = add(lift_line[0], *from_lift_line)
     else:
         attend_grad = scatter(attend_keep, attend_send)[0]
     input_grad = give_back(grad_raw).astype(f32)
 
-    squares = jnp.stack(
-        [jnp.sum(feed_square[0]), jnp.sum(attended_square), jnp.sum(feed_square[1]), used.astype(f32)]
-    )
-    small = jnp.concatenate(
-        [
-            grad_norm_first,
-            grad_norm_second,
-            grad_bias,
-            grad_mask,
-            jnp.pad(squares, (0, model_width - 4))[None],
-        ],
-        axis=0,
-    )
-    if cube:
-        small = after(small, plane)
-        for axis, bit in (("mp", 1), ("dp", 2), ("dp", 4)):
-            small = small + swap(small, axis, bit)
-        small = after(small, line)
-        for axis, bit in (("mp", 2), ("dp", 1)):
+    small = jnp.concatenate(small, axis=0)
+    if cube:
+        for axis, bit in (("mp", 1), ("dp", 1), ("mp", 2), ("dp", 2), ("dp", 4)):
             small = small + swap(small, axis, bit)
     else:
         small = lax.psum(small, ("dp", "mp"))

time: 444 us -> 417 us (0.939)
  waiting for transfers between devices: 105 us -> 76 us
  starting transfers between devices: 62.9 us -> 78.5 us
  between operations: 17.4 us -> 4.06 us
  Pallas kernels: 172 us -> 183 us
  other arithmetic: 58.9 us -> 51.1 us
    ppermute x53 -> x65, waiting for transfers between devices: 104 us -> 75 us  [swap(): return lax.ppermute(values, axis, [(i, i ^ bit) for i in range(size)])]
    ppermute x53 -> x65, starting transfers between devices: 47.1 us -> 62.4 us  [swap(): return lax.ppermute(values, axis, [(i, i ^ bit) for i in range(size)])]
    pallas_call x11 -> x12, Pallas kernels: 172 us -> 183 us  [call(): pl.pallas_call(kernel, name=name, grid_spec=pltpu.PrefetchScalarGridSpec(...]
    add x3, other arithmetic: 13.4 us -> 6.98 us  [add(): total = total + term.astype(f32)]
    convert_element_type x4 -> x7, other arithmetic: 8.51 us -> 13.4 us  [the longest x3 6.37 us: scatter_line(): return add(quarter(0, 0), from_x, from_y).astype(bf16)]
    unnamed x127 -> x125, local copies, waits for them, and re-layouts: 9.19 us -> 10.9 us
  transfers between devices with their start and end apart: 58 -> 69, of which waited for: 24 -> 23; matrix products, arithmetic and copies ran while one was open for 14% -> 11% of each run, Pallas kernels for 36% -> 44%
where the time goes in v4:
time: 417 us; the launch traced here: 413 us
  Pallas kernels  183 us (44%)
  starting transfers between devices  78.5 us (19%)
  waiting for transfers between devices  76 us (18%)
  other arithmetic  51.1 us (12%)
  local copies, waits for them, and re-layouts  20.7 us (5%)
    pallas_call x12, Pallas kernels, call(): pl.pallas_call(kernel, name=name, grid_spec=pltpu.PrefetchScalarGridSpec(...  183 us
    ppermute x65, waiting for transfers between devices, swap(): return lax.ppermute(values, axis, [(i, i ^ bit) for i in range(size)])  75 us
    ppermute x65, starting transfers between devices, swap(): return lax.ppermute(values, axis, [(i, i ^ bit) for i in range(size)])  62.4 us
    unnamed x125, local copies, waits for them, and re-layouts  10.9 us
    convert_element_type x6, other arithmetic, adamw(): return (weight_new, first_new, second_new, weight_new.astype(bf16))  8.58 us
    all_to_all x2, starting transfers between devices, exchange(): lax.all_to_all(values, 'mp', split_axis=0, concat_axis=1, tiled=True)[0]  8.51 us
  transfers between devices with their start and end apart: 69, of which 23 were waited for; matrix products, arithmetic and copies ran while one was open for 11% of the time, Pallas kernels for 44%

profile of v4, /device:TPU:0, one launch (start us, length us, event | category | flops | bytes accessed | tf_op | source)
XLA Modules:
  0.0 413.3 jit_solution(15181044240984211046)
XLA Ops:
  3.5 5.1 %collective-permute-start.2 = (bf16[1,96,768]{2,1,0:T(8,128)(2,1)S(1)}, bf16[1,96,768]{2,1,0:T(8,128)(2,1)S(1)}, u32[]{:S(2)}, u32[]{:S(2)}) collective-permute-start(bf16[1,96,768]{2,1,0:T(8,128)(2,1)S(1)} %pad_maximum_fusion.10), channel_id=1, source_target_pairs={{0,24},{4,28},{8,16},{12,20},{16,8},{20,12},{24,0},{28,4},{1,25},{... | collective-permute-start | bytes 442376 | tf_op jit(solution)/shard_map/ppermute | solution.py:771
  9.3 4.4 %all-to-all-start = ((bf16[4,240,768]{2,1,0:T(8,128)(2,1)}), bf16[4,240,768]{2,1,0:T(8,128)(2,1)}, u32[]{:S(2)}, u32[]{:S(2)}) async-start(bf16[4,240,768]{2,1,0:T(8,128)(2,1)} %param.23), calls=%async_computation | async-start | bytes 2949120 | tf_op jit(solution)/shard_map/all_to_all | solution.py:774
  16.0 1.9 fusion.24.valid_ref
  21.9 2.1 pad_maximum_fusion.6.refs_2_
  25.6 2.0 collective-permute-start.4
  28.4 11.6 %collective-permute-done.3.refs_3_ = bf16[4,1,96,768]{3,2,1,0:T(8,128)(2,1)} collective-permute-done((bf16[4,1,96,768]{3,2,1,0:T(8,128)(2,1)}, bf16[4,1,96,768]{3,2,1,0:T(8,128)(2,1)}, u32[]{:S(2)}, u32[]{:S(2)}) %collective-permute-start.3) | collective-permute-done | bytes 589856 | tf_op jit(solution)/shard_map/ppermute | solution.py:771
  40.0 5.4 %collective-permute-done.4.refs_3_ = bf16[4,1,96,768]{3,2,1,0:T(8,128)(2,1)} collective-permute-done((bf16[4,1,96,768]{3,2,1,0:T(8,128)(2,1)}, bf16[4,1,96,768]{3,2,1,0:T(8,128)(2,1)}, u32[]{:S(2)}, u32[]{:S(2)}) %collective-permute-start.4) | collective-permute-done | bytes 589856 | tf_op jit(solution)/shard_map/ppermute | solution.py:771
  49.9 2.9 collective-permute-start.8
  54.1 4.1 %all-to-all-start.1 = ((bf16[4,240,768]{2,1,0:T(8,128)(2,1)}), bf16[4,240,768]{2,1,0:T(8,128)(2,1)S(1)}, u32[]{:S(2)}, u32[]{:S(2)}) async-start(bf16[4,240,768]{2,1,0:T(8,128)(2,1)} %convert_element_type.394), calls=%async_computation.1 | async-start | bytes 2949120 | tf_op jit(solution)/shard_map/all_to_all | solution.py:774
  61.4 19.5 %attention.1 = (f32[1168,768]{1,0:T(8,128)}, bf16[1168,768]{1,0:T(8,128)(2,1)}, f32[1168,768]{1,0:T(8,128)}, bf16[1,4,768,768]{3,2,1,0:T(8,128)(2,1)}, bf16[4,11...) custom-call(s32[6]{0:T(128)} %pad_add_fusion.1.meta_ref, ...), custom_call_target="tpu_custom_call" | custom-call | flops 17999998976 | bytes 18000000 | tf_op jit(solution)/shard_map/attention/pallas_call | solution.py:690
  85.6 3.8 collective-permute-start.15
  90.1 20.1 %attention_end.1 = (f32[1168,768]{1,0:T(8,128)}, bf16[1168,768]{1,0:T(8,128)(2,1)}, f32[1,768]{1,0:T(1,128)}, bf16[1,4,768,768]{3,2,1,0:T(8,128)(2,1)}, bf16[4,1...) custom-call(s32[6]{0:T(128)} %pad_add_fusion.1.meta_ref, ...), custom_call_target="tpu_custom_call", output_to_operand_aliasing={{3}: (12, {}), {4}: (13, {}), {5}: (14, {}), {6}: (15, {})} | custom-call | flops 17999998976 | bytes 18000000 | tf_op jit(solution)/shard_map/attention_end/pallas_call | solution.py:690
  112.4 1.8 collective-permute-start.20
  115.5 5.1 %place_grad.1 = (bf16[1024,768]{1,0:T(8,128)(2,1)}, f32[2,768]{1,0:T(2,128)}) custom-call(bf16[960,768]{1,0:T(8,128)(2,1)} %bitcast.229, s32[1,960]{1,0:T(1,128)} %reshape_select_fusion.place_ref), custom_call_target="tpu_custom_call" | custom-call | flops 5000000000 | bytes 5000000 | tf_op jit(solution)/shard_map/place_grad/pallas_call | solution.py:690
  120.6 7.0 %collective-permute-done.20.refs_3_ = bf16[2,2,96,768]{3,2,1,0:T(8,128)(2,1)} collective-permute-done((bf16[2,2,96,768]{3,2,1,0:T(8,128)(2,1)S(1)}, bf16[2,2,96,768]{3,2,1,0:T(8,128)(2,1)}, u32[]{:S(2)}, u32[]{:S(2)}) %collective-permute-start.20) | collective-permute-done | bytes 589856 | tf_op jit(solution)/shard_map/ppermute | solution.py:771
  133.0 16.8 %lift.1 = (bf16[4,1168,768]{2,1,0:T(8,128)(2,1)}, bf16[4,1168,768]{2,1,0:T(8,128)(2,1)}, bf16[2,4,768,768]{3,2,1,0:T(8,128)(2,1)}) custom-call(s32[2]{0:T(128)} %pad_add_fusion.mine_ref, bf16[1168,768]{1,0:T(8,128)(2,1)} %get-tuple-element.260.feed_ref, bf16[4,2,96,768]{3,2,1,0:T(8,128)(2,1)} %copy-done.13, bf16[4,2,96,768]{3,2,1,0:T(8,128)(2,1)} %copy-done.34, ...), custom_call_target="tpu_custom_call" | custom-call | flops 16000000000 | bytes 16000000 | tf_op jit(solution)/shard_map/lift/pallas_call | solution.py:690
  149.8 8.1 %collective-permute-done.25.refs_1_ = bf16[4,2,96,768]{3,2,1,0:T(8,128)(2,1)S(1)} collective-permute-done((bf16[4,2,96,768]{3,2,1,0:T(8,128)(2,1)S(1)}, bf16[4,2,96,768]{3,2,1,0:T(8,128)(2,1)S(1)}, u32[]{:S(2)}, u32[]{:S(2)}) %collective-permute-start.25) | collective-permute-done | bytes 1179680 | tf_op jit(solution)/shard_map/ppermute | solution.py:771
  161.7 7.4 %drop_weight_grad.2 = bf16[2,8,2,96,768]{4,3,2,1,0:T(8,128)(2,1)} custom-call(s32[2]{0:T(128)} %pad_add_fusion.mine_ref, bf16[1024,768]{1,0:T(8,128)(2,1)} %get-tuple-element.282.grad_ref, bf16[4,1168,768]{2,1,0:T(8,128)(2,1)} %get-tuple-element.324.acted_ref), custom_call_target="tpu_custom_call" | custom-call | flops 7000000000 | bytes 7000000 | tf_op jit(solution)/shard_map/drop_weight_grad/pallas_call | solution.py:690
  169.1 6.1 %collective-permute-done.29.refs_3_ = bf16[2,2,96,768]{3,2,1,0:T(8,128)(2,1)} collective-permute-done((bf16[2,2,96,768]{3,2,1,0:T(8,128)(2,1)S(1)}, bf16[2,2,96,768]{3,2,1,0:T(8,128)(2,1)}, u32[]{:S(2)}, u32[]{:S(2)}) %collective-permute-start.29) | collective-permute-done | bytes 589856 | tf_op jit(solution)/shard_map/ppermute | solution.py:771
  176.3 7.5 %drop_weight_grad.3 = bf16[2,8,2,96,768]{4,3,2,1,0:T(8,128)(2,1)} custom-call(s32[2]{0:T(128)} %pad_add_fusion.mine_ref, bf16[1024,768]{1,0:T(8,128)(2,1)} %get-tuple-element.282.grad_ref, bf16[4,1168,768]{2,1,0:T(8,128)(2,1)} %get-tuple-element.324.acted_ref), custom_call_target="tpu_custom_call" | custom-call | flops 7000000000 | bytes 7000000 | tf_op jit(solution)/shard_map/drop_weight_grad/pallas_call | solution.py:690
  185.5 2.5 fusion.4
  191.0 18.7 %expert_back.1 = (bf16[2,8,2,96,768]{4,3,2,1,0:T(8,128)(2,1)}, bf16[2,4,768,768]{3,2,1,0:T(8,128)(2,1)}, f32[1024,768]{1,0:T(8,128)}) custom-call(s32[2]{0:T(128)} %pad_add_fusion.mine_ref, bf16[1024,768]{1,0:T(8,128)(2,1)} %get-tuple-element.282.grad_ref, bf16[4,1168,768]{2,1,0:T(8,128)(2,1)} %get-tuple-element.283.slope_ref, ...), custom_call_target="tpu_custom_call" | custom-call | flops 16999999488 | bytes 17000000 | tf_op jit(solution)/shard_map/expert_back/pallas_call | solution.py:690
  209.7 2.4 convert_add_fusion.2
  216.4 22.2 %expert_back_end.1 = (bf16[2,8,2,96,768]{4,3,2,1,0:T(8,128)(2,1)}, bf16[2,4,768,768]{3,2,1,0:T(8,128)(2,1)}, f32[1024,768]{1,0:T(8,128)}, bf16[1024,768]{1,0:T(8,128)(2,1)}, f32[2,768]{1,0:T(2,128)}) custom-call(s32[2]{0:T(128)} %pad_add_fusion.mine_ref, bf16[1024,768]{1,0:T(8,128)(2,1)} %get-tuple-element.282.grad_ref, ...), custom_call_target="tpu_custom_call", output_to_operand_aliasing={{1}: (10, {})} | custom-call | flops 16999999488 | bytes 17000000 | tf_op jit(solution)/shard_map/expert_back_end/pallas_call | solution.py:690
  238.6 3.9 collective-permute-done.40
  243.9 1.9 fusion.5
  245.8 2.4 fusion.3
  249.6 4.1 collective-permute-start.42
  256.1 16.7 %drop.1 = (bf16[960,768]{1,0:T(8,128)(2,1)}, f32[2,768]{1,0:T(2,128)}) custom-call(bf16[4,1168,768]{2,1,0:T(8,128)(2,1)} %get-tuple-element.324.acted_ref, f32[1168,768]{1,0:T(8,128)} %get-tuple-element.307.refs_7_.residual_ref, f32[1168,1]{1,0:T(8,128)} %fusion.24.valid_ref, s32[960,1]{1,0:T(8,128)} %select_select_fusion.place_ref, f32[3,768]{1,0:T(4,128)} %extra_ref.3, ...), custom_call_target="tpu_custom_call" | custom-call | flops 16999999488 | bytes 17000000 | tf_op jit(solution)/shard_map/drop/pallas_call | solution.py:690
  274.2 2.0 select_maximum_fusion
  276.2 2.9 convert_add_fusion
  282.5 19.0 %attention_back.1 = (bf16[2,8,1,96,768]{4,3,2,1,0:T(8,128)(2,1)}, f32[1024,768]{1,0:T(8,128)}) custom-call(s32[2]{0:T(128)} %pad_add_fusion.mine_ref, bf16[1024,768]{1,0:T(8,128)(2,1)} %get-tuple-element.335.grad_attended_ref, bf16[4,1168,576]{2,1,0:T(8,128)(2,1)} %get-tuple-element.336.joint_ref, bf16[4,1168,192]{2,1,0:T(8,128)(2,1)} %get-tuple-element.337.mixed_ref, ...), custom_call_target="tpu_custom_call" | custom-call | flops 19000000512 | bytes 19000000 | tf_op jit(solution)/shard_map/attention_back/pallas_call | solution.py:690
  301.5 5.3 %collective-permute-done.48 = bf16[4,2,96,768]{3,2,1,0:T(8,128)(2,1)S(1)} collective-permute-done((bf16[4,2,96,768]{3,2,1,0:T(8,128)(2,1)S(1)}, bf16[4,2,96,768]{3,2,1,0:T(8,128)(2,1)S(1)}, u32[]{:S(2)}, u32[]{:S(2)}) %collective-permute-start.48) | collective-permute-done | bytes 1179680 | tf_op jit(solution)/shard_map/ppermute | solution.py:771
  307.9 2.4 fusion.1
  313.1 2.2 collective-permute-start.51
  316.8 3.7 all-to-all-start.2
  320.5 19.4 %attention_back_end.1 = (bf16[2,8,1,96,768]{4,3,2,1,0:T(8,128)(2,1)}, f32[1024,768]{1,0:T(8,128)}) custom-call(s32[2]{0:T(128)} %pad_add_fusion.mine_ref, bf16[1024,768]{1,0:T(8,128)(2,1)} %get-tuple-element.335.grad_attended_ref, bf16[4,1168,576]{2,1,0:T(8,128)(2,1)} %get-tuple-element.336.joint_ref, bf16[4,1168,192]{2,1,0:T(8,128)(2,1)} %get-tuple-element.337.mixed_ref, ...), custom_call_target="tpu_custom_call" | custom-call | flops 19000000512 | bytes 19000000 | tf_op jit(solution)/shard_map/attention_back_end/pallas_call | solution.py:690
  342.8 2.0 collective-permute-start.54
  344.8 10.5 %input_grad.1 = (bf16[960,768]{1,0:T(8,128)(2,1)}, f32[2,768]{1,0:T(2,128)}, f32[1,768]{1,0:T(1,128)}) custom-call(f32[1024,768]{1,0:T(8,128)} %get-tuple-element.364.grad_normed_ref, f32[1024,768]{1,0:T(8,128)} %get-tuple-element.365.grad_residual_ref, f32[1168,768]{1,0:T(8,128)} %get-tuple-element.238.block_ref, s32[1168,1]{1,0:T(8,128)} %copy.131.hidden_ref, ...), custom_call_target="tpu_custom_call" | custom-call | flops 8999999488 | bytes 9000000 | tf_op jit(solution)/shard_map/input_grad/pallas_call | solution.py:690
  355.3 1.8 convert_element_type.438
  361.5 13.4 %collective-permute-done.55 = bf16[4,1,96,768]{3,2,1,0:T(8,128)(2,1)S(1)} collective-permute-done((bf16[4,1,96,768]{3,2,1,0:T(8,128)(2,1)S(1)}, bf16[4,1,96,768]{3,2,1,0:T(8,128)(2,1)S(1)}, u32[]{:S(2)}, u32[]{:S(2)}) %collective-permute-start.55) | collective-permute-done | bytes 589856 | tf_op jit(solution)/shard_map/ppermute | solution.py:771
  379.8 3.0 collective-permute-done.58
  383.9 3.0 collective-permute-start.63
  388.3 3.9 all-to-all-start.3
  392.4 3.4 fusion.61
  396.7 2.0 collective-permute-start.61
  398.8 2.7 fusion.63
  411.2 1.8 convert_element_type.444
  (321 shorter events, 86.9 us)
Async XLA Ops:
  3.5 17.6 %collective-permute-start.2 = (bf16[1,96,768]{2,1,0:T(8,128)(2,1)S(1)}, bf16[1,96,768]{2,1,0:T(8,128)(2,1)S(1)}, u32[]{:S(2)}, u32[]{:S(2)}) collective-permute-start(bf16[1,96,768]{2,1,0:T(8,128)(2,1)S(1)} %pad_maximum_fusion.10), channel_id=1, source_target_pairs={{0,24},{4,28},{8,16},{12,20},{16,8},{20,12},{24,0},{28,4},{1,25},{... | collective-permute-start | bytes 442376 | tf_op jit(solution)/shard_map/ppermute | solution.py:771
  9.3 36.1 %all-to-all-start = ((bf16[4,240,768]{2,1,0:T(8,128)(2,1)}), bf16[4,240,768]{2,1,0:T(8,128)(2,1)}, u32[]{:S(2)}, u32[]{:S(2)}) async-start(bf16[4,240,768]{2,1,0:T(8,128)(2,1)} %param.23), calls=%async_computation | async-start | bytes 2949120 | tf_op jit(solution)/shard_map/all_to_all | solution.py:774
  24.0 16.0 %collective-permute-start.3 = (bf16[4,1,96,768]{3,2,1,0:T(8,128)(2,1)}, bf16[4,1,96,768]{3,2,1,0:T(8,128)(2,1)}, u32[]{:S(2)}, u32[]{:S(2)}) collective-permute-start(bf16[4,1,96,768]{3,2,1,0:T(8,128)(2,1)} %pad_maximum_fusion.6.refs_2_), channel_id=1, source_target_pairs={{0,4},{4,0},{8,12},{12,8},{16,20},{20,16},{24,28},{28,24},{1,5},{5... | collective-permute-start | bytes 1769480 | tf_op jit(solution)/shard_map/ppermute | solution.py:771
  25.6 19.8 %collective-permute-start.4 = (bf16[4,1,96,768]{3,2,1,0:T(8,128)(2,1)}, bf16[4,1,96,768]{3,2,1,0:T(8,128)(2,1)}, u32[]{:S(2)}, u32[]{:S(2)}) collective-permute-start(bf16[4,1,96,768]{3,2,1,0:T(8,128)(2,1)} %pad_maximum_fusion.6.refs_2_), channel_id=1, source_target_pairs={{0,2},{1,3},{2,0},{3,1},{4,6},{5,7},{6,4},{7,5},{8,10},{9,11},{10,... | collective-permute-start | bytes 1769480 | tf_op jit(solution)/shard_map/ppermute | solution.py:771
  28.4 30.9 %collective-permute-start.10 = (bf16[4,1,96,768]{3,2,1,0:T(8,128)(2,1)}, bf16[4,1,96,768]{3,2,1,0:T(8,128)(2,1)}, u32[]{:S(2)}, u32[]{:S(2)}) collective-permute-start(bf16[4,1,96,768]{3,2,1,0:T(8,128)(2,1)} %pad_maximum_fusion.6.refs_2_), channel_id=1, source_target_pairs={{0,1},{1,0},{2,3},{3,2},{4,5},{5,4},{6,7},{7,6},{8,9},{9,8},{10,11... | collective-permute-start | bytes 1769480 | tf_op jit(solution)/shard_map/ppermute | solution.py:771
  48.5 32.4 %collective-permute-start.7 = (bf16[2,96,768]{2,1,0:T(8,128)(2,1)}, bf16[2,96,768]{2,1,0:T(8,128)(2,1)}, u32[]{:S(2)}, u32[]{:S(2)}) collective-permute-start(bf16[2,96,768]{2,1,0:T(8,128)(2,1)} %convert_element_type.393), channel_id=1, source_target_pairs={{0,8},{4,12},{8,0},{12,4},{16,24},{20,28},{24,16},{28,20},{1,9},{5... | collective-permute-start | bytes 884744 | tf_op jit(solution)/shard_map/ppermute | solution.py:771
  49.9 31.0 %collective-permute-start.8 = (bf16[2,96,768]{2,1,0:T(8,128)(2,1)}, bf16[2,96,768]{2,1,0:T(8,128)(2,1)}, u32[]{:S(2)}, u32[]{:S(2)}) collective-permute-start(bf16[2,96,768]{2,1,0:T(8,128)(2,1)} %convert_element_type.393), channel_id=1, source_target_pairs={{0,16},{4,20},{8,24},{12,28},{16,0},{20,4},{24,8},{28,12},{1,17},{... | collective-permute-start | bytes 884744 | tf_op jit(solution)/shard_map/ppermute | solution.py:771
  54.1 26.9 %all-to-all-start.1 = ((bf16[4,240,768]{2,1,0:T(8,128)(2,1)}), bf16[4,240,768]{2,1,0:T(8,128)(2,1)S(1)}, u32[]{:S(2)}, u32[]{:S(2)}) async-start(bf16[4,240,768]{2,1,0:T(8,128)(2,1)} %convert_element_type.394), calls=%async_computation.1 | async-start | bytes 2949120 | tf_op jit(solution)/shard_map/all_to_all | solution.py:774
  59.2 21.7 %collective-permute-start.9 = (bf16[2,96,768]{2,1,0:T(8,128)(2,1)}, bf16[2,96,768]{2,1,0:T(8,128)(2,1)S(1)}, u32[]{:S(2)}, u32[]{:S(2)}) collective-permute-start(bf16[2,96,768]{2,1,0:T(8,128)(2,1)} %convert_element_type.393), channel_id=1, source_target_pairs={{0,24},{4,28},{8,16},{12,20},{16,8},{20,12},{24,0},{28,4},{1,25},{... | collective-permute-start | bytes 884744 | tf_op jit(solution)/shard_map/ppermute | solution.py:771
  59.4 25.8 %collective-permute-start.17 = (bf16[4,1,96,768]{3,2,1,0:T(8,128)(2,1)}, bf16[4,1,96,768]{3,2,1,0:T(8,128)(2,1)}, u32[]{:S(2)}, u32[]{:S(2)}) collective-permute-start(bf16[4,1,96,768]{3,2,1,0:T(8,128)(2,1)} %collective-permute-done.4.refs_3_), channel_id=1, source_target_pairs={{0,1},{1,0},{2,3},{3,2},{4,5},{5,4},{6,7},{7,6},{8,9},{9,8},{10,11... | collective-permute-start | bytes 1769480 | tf_op jit(solution)/shard_map/ppermute | solution.py:771
  59.9 21.0 %collective-permute-start.6 = (bf16[2,1,96,768]{3,2,1,0:T(8,128)(2,1)S(1)}, bf16[2,1,96,768]{3,2,1,0:T(8,128)(2,1)S(1)}, u32[]{:S(2)}, u32[]{:S(2)}) collective-permute-start(bf16[2,1,96,768]{3,2,1,0:T(8,128)(2,1)S(1)} %slice.265), channel_id=1, source_target_pairs={{0,4},{4,0},{8,12},{12,8},{16,20},{20,16},{24,28},{28,24},{1,5},{5... | collective-permute-start | bytes 884744 | tf_op jit(solution)/shard_map/ppermute | solution.py:771
  82.9 28.0 %collective-permute-start.12 = (bf16[4,2,96,768]{3,2,1,0:T(8,128)(2,1)S(1)}, bf16[4,2,96,768]{3,2,1,0:T(8,128)(2,1)S(1)}, u32[]{:S(2)}, u32[]{:S(2)}) collective-permute-start(bf16[4,2,96,768]{3,2,1,0:T(8,128)(2,1)S(1)} %pad_maximum_fusion.refs_0_), channel_id=1, source_target_pairs={{0,4},{4,0},{8,12},{12,8},{16,20},{20,16},{24,28},{28,24},{1,5},{5... | collective-permute-start | bytes 3538952 | tf_op jit(solution)/shard_map/ppermute | solution.py:771
  83.5 27.7 %collective-permute-start.13 = (bf16[4,2,96,768]{3,2,1,0:T(8,128)(2,1)S(1)}, bf16[4,2,96,768]{3,2,1,0:T(8,128)(2,1)S(1)}, u32[]{:S(2)}, u32[]{:S(2)}) collective-permute-start(bf16[4,2,96,768]{3,2,1,0:T(8,128)(2,1)S(1)} %pad_maximum_fusion.refs_0_), channel_id=1, source_target_pairs={{0,2},{1,3},{2,0},{3,1},{4,6},{5,7},{6,4},{7,5},{8,10},{9,11},{10,... | collective-permute-start | bytes 3538952 | tf_op jit(solution)/shard_map/ppermute | solution.py:771
  85.2 25.0 %collective-permute-start.14 = (bf16[2,96,768]{2,1,0:T(8,128)(2,1)S(1)}, bf16[2,96,768]{2,1,0:T(8,128)(2,1)S(1)}, u32[]{:S(2)}, u32[]{:S(2)}) collective-permute-start(bf16[2,96,768]{2,1,0:T(8,128)(2,1)S(1)} %convert_bitcast_fusion), channel_id=1, source_target_pairs={{0,8},{4,12},{8,0},{12,4},{16,24},{20,28},{24,16},{28,20},{1,9},{5... | collective-permute-start | bytes 884744 | tf_op jit(solution)/shard_map/ppermute | solution.py:771
  85.6 24.7 %collective-permute-start.15 = (bf16[2,96,768]{2,1,0:T(8,128)(2,1)S(1)}, bf16[2,96,768]{2,1,0:T(8,128)(2,1)S(1)}, u32[]{:S(2)}, u32[]{:S(2)}) collective-permute-start(bf16[2,96,768]{2,1,0:T(8,128)(2,1)S(1)} %convert_bitcast_fusion), channel_id=1, source_target_pairs={{0,16},{4,20},{8,24},{12,28},{16,0},{20,4},{24,8},{28,12},{1,17},{... | collective-permute-start | bytes 884744 | tf_op jit(solution)/shard_map/ppermute | solution.py:771
  89.4 20.9 %collective-permute-start.16 = (bf16[2,96,768]{2,1,0:T(8,128)(2,1)S(1)}, bf16[2,96,768]{2,1,0:T(8,128)(2,1)S(1)}, u32[]{:S(2)}, u32[]{:S(2)}) collective-permute-start(bf16[2,96,768]{2,1,0:T(8,128)(2,1)S(1)} %convert_bitcast_fusion), channel_id=1, source_target_pairs={{0,24},{4,28},{8,16},{12,20},{16,8},{20,12},{24,0},{28,4},{1,25},{... | collective-permute-start | bytes 884744 | tf_op jit(solution)/shard_map/ppermute | solution.py:771
  111.2 17.5 %collective-permute-start.23 = (bf16[4,2,96,768]{3,2,1,0:T(8,128)(2,1)S(1)}, bf16[4,2,96,768]{3,2,1,0:T(8,128)(2,1)}, u32[]{:S(2)}, u32[]{:S(2)}) collective-permute-start(bf16[4,2,96,768]{3,2,1,0:T(8,128)(2,1)S(1)} %collective-permute-done.12.refs_1_), channel_id=1, source_target_pairs={{0,1},{1,0},{2,3},{3,2},{4,5},{5,4},{6,7},{7,6},{8,9},{9,8},{10,11... | collective-permute-start | bytes 3538952 | tf_op jit(solution)/shard_map/ppermute | solution.py:771
  111.2 17.5 %collective-permute-start.24 = (bf16[4,2,96,768]{3,2,1,0:T(8,128)(2,1)S(1)}, bf16[4,2,96,768]{3,2,1,0:T(8,128)(2,1)}, u32[]{:S(2)}, u32[]{:S(2)}) collective-permute-start(bf16[4,2,96,768]{3,2,1,0:T(8,128)(2,1)S(1)} %collective-permute-done.13.refs_2_), channel_id=1, source_target_pairs={{0,1},{1,0},{2,3},{3,2},{4,5},{5,4},{6,7},{7,6},{8,9},{9,8},{10,11... | collective-permute-start | bytes 3538952 | tf_op jit(solution)/shard_map/ppermute | solution.py:771
  112.4 15.2 %collective-permute-start.20 = (bf16[2,2,96,768]{3,2,1,0:T(8,128)(2,1)S(1)}, bf16[2,2,96,768]{3,2,1,0:T(8,128)(2,1)}, u32[]{:S(2)}, u32[]{:S(2)}) collective-permute-start(bf16[2,2,96,768]{3,2,1,0:T(8,128)(2,1)S(1)} %slice.266), channel_id=1, source_target_pairs={{0,2},{1,3},{2,0},{3,1},{4,6},{5,7},{6,4},{7,5},{8,10},{9,11},{10,... | collective-permute-start | bytes 1769480 | tf_op jit(solution)/shard_map/ppermute | solution.py:771
  129.9 28.0 %collective-permute-start.25 = (bf16[4,2,96,768]{3,2,1,0:T(8,128)(2,1)S(1)}, bf16[4,2,96,768]{3,2,1,0:T(8,128)(2,1)S(1)}, u32[]{:S(2)}, u32[]{:S(2)}) collective-permute-start(bf16[4,2,96,768]{3,2,1,0:T(8,128)(2,1)S(1)} %pad_maximum_fusion.1.refs_0_), channel_id=1, source_target_pairs={{0,4},{4,0},{8,12},{12,8},{16,20},{20,16},{24,28},{28,24},{1,5},{5... | collective-permute-start | bytes 3538952 | tf_op jit(solution)/shard_map/ppermute | solution.py:771
  131.6 27.7 %collective-permute-start.26 = (bf16[4,2,96,768]{3,2,1,0:T(8,128)(2,1)S(1)}, bf16[4,2,96,768]{3,2,1,0:T(8,128)(2,1)S(1)}, u32[]{:S(2)}, u32[]{:S(2)}) collective-permute-start(bf16[4,2,96,768]{3,2,1,0:T(8,128)(2,1)S(1)} %pad_maximum_fusion.1.refs_0_), channel_id=1, source_target_pairs={{0,2},{1,3},{2,0},{3,1},{4,6},{5,7},{6,4},{7,5},{8,10},{9,11},{10,... | collective-permute-start | bytes 3538952 | tf_op jit(solution)/shard_map/ppermute | solution.py:771
  132.2 36.9 %collective-permute-start.31 = (bf16[4,2,96,768]{3,2,1,0:T(8,128)(2,1)S(1)}, bf16[4,2,96,768]{3,2,1,0:T(8,128)(2,1)S(1)}, u32[]{:S(2)}, u32[]{:S(2)}) collective-permute-start(bf16[4,2,96,768]{3,2,1,0:T(8,128)(2,1)S(1)} %pad_maximum_fusion.1.refs_0_), channel_id=1, source_target_pairs={{0,1},{1,0},{2,3},{3,2},{4,5},{5,4},{6,7},{7,6},{8,9},{9,8},{10,11... | collective-permute-start | bytes 3538952 | tf_op jit(solution)/shard_map/ppermute | solution.py:771
  159.2 16.4 %collective-permute-start.32 = (bf16[4,2,96,768]{3,2,1,0:T(8,128)(2,1)S(1)}, bf16[4,2,96,768]{3,2,1,0:T(8,128)(2,1)}, u32[]{:S(2)}, u32[]{:S(2)}) collective-permute-start(bf16[4,2,96,768]{3,2,1,0:T(8,128)(2,1)S(1)} %collective-permute-done.25.refs_1_), channel_id=1, source_target_pairs={{0,1},{1,0},{2,3},{3,2},{4,5},{5,4},{6,7},{7,6},{8,9},{9,8},{10,11... | collective-permute-start | bytes 3538952 | tf_op jit(solution)/shard_map/ppermute | solution.py:771
  159.2 16.4 %collective-permute-start.33 = (bf16[4,2,96,768]{3,2,1,0:T(8,128)(2,1)S(1)}, bf16[4,2,96,768]{3,2,1,0:T(8,128)(2,1)}, u32[]{:S(2)}, u32[]{:S(2)}) collective-permute-start(bf16[4,2,96,768]{3,2,1,0:T(8,128)(2,1)S(1)} %collective-permute-done.26.refs_2_), channel_id=1, source_target_pairs={{0,1},{1,0},{2,3},{3,2},{4,5},{5,4},{6,7},{7,6},{8,9},{9,8},{10,11... | collective-permute-start | bytes 3538952 | tf_op jit(solution)/shard_map/ppermute | solution.py:771
  160.3 14.9 %collective-permute-start.29 = (bf16[2,2,96,768]{3,2,1,0:T(8,128)(2,1)S(1)}, bf16[2,2,96,768]{3,2,1,0:T(8,128)(2,1)}, u32[]{:S(2)}, u32[]{:S(2)}) collective-permute-start(bf16[2,2,96,768]{3,2,1,0:T(8,128)(2,1)S(1)} %slice.268), channel_id=1, source_target_pairs={{0,2},{1,3},{2,0},{3,1},{4,6},{5,7},{6,4},{7,5},{8,10},{9,11},{10,... | collective-permute-start | bytes 1769480 | tf_op jit(solution)/shard_map/ppermute | solution.py:771
  189.1 20.6 %collective-permute-start.37 = (bf16[2,2,96,768]{3,2,1,0:T(8,128)(2,1)}, bf16[2,2,96,768]{3,2,1,0:T(8,128)(2,1)S(1)}, u32[]{:S(2)}, u32[]{:S(2)}) collective-permute-start(bf16[2,2,96,768]{3,2,1,0:T(8,128)(2,1)} %get-tuple-element.566), channel_id=1, source_target_pairs={{0,4},{4,0},{8,12},{12,8},{16,20},{20,16},{24,28},{28,24},{1,5},{5... | collective-permute-start | bytes 1769480 | tf_op jit(solution)/shard_map/ppermute | solution.py:771
  189.7 20.0 %collective-permute-start.38 = (bf16[2,2,96,768]{3,2,1,0:T(8,128)(2,1)}, bf16[2,2,96,768]{3,2,1,0:T(8,128)(2,1)S(1)}, u32[]{:S(2)}, u32[]{:S(2)}) collective-permute-start(bf16[2,2,96,768]{3,2,1,0:T(8,128)(2,1)} %get-tuple-element.565), channel_id=1, source_target_pairs={{0,2},{1,3},{2,0},{3,1},{4,6},{5,7},{6,4},{7,5},{8,10},{9,11},{10,... | collective-permute-start | bytes 1769480 | tf_op jit(solution)/shard_map/ppermute | solution.py:771
  212.8 31.0 %collective-permute-start.39 = (bf16[2,8,2,96,768]{4,3,2,1,0:T(8,128)(2,1)}, bf16[2,8,2,96,768]{4,3,2,1,0:T(8,128)(2,1)}, u32[]{:S(2)}, u32[]{:S(2)}) collective-permute-start(bf16[2,8,2,96,768]{4,3,2,1,0:T(8,128)(2,1)} %get-tuple-element.309), channel_id=1, source_target_pairs={{0,1},{1,0},{2,3},{3,2},{4,5},{5,4},{6,7},{7,6},{8,9},{9,8},{10,11... | collective-permute-start | bytes 14155784 | tf_op jit(solution)/shard_map/ppermute | solution.py:771
  214.2 28.4 %collective-permute-start.40 = (bf16[4,2,96,768]{3,2,1,0:T(8,128)(2,1)S(1)}, bf16[4,2,96,768]{3,2,1,0:T(8,128)(2,1)S(1)}, u32[]{:S(2)}, u32[]{:S(2)}) collective-permute-start(bf16[4,2,96,768]{3,2,1,0:T(8,128)(2,1)S(1)} %pad_maximum_fusion.2), channel_id=1, source_target_pairs={{0,4},{4,0},{8,12},{12,8},{16,20},{20,16},{24,28},{28,24},{1,5},{5... | collective-permute-start | bytes 3538952 | tf_op jit(solution)/shard_map/ppermute | solution.py:771
  215.8 28.1 %collective-permute-start.41 = (bf16[4,2,96,768]{3,2,1,0:T(8,128)(2,1)S(1)}, bf16[4,2,96,768]{3,2,1,0:T(8,128)(2,1)S(1)}, u32[]{:S(2)}, u32[]{:S(2)}) collective-permute-start(bf16[4,2,96,768]{3,2,1,0:T(8,128)(2,1)S(1)} %pad_maximum_fusion.3), channel_id=1, source_target_pairs={{0,2},{1,3},{2,0},{3,1},{4,6},{5,7},{6,4},{7,5},{8,10},{9,11},{10,... | collective-permute-start | bytes 3538952 | tf_op jit(solution)/shard_map/ppermute | solution.py:771
  248.3 27.9 %collective-permute-start.45 = (bf16[2,2,96,768]{3,2,1,0:T(8,128)(2,1)S(1)}, bf16[2,2,96,768]{3,2,1,0:T(8,128)(2,1)S(1)}, u32[]{:S(2)}, u32[]{:S(2)}) collective-permute-start(bf16[2,2,96,768]{3,2,1,0:T(8,128)(2,1)S(1)} %get-tuple-element.561), channel_id=1, source_target_pairs={{0,4},{4,0},{8,12},{12,8},{16,20},{20,16},{24,28},{28,24},{1,5},{5... | collective-permute-start | bytes 1769480 | tf_op jit(solution)/shard_map/ppermute | solution.py:771
  248.8 27.4 %collective-permute-start.46 = (bf16[2,2,96,768]{3,2,1,0:T(8,128)(2,1)S(1)}, bf16[2,2,96,768]{3,2,1,0:T(8,128)(2,1)S(1)}, u32[]{:S(2)}, u32[]{:S(2)}) collective-permute-start(bf16[2,2,96,768]{3,2,1,0:T(8,128)(2,1)S(1)} %get-tuple-element.560), channel_id=1, source_target_pairs={{0,2},{1,3},{2,0},{3,1},{4,6},{5,7},{6,4},{7,5},{8,10},{9,11},{10,... | collective-permute-start | bytes 1769480 | tf_op jit(solution)/shard_map/ppermute | solution.py:771
  249.6 30.2 %collective-permute-start.42 = (bf16[2,96,768]{2,1,0:T(8,128)(2,1)S(1)}, bf16[2,96,768]{2,1,0:T(8,128)(2,1)S(1)}, u32[]{:S(2)}, u32[]{:S(2)}) collective-permute-start(bf16[2,96,768]{2,1,0:T(8,128)(2,1)S(1)} %get-tuple-element.564), channel_id=1, source_target_pairs={{0,8},{4,12},{8,0},{12,4},{16,24},{20,28},{24,16},{28,20},{1,9},{5... | collective-permute-start | bytes 884744 | tf_op jit(solution)/shard_map/ppermute | solution.py:771
  253.7 26.1 %collective-permute-start.43 = (bf16[2,96,768]{2,1,0:T(8,128)(2,1)S(1)}, bf16[2,96,768]{2,1,0:T(8,128)(2,1)S(1)}, u32[]{:S(2)}, u32[]{:S(2)}) collective-permute-start(bf16[2,96,768]{2,1,0:T(8,128)(2,1)S(1)} %get-tuple-element.563), channel_id=1, source_target_pairs={{0,16},{4,20},{8,24},{12,28},{16,0},{20,4},{24,8},{28,12},{1,17},{... | collective-permute-start | bytes 884744 | tf_op jit(solution)/shard_map/ppermute | solution.py:771
  254.7 25.8 %collective-permute-start.44 = (bf16[2,96,768]{2,1,0:T(8,128)(2,1)S(1)}, bf16[2,96,768]{2,1,0:T(8,128)(2,1)}, u32[]{:S(2)}, u32[]{:S(2)}) collective-permute-start(bf16[2,96,768]{2,1,0:T(8,128)(2,1)S(1)} %get-tuple-element.562), channel_id=1, source_target_pairs={{0,24},{4,28},{8,16},{12,20},{16,8},{20,12},{24,0},{28,4},{1,25},{... | collective-permute-start | bytes 884744 | tf_op jit(solution)/shard_map/ppermute | solution.py:771
  280.6 26.2 %collective-permute-start.48 = (bf16[4,2,96,768]{3,2,1,0:T(8,128)(2,1)S(1)}, bf16[4,2,96,768]{3,2,1,0:T(8,128)(2,1)S(1)}, u32[]{:S(2)}, u32[]{:S(2)}) collective-permute-start(bf16[4,2,96,768]{3,2,1,0:T(8,128)(2,1)S(1)} %pad_maximum_fusion.4), channel_id=1, source_target_pairs={{0,4},{4,0},{8,12},{12,8},{16,20},{20,16},{24,28},{28,24},{1,5},{5... | collective-permute-start | bytes 3538952 | tf_op jit(solution)/shard_map/ppermute | solution.py:771
  282.1 25.9 %collective-permute-start.49 = (bf16[4,2,96,768]{3,2,1,0:T(8,128)(2,1)S(1)}, bf16[4,2,96,768]{3,2,1,0:T(8,128)(2,1)S(1)}, u32[]{:S(2)}, u32[]{:S(2)}) collective-permute-start(bf16[4,2,96,768]{3,2,1,0:T(8,128)(2,1)S(1)} %pad_maximum_fusion.5), channel_id=1, source_target_pairs={{0,2},{1,3},{2,0},{3,1},{4,6},{5,7},{6,4},{7,5},{8,10},{9,11},{10,... | collective-permute-start | bytes 3538952 | tf_op jit(solution)/shard_map/ppermute | solution.py:771
  301.4 38.5 %collective-permute-start.47 = (bf16[2,8,1,96,768]{4,3,2,1,0:T(8,128)(2,1)}, bf16[2,8,1,96,768]{4,3,2,1,0:T(8,128)(2,1)}, u32[]{:S(2)}, u32[]{:S(2)}) collective-permute-start(bf16[2,8,1,96,768]{4,3,2,1,0:T(8,128)(2,1)} %get-tuple-element.340), channel_id=1, source_target_pairs={{0,1},{1,0},{2,3},{3,2},{4,5},{5,4},{6,7},{7,6},{8,9},{9,8},{10,11... | collective-permute-start | bytes 7077896 | tf_op jit(solution)/shard_map/ppermute | solution.py:771
  312.4 27.5 %collective-permute-start.50 = (bf16[2,96,768]{2,1,0:T(8,128)(2,1)}, bf16[2,96,768]{2,1,0:T(8,128)(2,1)S(1)}, u32[]{:S(2)}, u32[]{:S(2)}) collective-permute-start(bf16[2,96,768]{2,1,0:T(8,128)(2,1)} %get-tuple-element.559), channel_id=1, source_target_pairs={{0,8},{4,12},{8,0},{12,4},{16,24},{20,28},{24,16},{28,20},{1,9},{5... | collective-permute-start | bytes 884744 | tf_op jit(solution)/shard_map/ppermute | solution.py:771
  313.1 26.7 %collective-permute-start.51 = (bf16[2,96,768]{2,1,0:T(8,128)(2,1)}, bf16[2,96,768]{2,1,0:T(8,128)(2,1)S(1)}, u32[]{:S(2)}, u32[]{:S(2)}) collective-permute-start(bf16[2,96,768]{2,1,0:T(8,128)(2,1)} %get-tuple-element.558), channel_id=1, source_target_pairs={{0,16},{4,20},{8,24},{12,28},{16,0},{20,4},{24,8},{28,12},{1,17},{... | collective-permute-start | bytes 884744 | tf_op jit(solution)/shard_map/ppermute | solution.py:771
  315.4 24.5 %collective-permute-start.52 = (bf16[2,96,768]{2,1,0:T(8,128)(2,1)}, bf16[2,96,768]{2,1,0:T(8,128)(2,1)S(1)}, u32[]{:S(2)}, u32[]{:S(2)}) collective-permute-start(bf16[2,96,768]{2,1,0:T(8,128)(2,1)} %get-tuple-element.557), channel_id=1, source_target_pairs={{0,24},{4,28},{8,16},{12,20},{16,8},{20,12},{24,0},{28,4},{1,25},{... | collective-permute-start | bytes 884744 | tf_op jit(solution)/shard_map/ppermute | solution.py:771
  316.8 25.3 %all-to-all-start.2 = ((bf16[4,240,768]{2,1,0:T(8,128)(2,1)}), bf16[4,240,768]{2,1,0:T(8,128)(2,1)S(1)}, u32[]{:S(2)}, u32[]{:S(2)}) async-start(bf16[4,240,768]{2,1,0:T(8,128)(2,1)} %bitcast.230), calls=%async_computation.2 | async-start | bytes 2949120 | tf_op jit(solution)/shard_map/all_to_all | solution.py:777
  342.1 15.1 %collective-permute-start.53 = (bf16[2,1,96,768]{3,2,1,0:T(8,128)(2,1)S(1)}, bf16[2,1,96,768]{3,2,1,0:T(8,128)(2,1)S(1)}, u32[]{:S(2)}, u32[]{:S(2)}) collective-permute-start(bf16[2,1,96,768]{3,2,1,0:T(8,128)(2,1)S(1)} %get-tuple-element.571), channel_id=1, source_target_pairs={{0,4},{4,0},{8,12},{12,8},{16,20},{20,16},{24,28},{28,24},{1,5},{5... | collective-permute-start | bytes 884744 | tf_op jit(solution)/shard_map/ppermute | solution.py:771
  360.0 14.9 %collective-permute-start.55 = (bf16[4,1,96,768]{3,2,1,0:T(8,128)(2,1)S(1)}, bf16[4,1,96,768]{3,2,1,0:T(8,128)(2,1)S(1)}, u32[]{:S(2)}, u32[]{:S(2)}) collective-permute-start(bf16[4,1,96,768]{3,2,1,0:T(8,128)(2,1)S(1)} %pad_maximum_fusion.7), channel_id=1, source_target_pairs={{0,4},{4,0},{8,12},{12,8},{16,20},{20,16},{24,28},{28,24},{1,5},{5... | collective-permute-start | bytes 1769480 | tf_op jit(solution)/shard_map/ppermute | solution.py:771
  383.9 20.7 %collective-permute-start.62 = (bf16[1,96,768]{2,1,0:T(8,128)(2,1)}, bf16[1,96,768]{2,1,0:T(8,128)(2,1)}, u32[]{:S(2)}, u32[]{:S(2)}) collective-permute-start(bf16[1,96,768]{2,1,0:T(8,128)(2,1)} %get-tuple-element.567), channel_id=1, source_target_pairs={{0,8},{4,12},{8,0},{12,4},{16,24},{20,28},{24,16},{28,20},{1,9},{5... | collective-permute-start | bytes 442376 | tf_op jit(solution)/shard_map/ppermute | solution.py:771
  383.9 20.7 %collective-permute-start.63 = (bf16[1,96,768]{2,1,0:T(8,128)(2,1)}, bf16[1,96,768]{2,1,0:T(8,128)(2,1)}, u32[]{:S(2)}, u32[]{:S(2)}) collective-permute-start(bf16[1,96,768]{2,1,0:T(8,128)(2,1)} %get-tuple-element.569), channel_id=1, source_target_pairs={{0,16},{4,20},{8,24},{12,28},{16,0},{20,4},{24,8},{28,12},{1,17},{... | collective-permute-start | bytes 442376 | tf_op jit(solution)/shard_map/ppermute | solution.py:771
  386.9 17.7 %collective-permute-start.64 = (bf16[1,96,768]{2,1,0:T(8,128)(2,1)}, bf16[1,96,768]{2,1,0:T(8,128)(2,1)}, u32[]{:S(2)}, u32[]{:S(2)}) collective-permute-start(bf16[1,96,768]{2,1,0:T(8,128)(2,1)} %get-tuple-element.568), channel_id=1, source_target_pairs={{0,24},{4,28},{8,16},{12,20},{16,8},{20,12},{24,0},{28,4},{1,25},{... | collective-permute-start | bytes 442376 | tf_op jit(solution)/shard_map/ppermute | solution.py:771
  388.3 22.9 %all-to-all-start.3 = ((bf16[4,240,768]{2,1,0:T(8,128)(2,1)}), bf16[4,240,768]{2,1,0:T(8,128)(2,1)S(1)}, u32[]{:S(2)}, u32[]{:S(2)}) async-start(bf16[4,240,768]{2,1,0:T(8,128)(2,1)} %bitcast.228), calls=%async_computation.3 | async-start | bytes 2949120 | tf_op jit(solution)/shard_map/all_to_all | solution.py:777
  (80 other events, 552.3 us)

commit v5 on v4

--- a/solution.py
+++ b/solution.py
@@ -223,7 +223,7 @@
 
 
 def attention_end_kernel(meta_ref, normed_ref, block_ref, before_ref, valid_ref, norm_ref, *refs, **sizes):
-    parts, outs = (refs[:3], refs[3:6]), refs[10:]
+    parts, outs = (refs[:2], refs[2:4]), refs[8:]
     residual_ref, feed_ref, square_ref, out_ref, joint_ref, mixed_ref, probs_ref = outs[:7]
     weight_ref, sems, out_sems = outs[7:]
     items, main_rows, all_rows = sizes["items"], sizes["main_rows"], sizes["all_rows"]
@@ -387,22 +387,23 @@
     hidden_ref,
     place_ref,
     norm_ref,
-    grad_raw_ref,
-    grad_norm_ref,
-    grad_mask_ref,
-    grad_block_ref,
+    *refs,
 ):
-    grad_norm_ref[...] = jnp.zeros_like(grad_norm_ref)
-    grad_mask_ref[...] = jnp.zeros_like(grad_mask_ref)
+    small_refs, (grad_raw_ref, small_ref, grad_block_ref) = refs[:-3], refs[-3:]
+    small_ref[...] = jnp.zeros_like(small_ref)
+    first = 3
+    for ref in small_refs:
+        small_ref[first : first + ref.shape[0], :] = ref[...]
+        first += ref.shape[0]
 
     def chunk(i):
         rows = rows_at(i, ITEM_ROWS)
         grad, gain, shift = norm_backward(block_ref[rows, :], norm_ref[0:1, :], grad_normed_ref[rows, :])
-        grad_norm_ref[0:1, :] += gain
-        grad_norm_ref[1:2, :] += shift
+        small_ref[0:1, :] += gain
+        small_ref[1:2, :] += shift
         grad = grad + grad_residual_ref[rows, :]
         hidden = hidden_ref[rows, :] > 0
-        grad_mask_ref[...] += jnp.sum(jnp.where(hidden, grad, 0.0), axis=0, keepdims=True)
+        small_ref[2:3, :] += jnp.sum(jnp.where(hidden, grad, 0.0), axis=0, keepdims=True)
         grad_block_ref[rows, :] = jnp.where(hidden, 0.0, grad).astype(bf16)
 
     loop(grad_normed_ref.shape[0] // ITEM_ROWS, chunk)
@@ -873,8 +874,8 @@
             ),
         )
 
-    place_row = place_of(jnp.arange(block_rows, dtype=jnp.int32))[None, :]
-    place_column = place_of(jnp.arange(block_rows, dtype=jnp.int32))[:, None]
+    places = together(place_of(jnp.arange(block_rows, dtype=jnp.int32)))[0]
+    place_row, place_column = places[None, :], places[:, None]
     targets = (vision_rows + TEXT_STRIDE * item_ids[:, None] + masked).reshape(-1)
     spots = jnp.arange(all_rows, dtype=jnp.int32)
     hidden = jnp.any(spots[:, None] == targets[None, :], axis=1).astype(jnp.int32)[:, None]
@@ -948,7 +949,7 @@
             weight_scratch(1, 2),
             ATTENTION_US,
             (meta,),
-            {12 + i: 3 + i for i in range(4)},
+            {10 + i: 3 + i for i in range(4)},
         )
 
     def lift(feed_input, pieces):
@@ -1065,7 +1066,7 @@
             (mine,),
         )
 
-    def finish_input_grad(grad_normed, grad_residual, block_input):
+    def finish_input_grad(grad_normed, grad_residual, block_input, *sums):
         return call(
             input_grad_kernel,
             "input_grad",
@@ -1077,8 +1078,9 @@
                 (hidden, whole(main_rows, 1)),
                 plain(place_column),
                 plain(norm_params),
-            ],
-            [rows_of(block_rows, bf16), rows_of(2, f32), rows_of(1, f32)],
+            ]
+            + [plain(values) for values in sums],
+            [rows_of(block_rows, bf16), rows_of(16, f32)],
             [pltpu.VMEM((main_rows, model_width), bf16)],
             9,
         )
@@ -1096,30 +1098,30 @@
             DROP_US,
         )
 
+    used_row = jnp.where(jnp.arange(model_width)[None, :] == 0, used.astype(f32), 0.0)
     tables = (place_row, place_column, hidden, valid, meta)
     raw_tokens = exchange(tokens)
     if cube:
-        line, tables = together(gather_line(shard_attend), tables)
+        line = gather_line(shard_attend)
+        even, high = gather_plane(line)
+        even, high, raw_tokens, shard_lift, cotangent, tables = together(
+            even, high, raw_tokens, shard_lift, cotangent, tables
+        )
         place_row, place_column, hidden, valid, meta = tables
-        even, high = gather_plane(line)
-        even, high, raw_tokens, shard_lift, cotangent = together(
-            even, high, raw_tokens, shard_lift, cotangent
-        )
-        corner = gather_corner(even, high)
+        corner = swap(high, "dp", 1)
         line_lift = line_parts(shard_lift)
         raw_grad = exchange(cotangent.astype(bf16))
         early = over_cores(line, even) + (line, even)
     else:
         pieces = gather_pieces(shard_attend)
         early = [pieces[i] for i in (5, 6, 0, 1)]
-        late = [pieces[i] for i in (7, 8, 9, 2, 3, 4)]
+        late = [pieces[7], jnp.concatenate(pieces[8:10]), pieces[2], jnp.concatenate(pieces[3:5])]
         raw_grad = exchange(cotangent.astype(bf16))
 
     block_input, normed, residual, *made = attention(raw_tokens, early)
     if cube:
         corner, line_lift, raw_grad, residual = together(corner, line_lift, raw_grad, residual)
-        late = (high,) + corner
-        late = over_cores(*late) + late
+        late = over_cores(high, corner) + (high, corner)
         line_lift, shard_drop = together(jnp.stack(line_lift), shard_drop)
         plane_lift = gather_plane(line_lift)
         line_drop = line_parts(shard_drop)
@@ -1172,14 +1174,14 @@
     )
     if cube:
         lift_received, from_plane, grad_attended = together(lift_received, from_plane, grad_attended)
-        lift_corner = scatter_corner(lift_keep, lift_received)
+        corner = scatter_corner(lift_keep, lift_received)
         drop_line = scatter_line(drop_keep, drop_received, *from_plane)
-        lift_corner, drop_line, acted = together(lift_corner, drop_line, acted)
-        from_corner = send_corner(lift_corner)
+        corner, drop_line, acted = together(corner, drop_line, acted)
+        from_corner = send_corner(corner)
         from_drop_line = send_line(drop_line)
     else:
         lift_grad = scatter(lift_keep, lift_send)
-    raw_out, feed_square = drop(acted, residual, drop_all)
+    raw_out, squares = drop(acted, residual, drop_all)
     if cube:
         from_corner, raw_out = together(from_corner, raw_out)
         plane = scatter_plane(lift_keep, lift_received, *from_corner)
@@ -1195,25 +1197,28 @@
         from_lift_line = send_line(lift_line)
     block_output = give_back(raw_out)
     attend_keep, grad_normed = attention_back_end(grad_normed, grad_attended, normed, *made)
-    squares = jnp.stack(
-        [jnp.sum(feed_square[0]), jnp.sum(attended_square), jnp.sum(feed_square[1]), used.astype(f32)]
-    )
-    squares = jnp.pad(squares, (0, model_width - 4))[None]
-    if cube:
-        attend_received, from_lift_line, squares, attend_keep = together(
-            attend_received, from_lift_line, squares, attend_keep
+    if cube:
+        attend_received, from_lift_line, attend_keep = together(
+            attend_received, from_lift_line, attend_keep
         )
         corner = scatter_corner(attend_keep, attend_received)
         corner, block_output, grad_normed = together(corner, block_output, grad_normed)
         from_corner = send_corner(corner)
     block_output = block_output.astype(f32)
-    grad_raw, grad_norm_first, grad_mask = finish_input_grad(grad_normed, grad_residual, block_input)
-    small = (grad_norm_first, grad_norm_second, grad_bias, grad_mask, squares)
+    grad_raw, small = finish_input_grad(
+        grad_normed,
+        grad_residual,
+        block_input,
+        *(grad_norm_second, grad_bias, squares, attended_square, used_row),
+    )
     if cube:
         from_corner, small, grad_raw = together(from_corner, small, grad_raw)
         plane = scatter_plane(attend_keep, attend_received, *from_corner)
         plane, small, grad_raw, block_output = together(plane, small, grad_raw, block_output)
-        line = scatter_line(attend_keep, attend_received, *send_plane(*plane))
+        from_plane = send_plane(*plane)
+        for axis, bit in (("mp", 1), ("dp", 1)):
+            small = small + swap(small, axis, bit)
+        line = scatter_line(attend_keep, attend_received, *from_plane)
         line, small, grad_raw, drop_line, lift_line = together(line, small, grad_raw, drop_line, lift_line)
         attend_grad = add(line[0], *send_line(line))[0]
         drop_grad = add(drop_line[0], *from_drop_line)
@@ -1222,14 +1227,15 @@
         attend_grad = scatter(attend_keep, attend_send)[0]
     input_grad = give_back(grad_raw).astype(f32)
 
-    small = jnp.concatenate(small, axis=0)
-    if cube:
-        for axis, bit in (("mp", 1), ("dp", 1), ("mp", 2), ("dp", 2), ("dp", 4)):
+    if cube:
+        for axis, bit in (("mp", 2), ("dp", 2), ("dp", 4)):
             small = small + swap(small, axis, bit)
     else:
         small = lax.psum(small, ("dp", "mp"))
-    norm_total, extra_total = small[:4], small[4:7]
-    rms_values = jnp.sqrt(small[7, :3] / (small[7, 3] * model_width))
+    norm_total = jnp.concatenate([small[0:2], small[3:5]])
+    extra_total = jnp.concatenate([small[5:7], small[2:3]])
+    sums = jnp.sum(small[7:11], axis=1)
+    rms_values = jnp.sqrt(jnp.stack([sums[0], sums[2], sums[1]]) / (sums[3] * model_width))
 
     joint_grad = jnp.stack([attend_grad[:, k * width : (k + 1) * width] for k in range(3)])
     output_grad = attend_grad[:, 3 * width :].T

time: 417 us -> 414 us (level)
  waiting for transfers between devices: 76 us -> 69.8 us
    ppermute x65 -> x63, waiting for transfers between devices: 75 us -> 69.8 us  [swap(): return lax.ppermute(values, axis, [(i, i ^ bit) for i in range(size)])]
    unnamed x125 -> x121, local copies, waits for them, and re-layouts: 10.9 us -> 14.5 us
    ppermute x65 -> x63, starting transfers between devices: 62.4 us -> 62.1 us  [swap(): return lax.ppermute(values, axis, [(i, i ^ bit) for i in range(size)])]
  transfers between devices with their start and end apart: 69 -> 67, of which waited for: 23 -> 22; matrix products, arithmetic and copies ran while one was open for 11% -> 12% of each run, Pallas kernels for 44% -> 45%
where the time goes in v5:
time: 414 us; the launch traced here: 410 us
  Pallas kernels  183 us (44%)
  starting transfers between devices  78.3 us (19%)
  waiting for transfers between devices  69.8 us (17%)
  other arithmetic  53.2 us (13%)
  local copies, waits for them, and re-layouts  21.9 us (5%)
    pallas_call x12, Pallas kernels, call(): pl.pallas_call(kernel, name=name, grid_spec=pltpu.PrefetchScalarGridSpec(...  183 us
    ppermute x63, waiting for transfers between devices, swap(): return lax.ppermute(values, axis, [(i, i ^ bit) for i in range(size)])  69.8 us
    ppermute x63, starting transfers between devices, swap(): return lax.ppermute(values, axis, [(i, i ^ bit) for i in range(size)])  62.1 us
    unnamed x121, local copies, waits for them, and re-layouts  14.5 us
    all_to_all x2, starting transfers between devices, exchange(): lax.all_to_all(values, 'mp', split_axis=0, concat_axis=1, tiled=True)[0]  8.65 us
    convert_element_type x6, other arithmetic, adamw(): return (weight_new, first_new, second_new, weight_new.astype(bf16))  8.53 us
  transfers between devices with their start and end apart: 67, of which 22 were waited for; matrix products, arithmetic and copies ran while one was open for 12% of the time, Pallas kernels for 45%

profile of v5, /device:TPU:0, one launch (start us, length us, event | category | flops | bytes accessed | tf_op | source)
XLA Modules:
  0.0 410.0 jit_solution(14486305022949729609)
XLA Ops:
  3.5 5.1 %collective-permute-start.2 = (bf16[1,96,768]{2,1,0:T(8,128)(2,1)S(1)}, bf16[1,96,768]{2,1,0:T(8,128)(2,1)S(1)}, u32[]{:S(2)}, u32[]{:S(2)}) collective-permute-start(bf16[1,96,768]{2,1,0:T(8,128)(2,1)S(1)} %pad_maximum_fusion.10), channel_id=1, source_target_pairs={{0,24},{4,28},{8,16},{12,20},{16,8},{20,12},{24,0},{28,4},{1,25},{... | collective-permute-start | bytes 442376 | tf_op jit(solution)/shard_map/ppermute | solution.py:772
  9.3 4.5 %all-to-all-start = ((bf16[4,240,768]{2,1,0:T(8,128)(2,1)}), bf16[4,240,768]{2,1,0:T(8,128)(2,1)}, u32[]{:S(2)}, u32[]{:S(2)}) async-start(bf16[4,240,768]{2,1,0:T(8,128)(2,1)} %param.23), calls=%async_computation | async-start | bytes 2949120 | tf_op jit(solution)/shard_map/all_to_all | solution.py:775
  16.7 4.4 %collective-permute-done.1 = bf16[1,96,768]{2,1,0:T(8,128)(2,1)S(1)} collective-permute-done((bf16[1,96,768]{2,1,0:T(8,128)(2,1)S(1)}, bf16[1,96,768]{2,1,0:T(8,128)(2,1)S(1)}, u32[]{:S(2)}, u32[]{:S(2)}) %collective-permute-start.1) | collective-permute-done | bytes 147488 | tf_op jit(solution)/shard_map/ppermute | solution.py:772
  21.8 2.1 pad_maximum_fusion.6.refs_2_
  30.5 1.9 fusion.24.valid_ref
  32.4 6.3 %collective-permute-done.3.refs_3_ = bf16[4,1,96,768]{3,2,1,0:T(8,128)(2,1)} collective-permute-done((bf16[4,1,96,768]{3,2,1,0:T(8,128)(2,1)}, bf16[4,1,96,768]{3,2,1,0:T(8,128)(2,1)}, u32[]{:S(2)}, u32[]{:S(2)}) %collective-permute-start.3) | collective-permute-done | bytes 589856 | tf_op jit(solution)/shard_map/ppermute | solution.py:772
  38.6 6.9 %collective-permute-done.4.refs_2_ = bf16[4,1,96,768]{3,2,1,0:T(8,128)(2,1)} collective-permute-done((bf16[4,1,96,768]{3,2,1,0:T(8,128)(2,1)}, bf16[4,1,96,768]{3,2,1,0:T(8,128)(2,1)}, u32[]{:S(2)}, u32[]{:S(2)}) %collective-permute-start.4) | collective-permute-done | bytes 589856 | tf_op jit(solution)/shard_map/ppermute | solution.py:772
  47.0 2.9 collective-permute-start.7
  52.3 4.1 %all-to-all-start.1 = ((bf16[4,240,768]{2,1,0:T(8,128)(2,1)}), bf16[4,240,768]{2,1,0:T(8,128)(2,1)S(1)}, u32[]{:S(2)}, u32[]{:S(2)}) async-start(bf16[4,240,768]{2,1,0:T(8,128)(2,1)} %convert_element_type.391), calls=%async_computation.1 | async-start | bytes 2949120 | tf_op jit(solution)/shard_map/all_to_all | solution.py:775
  56.4 1.7 collective-permute-start.5
  58.3 19.5 %attention.1 = (f32[1168,768]{1,0:T(8,128)}, bf16[1168,768]{1,0:T(8,128)(2,1)}, f32[1168,768]{1,0:T(8,128)}, bf16[1,4,768,768]{3,2,1,0:T(8,128)(2,1)}, bf16[4,11...) custom-call(s32[6]{0:T(128)} %pad_add_fusion.1.meta_ref, ...), custom_call_target="tpu_custom_call" | custom-call | flops 17999998976 | bytes 18000000 | tf_op jit(solution)/shard_map/attention/pallas_call | solution.py:691
  80.2 1.9 collective-permute-start.12
  82.6 3.8 collective-permute-start.14
  87.3 20.1 %attention_end.1 = (f32[1168,768]{1,0:T(8,128)}, bf16[1168,768]{1,0:T(8,128)(2,1)}, f32[1,768]{1,0:T(1,128)}, bf16[1,4,768,768]{3,2,1,0:T(8,128)(2,1)}, bf16[4,1...) custom-call(s32[6]{0:T(128)} %pad_add_fusion.1.meta_ref, ...), custom_call_target="tpu_custom_call", output_to_operand_aliasing={{3}: (10, {}), {4}: (11, {}), {5}: (12, {}), {6}: (13, {})} | custom-call | flops 17999998976 | bytes 18000000 | tf_op jit(solution)/shard_map/attention_end/pallas_call | solution.py:691
  109.4 2.0 collective-permute-start.18
  112.8 5.1 %place_grad.1 = (bf16[1024,768]{1,0:T(8,128)(2,1)}, f32[2,768]{1,0:T(2,128)}) custom-call(bf16[960,768]{1,0:T(8,128)(2,1)} %bitcast.219, s32[1,960]{1,0:T(1,128)} %bitcast.233), custom_call_target="tpu_custom_call" | custom-call | flops 5000000000 | bytes 5000000 | tf_op jit(solution)/shard_map/place_grad/pallas_call | solution.py:691
  117.9 6.9 %collective-permute-done.18.refs_3_ = bf16[2,2,96,768]{3,2,1,0:T(8,128)(2,1)} collective-permute-done((bf16[2,2,96,768]{3,2,1,0:T(8,128)(2,1)S(1)}, bf16[2,2,96,768]{3,2,1,0:T(8,128)(2,1)}, u32[]{:S(2)}, u32[]{:S(2)}) %collective-permute-start.18) | collective-permute-done | bytes 589856 | tf_op jit(solution)/shard_map/ppermute | solution.py:772
  130.1 16.8 %lift.1 = (bf16[4,1168,768]{2,1,0:T(8,128)(2,1)}, bf16[4,1168,768]{2,1,0:T(8,128)(2,1)}, bf16[2,4,768,768]{3,2,1,0:T(8,128)(2,1)}) custom-call(s32[2]{0:T(128)} %pad_add_fusion.mine_ref, bf16[1168,768]{1,0:T(8,128)(2,1)} %get-tuple-element.242.feed_ref, bf16[4,2,96,768]{3,2,1,0:T(8,128)(2,1)} %copy-done.14, bf16[4,2,96,768]{3,2,1,0:T(8,128)(2,1)} %copy-done.38, ...), custom_call_target="tpu_custom_call" | custom-call | flops 16000000000 | bytes 16000000 | tf_op jit(solution)/shard_map/lift/pallas_call | solution.py:691
  146.9 8.5 %collective-permute-done.23.refs_1_ = bf16[4,2,96,768]{3,2,1,0:T(8,128)(2,1)S(1)} collective-permute-done((bf16[4,2,96,768]{3,2,1,0:T(8,128)(2,1)S(1)}, bf16[4,2,96,768]{3,2,1,0:T(8,128)(2,1)S(1)}, u32[]{:S(2)}, u32[]{:S(2)}) %collective-permute-start.23) | collective-permute-done | bytes 1179680 | tf_op jit(solution)/shard_map/ppermute | solution.py:772
  158.8 7.4 %drop_weight_grad.2 = bf16[2,8,2,96,768]{4,3,2,1,0:T(8,128)(2,1)} custom-call(s32[2]{0:T(128)} %pad_add_fusion.mine_ref, bf16[1024,768]{1,0:T(8,128)(2,1)} %get-tuple-element.264.grad_ref, bf16[4,1168,768]{2,1,0:T(8,128)(2,1)} %get-tuple-element.306.acted_ref), custom_call_target="tpu_custom_call" | custom-call | flops 7000000000 | bytes 7000000 | tf_op jit(solution)/shard_map/drop_weight_grad/pallas_call | solution.py:691
  166.3 6.3 %collective-permute-done.27.refs_3_ = bf16[2,2,96,768]{3,2,1,0:T(8,128)(2,1)} collective-permute-done((bf16[2,2,96,768]{3,2,1,0:T(8,128)(2,1)S(1)}, bf16[2,2,96,768]{3,2,1,0:T(8,128)(2,1)}, u32[]{:S(2)}, u32[]{:S(2)}) %collective-permute-start.27) | collective-permute-done | bytes 589856 | tf_op jit(solution)/shard_map/ppermute | solution.py:772
  173.4 7.5 %drop_weight_grad.3 = bf16[2,8,2,96,768]{4,3,2,1,0:T(8,128)(2,1)} custom-call(s32[2]{0:T(128)} %pad_add_fusion.mine_ref, bf16[1024,768]{1,0:T(8,128)(2,1)} %get-tuple-element.264.grad_ref, bf16[4,1168,768]{2,1,0:T(8,128)(2,1)} %get-tuple-element.306.acted_ref), custom_call_target="tpu_custom_call" | custom-call | flops 7000000000 | bytes 7000000 | tf_op jit(solution)/shard_map/drop_weight_grad/pallas_call | solution.py:691
  182.6 2.5 fusion.4
  188.5 18.7 %expert_back.1 = (bf16[2,8,2,96,768]{4,3,2,1,0:T(8,128)(2,1)}, bf16[2,4,768,768]{3,2,1,0:T(8,128)(2,1)}, f32[1024,768]{1,0:T(8,128)}) custom-call(s32[2]{0:T(128)} %pad_add_fusion.mine_ref, bf16[1024,768]{1,0:T(8,128)(2,1)} %get-tuple-element.264.grad_ref, bf16[4,1168,768]{2,1,0:T(8,128)(2,1)} %get-tuple-element.265.slope_ref, ...), custom_call_target="tpu_custom_call" | custom-call | flops 16999999488 | bytes 17000000 | tf_op jit(solution)/shard_map/expert_back/pallas_call | solution.py:691
  207.2 2.4 convert_add_fusion.2
  214.4 22.2 %expert_back_end.1 = (bf16[2,8,2,96,768]{4,3,2,1,0:T(8,128)(2,1)}, bf16[2,4,768,768]{3,2,1,0:T(8,128)(2,1)}, f32[1024,768]{1,0:T(8,128)}, bf16[1024,768]{1,0:T(8,128)(2,1)}, f32[2,768]{1,0:T(2,128)}) custom-call(s32[2]{0:T(128)} %pad_add_fusion.mine_ref, bf16[1024,768]{1,0:T(8,128)(2,1)} %get-tuple-element.264.grad_ref, ...), custom_call_target="tpu_custom_call", output_to_operand_aliasing={{1}: (10, {})} | custom-call | flops 16999999488 | bytes 17000000 | tf_op jit(solution)/shard_map/expert_back_end/pallas_call | solution.py:691
  236.7 4.3 %collective-permute-done.38 = bf16[4,2,96,768]{3,2,1,0:T(8,128)(2,1)S(1)} collective-permute-done((bf16[4,2,96,768]{3,2,1,0:T(8,128)(2,1)S(1)}, bf16[4,2,96,768]{3,2,1,0:T(8,128)(2,1)S(1)}, u32[]{:S(2)}, u32[]{:S(2)}) %collective-permute-start.38) | collective-permute-done | bytes 1179680 | tf_op jit(solution)/shard_map/ppermute | solution.py:772
  242.1 1.9 fusion.5
  244.0 2.4 fusion.3
  247.7 4.3 %collective-permute-start.40 = (bf16[2,96,768]{2,1,0:T(8,128)(2,1)S(1)}, bf16[2,96,768]{2,1,0:T(8,128)(2,1)S(1)}, u32[]{:S(2)}, u32[]{:S(2)}) collective-permute-start(bf16[2,96,768]{2,1,0:T(8,128)(2,1)S(1)} %get-tuple-element.530), channel_id=1, source_target_pairs={{0,8},{4,12},{8,0},{12,4},{16,24},{20,28},{24,16},{28,20},{1,9},{5... | collective-permute-start | bytes 884744 | tf_op jit(solution)/shard_map/ppermute | solution.py:772
  254.4 16.7 %drop.1 = (bf16[960,768]{1,0:T(8,128)(2,1)}, f32[2,768]{1,0:T(2,128)}) custom-call(bf16[4,1168,768]{2,1,0:T(8,128)(2,1)} %get-tuple-element.306.acted_ref, f32[1168,768]{1,0:T(8,128)} %get-tuple-element.289.refs_7_.residual_ref, f32[1168,1]{1,0:T(8,128)} %fusion.24.valid_ref, s32[960,1]{1,0:T(8,128)} %copy.124.place_ref, f32[3,768]{1,0:T(4,128)} %extra_ref.3, ...), custom_call_target="tpu_custom_call" | custom-call | flops 16999999488 | bytes 17000000 | tf_op jit(solution)/shard_map/drop/pallas_call | solution.py:691
  271.0 2.9 convert_add_fusion
  278.0 19.0 %attention_back.1 = (bf16[2,8,1,96,768]{4,3,2,1,0:T(8,128)(2,1)}, f32[1024,768]{1,0:T(8,128)}) custom-call(s32[2]{0:T(128)} %pad_add_fusion.mine_ref, bf16[1024,768]{1,0:T(8,128)(2,1)} %get-tuple-element.317.grad_attended_ref, bf16[4,1168,576]{2,1,0:T(8,128)(2,1)} %get-tuple-element.318.joint_ref, bf16[4,1168,192]{2,1,0:T(8,128)(2,1)} %get-tuple-element.319.mixed_ref, ...), custom_call_target="tpu_custom_call" | custom-call | flops 19000000512 | bytes 19000000 | tf_op jit(solution)/shard_map/attention_back/pallas_call | solution.py:691
  297.0 4.6 %collective-permute-done.46 = bf16[4,2,96,768]{3,2,1,0:T(8,128)(2,1)S(1)} collective-permute-done((bf16[4,2,96,768]{3,2,1,0:T(8,128)(2,1)S(1)}, bf16[4,2,96,768]{3,2,1,0:T(8,128)(2,1)S(1)}, u32[]{:S(2)}, u32[]{:S(2)}) %collective-permute-start.46) | collective-permute-done | bytes 1179680 | tf_op jit(solution)/shard_map/ppermute | solution.py:772
  302.8 2.4 fusion.1
  307.2 4.0 collective-permute-start.48
  313.5 3.7 all-to-all-start.2
  317.3 19.4 %attention_back_end.1 = (bf16[2,8,1,96,768]{4,3,2,1,0:T(8,128)(2,1)}, f32[1024,768]{1,0:T(8,128)}) custom-call(s32[2]{0:T(128)} %pad_add_fusion.mine_ref, bf16[1024,768]{1,0:T(8,128)(2,1)} %get-tuple-element.317.grad_attended_ref, bf16[4,1168,576]{2,1,0:T(8,128)(2,1)} %get-tuple-element.318.joint_ref, bf16[4,1168,192]{2,1,0:T(8,128)(2,1)} %get-tuple-element.319.mixed_ref, ...), custom_call_target="tpu_custom_call" | custom-call | flops 19000000512 | bytes 19000000 | tf_op jit(solution)/shard_map/attention_back_end/pallas_call | solution.py:691
  339.6 2.0 collective-permute-start.52
  341.6 10.5 %input_grad.1 = (bf16[960,768]{1,0:T(8,128)(2,1)}, f32[16,768]{1,0:T(8,128)}) custom-call(f32[1024,768]{1,0:T(8,128)} %get-tuple-element.344.grad_normed_ref, f32[1024,768]{1,0:T(8,128)} %get-tuple-element.345.grad_residual_ref, f32[1168,768]{1,0:T(8,128)} %get-tuple-element.221.block_ref, s32[1168,1]{1,0:T(8,128)} %copy.123.hidden_ref, ...), custom_call_target="tpu_custom_call" | custom-call | flops 8999999488 | bytes 9000000 | tf_op jit(solution)/shard_map/input_grad/pallas_call | solution.py:691
  352.1 1.8 convert_element_type.435
  364.1 8.8 %collective-permute-done.56 = f32[16,768]{1,0:T(8,128)} collective-permute-done((f32[16,768]{1,0:T(8,128)}, f32[16,768]{1,0:T(8,128)}, u32[]{:S(2)}, u32[]{:S(2)}) %collective-permute-start.56) | collective-permute-done | bytes 49184 | tf_op jit(solution)/shard_map/ppermute | solution.py:772
  378.3 1.8 collective-permute-start.61
  381.6 3.9 all-to-all-start.3
  386.7 3.3 fusion.60
  392.7 2.7 fusion.62
  402.8 2.5 fusion.54
  407.9 1.8 convert_element_type.441
  (305 shorter events, 89.7 us)
Async XLA Ops:
  9.3 36.2 %all-to-all-start = ((bf16[4,240,768]{2,1,0:T(8,128)(2,1)}), bf16[4,240,768]{2,1,0:T(8,128)(2,1)}, u32[]{:S(2)}, u32[]{:S(2)}) async-start(bf16[4,240,768]{2,1,0:T(8,128)(2,1)} %param.23), calls=%async_computation | async-start | bytes 2949120 | tf_op jit(solution)/shard_map/all_to_all | solution.py:775
  23.9 14.7 %collective-permute-start.3 = (bf16[4,1,96,768]{3,2,1,0:T(8,128)(2,1)}, bf16[4,1,96,768]{3,2,1,0:T(8,128)(2,1)}, u32[]{:S(2)}, u32[]{:S(2)}) collective-permute-start(bf16[4,1,96,768]{3,2,1,0:T(8,128)(2,1)} %pad_maximum_fusion.6.refs_2_), channel_id=1, source_target_pairs={{0,4},{4,0},{8,12},{12,8},{16,20},{20,16},{24,28},{28,24},{1,5},{5... | collective-permute-start | bytes 1769480 | tf_op jit(solution)/shard_map/ppermute | solution.py:772
  25.4 20.1 %collective-permute-start.4 = (bf16[4,1,96,768]{3,2,1,0:T(8,128)(2,1)}, bf16[4,1,96,768]{3,2,1,0:T(8,128)(2,1)}, u32[]{:S(2)}, u32[]{:S(2)}) collective-permute-start(bf16[4,1,96,768]{3,2,1,0:T(8,128)(2,1)} %pad_maximum_fusion.6.refs_2_), channel_id=1, source_target_pairs={{0,2},{1,3},{2,0},{3,1},{4,6},{5,7},{6,4},{7,5},{8,10},{9,11},{10,... | collective-permute-start | bytes 1769480 | tf_op jit(solution)/shard_map/ppermute | solution.py:772
  32.4 24.1 %collective-permute-start.9 = (bf16[4,1,96,768]{3,2,1,0:T(8,128)(2,1)}, bf16[4,1,96,768]{3,2,1,0:T(8,128)(2,1)}, u32[]{:S(2)}, u32[]{:S(2)}) collective-permute-start(bf16[4,1,96,768]{3,2,1,0:T(8,128)(2,1)} %pad_maximum_fusion.6.refs_2_), channel_id=1, source_target_pairs={{0,1},{1,0},{2,3},{3,2},{4,5},{5,4},{6,7},{7,6},{8,9},{9,8},{10,11... | collective-permute-start | bytes 1769480 | tf_op jit(solution)/shard_map/ppermute | solution.py:772
  45.5 32.3 %collective-permute-start.6 = (bf16[2,96,768]{2,1,0:T(8,128)(2,1)}, bf16[2,96,768]{2,1,0:T(8,128)(2,1)}, u32[]{:S(2)}, u32[]{:S(2)}) collective-permute-start(bf16[2,96,768]{2,1,0:T(8,128)(2,1)} %convert_element_type.386), channel_id=1, source_target_pairs={{0,8},{4,12},{8,0},{12,4},{16,24},{20,28},{24,16},{28,20},{1,9},{5... | collective-permute-start | bytes 884744 | tf_op jit(solution)/shard_map/ppermute | solution.py:772
  47.0 30.9 %collective-permute-start.7 = (bf16[2,96,768]{2,1,0:T(8,128)(2,1)}, bf16[2,96,768]{2,1,0:T(8,128)(2,1)}, u32[]{:S(2)}, u32[]{:S(2)}) collective-permute-start(bf16[2,96,768]{2,1,0:T(8,128)(2,1)} %convert_element_type.386), channel_id=1, source_target_pairs={{0,16},{4,20},{8,24},{12,28},{16,0},{20,4},{24,8},{28,12},{1,17},{... | collective-permute-start | bytes 884744 | tf_op jit(solution)/shard_map/ppermute | solution.py:772
  49.9 28.0 %collective-permute-start.8 = (bf16[2,96,768]{2,1,0:T(8,128)(2,1)}, bf16[2,96,768]{2,1,0:T(8,128)(2,1)}, u32[]{:S(2)}, u32[]{:S(2)}) collective-permute-start(bf16[2,96,768]{2,1,0:T(8,128)(2,1)} %convert_element_type.386), channel_id=1, source_target_pairs={{0,24},{4,28},{8,16},{12,20},{16,8},{20,12},{24,0},{28,4},{1,25},{... | collective-permute-start | bytes 884744 | tf_op jit(solution)/shard_map/ppermute | solution.py:772
  52.3 25.7 %all-to-all-start.1 = ((bf16[4,240,768]{2,1,0:T(8,128)(2,1)}), bf16[4,240,768]{2,1,0:T(8,128)(2,1)S(1)}, u32[]{:S(2)}, u32[]{:S(2)}) async-start(bf16[4,240,768]{2,1,0:T(8,128)(2,1)} %convert_element_type.391), calls=%async_computation.1 | async-start | bytes 2949120 | tf_op jit(solution)/shard_map/all_to_all | solution.py:775
  56.4 21.5 %collective-permute-start.5 = (bf16[4,1,96,768]{3,2,1,0:T(8,128)(2,1)}, bf16[4,1,96,768]{3,2,1,0:T(8,128)(2,1)}, u32[]{:S(2)}, u32[]{:S(2)}) collective-permute-start(bf16[4,1,96,768]{3,2,1,0:T(8,128)(2,1)} %collective-permute-done.4.refs_2_), channel_id=1, source_target_pairs={{0,4},{4,0},{8,12},{12,8},{16,20},{20,16},{24,28},{28,24},{1,5},{5... | collective-permute-start | bytes 1769480 | tf_op jit(solution)/shard_map/ppermute | solution.py:772
  58.1 24.5 %collective-permute-start.16 = (bf16[4,1,96,768]{3,2,1,0:T(8,128)(2,1)}, bf16[4,1,96,768]{3,2,1,0:T(8,128)(2,1)}, u32[]{:S(2)}, u32[]{:S(2)}) collective-permute-start(bf16[4,1,96,768]{3,2,1,0:T(8,128)(2,1)} %collective-permute-done.4.refs_2_), channel_id=1, source_target_pairs={{0,1},{1,0},{2,3},{3,2},{4,5},{5,4},{6,7},{7,6},{8,9},{9,8},{10,11... | collective-permute-start | bytes 1769480 | tf_op jit(solution)/shard_map/ppermute | solution.py:772
  79.7 28.3 %collective-permute-start.11 = (bf16[4,2,96,768]{3,2,1,0:T(8,128)(2,1)S(1)}, bf16[4,2,96,768]{3,2,1,0:T(8,128)(2,1)S(1)}, u32[]{:S(2)}, u32[]{:S(2)}) collective-permute-start(bf16[4,2,96,768]{3,2,1,0:T(8,128)(2,1)S(1)} %pad_maximum_fusion.refs_0_), channel_id=1, source_target_pairs={{0,4},{4,0},{8,12},{12,8},{16,20},{20,16},{24,28},{28,24},{1,5},{5... | collective-permute-start | bytes 3538952 | tf_op jit(solution)/shard_map/ppermute | solution.py:772
  80.2 28.2 %collective-permute-start.12 = (bf16[4,2,96,768]{3,2,1,0:T(8,128)(2,1)S(1)}, bf16[4,2,96,768]{3,2,1,0:T(8,128)(2,1)S(1)}, u32[]{:S(2)}, u32[]{:S(2)}) collective-permute-start(bf16[4,2,96,768]{3,2,1,0:T(8,128)(2,1)S(1)} %pad_maximum_fusion.refs_0_), channel_id=1, source_target_pairs={{0,2},{1,3},{2,0},{3,1},{4,6},{5,7},{6,4},{7,5},{8,10},{9,11},{10,... | collective-permute-start | bytes 3538952 | tf_op jit(solution)/shard_map/ppermute | solution.py:772
  82.1 25.3 %collective-permute-start.13 = (bf16[2,96,768]{2,1,0:T(8,128)(2,1)S(1)}, bf16[2,96,768]{2,1,0:T(8,128)(2,1)S(1)}, u32[]{:S(2)}, u32[]{:S(2)}) collective-permute-start(bf16[2,96,768]{2,1,0:T(8,128)(2,1)S(1)} %convert_bitcast_fusion), channel_id=1, source_target_pairs={{0,8},{4,12},{8,0},{12,4},{16,24},{20,28},{24,16},{28,20},{1,9},{5... | collective-permute-start | bytes 884744 | tf_op jit(solution)/shard_map/ppermute | solution.py:772
  82.6 24.9 %collective-permute-start.14 = (bf16[2,96,768]{2,1,0:T(8,128)(2,1)S(1)}, bf16[2,96,768]{2,1,0:T(8,128)(2,1)S(1)}, u32[]{:S(2)}, u32[]{:S(2)}) collective-permute-start(bf16[2,96,768]{2,1,0:T(8,128)(2,1)S(1)} %convert_bitcast_fusion), channel_id=1, source_target_pairs={{0,16},{4,20},{8,24},{12,28},{16,0},{20,4},{24,8},{28,12},{1,17},{... | collective-permute-start | bytes 884744 | tf_op jit(solution)/shard_map/ppermute | solution.py:772
  86.4 21.1 %collective-permute-start.15 = (bf16[2,96,768]{2,1,0:T(8,128)(2,1)S(1)}, bf16[2,96,768]{2,1,0:T(8,128)(2,1)S(1)}, u32[]{:S(2)}, u32[]{:S(2)}) collective-permute-start(bf16[2,96,768]{2,1,0:T(8,128)(2,1)S(1)} %convert_bitcast_fusion), channel_id=1, source_target_pairs={{0,24},{4,28},{8,16},{12,20},{16,8},{20,12},{24,0},{28,4},{1,25},{... | collective-permute-start | bytes 884744 | tf_op jit(solution)/shard_map/ppermute | solution.py:772
  108.4 17.7 %collective-permute-start.21 = (bf16[4,2,96,768]{3,2,1,0:T(8,128)(2,1)S(1)}, bf16[4,2,96,768]{3,2,1,0:T(8,128)(2,1)}, u32[]{:S(2)}, u32[]{:S(2)}) collective-permute-start(bf16[4,2,96,768]{3,2,1,0:T(8,128)(2,1)S(1)} %collective-permute-done.11.refs_1_), channel_id=1, source_target_pairs={{0,1},{1,0},{2,3},{3,2},{4,5},{5,4},{6,7},{7,6},{8,9},{9,8},{10,11... | collective-permute-start | bytes 3538952 | tf_op jit(solution)/shard_map/ppermute | solution.py:772
  108.4 17.7 %collective-permute-start.22 = (bf16[4,2,96,768]{3,2,1,0:T(8,128)(2,1)S(1)}, bf16[4,2,96,768]{3,2,1,0:T(8,128)(2,1)}, u32[]{:S(2)}, u32[]{:S(2)}) collective-permute-start(bf16[4,2,96,768]{3,2,1,0:T(8,128)(2,1)S(1)} %collective-permute-done.12.refs_2_), channel_id=1, source_target_pairs={{0,1},{1,0},{2,3},{3,2},{4,5},{5,4},{6,7},{7,6},{8,9},{9,8},{10,11... | collective-permute-start | bytes 3538952 | tf_op jit(solution)/shard_map/ppermute | solution.py:772
  109.4 15.3 %collective-permute-start.18 = (bf16[2,2,96,768]{3,2,1,0:T(8,128)(2,1)S(1)}, bf16[2,2,96,768]{3,2,1,0:T(8,128)(2,1)}, u32[]{:S(2)}, u32[]{:S(2)}) collective-permute-start(bf16[2,2,96,768]{3,2,1,0:T(8,128)(2,1)S(1)} %slice.267), channel_id=1, source_target_pairs={{0,2},{1,3},{2,0},{3,1},{4,6},{5,7},{6,4},{7,5},{8,10},{9,11},{10,... | collective-permute-start | bytes 1769480 | tf_op jit(solution)/shard_map/ppermute | solution.py:772
  127.4 28.0 %collective-permute-start.23 = (bf16[4,2,96,768]{3,2,1,0:T(8,128)(2,1)S(1)}, bf16[4,2,96,768]{3,2,1,0:T(8,128)(2,1)S(1)}, u32[]{:S(2)}, u32[]{:S(2)}) collective-permute-start(bf16[4,2,96,768]{3,2,1,0:T(8,128)(2,1)S(1)} %pad_maximum_fusion.1.refs_0_), channel_id=1, source_target_pairs={{0,4},{4,0},{8,12},{12,8},{16,20},{20,16},{24,28},{28,24},{1,5},{5... | collective-permute-start | bytes 3538952 | tf_op jit(solution)/shard_map/ppermute | solution.py:772
  128.9 27.7 %collective-permute-start.24 = (bf16[4,2,96,768]{3,2,1,0:T(8,128)(2,1)S(1)}, bf16[4,2,96,768]{3,2,1,0:T(8,128)(2,1)S(1)}, u32[]{:S(2)}, u32[]{:S(2)}) collective-permute-start(bf16[4,2,96,768]{3,2,1,0:T(8,128)(2,1)S(1)} %pad_maximum_fusion.1.refs_0_), channel_id=1, source_target_pairs={{0,2},{1,3},{2,0},{3,1},{4,6},{5,7},{6,4},{7,5},{8,10},{9,11},{10,... | collective-permute-start | bytes 3538952 | tf_op jit(solution)/shard_map/ppermute | solution.py:772
  129.3 37.0 %collective-permute-start.29 = (bf16[4,2,96,768]{3,2,1,0:T(8,128)(2,1)S(1)}, bf16[4,2,96,768]{3,2,1,0:T(8,128)(2,1)S(1)}, u32[]{:S(2)}, u32[]{:S(2)}) collective-permute-start(bf16[4,2,96,768]{3,2,1,0:T(8,128)(2,1)S(1)} %pad_maximum_fusion.1.refs_0_), channel_id=1, source_target_pairs={{0,1},{1,0},{2,3},{3,2},{4,5},{5,4},{6,7},{7,6},{8,9},{9,8},{10,11... | collective-permute-start | bytes 3538952 | tf_op jit(solution)/shard_map/ppermute | solution.py:772
  156.5 16.2 %collective-permute-start.30 = (bf16[4,2,96,768]{3,2,1,0:T(8,128)(2,1)S(1)}, bf16[4,2,96,768]{3,2,1,0:T(8,128)(2,1)}, u32[]{:S(2)}, u32[]{:S(2)}) collective-permute-start(bf16[4,2,96,768]{3,2,1,0:T(8,128)(2,1)S(1)} %collective-permute-done.23.refs_1_), channel_id=1, source_target_pairs={{0,1},{1,0},{2,3},{3,2},{4,5},{5,4},{6,7},{7,6},{8,9},{9,8},{10,11... | collective-permute-start | bytes 3538952 | tf_op jit(solution)/shard_map/ppermute | solution.py:772
  156.5 16.2 %collective-permute-start.31 = (bf16[4,2,96,768]{3,2,1,0:T(8,128)(2,1)S(1)}, bf16[4,2,96,768]{3,2,1,0:T(8,128)(2,1)}, u32[]{:S(2)}, u32[]{:S(2)}) collective-permute-start(bf16[4,2,96,768]{3,2,1,0:T(8,128)(2,1)S(1)} %collective-permute-done.24.refs_2_), channel_id=1, source_target_pairs={{0,1},{1,0},{2,3},{3,2},{4,5},{5,4},{6,7},{7,6},{8,9},{9,8},{10,11... | collective-permute-start | bytes 3538952 | tf_op jit(solution)/shard_map/ppermute | solution.py:772
  157.6 14.9 %collective-permute-start.27 = (bf16[2,2,96,768]{3,2,1,0:T(8,128)(2,1)S(1)}, bf16[2,2,96,768]{3,2,1,0:T(8,128)(2,1)}, u32[]{:S(2)}, u32[]{:S(2)}) collective-permute-start(bf16[2,2,96,768]{3,2,1,0:T(8,128)(2,1)S(1)} %slice.269), channel_id=1, source_target_pairs={{0,2},{1,3},{2,0},{3,1},{4,6},{5,7},{6,4},{7,5},{8,10},{9,11},{10,... | collective-permute-start | bytes 1769480 | tf_op jit(solution)/shard_map/ppermute | solution.py:772
  186.3 20.9 %collective-permute-start.35 = (bf16[2,2,96,768]{3,2,1,0:T(8,128)(2,1)}, bf16[2,2,96,768]{3,2,1,0:T(8,128)(2,1)S(1)}, u32[]{:S(2)}, u32[]{:S(2)}) collective-permute-start(bf16[2,2,96,768]{3,2,1,0:T(8,128)(2,1)} %get-tuple-element.532), channel_id=1, source_target_pairs={{0,4},{4,0},{8,12},{12,8},{16,20},{20,16},{24,28},{28,24},{1,5},{5... | collective-permute-start | bytes 1769480 | tf_op jit(solution)/shard_map/ppermute | solution.py:772
  186.9 20.3 %collective-permute-start.36 = (bf16[2,2,96,768]{3,2,1,0:T(8,128)(2,1)}, bf16[2,2,96,768]{3,2,1,0:T(8,128)(2,1)S(1)}, u32[]{:S(2)}, u32[]{:S(2)}) collective-permute-start(bf16[2,2,96,768]{3,2,1,0:T(8,128)(2,1)} %get-tuple-element.531), channel_id=1, source_target_pairs={{0,2},{1,3},{2,0},{3,1},{4,6},{5,7},{6,4},{7,5},{8,10},{9,11},{10,... | collective-permute-start | bytes 1769480 | tf_op jit(solution)/shard_map/ppermute | solution.py:772
  210.3 31.8 %collective-permute-start.37 = (bf16[2,8,2,96,768]{4,3,2,1,0:T(8,128)(2,1)}, bf16[2,8,2,96,768]{4,3,2,1,0:T(8,128)(2,1)}, u32[]{:S(2)}, u32[]{:S(2)}) collective-permute-start(bf16[2,8,2,96,768]{4,3,2,1,0:T(8,128)(2,1)} %get-tuple-element.291), channel_id=1, source_target_pairs={{0,1},{1,0},{2,3},{3,2},{4,5},{5,4},{6,7},{7,6},{8,9},{9,8},{10,11... | collective-permute-start | bytes 14155784 | tf_op jit(solution)/shard_map/ppermute | solution.py:772
  212.6 28.4 %collective-permute-start.38 = (bf16[4,2,96,768]{3,2,1,0:T(8,128)(2,1)S(1)}, bf16[4,2,96,768]{3,2,1,0:T(8,128)(2,1)S(1)}, u32[]{:S(2)}, u32[]{:S(2)}) collective-permute-start(bf16[4,2,96,768]{3,2,1,0:T(8,128)(2,1)S(1)} %pad_maximum_fusion.2), channel_id=1, source_target_pairs={{0,4},{4,0},{8,12},{12,8},{16,20},{20,16},{24,28},{28,24},{1,5},{5... | collective-permute-start | bytes 3538952 | tf_op jit(solution)/shard_map/ppermute | solution.py:772
  214.0 28.1 %collective-permute-start.39 = (bf16[4,2,96,768]{3,2,1,0:T(8,128)(2,1)S(1)}, bf16[4,2,96,768]{3,2,1,0:T(8,128)(2,1)S(1)}, u32[]{:S(2)}, u32[]{:S(2)}) collective-permute-start(bf16[4,2,96,768]{3,2,1,0:T(8,128)(2,1)S(1)} %pad_maximum_fusion.3), channel_id=1, source_target_pairs={{0,2},{1,3},{2,0},{3,1},{4,6},{5,7},{6,4},{7,5},{8,10},{9,11},{10,... | collective-permute-start | bytes 3538952 | tf_op jit(solution)/shard_map/ppermute | solution.py:772
  246.5 24.5 %collective-permute-start.43 = (bf16[2,2,96,768]{3,2,1,0:T(8,128)(2,1)S(1)}, bf16[2,2,96,768]{3,2,1,0:T(8,128)(2,1)S(1)}, u32[]{:S(2)}, u32[]{:S(2)}) collective-permute-start(bf16[2,2,96,768]{3,2,1,0:T(8,128)(2,1)S(1)} %get-tuple-element.527), channel_id=1, source_target_pairs={{0,4},{4,0},{8,12},{12,8},{16,20},{20,16},{24,28},{28,24},{1,5},{5... | collective-permute-start | bytes 1769480 | tf_op jit(solution)/shard_map/ppermute | solution.py:772
  247.2 23.8 %collective-permute-start.44 = (bf16[2,2,96,768]{3,2,1,0:T(8,128)(2,1)S(1)}, bf16[2,2,96,768]{3,2,1,0:T(8,128)(2,1)S(1)}, u32[]{:S(2)}, u32[]{:S(2)}) collective-permute-start(bf16[2,2,96,768]{3,2,1,0:T(8,128)(2,1)S(1)} %get-tuple-element.526), channel_id=1, source_target_pairs={{0,2},{1,3},{2,0},{3,1},{4,6},{5,7},{6,4},{7,5},{8,10},{9,11},{10,... | collective-permute-start | bytes 1769480 | tf_op jit(solution)/shard_map/ppermute | solution.py:772
  247.7 27.0 %collective-permute-start.40 = (bf16[2,96,768]{2,1,0:T(8,128)(2,1)S(1)}, bf16[2,96,768]{2,1,0:T(8,128)(2,1)S(1)}, u32[]{:S(2)}, u32[]{:S(2)}) collective-permute-start(bf16[2,96,768]{2,1,0:T(8,128)(2,1)S(1)} %get-tuple-element.530), channel_id=1, source_target_pairs={{0,8},{4,12},{8,0},{12,4},{16,24},{20,28},{24,16},{28,20},{1,9},{5... | collective-permute-start | bytes 884744 | tf_op jit(solution)/shard_map/ppermute | solution.py:772
  251.9 23.5 %collective-permute-start.41 = (bf16[2,96,768]{2,1,0:T(8,128)(2,1)S(1)}, bf16[2,96,768]{2,1,0:T(8,128)(2,1)S(1)}, u32[]{:S(2)}, u32[]{:S(2)}) collective-permute-start(bf16[2,96,768]{2,1,0:T(8,128)(2,1)S(1)} %get-tuple-element.529), channel_id=1, source_target_pairs={{0,16},{4,20},{8,24},{12,28},{16,0},{20,4},{24,8},{28,12},{1,17},{... | collective-permute-start | bytes 884744 | tf_op jit(solution)/shard_map/ppermute | solution.py:772
  252.9 23.2 %collective-permute-start.42 = (bf16[2,96,768]{2,1,0:T(8,128)(2,1)S(1)}, bf16[2,96,768]{2,1,0:T(8,128)(2,1)}, u32[]{:S(2)}, u32[]{:S(2)}) collective-permute-start(bf16[2,96,768]{2,1,0:T(8,128)(2,1)S(1)} %get-tuple-element.528), channel_id=1, source_target_pairs={{0,24},{4,28},{8,16},{12,20},{16,8},{20,12},{24,0},{28,4},{1,25},{... | collective-permute-start | bytes 884744 | tf_op jit(solution)/shard_map/ppermute | solution.py:772
  276.1 25.5 %collective-permute-start.46 = (bf16[4,2,96,768]{3,2,1,0:T(8,128)(2,1)S(1)}, bf16[4,2,96,768]{3,2,1,0:T(8,128)(2,1)S(1)}, u32[]{:S(2)}, u32[]{:S(2)}) collective-permute-start(bf16[4,2,96,768]{3,2,1,0:T(8,128)(2,1)S(1)} %pad_maximum_fusion.4), channel_id=1, source_target_pairs={{0,4},{4,0},{8,12},{12,8},{16,20},{20,16},{24,28},{28,24},{1,5},{5... | collective-permute-start | bytes 3538952 | tf_op jit(solution)/shard_map/ppermute | solution.py:772
  277.6 25.2 %collective-permute-start.47 = (bf16[4,2,96,768]{3,2,1,0:T(8,128)(2,1)S(1)}, bf16[4,2,96,768]{3,2,1,0:T(8,128)(2,1)S(1)}, u32[]{:S(2)}, u32[]{:S(2)}) collective-permute-start(bf16[4,2,96,768]{3,2,1,0:T(8,128)(2,1)S(1)} %pad_maximum_fusion.5), channel_id=1, source_target_pairs={{0,2},{1,3},{2,0},{3,1},{4,6},{5,7},{6,4},{7,5},{8,10},{9,11},{10,... | collective-permute-start | bytes 3538952 | tf_op jit(solution)/shard_map/ppermute | solution.py:772
  297.0 39.7 %collective-permute-start.45 = (bf16[2,8,1,96,768]{4,3,2,1,0:T(8,128)(2,1)}, bf16[2,8,1,96,768]{4,3,2,1,0:T(8,128)(2,1)}, u32[]{:S(2)}, u32[]{:S(2)}) collective-permute-start(bf16[2,8,1,96,768]{4,3,2,1,0:T(8,128)(2,1)} %get-tuple-element.322), channel_id=1, source_target_pairs={{0,1},{1,0},{2,3},{3,2},{4,5},{5,4},{6,7},{7,6},{8,9},{9,8},{10,11... | collective-permute-start | bytes 7077896 | tf_op jit(solution)/shard_map/ppermute | solution.py:772
  307.2 29.4 %collective-permute-start.48 = (bf16[2,96,768]{2,1,0:T(8,128)(2,1)}, bf16[2,96,768]{2,1,0:T(8,128)(2,1)S(1)}, u32[]{:S(2)}, u32[]{:S(2)}) collective-permute-start(bf16[2,96,768]{2,1,0:T(8,128)(2,1)} %get-tuple-element.525), channel_id=1, source_target_pairs={{0,8},{4,12},{8,0},{12,4},{16,24},{20,28},{24,16},{28,20},{1,9},{5... | collective-permute-start | bytes 884744 | tf_op jit(solution)/shard_map/ppermute | solution.py:772
  311.2 25.5 %collective-permute-start.49 = (bf16[2,96,768]{2,1,0:T(8,128)(2,1)}, bf16[2,96,768]{2,1,0:T(8,128)(2,1)S(1)}, u32[]{:S(2)}, u32[]{:S(2)}) collective-permute-start(bf16[2,96,768]{2,1,0:T(8,128)(2,1)} %get-tuple-element.524), channel_id=1, source_target_pairs={{0,16},{4,20},{8,24},{12,28},{16,0},{20,4},{24,8},{28,12},{1,17},{... | collective-permute-start | bytes 884744 | tf_op jit(solution)/shard_map/ppermute | solution.py:772
  312.1 24.6 %collective-permute-start.50 = (bf16[2,96,768]{2,1,0:T(8,128)(2,1)}, bf16[2,96,768]{2,1,0:T(8,128)(2,1)S(1)}, u32[]{:S(2)}, u32[]{:S(2)}) collective-permute-start(bf16[2,96,768]{2,1,0:T(8,128)(2,1)} %get-tuple-element.523), channel_id=1, source_target_pairs={{0,24},{4,28},{8,16},{12,20},{16,8},{20,12},{24,0},{28,4},{1,25},{... | collective-permute-start | bytes 884744 | tf_op jit(solution)/shard_map/ppermute | solution.py:772
  313.5 25.3 %all-to-all-start.2 = ((bf16[4,240,768]{2,1,0:T(8,128)(2,1)}), bf16[4,240,768]{2,1,0:T(8,128)(2,1)S(1)}, u32[]{:S(2)}, u32[]{:S(2)}) async-start(bf16[4,240,768]{2,1,0:T(8,128)(2,1)} %bitcast.220), calls=%async_computation.2 | async-start | bytes 2949120 | tf_op jit(solution)/shard_map/all_to_all | solution.py:778
  338.9 15.1 %collective-permute-start.51 = (bf16[2,1,96,768]{3,2,1,0:T(8,128)(2,1)S(1)}, bf16[2,1,96,768]{3,2,1,0:T(8,128)(2,1)S(1)}, u32[]{:S(2)}, u32[]{:S(2)}) collective-permute-start(bf16[2,1,96,768]{3,2,1,0:T(8,128)(2,1)S(1)} %get-tuple-element.537), channel_id=1, source_target_pairs={{0,4},{4,0},{8,12},{12,8},{16,20},{20,16},{24,28},{28,24},{1,5},{5... | collective-permute-start | bytes 884744 | tf_op jit(solution)/shard_map/ppermute | solution.py:772
  356.8 17.5 %collective-permute-start.53 = (bf16[4,1,96,768]{3,2,1,0:T(8,128)(2,1)S(1)}, bf16[4,1,96,768]{3,2,1,0:T(8,128)(2,1)S(1)}, u32[]{:S(2)}, u32[]{:S(2)}) collective-permute-start(bf16[4,1,96,768]{3,2,1,0:T(8,128)(2,1)S(1)} %pad_maximum_fusion.7), channel_id=1, source_target_pairs={{0,4},{4,0},{8,12},{12,8},{16,20},{20,16},{24,28},{28,24},{1,5},{5... | collective-permute-start | bytes 1769480 | tf_op jit(solution)/shard_map/ppermute | solution.py:772
  358.3 16.1 %collective-permute-start.54 = (bf16[4,1,96,768]{3,2,1,0:T(8,128)(2,1)S(1)}, bf16[4,1,96,768]{3,2,1,0:T(8,128)(2,1)S(1)}, u32[]{:S(2)}, u32[]{:S(2)}) collective-permute-start(bf16[4,1,96,768]{3,2,1,0:T(8,128)(2,1)S(1)} %pad_maximum_fusion.8), channel_id=1, source_target_pairs={{0,2},{1,3},{2,0},{3,1},{4,6},{5,7},{6,4},{7,5},{8,10},{9,11},{10,... | collective-permute-start | bytes 1769480 | tf_op jit(solution)/shard_map/ppermute | solution.py:772
  377.2 20.0 %collective-permute-start.60 = (bf16[1,96,768]{2,1,0:T(8,128)(2,1)}, bf16[1,96,768]{2,1,0:T(8,128)(2,1)}, u32[]{:S(2)}, u32[]{:S(2)}) collective-permute-start(bf16[1,96,768]{2,1,0:T(8,128)(2,1)} %get-tuple-element.533), channel_id=1, source_target_pairs={{0,8},{4,12},{8,0},{12,4},{16,24},{20,28},{24,16},{28,20},{1,9},{5... | collective-permute-start | bytes 442376 | tf_op jit(solution)/shard_map/ppermute | solution.py:772
  378.3 18.9 %collective-permute-start.61 = (bf16[1,96,768]{2,1,0:T(8,128)(2,1)}, bf16[1,96,768]{2,1,0:T(8,128)(2,1)}, u32[]{:S(2)}, u32[]{:S(2)}) collective-permute-start(bf16[1,96,768]{2,1,0:T(8,128)(2,1)} %get-tuple-element.535), channel_id=1, source_target_pairs={{0,16},{4,20},{8,24},{12,28},{16,0},{20,4},{24,8},{28,12},{1,17},{... | collective-permute-start | bytes 442376 | tf_op jit(solution)/shard_map/ppermute | solution.py:772
  380.1 17.1 %collective-permute-start.62 = (bf16[1,96,768]{2,1,0:T(8,128)(2,1)}, bf16[1,96,768]{2,1,0:T(8,128)(2,1)}, u32[]{:S(2)}, u32[]{:S(2)}) collective-permute-start(bf16[1,96,768]{2,1,0:T(8,128)(2,1)} %get-tuple-element.534), channel_id=1, source_target_pairs={{0,24},{4,28},{8,16},{12,20},{16,8},{20,12},{24,0},{28,4},{1,25},{... | collective-permute-start | bytes 442376 | tf_op jit(solution)/shard_map/ppermute | solution.py:772
  381.6 26.4 %all-to-all-start.3 = ((bf16[4,240,768]{2,1,0:T(8,128)(2,1)}), bf16[4,240,768]{2,1,0:T(8,128)(2,1)S(1)}, u32[]{:S(2)}, u32[]{:S(2)}) async-start(bf16[4,240,768]{2,1,0:T(8,128)(2,1)} %bitcast.218), calls=%async_computation.3 | async-start | bytes 2949120 | tf_op jit(solution)/shard_map/all_to_all | solution.py:778
  (76 other events, 602.1 us)

commit v6 on v5

--- a/solution.py
+++ b/solution.py
@@ -390,24 +390,27 @@
     *refs,
 ):
     small_refs, (grad_raw_ref, small_ref, grad_block_ref) = refs[:-3], refs[-3:]
-    small_ref[...] = jnp.zeros_like(small_ref)
-    first = 3
-    for ref in small_refs:
-        small_ref[first : first + ref.shape[0], :] = ref[...]
-        first += ref.shape[0]
-
-    def chunk(i):
-        rows = rows_at(i, ITEM_ROWS)
-        grad, gain, shift = norm_backward(block_ref[rows, :], norm_ref[0:1, :], grad_normed_ref[rows, :])
-        small_ref[0:1, :] += gain
-        small_ref[1:2, :] += shift
-        grad = grad + grad_residual_ref[rows, :]
-        hidden = hidden_ref[rows, :] > 0
-        small_ref[2:3, :] += jnp.sum(jnp.where(hidden, grad, 0.0), axis=0, keepdims=True)
-        grad_block_ref[rows, :] = jnp.where(hidden, 0.0, grad).astype(bf16)
-
-    loop(grad_normed_ref.shape[0] // ITEM_ROWS, chunk)
-    unplace(place_ref, grad_block_ref, grad_raw_ref, grad_block_ref.shape[0])
+    step = pl.program_id(0)
+
+    @pl.when(step == 0)
+    def _():
+        small_ref[...] = jnp.zeros_like(small_ref)
+        first = 3
+        for ref in small_refs:
+            small_ref[first : first + ref.shape[0], :] = ref[...]
+            first += ref.shape[0]
+
+    grad, gain, shift = norm_backward(block_ref[...], norm_ref[0:1, :], grad_normed_ref[...])
+    small_ref[0:1, :] += gain
+    small_ref[1:2, :] += shift
+    grad = grad + grad_residual_ref[...]
+    hidden = hidden_ref[...] > 0
+    small_ref[2:3, :] += jnp.sum(jnp.where(hidden, grad, 0.0), axis=0, keepdims=True)
+    grad_block_ref[rows_at(step, ITEM_ROWS), :] = jnp.where(hidden, 0.0, grad).astype(bf16)
+
+    @pl.when(step == pl.num_programs(0) - 1)
+    def _():
+        unplace(place_ref, grad_block_ref, grad_raw_ref, grad_block_ref.shape[0])
 
 
 def heads_back(
@@ -1070,12 +1073,12 @@
         return call(
             input_grad_kernel,
             "input_grad",
-            1,
+            main_rows // ITEM_ROWS,
             [
-                plain(grad_normed),
-                plain(grad_residual),
-                (block_input, whole(main_rows, model_width)),
-                (hidden, whole(main_rows, 1)),
+                (grad_normed, stepped(ITEM_ROWS, model_width)),
+                (grad_residual, stepped(ITEM_ROWS, model_width)),
+                (block_input, stepped(ITEM_ROWS, model_width)),
+                (hidden, stepped(ITEM_ROWS, 1)),
                 plain(place_column),
                 plain(norm_params),
             ]
@@ -1198,13 +1201,12 @@
     block_output = give_back(raw_out)
     attend_keep, grad_normed = attention_back_end(grad_normed, grad_attended, normed, *made)
     if cube:
-        attend_received, from_lift_line, attend_keep = together(
-            attend_received, from_lift_line, attend_keep
+        attend_received, from_lift_line, block_output, attend_keep = together(
+            attend_received, from_lift_line, block_output, attend_keep
         )
         corner = scatter_corner(attend_keep, attend_received)
-        corner, block_output, grad_normed = together(corner, block_output, grad_normed)
+        corner, grad_normed = together(corner, grad_normed)
         from_corner = send_corner(corner)
-    block_output = block_output.astype(f32)
     grad_raw, small = finish_input_grad(
         grad_normed,
         grad_residual,
@@ -1214,18 +1216,21 @@
     if cube:
         from_corner, small, grad_raw = together(from_corner, small, grad_raw)
         plane = scatter_plane(attend_keep, attend_received, *from_corner)
-        plane, small, grad_raw, block_output = together(plane, small, grad_raw, block_output)
+        plane, small, grad_raw = together(plane, small, grad_raw)
         from_plane = send_plane(*plane)
         for axis, bit in (("mp", 1), ("dp", 1)):
             small = small + swap(small, axis, bit)
         line = scatter_line(attend_keep, attend_received, *from_plane)
-        line, small, grad_raw, drop_line, lift_line = together(line, small, grad_raw, drop_line, lift_line)
+        line, small, grad_raw, drop_line, lift_line, block_output = together(
+            line, small, grad_raw, drop_line, lift_line, block_output
+        )
         attend_grad = add(line[0], *send_line(line))[0]
         drop_grad = add(drop_line[0], *from_drop_line)
         lift_grad = add(lift_line[0], *from_lift_line)
     else:
         attend_grad = scatter(attend_keep, attend_send)[0]
     input_grad = give_back(grad_raw).astype(f32)
+    block_output = block_output.astype(f32)
 
     if cube:
         for axis, bit in (("mp", 2), ("dp", 2), ("dp", 4)):

time: 414 us -> 411 us (level)
    unnamed x121 -> x127, local copies, waits for them, and re-layouts: 14.5 us -> 10.3 us
  transfers between devices with their start and end apart: 67 -> 67, of which waited for: 22 -> 21; matrix products, arithmetic and copies ran while one was open for 12% -> 11% of each run, Pallas kernels for 45% -> 45%
where the time goes in v6:
time: 411 us; the launch traced here: 407 us
  Pallas kernels  182 us (44%)
  starting transfers between devices  78.6 us (19%)
  waiting for transfers between devices  70.7 us (17%)
  other arithmetic  53 us (13%)
  local copies, waits for them, and re-layouts  18.8 us (5%)
    pallas_call x12, Pallas kernels, call(): pl.pallas_call(kernel, name=name, grid_spec=pltpu.PrefetchScalarGridSpec(...  182 us
    ppermute x63, waiting for transfers between devices, swap(): return lax.ppermute(values, axis, [(i, i ^ bit) for i in range(size)])  70.7 us
    ppermute x63, starting transfers between devices, swap(): return lax.ppermute(values, axis, [(i, i ^ bit) for i in range(size)])  62.4 us
    unnamed x127, local copies, waits for them, and re-layouts  10.3 us
    all_to_all x2, starting transfers between devices, exchange(): lax.all_to_all(values, 'mp', split_axis=0, concat_axis=1, tiled=True)[0]  8.67 us
    convert_element_type x6, other arithmetic, adamw(): return (weight_new, first_new, second_new, weight_new.astype(bf16))  8.63 us
  transfers between devices with their start and end apart: 67, of which 21 were waited for; matrix products, arithmetic and copies ran while one was open for 11% of the time, Pallas kernels for 45%

profile of v6, /device:TPU:0, one launch (start us, length us, event | category | flops | bytes accessed | tf_op | source)
XLA Modules:
  0.0 407.1 jit_solution(9418886246483046271)
XLA Ops:
  3.5 5.1 %collective-permute-start.2 = (bf16[1,96,768]{2,1,0:T(8,128)(2,1)S(1)}, bf16[1,96,768]{2,1,0:T(8,128)(2,1)S(1)}, u32[]{:S(2)}, u32[]{:S(2)}) collective-permute-start(bf16[1,96,768]{2,1,0:T(8,128)(2,1)S(1)} %pad_maximum_fusion.10), channel_id=1, source_target_pairs={{0,24},{4,28},{8,16},{12,20},{16,8},{20,12},{24,0},{28,4},{1,25},{... | collective-permute-start | bytes 442376 | tf_op jit(solution)/shard_map/ppermute | solution.py:775
  9.3 4.5 %all-to-all-start = ((bf16[4,240,768]{2,1,0:T(8,128)(2,1)}), bf16[4,240,768]{2,1,0:T(8,128)(2,1)}, u32[]{:S(2)}, u32[]{:S(2)}) async-start(bf16[4,240,768]{2,1,0:T(8,128)(2,1)} %param.23), calls=%async_computation | async-start | bytes 2949120 | tf_op jit(solution)/shard_map/all_to_all | solution.py:778
  16.8 4.3 %collective-permute-done.1 = bf16[1,96,768]{2,1,0:T(8,128)(2,1)S(1)} collective-permute-done((bf16[1,96,768]{2,1,0:T(8,128)(2,1)S(1)}, bf16[1,96,768]{2,1,0:T(8,128)(2,1)S(1)}, u32[]{:S(2)}, u32[]{:S(2)}) %collective-permute-start.1) | collective-permute-done | bytes 147488 | tf_op jit(solution)/shard_map/ppermute | solution.py:775
  21.8 2.1 pad_maximum_fusion.6.refs_2_
  30.5 1.9 fusion.24.valid_ref
  32.4 6.3 %collective-permute-done.3.refs_3_ = bf16[4,1,96,768]{3,2,1,0:T(8,128)(2,1)} collective-permute-done((bf16[4,1,96,768]{3,2,1,0:T(8,128)(2,1)}, bf16[4,1,96,768]{3,2,1,0:T(8,128)(2,1)}, u32[]{:S(2)}, u32[]{:S(2)}) %collective-permute-start.3) | collective-permute-done | bytes 589856 | tf_op jit(solution)/shard_map/ppermute | solution.py:775
  38.6 6.9 %collective-permute-done.4.refs_2_ = bf16[4,1,96,768]{3,2,1,0:T(8,128)(2,1)} collective-permute-done((bf16[4,1,96,768]{3,2,1,0:T(8,128)(2,1)}, bf16[4,1,96,768]{3,2,1,0:T(8,128)(2,1)}, u32[]{:S(2)}, u32[]{:S(2)}) %collective-permute-start.4) | collective-permute-done | bytes 589856 | tf_op jit(solution)/shard_map/ppermute | solution.py:775
  47.0 2.9 collective-permute-start.7
  52.3 4.1 %all-to-all-start.1 = ((bf16[4,240,768]{2,1,0:T(8,128)(2,1)}), bf16[4,240,768]{2,1,0:T(8,128)(2,1)S(1)}, u32[]{:S(2)}, u32[]{:S(2)}) async-start(bf16[4,240,768]{2,1,0:T(8,128)(2,1)} %convert_element_type.391), calls=%async_computation.1 | async-start | bytes 2949120 | tf_op jit(solution)/shard_map/all_to_all | solution.py:778
  58.4 19.5 %attention.1 = (f32[1168,768]{1,0:T(8,128)}, bf16[1168,768]{1,0:T(8,128)(2,1)}, f32[1168,768]{1,0:T(8,128)}, bf16[1,4,768,768]{3,2,1,0:T(8,128)(2,1)}, bf16[4,11...) custom-call(s32[6]{0:T(128)} %pad_add_fusion.1.meta_ref, ...), custom_call_target="tpu_custom_call" | custom-call | flops 17999998976 | bytes 18000000 | tf_op jit(solution)/shard_map/attention/pallas_call | solution.py:694
  80.2 1.9 collective-permute-start.12
  82.7 3.8 collective-permute-start.14
  87.3 20.1 %attention_end.1 = (f32[1168,768]{1,0:T(8,128)}, bf16[1168,768]{1,0:T(8,128)(2,1)}, f32[1,768]{1,0:T(1,128)}, bf16[1,4,768,768]{3,2,1,0:T(8,128)(2,1)}, bf16[4,1...) custom-call(s32[6]{0:T(128)} %pad_add_fusion.1.meta_ref, ...), custom_call_target="tpu_custom_call", output_to_operand_aliasing={{3}: (10, {}), {4}: (11, {}), {5}: (12, {}), {6}: (13, {})} | custom-call | flops 17999998976 | bytes 18000000 | tf_op jit(solution)/shard_map/attention_end/pallas_call | solution.py:694
  109.5 2.0 collective-permute-start.18
  112.9 5.0 %place_grad.1 = (bf16[1024,768]{1,0:T(8,128)(2,1)}, f32[2,768]{1,0:T(2,128)}) custom-call(bf16[960,768]{1,0:T(8,128)(2,1)} %bitcast.221, s32[1,960]{1,0:T(1,128)} %bitcast.234), custom_call_target="tpu_custom_call" | custom-call | flops 5000000000 | bytes 5000000 | tf_op jit(solution)/shard_map/place_grad/pallas_call | solution.py:694
  117.9 6.9 %collective-permute-done.18.refs_3_ = bf16[2,2,96,768]{3,2,1,0:T(8,128)(2,1)} collective-permute-done((bf16[2,2,96,768]{3,2,1,0:T(8,128)(2,1)S(1)}, bf16[2,2,96,768]{3,2,1,0:T(8,128)(2,1)}, u32[]{:S(2)}, u32[]{:S(2)}) %collective-permute-start.18) | collective-permute-done | bytes 589856 | tf_op jit(solution)/shard_map/ppermute | solution.py:775
  130.2 16.8 %lift.1 = (bf16[4,1168,768]{2,1,0:T(8,128)(2,1)}, bf16[4,1168,768]{2,1,0:T(8,128)(2,1)}, bf16[2,4,768,768]{3,2,1,0:T(8,128)(2,1)}) custom-call(s32[2]{0:T(128)} %pad_add_fusion.mine_ref, bf16[1168,768]{1,0:T(8,128)(2,1)} %get-tuple-element.242.feed_ref, bf16[4,2,96,768]{3,2,1,0:T(8,128)(2,1)} %copy-done.15, bf16[4,2,96,768]{3,2,1,0:T(8,128)(2,1)} %copy-done.37, ...), custom_call_target="tpu_custom_call" | custom-call | flops 16000000000 | bytes 16000000 | tf_op jit(solution)/shard_map/lift/pallas_call | solution.py:694
  147.0 8.5 %collective-permute-done.23.refs_1_ = bf16[4,2,96,768]{3,2,1,0:T(8,128)(2,1)S(1)} collective-permute-done((bf16[4,2,96,768]{3,2,1,0:T(8,128)(2,1)S(1)}, bf16[4,2,96,768]{3,2,1,0:T(8,128)(2,1)S(1)}, u32[]{:S(2)}, u32[]{:S(2)}) %collective-permute-start.23) | collective-permute-done | bytes 1179680 | tf_op jit(solution)/shard_map/ppermute | solution.py:775
  158.9 7.4 %drop_weight_grad.2 = bf16[2,8,2,96,768]{4,3,2,1,0:T(8,128)(2,1)} custom-call(s32[2]{0:T(128)} %pad_add_fusion.mine_ref, bf16[1024,768]{1,0:T(8,128)(2,1)} %get-tuple-element.264.grad_ref, bf16[4,1168,768]{2,1,0:T(8,128)(2,1)} %get-tuple-element.306.acted_ref), custom_call_target="tpu_custom_call" | custom-call | flops 7000000000 | bytes 7000000 | tf_op jit(solution)/shard_map/drop_weight_grad/pallas_call | solution.py:694
  166.3 6.3 %collective-permute-done.27.refs_3_ = bf16[2,2,96,768]{3,2,1,0:T(8,128)(2,1)} collective-permute-done((bf16[2,2,96,768]{3,2,1,0:T(8,128)(2,1)S(1)}, bf16[2,2,96,768]{3,2,1,0:T(8,128)(2,1)}, u32[]{:S(2)}, u32[]{:S(2)}) %collective-permute-start.27) | collective-permute-done | bytes 589856 | tf_op jit(solution)/shard_map/ppermute | solution.py:775
  173.4 7.4 %drop_weight_grad.3 = bf16[2,8,2,96,768]{4,3,2,1,0:T(8,128)(2,1)} custom-call(s32[2]{0:T(128)} %pad_add_fusion.mine_ref, bf16[1024,768]{1,0:T(8,128)(2,1)} %get-tuple-element.264.grad_ref, bf16[4,1168,768]{2,1,0:T(8,128)(2,1)} %get-tuple-element.306.acted_ref), custom_call_target="tpu_custom_call" | custom-call | flops 7000000000 | bytes 7000000 | tf_op jit(solution)/shard_map/drop_weight_grad/pallas_call | solution.py:694
  182.7 2.5 fusion.4
  188.5 18.7 %expert_back.1 = (bf16[2,8,2,96,768]{4,3,2,1,0:T(8,128)(2,1)}, bf16[2,4,768,768]{3,2,1,0:T(8,128)(2,1)}, f32[1024,768]{1,0:T(8,128)}) custom-call(s32[2]{0:T(128)} %pad_add_fusion.mine_ref, bf16[1024,768]{1,0:T(8,128)(2,1)} %get-tuple-element.264.grad_ref, bf16[4,1168,768]{2,1,0:T(8,128)(2,1)} %get-tuple-element.265.slope_ref, ...), custom_call_target="tpu_custom_call" | custom-call | flops 16999999488 | bytes 17000000 | tf_op jit(solution)/shard_map/expert_back/pallas_call | solution.py:694
  207.3 2.4 convert_add_fusion.2
  214.5 22.2 %expert_back_end.1 = (bf16[2,8,2,96,768]{4,3,2,1,0:T(8,128)(2,1)}, bf16[2,4,768,768]{3,2,1,0:T(8,128)(2,1)}, f32[1024,768]{1,0:T(8,128)}, bf16[1024,768]{1,0:T(8,128)(2,1)}, f32[2,768]{1,0:T(2,128)}) custom-call(s32[2]{0:T(128)} %pad_add_fusion.mine_ref, bf16[1024,768]{1,0:T(8,128)(2,1)} %get-tuple-element.264.grad_ref, ...), custom_call_target="tpu_custom_call", output_to_operand_aliasing={{1}: (10, {})} | custom-call | flops 16999999488 | bytes 17000000 | tf_op jit(solution)/shard_map/expert_back_end/pallas_call | solution.py:694
  236.7 4.3 %collective-permute-done.38 = bf16[4,2,96,768]{3,2,1,0:T(8,128)(2,1)S(1)} collective-permute-done((bf16[4,2,96,768]{3,2,1,0:T(8,128)(2,1)S(1)}, bf16[4,2,96,768]{3,2,1,0:T(8,128)(2,1)S(1)}, u32[]{:S(2)}, u32[]{:S(2)}) %collective-permute-start.38) | collective-permute-done | bytes 1179680 | tf_op jit(solution)/shard_map/ppermute | solution.py:775
  242.1 1.9 fusion.5
  244.1 2.4 fusion.3
  249.6 4.2 %collective-permute-start.40 = (bf16[2,96,768]{2,1,0:T(8,128)(2,1)}, bf16[2,96,768]{2,1,0:T(8,128)(2,1)S(1)}, u32[]{:S(2)}, u32[]{:S(2)}) collective-permute-start(bf16[2,96,768]{2,1,0:T(8,128)(2,1)} %get-tuple-element.530), channel_id=1, source_target_pairs={{0,8},{4,12},{8,0},{12,4},{16,24},{20,28},{24,16},{28,20},{1,9},{5... | collective-permute-start | bytes 884744 | tf_op jit(solution)/shard_map/ppermute | solution.py:775
  256.1 16.8 %drop.1 = (bf16[960,768]{1,0:T(8,128)(2,1)}, f32[2,768]{1,0:T(2,128)}) custom-call(bf16[4,1168,768]{2,1,0:T(8,128)(2,1)} %get-tuple-element.306.acted_ref, f32[1168,768]{1,0:T(8,128)} %get-tuple-element.289.refs_7_.residual_ref, f32[1168,1]{1,0:T(8,128)} %fusion.24.valid_ref, s32[960,1]{1,0:T(8,128)} %copy.124.place_ref, f32[3,768]{1,0:T(4,128)} %extra_ref.3, ...), custom_call_target="tpu_custom_call" | custom-call | flops 16999999488 | bytes 17000000 | tf_op jit(solution)/shard_map/drop/pallas_call | solution.py:694
  273.0 2.4 convert_add_fusion
  279.5 18.9 %attention_back.1 = (bf16[2,8,1,96,768]{4,3,2,1,0:T(8,128)(2,1)}, f32[1024,768]{1,0:T(8,128)}) custom-call(s32[2]{0:T(128)} %pad_add_fusion.mine_ref, bf16[1024,768]{1,0:T(8,128)(2,1)} %get-tuple-element.317.grad_attended_ref, bf16[4,1168,576]{2,1,0:T(8,128)(2,1)} %get-tuple-element.318.joint_ref, bf16[4,1168,192]{2,1,0:T(8,128)(2,1)} %get-tuple-element.319.mixed_ref, ...), custom_call_target="tpu_custom_call" | custom-call | flops 19000000512 | bytes 19000000 | tf_op jit(solution)/shard_map/attention_back/pallas_call | solution.py:694
  298.5 5.2 %collective-permute-done.46 = bf16[4,2,96,768]{3,2,1,0:T(8,128)(2,1)} collective-permute-done((bf16[4,2,96,768]{3,2,1,0:T(8,128)(2,1)}, bf16[4,2,96,768]{3,2,1,0:T(8,128)(2,1)}, u32[]{:S(2)}, u32[]{:S(2)}) %collective-permute-start.46) | collective-permute-done | bytes 1179680 | tf_op jit(solution)/shard_map/ppermute | solution.py:775
  304.6 2.7 fusion.1
  308.4 4.4 %collective-permute-start.48 = (bf16[2,96,768]{2,1,0:T(8,128)(2,1)S(1)}, bf16[2,96,768]{2,1,0:T(8,128)(2,1)S(1)}, u32[]{:S(2)}, u32[]{:S(2)}) collective-permute-start(bf16[2,96,768]{2,1,0:T(8,128)(2,1)S(1)} %get-tuple-element.525), channel_id=1, source_target_pairs={{0,8},{4,12},{8,0},{12,4},{16,24},{20,28},{24,16},{28,20},{1,9},{5... | collective-permute-start | bytes 884744 | tf_op jit(solution)/shard_map/ppermute | solution.py:775
  315.2 3.7 all-to-all-start.2
  318.9 19.3 %attention_back_end.1 = (bf16[2,8,1,96,768]{4,3,2,1,0:T(8,128)(2,1)}, f32[1024,768]{1,0:T(8,128)}) custom-call(s32[2]{0:T(128)} %pad_add_fusion.mine_ref, bf16[1024,768]{1,0:T(8,128)(2,1)} %get-tuple-element.317.grad_attended_ref, bf16[4,1168,576]{2,1,0:T(8,128)(2,1)} %get-tuple-element.318.joint_ref, bf16[4,1168,192]{2,1,0:T(8,128)(2,1)} %get-tuple-element.319.mixed_ref, ...), custom_call_target="tpu_custom_call" | custom-call | flops 19000000512 | bytes 19000000 | tf_op jit(solution)/shard_map/attention_back_end/pallas_call | solution.py:694
  340.8 2.0 collective-permute-start.52
  342.8 9.5 %input_grad.1 = (bf16[960,768]{1,0:T(8,128)(2,1)}, f32[16,768]{1,0:T(8,128)}) custom-call(f32[1024,768]{1,0:T(8,128)} %get-tuple-element.344.grad_normed_ref, f32[1024,768]{1,0:T(8,128)} %get-tuple-element.345.grad_residual_ref, f32[1168,768]{1,0:T(8,128)} %get-tuple-element.221.block_ref, s32[1168,1]{1,0:T(8,128)} %copy.123.hidden_ref, ...), custom_call_target="tpu_custom_call" | custom-call | flops 8999999488 | bytes 9000000 | tf_op jit(solution)/shard_map/input_grad/pallas_call | solution.py:694
  359.3 11.0 %collective-permute-done.56 = f32[16,768]{1,0:T(8,128)S(1)} collective-permute-done((f32[16,768]{1,0:T(8,128)S(1)}, f32[16,768]{1,0:T(8,128)S(1)}, u32[]{:S(2)}, u32[]{:S(2)}) %collective-permute-start.56) | collective-permute-done | bytes 49184 | tf_op jit(solution)/shard_map/ppermute | solution.py:775
  370.9 1.8 fusion.15
  375.0 1.9 collective-permute-start.61
  378.3 3.9 all-to-all-start.3
  383.4 3.4 fusion.60
  389.6 2.7 fusion.62
  392.2 1.8 convert_element_type.440
  399.9 2.5 fusion.54
  405.0 1.8 convert_element_type.441
  (312 shorter events, 84.5 us)
Async XLA Ops:
  9.3 36.3 %all-to-all-start = ((bf16[4,240,768]{2,1,0:T(8,128)(2,1)}), bf16[4,240,768]{2,1,0:T(8,128)(2,1)}, u32[]{:S(2)}, u32[]{:S(2)}) async-start(bf16[4,240,768]{2,1,0:T(8,128)(2,1)} %param.23), calls=%async_computation | async-start | bytes 2949120 | tf_op jit(solution)/shard_map/all_to_all | solution.py:778
  23.9 14.7 %collective-permute-start.3 = (bf16[4,1,96,768]{3,2,1,0:T(8,128)(2,1)}, bf16[4,1,96,768]{3,2,1,0:T(8,128)(2,1)}, u32[]{:S(2)}, u32[]{:S(2)}) collective-permute-start(bf16[4,1,96,768]{3,2,1,0:T(8,128)(2,1)} %pad_maximum_fusion.6.refs_2_), channel_id=1, source_target_pairs={{0,4},{4,0},{8,12},{12,8},{16,20},{20,16},{24,28},{28,24},{1,5},{5... | collective-permute-start | bytes 1769480 | tf_op jit(solution)/shard_map/ppermute | solution.py:775
  25.4 20.1 %collective-permute-start.4 = (bf16[4,1,96,768]{3,2,1,0:T(8,128)(2,1)}, bf16[4,1,96,768]{3,2,1,0:T(8,128)(2,1)}, u32[]{:S(2)}, u32[]{:S(2)}) collective-permute-start(bf16[4,1,96,768]{3,2,1,0:T(8,128)(2,1)} %pad_maximum_fusion.6.refs_2_), channel_id=1, source_target_pairs={{0,2},{1,3},{2,0},{3,1},{4,6},{5,7},{6,4},{7,5},{8,10},{9,11},{10,... | collective-permute-start | bytes 1769480 | tf_op jit(solution)/shard_map/ppermute | solution.py:775
  32.4 24.1 %collective-permute-start.9 = (bf16[4,1,96,768]{3,2,1,0:T(8,128)(2,1)}, bf16[4,1,96,768]{3,2,1,0:T(8,128)(2,1)}, u32[]{:S(2)}, u32[]{:S(2)}) collective-permute-start(bf16[4,1,96,768]{3,2,1,0:T(8,128)(2,1)} %pad_maximum_fusion.6.refs_2_), channel_id=1, source_target_pairs={{0,1},{1,0},{2,3},{3,2},{4,5},{5,4},{6,7},{7,6},{8,9},{9,8},{10,11... | collective-permute-start | bytes 1769480 | tf_op jit(solution)/shard_map/ppermute | solution.py:775
  45.6 32.4 %collective-permute-start.6 = (bf16[2,96,768]{2,1,0:T(8,128)(2,1)}, bf16[2,96,768]{2,1,0:T(8,128)(2,1)}, u32[]{:S(2)}, u32[]{:S(2)}) collective-permute-start(bf16[2,96,768]{2,1,0:T(8,128)(2,1)} %convert_element_type.386), channel_id=1, source_target_pairs={{0,8},{4,12},{8,0},{12,4},{16,24},{20,28},{24,16},{28,20},{1,9},{5... | collective-permute-start | bytes 884744 | tf_op jit(solution)/shard_map/ppermute | solution.py:775
  47.0 31.0 %collective-permute-start.7 = (bf16[2,96,768]{2,1,0:T(8,128)(2,1)}, bf16[2,96,768]{2,1,0:T(8,128)(2,1)}, u32[]{:S(2)}, u32[]{:S(2)}) collective-permute-start(bf16[2,96,768]{2,1,0:T(8,128)(2,1)} %convert_element_type.386), channel_id=1, source_target_pairs={{0,16},{4,20},{8,24},{12,28},{16,0},{20,4},{24,8},{28,12},{1,17},{... | collective-permute-start | bytes 884744 | tf_op jit(solution)/shard_map/ppermute | solution.py:775
  49.9 28.1 %collective-permute-start.8 = (bf16[2,96,768]{2,1,0:T(8,128)(2,1)}, bf16[2,96,768]{2,1,0:T(8,128)(2,1)}, u32[]{:S(2)}, u32[]{:S(2)}) collective-permute-start(bf16[2,96,768]{2,1,0:T(8,128)(2,1)} %convert_element_type.386), channel_id=1, source_target_pairs={{0,24},{4,28},{8,16},{12,20},{16,8},{20,12},{24,0},{28,4},{1,25},{... | collective-permute-start | bytes 884744 | tf_op jit(solution)/shard_map/ppermute | solution.py:775
  52.3 25.7 %all-to-all-start.1 = ((bf16[4,240,768]{2,1,0:T(8,128)(2,1)}), bf16[4,240,768]{2,1,0:T(8,128)(2,1)S(1)}, u32[]{:S(2)}, u32[]{:S(2)}) async-start(bf16[4,240,768]{2,1,0:T(8,128)(2,1)} %convert_element_type.391), calls=%async_computation.1 | async-start | bytes 2949120 | tf_op jit(solution)/shard_map/all_to_all | solution.py:778
  56.5 21.5 %collective-permute-start.5 = (bf16[4,1,96,768]{3,2,1,0:T(8,128)(2,1)}, bf16[4,1,96,768]{3,2,1,0:T(8,128)(2,1)}, u32[]{:S(2)}, u32[]{:S(2)}) collective-permute-start(bf16[4,1,96,768]{3,2,1,0:T(8,128)(2,1)} %collective-permute-done.4.refs_2_), channel_id=1, source_target_pairs={{0,4},{4,0},{8,12},{12,8},{16,20},{20,16},{24,28},{28,24},{1,5},{5... | collective-permute-start | bytes 1769480 | tf_op jit(solution)/shard_map/ppermute | solution.py:775
  58.2 24.5 %collective-permute-start.16 = (bf16[4,1,96,768]{3,2,1,0:T(8,128)(2,1)}, bf16[4,1,96,768]{3,2,1,0:T(8,128)(2,1)}, u32[]{:S(2)}, u32[]{:S(2)}) collective-permute-start(bf16[4,1,96,768]{3,2,1,0:T(8,128)(2,1)} %collective-permute-done.4.refs_2_), channel_id=1, source_target_pairs={{0,1},{1,0},{2,3},{3,2},{4,5},{5,4},{6,7},{7,6},{8,9},{9,8},{10,11... | collective-permute-start | bytes 1769480 | tf_op jit(solution)/shard_map/ppermute | solution.py:775
  79.8 28.3 %collective-permute-start.11 = (bf16[4,2,96,768]{3,2,1,0:T(8,128)(2,1)S(1)}, bf16[4,2,96,768]{3,2,1,0:T(8,128)(2,1)S(1)}, u32[]{:S(2)}, u32[]{:S(2)}) collective-permute-start(bf16[4,2,96,768]{3,2,1,0:T(8,128)(2,1)S(1)} %pad_maximum_fusion.refs_0_), channel_id=1, source_target_pairs={{0,4},{4,0},{8,12},{12,8},{16,20},{20,16},{24,28},{28,24},{1,5},{5... | collective-permute-start | bytes 3538952 | tf_op jit(solution)/shard_map/ppermute | solution.py:775
  80.2 28.2 %collective-permute-start.12 = (bf16[4,2,96,768]{3,2,1,0:T(8,128)(2,1)S(1)}, bf16[4,2,96,768]{3,2,1,0:T(8,128)(2,1)S(1)}, u32[]{:S(2)}, u32[]{:S(2)}) collective-permute-start(bf16[4,2,96,768]{3,2,1,0:T(8,128)(2,1)S(1)} %pad_maximum_fusion.refs_0_), channel_id=1, source_target_pairs={{0,2},{1,3},{2,0},{3,1},{4,6},{5,7},{6,4},{7,5},{8,10},{9,11},{10,... | collective-permute-start | bytes 3538952 | tf_op jit(solution)/shard_map/ppermute | solution.py:775
  82.2 25.3 %collective-permute-start.13 = (bf16[2,96,768]{2,1,0:T(8,128)(2,1)S(1)}, bf16[2,96,768]{2,1,0:T(8,128)(2,1)S(1)}, u32[]{:S(2)}, u32[]{:S(2)}) collective-permute-start(bf16[2,96,768]{2,1,0:T(8,128)(2,1)S(1)} %convert_bitcast_fusion), channel_id=1, source_target_pairs={{0,8},{4,12},{8,0},{12,4},{16,24},{20,28},{24,16},{28,20},{1,9},{5... | collective-permute-start | bytes 884744 | tf_op jit(solution)/shard_map/ppermute | solution.py:775
  82.7 24.9 %collective-permute-start.14 = (bf16[2,96,768]{2,1,0:T(8,128)(2,1)S(1)}, bf16[2,96,768]{2,1,0:T(8,128)(2,1)S(1)}, u32[]{:S(2)}, u32[]{:S(2)}) collective-permute-start(bf16[2,96,768]{2,1,0:T(8,128)(2,1)S(1)} %convert_bitcast_fusion), channel_id=1, source_target_pairs={{0,16},{4,20},{8,24},{12,28},{16,0},{20,4},{24,8},{28,12},{1,17},{... | collective-permute-start | bytes 884744 | tf_op jit(solution)/shard_map/ppermute | solution.py:775
  86.5 21.1 %collective-permute-start.15 = (bf16[2,96,768]{2,1,0:T(8,128)(2,1)S(1)}, bf16[2,96,768]{2,1,0:T(8,128)(2,1)S(1)}, u32[]{:S(2)}, u32[]{:S(2)}) collective-permute-start(bf16[2,96,768]{2,1,0:T(8,128)(2,1)S(1)} %convert_bitcast_fusion), channel_id=1, source_target_pairs={{0,24},{4,28},{8,16},{12,20},{16,8},{20,12},{24,0},{28,4},{1,25},{... | collective-permute-start | bytes 884744 | tf_op jit(solution)/shard_map/ppermute | solution.py:775
  108.5 17.7 %collective-permute-start.21 = (bf16[4,2,96,768]{3,2,1,0:T(8,128)(2,1)S(1)}, bf16[4,2,96,768]{3,2,1,0:T(8,128)(2,1)}, u32[]{:S(2)}, u32[]{:S(2)}) collective-permute-start(bf16[4,2,96,768]{3,2,1,0:T(8,128)(2,1)S(1)} %collective-permute-done.11.refs_1_), channel_id=1, source_target_pairs={{0,1},{1,0},{2,3},{3,2},{4,5},{5,4},{6,7},{7,6},{8,9},{9,8},{10,11... | collective-permute-start | bytes 3538952 | tf_op jit(solution)/shard_map/ppermute | solution.py:775
  108.5 17.7 %collective-permute-start.22 = (bf16[4,2,96,768]{3,2,1,0:T(8,128)(2,1)S(1)}, bf16[4,2,96,768]{3,2,1,0:T(8,128)(2,1)}, u32[]{:S(2)}, u32[]{:S(2)}) collective-permute-start(bf16[4,2,96,768]{3,2,1,0:T(8,128)(2,1)S(1)} %collective-permute-done.12.refs_2_), channel_id=1, source_target_pairs={{0,1},{1,0},{2,3},{3,2},{4,5},{5,4},{6,7},{7,6},{8,9},{9,8},{10,11... | collective-permute-start | bytes 3538952 | tf_op jit(solution)/shard_map/ppermute | solution.py:775
  109.5 15.3 %collective-permute-start.18 = (bf16[2,2,96,768]{3,2,1,0:T(8,128)(2,1)S(1)}, bf16[2,2,96,768]{3,2,1,0:T(8,128)(2,1)}, u32[]{:S(2)}, u32[]{:S(2)}) collective-permute-start(bf16[2,2,96,768]{3,2,1,0:T(8,128)(2,1)S(1)} %slice.267), channel_id=1, source_target_pairs={{0,2},{1,3},{2,0},{3,1},{4,6},{5,7},{6,4},{7,5},{8,10},{9,11},{10,... | collective-permute-start | bytes 1769480 | tf_op jit(solution)/shard_map/ppermute | solution.py:775
  111.5 14.7 %collective-permute-start.19 = (bf16[2,2,96,768]{3,2,1,0:T(8,128)(2,1)S(1)}, bf16[2,2,96,768]{3,2,1,0:T(8,128)(2,1)}, u32[]{:S(2)}, u32[]{:S(2)}) collective-permute-start(bf16[2,2,96,768]{3,2,1,0:T(8,128)(2,1)S(1)} %slice.268), channel_id=1, source_target_pairs={{0,4},{4,0},{8,12},{12,8},{16,20},{20,16},{24,28},{28,24},{1,5},{5... | collective-permute-start | bytes 1769480 | tf_op jit(solution)/shard_map/ppermute | solution.py:775
  127.5 28.0 %collective-permute-start.23 = (bf16[4,2,96,768]{3,2,1,0:T(8,128)(2,1)S(1)}, bf16[4,2,96,768]{3,2,1,0:T(8,128)(2,1)S(1)}, u32[]{:S(2)}, u32[]{:S(2)}) collective-permute-start(bf16[4,2,96,768]{3,2,1,0:T(8,128)(2,1)S(1)} %pad_maximum_fusion.1.refs_0_), channel_id=1, source_target_pairs={{0,4},{4,0},{8,12},{12,8},{16,20},{20,16},{24,28},{28,24},{1,5},{5... | collective-permute-start | bytes 3538952 | tf_op jit(solution)/shard_map/ppermute | solution.py:775
  128.9 27.7 %collective-permute-start.24 = (bf16[4,2,96,768]{3,2,1,0:T(8,128)(2,1)S(1)}, bf16[4,2,96,768]{3,2,1,0:T(8,128)(2,1)S(1)}, u32[]{:S(2)}, u32[]{:S(2)}) collective-permute-start(bf16[4,2,96,768]{3,2,1,0:T(8,128)(2,1)S(1)} %pad_maximum_fusion.1.refs_0_), channel_id=1, source_target_pairs={{0,2},{1,3},{2,0},{3,1},{4,6},{5,7},{6,4},{7,5},{8,10},{9,11},{10,... | collective-permute-start | bytes 3538952 | tf_op jit(solution)/shard_map/ppermute | solution.py:775
  129.4 36.9 %collective-permute-start.29 = (bf16[4,2,96,768]{3,2,1,0:T(8,128)(2,1)S(1)}, bf16[4,2,96,768]{3,2,1,0:T(8,128)(2,1)S(1)}, u32[]{:S(2)}, u32[]{:S(2)}) collective-permute-start(bf16[4,2,96,768]{3,2,1,0:T(8,128)(2,1)S(1)} %pad_maximum_fusion.1.refs_0_), channel_id=1, source_target_pairs={{0,1},{1,0},{2,3},{3,2},{4,5},{5,4},{6,7},{7,6},{8,9},{9,8},{10,11... | collective-permute-start | bytes 3538952 | tf_op jit(solution)/shard_map/ppermute | solution.py:775
  156.6 16.2 %collective-permute-start.30 = (bf16[4,2,96,768]{3,2,1,0:T(8,128)(2,1)S(1)}, bf16[4,2,96,768]{3,2,1,0:T(8,128)(2,1)}, u32[]{:S(2)}, u32[]{:S(2)}) collective-permute-start(bf16[4,2,96,768]{3,2,1,0:T(8,128)(2,1)S(1)} %collective-permute-done.23.refs_1_), channel_id=1, source_target_pairs={{0,1},{1,0},{2,3},{3,2},{4,5},{5,4},{6,7},{7,6},{8,9},{9,8},{10,11... | collective-permute-start | bytes 3538952 | tf_op jit(solution)/shard_map/ppermute | solution.py:775
  156.6 16.2 %collective-permute-start.31 = (bf16[4,2,96,768]{3,2,1,0:T(8,128)(2,1)S(1)}, bf16[4,2,96,768]{3,2,1,0:T(8,128)(2,1)}, u32[]{:S(2)}, u32[]{:S(2)}) collective-permute-start(bf16[4,2,96,768]{3,2,1,0:T(8,128)(2,1)S(1)} %collective-permute-done.24.refs_2_), channel_id=1, source_target_pairs={{0,1},{1,0},{2,3},{3,2},{4,5},{5,4},{6,7},{7,6},{8,9},{9,8},{10,11... | collective-permute-start | bytes 3538952 | tf_op jit(solution)/shard_map/ppermute | solution.py:775
  157.6 15.0 %collective-permute-start.27 = (bf16[2,2,96,768]{3,2,1,0:T(8,128)(2,1)S(1)}, bf16[2,2,96,768]{3,2,1,0:T(8,128)(2,1)}, u32[]{:S(2)}, u32[]{:S(2)}) collective-permute-start(bf16[2,2,96,768]{3,2,1,0:T(8,128)(2,1)S(1)} %slice.269), channel_id=1, source_target_pairs={{0,2},{1,3},{2,0},{3,1},{4,6},{5,7},{6,4},{7,5},{8,10},{9,11},{10,... | collective-permute-start | bytes 1769480 | tf_op jit(solution)/shard_map/ppermute | solution.py:775
  186.3 20.9 %collective-permute-start.35 = (bf16[2,2,96,768]{3,2,1,0:T(8,128)(2,1)}, bf16[2,2,96,768]{3,2,1,0:T(8,128)(2,1)S(1)}, u32[]{:S(2)}, u32[]{:S(2)}) collective-permute-start(bf16[2,2,96,768]{3,2,1,0:T(8,128)(2,1)} %get-tuple-element.532), channel_id=1, source_target_pairs={{0,4},{4,0},{8,12},{12,8},{16,20},{20,16},{24,28},{28,24},{1,5},{5... | collective-permute-start | bytes 1769480 | tf_op jit(solution)/shard_map/ppermute | solution.py:775
  186.9 20.3 %collective-permute-start.36 = (bf16[2,2,96,768]{3,2,1,0:T(8,128)(2,1)}, bf16[2,2,96,768]{3,2,1,0:T(8,128)(2,1)S(1)}, u32[]{:S(2)}, u32[]{:S(2)}) collective-permute-start(bf16[2,2,96,768]{3,2,1,0:T(8,128)(2,1)} %get-tuple-element.531), channel_id=1, source_target_pairs={{0,2},{1,3},{2,0},{3,1},{4,6},{5,7},{6,4},{7,5},{8,10},{9,11},{10,... | collective-permute-start | bytes 1769480 | tf_op jit(solution)/shard_map/ppermute | solution.py:775
  210.3 31.8 %collective-permute-start.37 = (bf16[2,8,2,96,768]{4,3,2,1,0:T(8,128)(2,1)}, bf16[2,8,2,96,768]{4,3,2,1,0:T(8,128)(2,1)}, u32[]{:S(2)}, u32[]{:S(2)}) collective-permute-start(bf16[2,8,2,96,768]{4,3,2,1,0:T(8,128)(2,1)} %get-tuple-element.291), channel_id=1, source_target_pairs={{0,1},{1,0},{2,3},{3,2},{4,5},{5,4},{6,7},{7,6},{8,9},{9,8},{10,11... | collective-permute-start | bytes 14155784 | tf_op jit(solution)/shard_map/ppermute | solution.py:775
  212.7 28.4 %collective-permute-start.38 = (bf16[4,2,96,768]{3,2,1,0:T(8,128)(2,1)S(1)}, bf16[4,2,96,768]{3,2,1,0:T(8,128)(2,1)S(1)}, u32[]{:S(2)}, u32[]{:S(2)}) collective-permute-start(bf16[4,2,96,768]{3,2,1,0:T(8,128)(2,1)S(1)} %pad_maximum_fusion.2), channel_id=1, source_target_pairs={{0,4},{4,0},{8,12},{12,8},{16,20},{20,16},{24,28},{28,24},{1,5},{5... | collective-permute-start | bytes 3538952 | tf_op jit(solution)/shard_map/ppermute | solution.py:775
  214.1 28.1 %collective-permute-start.39 = (bf16[4,2,96,768]{3,2,1,0:T(8,128)(2,1)S(1)}, bf16[4,2,96,768]{3,2,1,0:T(8,128)(2,1)S(1)}, u32[]{:S(2)}, u32[]{:S(2)}) collective-permute-start(bf16[4,2,96,768]{3,2,1,0:T(8,128)(2,1)S(1)} %pad_maximum_fusion.3), channel_id=1, source_target_pairs={{0,2},{1,3},{2,0},{3,1},{4,6},{5,7},{6,4},{7,5},{8,10},{9,11},{10,... | collective-permute-start | bytes 3538952 | tf_op jit(solution)/shard_map/ppermute | solution.py:775
  247.6 25.3 %collective-permute-start.43 = (bf16[2,2,96,768]{3,2,1,0:T(8,128)(2,1)}, bf16[2,2,96,768]{3,2,1,0:T(8,128)(2,1)S(1)}, u32[]{:S(2)}, u32[]{:S(2)}) collective-permute-start(bf16[2,2,96,768]{3,2,1,0:T(8,128)(2,1)} %get-tuple-element.527), channel_id=1, source_target_pairs={{0,4},{4,0},{8,12},{12,8},{16,20},{20,16},{24,28},{28,24},{1,5},{5... | collective-permute-start | bytes 1769480 | tf_op jit(solution)/shard_map/ppermute | solution.py:775
  248.3 24.7 %collective-permute-start.44 = (bf16[2,2,96,768]{3,2,1,0:T(8,128)(2,1)}, bf16[2,2,96,768]{3,2,1,0:T(8,128)(2,1)S(1)}, u32[]{:S(2)}, u32[]{:S(2)}) collective-permute-start(bf16[2,2,96,768]{3,2,1,0:T(8,128)(2,1)} %get-tuple-element.526), channel_id=1, source_target_pairs={{0,2},{1,3},{2,0},{3,1},{4,6},{5,7},{6,4},{7,5},{8,10},{9,11},{10,... | collective-permute-start | bytes 1769480 | tf_op jit(solution)/shard_map/ppermute | solution.py:775
  249.6 27.5 %collective-permute-start.40 = (bf16[2,96,768]{2,1,0:T(8,128)(2,1)}, bf16[2,96,768]{2,1,0:T(8,128)(2,1)S(1)}, u32[]{:S(2)}, u32[]{:S(2)}) collective-permute-start(bf16[2,96,768]{2,1,0:T(8,128)(2,1)} %get-tuple-element.530), channel_id=1, source_target_pairs={{0,8},{4,12},{8,0},{12,4},{16,24},{20,28},{24,16},{28,20},{1,9},{5... | collective-permute-start | bytes 884744 | tf_op jit(solution)/shard_map/ppermute | solution.py:775
  253.8 23.8 %collective-permute-start.41 = (bf16[2,96,768]{2,1,0:T(8,128)(2,1)}, bf16[2,96,768]{2,1,0:T(8,128)(2,1)}, u32[]{:S(2)}, u32[]{:S(2)}) collective-permute-start(bf16[2,96,768]{2,1,0:T(8,128)(2,1)} %get-tuple-element.529), channel_id=1, source_target_pairs={{0,16},{4,20},{8,24},{12,28},{16,0},{20,4},{24,8},{28,12},{1,17},{... | collective-permute-start | bytes 884744 | tf_op jit(solution)/shard_map/ppermute | solution.py:775
  254.7 22.9 %collective-permute-start.42 = (bf16[2,96,768]{2,1,0:T(8,128)(2,1)}, bf16[2,96,768]{2,1,0:T(8,128)(2,1)}, u32[]{:S(2)}, u32[]{:S(2)}) collective-permute-start(bf16[2,96,768]{2,1,0:T(8,128)(2,1)} %get-tuple-element.528), channel_id=1, source_target_pairs={{0,24},{4,28},{8,16},{12,20},{16,8},{20,12},{24,0},{28,4},{1,25},{... | collective-permute-start | bytes 884744 | tf_op jit(solution)/shard_map/ppermute | solution.py:775
  277.6 26.1 %collective-permute-start.46 = (bf16[4,2,96,768]{3,2,1,0:T(8,128)(2,1)}, bf16[4,2,96,768]{3,2,1,0:T(8,128)(2,1)}, u32[]{:S(2)}, u32[]{:S(2)}) collective-permute-start(bf16[4,2,96,768]{3,2,1,0:T(8,128)(2,1)} %pad_maximum_fusion.4), channel_id=1, source_target_pairs={{0,4},{4,0},{8,12},{12,8},{16,20},{20,16},{24,28},{28,24},{1,5},{5... | collective-permute-start | bytes 3538952 | tf_op jit(solution)/shard_map/ppermute | solution.py:775
  279.1 25.5 %collective-permute-start.47 = (bf16[4,2,96,768]{3,2,1,0:T(8,128)(2,1)S(1)}, bf16[4,2,96,768]{3,2,1,0:T(8,128)(2,1)}, u32[]{:S(2)}, u32[]{:S(2)}) collective-permute-start(bf16[4,2,96,768]{3,2,1,0:T(8,128)(2,1)S(1)} %pad_maximum_fusion.5), channel_id=1, source_target_pairs={{0,2},{1,3},{2,0},{3,1},{4,6},{5,7},{6,4},{7,5},{8,10},{9,11},{10,... | collective-permute-start | bytes 3538952 | tf_op jit(solution)/shard_map/ppermute | solution.py:775
  298.4 39.9 %collective-permute-start.45 = (bf16[2,8,1,96,768]{4,3,2,1,0:T(8,128)(2,1)}, bf16[2,8,1,96,768]{4,3,2,1,0:T(8,128)(2,1)}, u32[]{:S(2)}, u32[]{:S(2)}) collective-permute-start(bf16[2,8,1,96,768]{4,3,2,1,0:T(8,128)(2,1)} %get-tuple-element.322), channel_id=1, source_target_pairs={{0,1},{1,0},{2,3},{3,2},{4,5},{5,4},{6,7},{7,6},{8,9},{9,8},{10,11... | collective-permute-start | bytes 7077896 | tf_op jit(solution)/shard_map/ppermute | solution.py:775
  308.4 29.9 %collective-permute-start.48 = (bf16[2,96,768]{2,1,0:T(8,128)(2,1)S(1)}, bf16[2,96,768]{2,1,0:T(8,128)(2,1)S(1)}, u32[]{:S(2)}, u32[]{:S(2)}) collective-permute-start(bf16[2,96,768]{2,1,0:T(8,128)(2,1)S(1)} %get-tuple-element.525), channel_id=1, source_target_pairs={{0,8},{4,12},{8,0},{12,4},{16,24},{20,28},{24,16},{28,20},{1,9},{5... | collective-permute-start | bytes 884744 | tf_op jit(solution)/shard_map/ppermute | solution.py:775
  312.8 25.5 %collective-permute-start.49 = (bf16[2,96,768]{2,1,0:T(8,128)(2,1)S(1)}, bf16[2,96,768]{2,1,0:T(8,128)(2,1)S(1)}, u32[]{:S(2)}, u32[]{:S(2)}) collective-permute-start(bf16[2,96,768]{2,1,0:T(8,128)(2,1)S(1)} %get-tuple-element.524), channel_id=1, source_target_pairs={{0,16},{4,20},{8,24},{12,28},{16,0},{20,4},{24,8},{28,12},{1,17},{... | collective-permute-start | bytes 884744 | tf_op jit(solution)/shard_map/ppermute | solution.py:775
  313.7 24.6 %collective-permute-start.50 = (bf16[2,96,768]{2,1,0:T(8,128)(2,1)S(1)}, bf16[2,96,768]{2,1,0:T(8,128)(2,1)S(1)}, u32[]{:S(2)}, u32[]{:S(2)}) collective-permute-start(bf16[2,96,768]{2,1,0:T(8,128)(2,1)S(1)} %get-tuple-element.523), channel_id=1, source_target_pairs={{0,24},{4,28},{8,16},{12,20},{16,8},{20,12},{24,0},{28,4},{1,25},{... | collective-permute-start | bytes 884744 | tf_op jit(solution)/shard_map/ppermute | solution.py:775
  315.2 23.1 %all-to-all-start.2 = ((bf16[4,240,768]{2,1,0:T(8,128)(2,1)}), bf16[4,240,768]{2,1,0:T(8,128)(2,1)S(1)}, u32[]{:S(2)}, u32[]{:S(2)}) async-start(bf16[4,240,768]{2,1,0:T(8,128)(2,1)} %bitcast.57), calls=%async_computation.2 | async-start | bytes 2949120 | tf_op jit(solution)/shard_map/all_to_all | solution.py:781
  354.4 16.6 %collective-permute-start.53 = (bf16[4,1,96,768]{3,2,1,0:T(8,128)(2,1)S(1)}, bf16[4,1,96,768]{3,2,1,0:T(8,128)(2,1)S(1)}, u32[]{:S(2)}, u32[]{:S(2)}) collective-permute-start(bf16[4,1,96,768]{3,2,1,0:T(8,128)(2,1)S(1)} %pad_maximum_fusion.7), channel_id=1, source_target_pairs={{0,4},{4,0},{8,12},{12,8},{16,20},{20,16},{24,28},{28,24},{1,5},{5... | collective-permute-start | bytes 1769480 | tf_op jit(solution)/shard_map/ppermute | solution.py:775
  355.8 15.2 %collective-permute-start.54 = (bf16[4,1,96,768]{3,2,1,0:T(8,128)(2,1)S(1)}, bf16[4,1,96,768]{3,2,1,0:T(8,128)(2,1)}, u32[]{:S(2)}, u32[]{:S(2)}) collective-permute-start(bf16[4,1,96,768]{3,2,1,0:T(8,128)(2,1)S(1)} %pad_maximum_fusion.8), channel_id=1, source_target_pairs={{0,2},{1,3},{2,0},{3,1},{4,6},{5,7},{6,4},{7,5},{8,10},{9,11},{10,... | collective-permute-start | bytes 1769480 | tf_op jit(solution)/shard_map/ppermute | solution.py:775
  373.9 20.3 %collective-permute-start.60 = (bf16[1,96,768]{2,1,0:T(8,128)(2,1)}, bf16[1,96,768]{2,1,0:T(8,128)(2,1)}, u32[]{:S(2)}, u32[]{:S(2)}) collective-permute-start(bf16[1,96,768]{2,1,0:T(8,128)(2,1)} %get-tuple-element.533), channel_id=1, source_target_pairs={{0,8},{4,12},{8,0},{12,4},{16,24},{20,28},{24,16},{28,20},{1,9},{5... | collective-permute-start | bytes 442376 | tf_op jit(solution)/shard_map/ppermute | solution.py:775
  375.0 19.3 %collective-permute-start.61 = (bf16[1,96,768]{2,1,0:T(8,128)(2,1)}, bf16[1,96,768]{2,1,0:T(8,128)(2,1)}, u32[]{:S(2)}, u32[]{:S(2)}) collective-permute-start(bf16[1,96,768]{2,1,0:T(8,128)(2,1)} %get-tuple-element.535), channel_id=1, source_target_pairs={{0,16},{4,20},{8,24},{12,28},{16,0},{20,4},{24,8},{28,12},{1,17},{... | collective-permute-start | bytes 442376 | tf_op jit(solution)/shard_map/ppermute | solution.py:775
  376.9 17.4 %collective-permute-start.62 = (bf16[1,96,768]{2,1,0:T(8,128)(2,1)}, bf16[1,96,768]{2,1,0:T(8,128)(2,1)}, u32[]{:S(2)}, u32[]{:S(2)}) collective-permute-start(bf16[1,96,768]{2,1,0:T(8,128)(2,1)} %get-tuple-element.534), channel_id=1, source_target_pairs={{0,24},{4,28},{8,16},{12,20},{16,8},{20,12},{24,0},{28,4},{1,25},{... | collective-permute-start | bytes 442376 | tf_op jit(solution)/shard_map/ppermute | solution.py:775
  378.3 26.7 %all-to-all-start.3 = ((bf16[4,240,768]{2,1,0:T(8,128)(2,1)}), bf16[4,240,768]{2,1,0:T(8,128)(2,1)S(1)}, u32[]{:S(2)}, u32[]{:S(2)}) async-start(bf16[4,240,768]{2,1,0:T(8,128)(2,1)} %bitcast.220), calls=%async_computation.3 | async-start | bytes 2949120 | tf_op jit(solution)/shard_map/all_to_all | solution.py:781
  (79 other events, 633.1 us)

commit v7 on v6

--- a/solution.py
+++ b/solution.py
@@ -583,8 +583,8 @@
             square_ref[1:2, :] += jnp.sum(valid * fed * fed, axis=0, keepdims=True)
             total_ref[rows, :] = out
 
-        loop(vision_rows // PATCH_STRIDE, lambda i: finish(rows_at(i, PATCH_STRIDE), 0))
-        loop(3, lambda i: finish(pl.ds(pl.multiple_of(vision_rows + i * (text // 3), 16), text // 3), 1))
+        loop(2, lambda i: finish(rows_at(i, vision_rows // 2), 0))
+        finish(pl.ds(vision_rows, text), 1)
         unplace(place_ref, total_ref, raw_ref, all_rows)
 
 

time: 411 us -> 411 us (level)
  no operation moved by 1% of the time
where the time goes in v7:
time: 411 us; the launch traced here: 407 us
  Pallas kernels  182 us (44%)
  starting transfers between devices  79 us (19%)
  waiting for transfers between devices  70.7 us (17%)
  other arithmetic  53 us (13%)
  local copies, waits for them, and re-layouts  18.8 us (5%)
    pallas_call x12, Pallas kernels, call(): pl.pallas_call(kernel, name=name, grid_spec=pltpu.PrefetchScalarGridSpec(...  182 us
    ppermute x63, waiting for transfers between devices, swap(): return lax.ppermute(values, axis, [(i, i ^ bit) for i in range(size)])  70.7 us
    ppermute x63, starting transfers between devices, swap(): return lax.ppermute(values, axis, [(i, i ^ bit) for i in range(size)])  62.7 us
    unnamed x127, local copies, waits for them, and re-layouts  10.3 us
    all_to_all x2, starting transfers between devices, exchange(): lax.all_to_all(values, 'mp', split_axis=0, concat_axis=1, tiled=True)[0]  8.67 us
    convert_element_type x6, other arithmetic, adamw(): return (weight_new, first_new, second_new, weight_new.astype(bf16))  8.63 us
  transfers between devices with their start and end apart: 67, of which 21 were waited for; matrix products, arithmetic and copies ran while one was open for 11% of the time, Pallas kernels for 45%

profile of v7, /device:TPU:0, one launch (start us, length us, event | category | flops | bytes accessed | tf_op | source)
XLA Modules:
  0.0 407.1 jit_solution(8917842765978341306)
XLA Ops:
  3.5 5.1 %collective-permute-start.2 = (bf16[1,96,768]{2,1,0:T(8,128)(2,1)S(1)}, bf16[1,96,768]{2,1,0:T(8,128)(2,1)S(1)}, u32[]{:S(2)}, u32[]{:S(2)}) collective-permute-start(bf16[1,96,768]{2,1,0:T(8,128)(2,1)S(1)} %pad_maximum_fusion.10), channel_id=1, source_target_pairs={{0,24},{4,28},{8,16},{12,20},{16,8},{20,12},{24,0},{28,4},{1,25},{... | collective-permute-start | bytes 442376 | tf_op jit(solution)/shard_map/ppermute | solution.py:775
  9.3 4.5 %all-to-all-start = ((bf16[4,240,768]{2,1,0:T(8,128)(2,1)}), bf16[4,240,768]{2,1,0:T(8,128)(2,1)}, u32[]{:S(2)}, u32[]{:S(2)}) async-start(bf16[4,240,768]{2,1,0:T(8,128)(2,1)} %param.23), calls=%async_computation | async-start | bytes 2949120 | tf_op jit(solution)/shard_map/all_to_all | solution.py:778
  16.8 4.3 %collective-permute-done.1 = bf16[1,96,768]{2,1,0:T(8,128)(2,1)S(1)} collective-permute-done((bf16[1,96,768]{2,1,0:T(8,128)(2,1)S(1)}, bf16[1,96,768]{2,1,0:T(8,128)(2,1)S(1)}, u32[]{:S(2)}, u32[]{:S(2)}) %collective-permute-start.1) | collective-permute-done | bytes 147488 | tf_op jit(solution)/shard_map/ppermute | solution.py:775
  21.8 2.1 pad_maximum_fusion.6.refs_2_
  30.5 1.9 fusion.24.valid_ref
  32.4 6.3 %collective-permute-done.3.refs_3_ = bf16[4,1,96,768]{3,2,1,0:T(8,128)(2,1)} collective-permute-done((bf16[4,1,96,768]{3,2,1,0:T(8,128)(2,1)}, bf16[4,1,96,768]{3,2,1,0:T(8,128)(2,1)}, u32[]{:S(2)}, u32[]{:S(2)}) %collective-permute-start.3) | collective-permute-done | bytes 589856 | tf_op jit(solution)/shard_map/ppermute | solution.py:775
  38.6 6.9 %collective-permute-done.4.refs_2_ = bf16[4,1,96,768]{3,2,1,0:T(8,128)(2,1)} collective-permute-done((bf16[4,1,96,768]{3,2,1,0:T(8,128)(2,1)}, bf16[4,1,96,768]{3,2,1,0:T(8,128)(2,1)}, u32[]{:S(2)}, u32[]{:S(2)}) %collective-permute-start.4) | collective-permute-done | bytes 589856 | tf_op jit(solution)/shard_map/ppermute | solution.py:775
  47.0 2.9 collective-permute-start.7
  52.3 4.1 %all-to-all-start.1 = ((bf16[4,240,768]{2,1,0:T(8,128)(2,1)}), bf16[4,240,768]{2,1,0:T(8,128)(2,1)S(1)}, u32[]{:S(2)}, u32[]{:S(2)}) async-start(bf16[4,240,768]{2,1,0:T(8,128)(2,1)} %convert_element_type.391), calls=%async_computation.1 | async-start | bytes 2949120 | tf_op jit(solution)/shard_map/all_to_all | solution.py:778
  58.4 19.5 %attention.1 = (f32[1168,768]{1,0:T(8,128)}, bf16[1168,768]{1,0:T(8,128)(2,1)}, f32[1168,768]{1,0:T(8,128)}, bf16[1,4,768,768]{3,2,1,0:T(8,128)(2,1)}, bf16[4,11...) custom-call(s32[6]{0:T(128)} %pad_add_fusion.1.meta_ref, ...), custom_call_target="tpu_custom_call" | custom-call | flops 17999998976 | bytes 18000000 | tf_op jit(solution)/shard_map/attention/pallas_call | solution.py:694
  80.2 1.9 collective-permute-start.12
  82.7 3.8 collective-permute-start.14
  87.3 20.1 %attention_end.1 = (f32[1168,768]{1,0:T(8,128)}, bf16[1168,768]{1,0:T(8,128)(2,1)}, f32[1,768]{1,0:T(1,128)}, bf16[1,4,768,768]{3,2,1,0:T(8,128)(2,1)}, bf16[4,1...) custom-call(s32[6]{0:T(128)} %pad_add_fusion.1.meta_ref, ...), custom_call_target="tpu_custom_call", output_to_operand_aliasing={{3}: (10, {}), {4}: (11, {}), {5}: (12, {}), {6}: (13, {})} | custom-call | flops 17999998976 | bytes 18000000 | tf_op jit(solution)/shard_map/attention_end/pallas_call | solution.py:694
  109.5 2.0 collective-permute-start.18
  112.9 5.0 %place_grad.1 = (bf16[1024,768]{1,0:T(8,128)(2,1)}, f32[2,768]{1,0:T(2,128)}) custom-call(bf16[960,768]{1,0:T(8,128)(2,1)} %bitcast.221, s32[1,960]{1,0:T(1,128)} %bitcast.234), custom_call_target="tpu_custom_call" | custom-call | flops 5000000000 | bytes 5000000 | tf_op jit(solution)/shard_map/place_grad/pallas_call | solution.py:694
  117.9 6.9 %collective-permute-done.18.refs_3_ = bf16[2,2,96,768]{3,2,1,0:T(8,128)(2,1)} collective-permute-done((bf16[2,2,96,768]{3,2,1,0:T(8,128)(2,1)S(1)}, bf16[2,2,96,768]{3,2,1,0:T(8,128)(2,1)}, u32[]{:S(2)}, u32[]{:S(2)}) %collective-permute-start.18) | collective-permute-done | bytes 589856 | tf_op jit(solution)/shard_map/ppermute | solution.py:775
  130.2 16.8 %lift.1 = (bf16[4,1168,768]{2,1,0:T(8,128)(2,1)}, bf16[4,1168,768]{2,1,0:T(8,128)(2,1)}, bf16[2,4,768,768]{3,2,1,0:T(8,128)(2,1)}) custom-call(s32[2]{0:T(128)} %pad_add_fusion.mine_ref, bf16[1168,768]{1,0:T(8,128)(2,1)} %get-tuple-element.242.feed_ref, bf16[4,2,96,768]{3,2,1,0:T(8,128)(2,1)} %copy-done.15, bf16[4,2,96,768]{3,2,1,0:T(8,128)(2,1)} %copy-done.37, ...), custom_call_target="tpu_custom_call" | custom-call | flops 16000000000 | bytes 16000000 | tf_op jit(solution)/shard_map/lift/pallas_call | solution.py:694
  147.0 8.5 %collective-permute-done.23.refs_1_ = bf16[4,2,96,768]{3,2,1,0:T(8,128)(2,1)S(1)} collective-permute-done((bf16[4,2,96,768]{3,2,1,0:T(8,128)(2,1)S(1)}, bf16[4,2,96,768]{3,2,1,0:T(8,128)(2,1)S(1)}, u32[]{:S(2)}, u32[]{:S(2)}) %collective-permute-start.23) | collective-permute-done | bytes 1179680 | tf_op jit(solution)/shard_map/ppermute | solution.py:775
  158.9 7.4 %drop_weight_grad.2 = bf16[2,8,2,96,768]{4,3,2,1,0:T(8,128)(2,1)} custom-call(s32[2]{0:T(128)} %pad_add_fusion.mine_ref, bf16[1024,768]{1,0:T(8,128)(2,1)} %get-tuple-element.264.grad_ref, bf16[4,1168,768]{2,1,0:T(8,128)(2,1)} %get-tuple-element.306.acted_ref), custom_call_target="tpu_custom_call" | custom-call | flops 7000000000 | bytes 7000000 | tf_op jit(solution)/shard_map/drop_weight_grad/pallas_call | solution.py:694
  166.3 6.3 %collective-permute-done.27.refs_3_ = bf16[2,2,96,768]{3,2,1,0:T(8,128)(2,1)} collective-permute-done((bf16[2,2,96,768]{3,2,1,0:T(8,128)(2,1)S(1)}, bf16[2,2,96,768]{3,2,1,0:T(8,128)(2,1)}, u32[]{:S(2)}, u32[]{:S(2)}) %collective-permute-start.27) | collective-permute-done | bytes 589856 | tf_op jit(solution)/shard_map/ppermute | solution.py:775
  173.4 7.4 %drop_weight_grad.3 = bf16[2,8,2,96,768]{4,3,2,1,0:T(8,128)(2,1)} custom-call(s32[2]{0:T(128)} %pad_add_fusion.mine_ref, bf16[1024,768]{1,0:T(8,128)(2,1)} %get-tuple-element.264.grad_ref, bf16[4,1168,768]{2,1,0:T(8,128)(2,1)} %get-tuple-element.306.acted_ref), custom_call_target="tpu_custom_call" | custom-call | flops 7000000000 | bytes 7000000 | tf_op jit(solution)/shard_map/drop_weight_grad/pallas_call | solution.py:694
  182.7 2.5 fusion.4
  188.5 18.7 %expert_back.1 = (bf16[2,8,2,96,768]{4,3,2,1,0:T(8,128)(2,1)}, bf16[2,4,768,768]{3,2,1,0:T(8,128)(2,1)}, f32[1024,768]{1,0:T(8,128)}) custom-call(s32[2]{0:T(128)} %pad_add_fusion.mine_ref, bf16[1024,768]{1,0:T(8,128)(2,1)} %get-tuple-element.264.grad_ref, bf16[4,1168,768]{2,1,0:T(8,128)(2,1)} %get-tuple-element.265.slope_ref, ...), custom_call_target="tpu_custom_call" | custom-call | flops 16999999488 | bytes 17000000 | tf_op jit(solution)/shard_map/expert_back/pallas_call | solution.py:694
  207.3 2.4 convert_add_fusion.2
  214.5 22.2 %expert_back_end.1 = (bf16[2,8,2,96,768]{4,3,2,1,0:T(8,128)(2,1)}, bf16[2,4,768,768]{3,2,1,0:T(8,128)(2,1)}, f32[1024,768]{1,0:T(8,128)}, bf16[1024,768]{1,0:T(8,128)(2,1)}, f32[2,768]{1,0:T(2,128)}) custom-call(s32[2]{0:T(128)} %pad_add_fusion.mine_ref, bf16[1024,768]{1,0:T(8,128)(2,1)} %get-tuple-element.264.grad_ref, ...), custom_call_target="tpu_custom_call", output_to_operand_aliasing={{1}: (10, {})} | custom-call | flops 16999999488 | bytes 17000000 | tf_op jit(solution)/shard_map/expert_back_end/pallas_call | solution.py:694
  236.7 4.3 %collective-permute-done.38 = bf16[4,2,96,768]{3,2,1,0:T(8,128)(2,1)S(1)} collective-permute-done((bf16[4,2,96,768]{3,2,1,0:T(8,128)(2,1)S(1)}, bf16[4,2,96,768]{3,2,1,0:T(8,128)(2,1)S(1)}, u32[]{:S(2)}, u32[]{:S(2)}) %collective-permute-start.38) | collective-permute-done | bytes 1179680 | tf_op jit(solution)/shard_map/ppermute | solution.py:775
  242.1 1.9 fusion.5
  244.1 2.4 fusion.3
  249.6 4.2 %collective-permute-start.40 = (bf16[2,96,768]{2,1,0:T(8,128)(2,1)}, bf16[2,96,768]{2,1,0:T(8,128)(2,1)S(1)}, u32[]{:S(2)}, u32[]{:S(2)}) collective-permute-start(bf16[2,96,768]{2,1,0:T(8,128)(2,1)} %get-tuple-element.530), channel_id=1, source_target_pairs={{0,8},{4,12},{8,0},{12,4},{16,24},{20,28},{24,16},{28,20},{1,9},{5... | collective-permute-start | bytes 884744 | tf_op jit(solution)/shard_map/ppermute | solution.py:775
  256.1 16.5 %drop.1 = (bf16[960,768]{1,0:T(8,128)(2,1)}, f32[2,768]{1,0:T(2,128)}) custom-call(bf16[4,1168,768]{2,1,0:T(8,128)(2,1)} %get-tuple-element.306.acted_ref, f32[1168,768]{1,0:T(8,128)} %get-tuple-element.289.refs_7_.residual_ref, f32[1168,1]{1,0:T(8,128)} %fusion.24.valid_ref, s32[960,1]{1,0:T(8,128)} %copy.124.place_ref, f32[3,768]{1,0:T(4,128)} %extra_ref.3, ...), custom_call_target="tpu_custom_call" | custom-call | flops 16999999488 | bytes 17000000 | tf_op jit(solution)/shard_map/drop/pallas_call | solution.py:694
  272.7 2.4 convert_add_fusion
  279.5 18.9 %attention_back.1 = (bf16[2,8,1,96,768]{4,3,2,1,0:T(8,128)(2,1)}, f32[1024,768]{1,0:T(8,128)}) custom-call(s32[2]{0:T(128)} %pad_add_fusion.mine_ref, bf16[1024,768]{1,0:T(8,128)(2,1)} %get-tuple-element.317.grad_attended_ref, bf16[4,1168,576]{2,1,0:T(8,128)(2,1)} %get-tuple-element.318.joint_ref, bf16[4,1168,192]{2,1,0:T(8,128)(2,1)} %get-tuple-element.319.mixed_ref, ...), custom_call_target="tpu_custom_call" | custom-call | flops 19000000512 | bytes 19000000 | tf_op jit(solution)/shard_map/attention_back/pallas_call | solution.py:694
  298.5 4.9 %collective-permute-done.46 = bf16[4,2,96,768]{3,2,1,0:T(8,128)(2,1)} collective-permute-done((bf16[4,2,96,768]{3,2,1,0:T(8,128)(2,1)}, bf16[4,2,96,768]{3,2,1,0:T(8,128)(2,1)}, u32[]{:S(2)}, u32[]{:S(2)}) %collective-permute-start.46) | collective-permute-done | bytes 1179680 | tf_op jit(solution)/shard_map/ppermute | solution.py:775
  304.3 2.7 fusion.1
  308.1 4.7 %collective-permute-start.48 = (bf16[2,96,768]{2,1,0:T(8,128)(2,1)S(1)}, bf16[2,96,768]{2,1,0:T(8,128)(2,1)S(1)}, u32[]{:S(2)}, u32[]{:S(2)}) collective-permute-start(bf16[2,96,768]{2,1,0:T(8,128)(2,1)S(1)} %get-tuple-element.525), channel_id=1, source_target_pairs={{0,8},{4,12},{8,0},{12,4},{16,24},{20,28},{24,16},{28,20},{1,9},{5... | collective-permute-start | bytes 884744 | tf_op jit(solution)/shard_map/ppermute | solution.py:775
  315.2 3.7 all-to-all-start.2
  318.9 19.3 %attention_back_end.1 = (bf16[2,8,1,96,768]{4,3,2,1,0:T(8,128)(2,1)}, f32[1024,768]{1,0:T(8,128)}) custom-call(s32[2]{0:T(128)} %pad_add_fusion.mine_ref, bf16[1024,768]{1,0:T(8,128)(2,1)} %get-tuple-element.317.grad_attended_ref, bf16[4,1168,576]{2,1,0:T(8,128)(2,1)} %get-tuple-element.318.joint_ref, bf16[4,1168,192]{2,1,0:T(8,128)(2,1)} %get-tuple-element.319.mixed_ref, ...), custom_call_target="tpu_custom_call" | custom-call | flops 19000000512 | bytes 19000000 | tf_op jit(solution)/shard_map/attention_back_end/pallas_call | solution.py:694
  340.8 2.0 collective-permute-start.52
  342.8 9.5 %input_grad.1 = (bf16[960,768]{1,0:T(8,128)(2,1)}, f32[16,768]{1,0:T(8,128)}) custom-call(f32[1024,768]{1,0:T(8,128)} %get-tuple-element.344.grad_normed_ref, f32[1024,768]{1,0:T(8,128)} %get-tuple-element.345.grad_residual_ref, f32[1168,768]{1,0:T(8,128)} %get-tuple-element.221.block_ref, s32[1168,1]{1,0:T(8,128)} %copy.123.hidden_ref, ...), custom_call_target="tpu_custom_call" | custom-call | flops 8999999488 | bytes 9000000 | tf_op jit(solution)/shard_map/input_grad/pallas_call | solution.py:694
  359.3 11.0 %collective-permute-done.56 = f32[16,768]{1,0:T(8,128)S(1)} collective-permute-done((f32[16,768]{1,0:T(8,128)S(1)}, f32[16,768]{1,0:T(8,128)S(1)}, u32[]{:S(2)}, u32[]{:S(2)}) %collective-permute-start.56) | collective-permute-done | bytes 49184 | tf_op jit(solution)/shard_map/ppermute | solution.py:775
  370.9 1.8 fusion.15
  375.0 1.9 collective-permute-start.61
  378.3 3.9 all-to-all-start.3
  383.4 3.4 fusion.60
  389.6 2.7 fusion.62
  392.2 1.8 convert_element_type.440
  399.9 2.5 fusion.54
  405.0 1.8 convert_element_type.441
  (312 shorter events, 84.8 us)
Async XLA Ops:
  9.3 36.3 %all-to-all-start = ((bf16[4,240,768]{2,1,0:T(8,128)(2,1)}), bf16[4,240,768]{2,1,0:T(8,128)(2,1)}, u32[]{:S(2)}, u32[]{:S(2)}) async-start(bf16[4,240,768]{2,1,0:T(8,128)(2,1)} %param.23), calls=%async_computation | async-start | bytes 2949120 | tf_op jit(solution)/shard_map/all_to_all | solution.py:778
  23.9 14.7 %collective-permute-start.3 = (bf16[4,1,96,768]{3,2,1,0:T(8,128)(2,1)}, bf16[4,1,96,768]{3,2,1,0:T(8,128)(2,1)}, u32[]{:S(2)}, u32[]{:S(2)}) collective-permute-start(bf16[4,1,96,768]{3,2,1,0:T(8,128)(2,1)} %pad_maximum_fusion.6.refs_2_), channel_id=1, source_target_pairs={{0,4},{4,0},{8,12},{12,8},{16,20},{20,16},{24,28},{28,24},{1,5},{5... | collective-permute-start | bytes 1769480 | tf_op jit(solution)/shard_map/ppermute | solution.py:775
  25.4 20.1 %collective-permute-start.4 = (bf16[4,1,96,768]{3,2,1,0:T(8,128)(2,1)}, bf16[4,1,96,768]{3,2,1,0:T(8,128)(2,1)}, u32[]{:S(2)}, u32[]{:S(2)}) collective-permute-start(bf16[4,1,96,768]{3,2,1,0:T(8,128)(2,1)} %pad_maximum_fusion.6.refs_2_), channel_id=1, source_target_pairs={{0,2},{1,3},{2,0},{3,1},{4,6},{5,7},{6,4},{7,5},{8,10},{9,11},{10,... | collective-permute-start | bytes 1769480 | tf_op jit(solution)/shard_map/ppermute | solution.py:775
  32.4 24.1 %collective-permute-start.9 = (bf16[4,1,96,768]{3,2,1,0:T(8,128)(2,1)}, bf16[4,1,96,768]{3,2,1,0:T(8,128)(2,1)}, u32[]{:S(2)}, u32[]{:S(2)}) collective-permute-start(bf16[4,1,96,768]{3,2,1,0:T(8,128)(2,1)} %pad_maximum_fusion.6.refs_2_), channel_id=1, source_target_pairs={{0,1},{1,0},{2,3},{3,2},{4,5},{5,4},{6,7},{7,6},{8,9},{9,8},{10,11... | collective-permute-start | bytes 1769480 | tf_op jit(solution)/shard_map/ppermute | solution.py:775
  45.6 32.4 %collective-permute-start.6 = (bf16[2,96,768]{2,1,0:T(8,128)(2,1)}, bf16[2,96,768]{2,1,0:T(8,128)(2,1)}, u32[]{:S(2)}, u32[]{:S(2)}) collective-permute-start(bf16[2,96,768]{2,1,0:T(8,128)(2,1)} %convert_element_type.386), channel_id=1, source_target_pairs={{0,8},{4,12},{8,0},{12,4},{16,24},{20,28},{24,16},{28,20},{1,9},{5... | collective-permute-start | bytes 884744 | tf_op jit(solution)/shard_map/ppermute | solution.py:775
  47.0 31.0 %collective-permute-start.7 = (bf16[2,96,768]{2,1,0:T(8,128)(2,1)}, bf16[2,96,768]{2,1,0:T(8,128)(2,1)}, u32[]{:S(2)}, u32[]{:S(2)}) collective-permute-start(bf16[2,96,768]{2,1,0:T(8,128)(2,1)} %convert_element_type.386), channel_id=1, source_target_pairs={{0,16},{4,20},{8,24},{12,28},{16,0},{20,4},{24,8},{28,12},{1,17},{... | collective-permute-start | bytes 884744 | tf_op jit(solution)/shard_map/ppermute | solution.py:775
  49.9 28.1 %collective-permute-start.8 = (bf16[2,96,768]{2,1,0:T(8,128)(2,1)}, bf16[2,96,768]{2,1,0:T(8,128)(2,1)}, u32[]{:S(2)}, u32[]{:S(2)}) collective-permute-start(bf16[2,96,768]{2,1,0:T(8,128)(2,1)} %convert_element_type.386), channel_id=1, source_target_pairs={{0,24},{4,28},{8,16},{12,20},{16,8},{20,12},{24,0},{28,4},{1,25},{... | collective-permute-start | bytes 884744 | tf_op jit(solution)/shard_map/ppermute | solution.py:775
  52.3 25.7 %all-to-all-start.1 = ((bf16[4,240,768]{2,1,0:T(8,128)(2,1)}), bf16[4,240,768]{2,1,0:T(8,128)(2,1)S(1)}, u32[]{:S(2)}, u32[]{:S(2)}) async-start(bf16[4,240,768]{2,1,0:T(8,128)(2,1)} %convert_element_type.391), calls=%async_computation.1 | async-start | bytes 2949120 | tf_op jit(solution)/shard_map/all_to_all | solution.py:778
  56.5 21.5 %collective-permute-start.5 = (bf16[4,1,96,768]{3,2,1,0:T(8,128)(2,1)}, bf16[4,1,96,768]{3,2,1,0:T(8,128)(2,1)}, u32[]{:S(2)}, u32[]{:S(2)}) collective-permute-start(bf16[4,1,96,768]{3,2,1,0:T(8,128)(2,1)} %collective-permute-done.4.refs_2_), channel_id=1, source_target_pairs={{0,4},{4,0},{8,12},{12,8},{16,20},{20,16},{24,28},{28,24},{1,5},{5... | collective-permute-start | bytes 1769480 | tf_op jit(solution)/shard_map/ppermute | solution.py:775
  58.2 24.5 %collective-permute-start.16 = (bf16[4,1,96,768]{3,2,1,0:T(8,128)(2,1)}, bf16[4,1,96,768]{3,2,1,0:T(8,128)(2,1)}, u32[]{:S(2)}, u32[]{:S(2)}) collective-permute-start(bf16[4,1,96,768]{3,2,1,0:T(8,128)(2,1)} %collective-permute-done.4.refs_2_), channel_id=1, source_target_pairs={{0,1},{1,0},{2,3},{3,2},{4,5},{5,4},{6,7},{7,6},{8,9},{9,8},{10,11... | collective-permute-start | bytes 1769480 | tf_op jit(solution)/shard_map/ppermute | solution.py:775
  79.8 28.3 %collective-permute-start.11 = (bf16[4,2,96,768]{3,2,1,0:T(8,128)(2,1)S(1)}, bf16[4,2,96,768]{3,2,1,0:T(8,128)(2,1)S(1)}, u32[]{:S(2)}, u32[]{:S(2)}) collective-permute-start(bf16[4,2,96,768]{3,2,1,0:T(8,128)(2,1)S(1)} %pad_maximum_fusion.refs_0_), channel_id=1, source_target_pairs={{0,4},{4,0},{8,12},{12,8},{16,20},{20,16},{24,28},{28,24},{1,5},{5... | collective-permute-start | bytes 3538952 | tf_op jit(solution)/shard_map/ppermute | solution.py:775
  80.2 28.2 %collective-permute-start.12 = (bf16[4,2,96,768]{3,2,1,0:T(8,128)(2,1)S(1)}, bf16[4,2,96,768]{3,2,1,0:T(8,128)(2,1)S(1)}, u32[]{:S(2)}, u32[]{:S(2)}) collective-permute-start(bf16[4,2,96,768]{3,2,1,0:T(8,128)(2,1)S(1)} %pad_maximum_fusion.refs_0_), channel_id=1, source_target_pairs={{0,2},{1,3},{2,0},{3,1},{4,6},{5,7},{6,4},{7,5},{8,10},{9,11},{10,... | collective-permute-start | bytes 3538952 | tf_op jit(solution)/shard_map/ppermute | solution.py:775
  82.2 25.3 %collective-permute-start.13 = (bf16[2,96,768]{2,1,0:T(8,128)(2,1)S(1)}, bf16[2,96,768]{2,1,0:T(8,128)(2,1)S(1)}, u32[]{:S(2)}, u32[]{:S(2)}) collective-permute-start(bf16[2,96,768]{2,1,0:T(8,128)(2,1)S(1)} %convert_bitcast_fusion), channel_id=1, source_target_pairs={{0,8},{4,12},{8,0},{12,4},{16,24},{20,28},{24,16},{28,20},{1,9},{5... | collective-permute-start | bytes 884744 | tf_op jit(solution)/shard_map/ppermute | solution.py:775
  82.7 24.9 %collective-permute-start.14 = (bf16[2,96,768]{2,1,0:T(8,128)(2,1)S(1)}, bf16[2,96,768]{2,1,0:T(8,128)(2,1)S(1)}, u32[]{:S(2)}, u32[]{:S(2)}) collective-permute-start(bf16[2,96,768]{2,1,0:T(8,128)(2,1)S(1)} %convert_bitcast_fusion), channel_id=1, source_target_pairs={{0,16},{4,20},{8,24},{12,28},{16,0},{20,4},{24,8},{28,12},{1,17},{... | collective-permute-start | bytes 884744 | tf_op jit(solution)/shard_map/ppermute | solution.py:775
  86.5 21.1 %collective-permute-start.15 = (bf16[2,96,768]{2,1,0:T(8,128)(2,1)S(1)}, bf16[2,96,768]{2,1,0:T(8,128)(2,1)S(1)}, u32[]{:S(2)}, u32[]{:S(2)}) collective-permute-start(bf16[2,96,768]{2,1,0:T(8,128)(2,1)S(1)} %convert_bitcast_fusion), channel_id=1, source_target_pairs={{0,24},{4,28},{8,16},{12,20},{16,8},{20,12},{24,0},{28,4},{1,25},{... | collective-permute-start | bytes 884744 | tf_op jit(solution)/shard_map/ppermute | solution.py:775
  108.5 17.7 %collective-permute-start.21 = (bf16[4,2,96,768]{3,2,1,0:T(8,128)(2,1)S(1)}, bf16[4,2,96,768]{3,2,1,0:T(8,128)(2,1)}, u32[]{:S(2)}, u32[]{:S(2)}) collective-permute-start(bf16[4,2,96,768]{3,2,1,0:T(8,128)(2,1)S(1)} %collective-permute-done.11.refs_1_), channel_id=1, source_target_pairs={{0,1},{1,0},{2,3},{3,2},{4,5},{5,4},{6,7},{7,6},{8,9},{9,8},{10,11... | collective-permute-start | bytes 3538952 | tf_op jit(solution)/shard_map/ppermute | solution.py:775
  108.5 17.7 %collective-permute-start.22 = (bf16[4,2,96,768]{3,2,1,0:T(8,128)(2,1)S(1)}, bf16[4,2,96,768]{3,2,1,0:T(8,128)(2,1)}, u32[]{:S(2)}, u32[]{:S(2)}) collective-permute-start(bf16[4,2,96,768]{3,2,1,0:T(8,128)(2,1)S(1)} %collective-permute-done.12.refs_2_), channel_id=1, source_target_pairs={{0,1},{1,0},{2,3},{3,2},{4,5},{5,4},{6,7},{7,6},{8,9},{9,8},{10,11... | collective-permute-start | bytes 3538952 | tf_op jit(solution)/shard_map/ppermute | solution.py:775
  109.5 15.3 %collective-permute-start.18 = (bf16[2,2,96,768]{3,2,1,0:T(8,128)(2,1)S(1)}, bf16[2,2,96,768]{3,2,1,0:T(8,128)(2,1)}, u32[]{:S(2)}, u32[]{:S(2)}) collective-permute-start(bf16[2,2,96,768]{3,2,1,0:T(8,128)(2,1)S(1)} %slice.267), channel_id=1, source_target_pairs={{0,2},{1,3},{2,0},{3,1},{4,6},{5,7},{6,4},{7,5},{8,10},{9,11},{10,... | collective-permute-start | bytes 1769480 | tf_op jit(solution)/shard_map/ppermute | solution.py:775
  111.5 14.7 %collective-permute-start.19 = (bf16[2,2,96,768]{3,2,1,0:T(8,128)(2,1)S(1)}, bf16[2,2,96,768]{3,2,1,0:T(8,128)(2,1)}, u32[]{:S(2)}, u32[]{:S(2)}) collective-permute-start(bf16[2,2,96,768]{3,2,1,0:T(8,128)(2,1)S(1)} %slice.268), channel_id=1, source_target_pairs={{0,4},{4,0},{8,12},{12,8},{16,20},{20,16},{24,28},{28,24},{1,5},{5... | collective-permute-start | bytes 1769480 | tf_op jit(solution)/shard_map/ppermute | solution.py:775
  127.5 28.0 %collective-permute-start.23 = (bf16[4,2,96,768]{3,2,1,0:T(8,128)(2,1)S(1)}, bf16[4,2,96,768]{3,2,1,0:T(8,128)(2,1)S(1)}, u32[]{:S(2)}, u32[]{:S(2)}) collective-permute-start(bf16[4,2,96,768]{3,2,1,0:T(8,128)(2,1)S(1)} %pad_maximum_fusion.1.refs_0_), channel_id=1, source_target_pairs={{0,4},{4,0},{8,12},{12,8},{16,20},{20,16},{24,28},{28,24},{1,5},{5... | collective-permute-start | bytes 3538952 | tf_op jit(solution)/shard_map/ppermute | solution.py:775
  128.9 27.7 %collective-permute-start.24 = (bf16[4,2,96,768]{3,2,1,0:T(8,128)(2,1)S(1)}, bf16[4,2,96,768]{3,2,1,0:T(8,128)(2,1)S(1)}, u32[]{:S(2)}, u32[]{:S(2)}) collective-permute-start(bf16[4,2,96,768]{3,2,1,0:T(8,128)(2,1)S(1)} %pad_maximum_fusion.1.refs_0_), channel_id=1, source_target_pairs={{0,2},{1,3},{2,0},{3,1},{4,6},{5,7},{6,4},{7,5},{8,10},{9,11},{10,... | collective-permute-start | bytes 3538952 | tf_op jit(solution)/shard_map/ppermute | solution.py:775
  129.4 36.9 %collective-permute-start.29 = (bf16[4,2,96,768]{3,2,1,0:T(8,128)(2,1)S(1)}, bf16[4,2,96,768]{3,2,1,0:T(8,128)(2,1)S(1)}, u32[]{:S(2)}, u32[]{:S(2)}) collective-permute-start(bf16[4,2,96,768]{3,2,1,0:T(8,128)(2,1)S(1)} %pad_maximum_fusion.1.refs_0_), channel_id=1, source_target_pairs={{0,1},{1,0},{2,3},{3,2},{4,5},{5,4},{6,7},{7,6},{8,9},{9,8},{10,11... | collective-permute-start | bytes 3538952 | tf_op jit(solution)/shard_map/ppermute | solution.py:775
  156.6 16.2 %collective-permute-start.30 = (bf16[4,2,96,768]{3,2,1,0:T(8,128)(2,1)S(1)}, bf16[4,2,96,768]{3,2,1,0:T(8,128)(2,1)}, u32[]{:S(2)}, u32[]{:S(2)}) collective-permute-start(bf16[4,2,96,768]{3,2,1,0:T(8,128)(2,1)S(1)} %collective-permute-done.23.refs_1_), channel_id=1, source_target_pairs={{0,1},{1,0},{2,3},{3,2},{4,5},{5,4},{6,7},{7,6},{8,9},{9,8},{10,11... | collective-permute-start | bytes 3538952 | tf_op jit(solution)/shard_map/ppermute | solution.py:775
  156.6 16.2 %collective-permute-start.31 = (bf16[4,2,96,768]{3,2,1,0:T(8,128)(2,1)S(1)}, bf16[4,2,96,768]{3,2,1,0:T(8,128)(2,1)}, u32[]{:S(2)}, u32[]{:S(2)}) collective-permute-start(bf16[4,2,96,768]{3,2,1,0:T(8,128)(2,1)S(1)} %collective-permute-done.24.refs_2_), channel_id=1, source_target_pairs={{0,1},{1,0},{2,3},{3,2},{4,5},{5,4},{6,7},{7,6},{8,9},{9,8},{10,11... | collective-permute-start | bytes 3538952 | tf_op jit(solution)/shard_map/ppermute | solution.py:775
  157.6 15.0 %collective-permute-start.27 = (bf16[2,2,96,768]{3,2,1,0:T(8,128)(2,1)S(1)}, bf16[2,2,96,768]{3,2,1,0:T(8,128)(2,1)}, u32[]{:S(2)}, u32[]{:S(2)}) collective-permute-start(bf16[2,2,96,768]{3,2,1,0:T(8,128)(2,1)S(1)} %slice.269), channel_id=1, source_target_pairs={{0,2},{1,3},{2,0},{3,1},{4,6},{5,7},{6,4},{7,5},{8,10},{9,11},{10,... | collective-permute-start | bytes 1769480 | tf_op jit(solution)/shard_map/ppermute | solution.py:775
  186.3 20.9 %collective-permute-start.35 = (bf16[2,2,96,768]{3,2,1,0:T(8,128)(2,1)}, bf16[2,2,96,768]{3,2,1,0:T(8,128)(2,1)S(1)}, u32[]{:S(2)}, u32[]{:S(2)}) collective-permute-start(bf16[2,2,96,768]{3,2,1,0:T(8,128)(2,1)} %get-tuple-element.532), channel_id=1, source_target_pairs={{0,4},{4,0},{8,12},{12,8},{16,20},{20,16},{24,28},{28,24},{1,5},{5... | collective-permute-start | bytes 1769480 | tf_op jit(solution)/shard_map/ppermute | solution.py:775
  186.9 20.3 %collective-permute-start.36 = (bf16[2,2,96,768]{3,2,1,0:T(8,128)(2,1)}, bf16[2,2,96,768]{3,2,1,0:T(8,128)(2,1)S(1)}, u32[]{:S(2)}, u32[]{:S(2)}) collective-permute-start(bf16[2,2,96,768]{3,2,1,0:T(8,128)(2,1)} %get-tuple-element.531), channel_id=1, source_target_pairs={{0,2},{1,3},{2,0},{3,1},{4,6},{5,7},{6,4},{7,5},{8,10},{9,11},{10,... | collective-permute-start | bytes 1769480 | tf_op jit(solution)/shard_map/ppermute | solution.py:775
  210.3 31.8 %collective-permute-start.37 = (bf16[2,8,2,96,768]{4,3,2,1,0:T(8,128)(2,1)}, bf16[2,8,2,96,768]{4,3,2,1,0:T(8,128)(2,1)}, u32[]{:S(2)}, u32[]{:S(2)}) collective-permute-start(bf16[2,8,2,96,768]{4,3,2,1,0:T(8,128)(2,1)} %get-tuple-element.291), channel_id=1, source_target_pairs={{0,1},{1,0},{2,3},{3,2},{4,5},{5,4},{6,7},{7,6},{8,9},{9,8},{10,11... | collective-permute-start | bytes 14155784 | tf_op jit(solution)/shard_map/ppermute | solution.py:775
  212.7 28.4 %collective-permute-start.38 = (bf16[4,2,96,768]{3,2,1,0:T(8,128)(2,1)S(1)}, bf16[4,2,96,768]{3,2,1,0:T(8,128)(2,1)S(1)}, u32[]{:S(2)}, u32[]{:S(2)}) collective-permute-start(bf16[4,2,96,768]{3,2,1,0:T(8,128)(2,1)S(1)} %pad_maximum_fusion.2), channel_id=1, source_target_pairs={{0,4},{4,0},{8,12},{12,8},{16,20},{20,16},{24,28},{28,24},{1,5},{5... | collective-permute-start | bytes 3538952 | tf_op jit(solution)/shard_map/ppermute | solution.py:775
  214.1 28.1 %collective-permute-start.39 = (bf16[4,2,96,768]{3,2,1,0:T(8,128)(2,1)S(1)}, bf16[4,2,96,768]{3,2,1,0:T(8,128)(2,1)S(1)}, u32[]{:S(2)}, u32[]{:S(2)}) collective-permute-start(bf16[4,2,96,768]{3,2,1,0:T(8,128)(2,1)S(1)} %pad_maximum_fusion.3), channel_id=1, source_target_pairs={{0,2},{1,3},{2,0},{3,1},{4,6},{5,7},{6,4},{7,5},{8,10},{9,11},{10,... | collective-permute-start | bytes 3538952 | tf_op jit(solution)/shard_map/ppermute | solution.py:775
  247.6 25.0 %collective-permute-start.43 = (bf16[2,2,96,768]{3,2,1,0:T(8,128)(2,1)}, bf16[2,2,96,768]{3,2,1,0:T(8,128)(2,1)S(1)}, u32[]{:S(2)}, u32[]{:S(2)}) collective-permute-start(bf16[2,2,96,768]{3,2,1,0:T(8,128)(2,1)} %get-tuple-element.527), channel_id=1, source_target_pairs={{0,4},{4,0},{8,12},{12,8},{16,20},{20,16},{24,28},{28,24},{1,5},{5... | collective-permute-start | bytes 1769480 | tf_op jit(solution)/shard_map/ppermute | solution.py:775
  248.3 24.4 %collective-permute-start.44 = (bf16[2,2,96,768]{3,2,1,0:T(8,128)(2,1)}, bf16[2,2,96,768]{3,2,1,0:T(8,128)(2,1)S(1)}, u32[]{:S(2)}, u32[]{:S(2)}) collective-permute-start(bf16[2,2,96,768]{3,2,1,0:T(8,128)(2,1)} %get-tuple-element.526), channel_id=1, source_target_pairs={{0,2},{1,3},{2,0},{3,1},{4,6},{5,7},{6,4},{7,5},{8,10},{9,11},{10,... | collective-permute-start | bytes 1769480 | tf_op jit(solution)/shard_map/ppermute | solution.py:775
  249.6 27.2 %collective-permute-start.40 = (bf16[2,96,768]{2,1,0:T(8,128)(2,1)}, bf16[2,96,768]{2,1,0:T(8,128)(2,1)S(1)}, u32[]{:S(2)}, u32[]{:S(2)}) collective-permute-start(bf16[2,96,768]{2,1,0:T(8,128)(2,1)} %get-tuple-element.530), channel_id=1, source_target_pairs={{0,8},{4,12},{8,0},{12,4},{16,24},{20,28},{24,16},{28,20},{1,9},{5... | collective-permute-start | bytes 884744 | tf_op jit(solution)/shard_map/ppermute | solution.py:775
  253.8 23.8 %collective-permute-start.41 = (bf16[2,96,768]{2,1,0:T(8,128)(2,1)}, bf16[2,96,768]{2,1,0:T(8,128)(2,1)}, u32[]{:S(2)}, u32[]{:S(2)}) collective-permute-start(bf16[2,96,768]{2,1,0:T(8,128)(2,1)} %get-tuple-element.529), channel_id=1, source_target_pairs={{0,16},{4,20},{8,24},{12,28},{16,0},{20,4},{24,8},{28,12},{1,17},{... | collective-permute-start | bytes 884744 | tf_op jit(solution)/shard_map/ppermute | solution.py:775
  254.7 22.9 %collective-permute-start.42 = (bf16[2,96,768]{2,1,0:T(8,128)(2,1)}, bf16[2,96,768]{2,1,0:T(8,128)(2,1)}, u32[]{:S(2)}, u32[]{:S(2)}) collective-permute-start(bf16[2,96,768]{2,1,0:T(8,128)(2,1)} %get-tuple-element.528), channel_id=1, source_target_pairs={{0,24},{4,28},{8,16},{12,20},{16,8},{20,12},{24,0},{28,4},{1,25},{... | collective-permute-start | bytes 884744 | tf_op jit(solution)/shard_map/ppermute | solution.py:775
  277.6 25.8 %collective-permute-start.46 = (bf16[4,2,96,768]{3,2,1,0:T(8,128)(2,1)}, bf16[4,2,96,768]{3,2,1,0:T(8,128)(2,1)}, u32[]{:S(2)}, u32[]{:S(2)}) collective-permute-start(bf16[4,2,96,768]{3,2,1,0:T(8,128)(2,1)} %pad_maximum_fusion.4), channel_id=1, source_target_pairs={{0,4},{4,0},{8,12},{12,8},{16,20},{20,16},{24,28},{28,24},{1,5},{5... | collective-permute-start | bytes 3538952 | tf_op jit(solution)/shard_map/ppermute | solution.py:775
  279.1 25.2 %collective-permute-start.47 = (bf16[4,2,96,768]{3,2,1,0:T(8,128)(2,1)S(1)}, bf16[4,2,96,768]{3,2,1,0:T(8,128)(2,1)}, u32[]{:S(2)}, u32[]{:S(2)}) collective-permute-start(bf16[4,2,96,768]{3,2,1,0:T(8,128)(2,1)S(1)} %pad_maximum_fusion.5), channel_id=1, source_target_pairs={{0,2},{1,3},{2,0},{3,1},{4,6},{5,7},{6,4},{7,5},{8,10},{9,11},{10,... | collective-permute-start | bytes 3538952 | tf_op jit(solution)/shard_map/ppermute | solution.py:775
  298.4 39.9 %collective-permute-start.45 = (bf16[2,8,1,96,768]{4,3,2,1,0:T(8,128)(2,1)}, bf16[2,8,1,96,768]{4,3,2,1,0:T(8,128)(2,1)}, u32[]{:S(2)}, u32[]{:S(2)}) collective-permute-start(bf16[2,8,1,96,768]{4,3,2,1,0:T(8,128)(2,1)} %get-tuple-element.322), channel_id=1, source_target_pairs={{0,1},{1,0},{2,3},{3,2},{4,5},{5,4},{6,7},{7,6},{8,9},{9,8},{10,11... | collective-permute-start | bytes 7077896 | tf_op jit(solution)/shard_map/ppermute | solution.py:775
  308.1 30.2 %collective-permute-start.48 = (bf16[2,96,768]{2,1,0:T(8,128)(2,1)S(1)}, bf16[2,96,768]{2,1,0:T(8,128)(2,1)S(1)}, u32[]{:S(2)}, u32[]{:S(2)}) collective-permute-start(bf16[2,96,768]{2,1,0:T(8,128)(2,1)S(1)} %get-tuple-element.525), channel_id=1, source_target_pairs={{0,8},{4,12},{8,0},{12,4},{16,24},{20,28},{24,16},{28,20},{1,9},{5... | collective-permute-start | bytes 884744 | tf_op jit(solution)/shard_map/ppermute | solution.py:775
  312.8 25.5 %collective-permute-start.49 = (bf16[2,96,768]{2,1,0:T(8,128)(2,1)S(1)}, bf16[2,96,768]{2,1,0:T(8,128)(2,1)S(1)}, u32[]{:S(2)}, u32[]{:S(2)}) collective-permute-start(bf16[2,96,768]{2,1,0:T(8,128)(2,1)S(1)} %get-tuple-element.524), channel_id=1, source_target_pairs={{0,16},{4,20},{8,24},{12,28},{16,0},{20,4},{24,8},{28,12},{1,17},{... | collective-permute-start | bytes 884744 | tf_op jit(solution)/shard_map/ppermute | solution.py:775
  313.7 24.6 %collective-permute-start.50 = (bf16[2,96,768]{2,1,0:T(8,128)(2,1)S(1)}, bf16[2,96,768]{2,1,0:T(8,128)(2,1)S(1)}, u32[]{:S(2)}, u32[]{:S(2)}) collective-permute-start(bf16[2,96,768]{2,1,0:T(8,128)(2,1)S(1)} %get-tuple-element.523), channel_id=1, source_target_pairs={{0,24},{4,28},{8,16},{12,20},{16,8},{20,12},{24,0},{28,4},{1,25},{... | collective-permute-start | bytes 884744 | tf_op jit(solution)/shard_map/ppermute | solution.py:775
  315.2 23.1 %all-to-all-start.2 = ((bf16[4,240,768]{2,1,0:T(8,128)(2,1)}), bf16[4,240,768]{2,1,0:T(8,128)(2,1)S(1)}, u32[]{:S(2)}, u32[]{:S(2)}) async-start(bf16[4,240,768]{2,1,0:T(8,128)(2,1)} %bitcast.57), calls=%async_computation.2 | async-start | bytes 2949120 | tf_op jit(solution)/shard_map/all_to_all | solution.py:781
  354.4 16.6 %collective-permute-start.53 = (bf16[4,1,96,768]{3,2,1,0:T(8,128)(2,1)S(1)}, bf16[4,1,96,768]{3,2,1,0:T(8,128)(2,1)S(1)}, u32[]{:S(2)}, u32[]{:S(2)}) collective-permute-start(bf16[4,1,96,768]{3,2,1,0:T(8,128)(2,1)S(1)} %pad_maximum_fusion.7), channel_id=1, source_target_pairs={{0,4},{4,0},{8,12},{12,8},{16,20},{20,16},{24,28},{28,24},{1,5},{5... | collective-permute-start | bytes 1769480 | tf_op jit(solution)/shard_map/ppermute | solution.py:775
  355.8 15.2 %collective-permute-start.54 = (bf16[4,1,96,768]{3,2,1,0:T(8,128)(2,1)S(1)}, bf16[4,1,96,768]{3,2,1,0:T(8,128)(2,1)}, u32[]{:S(2)}, u32[]{:S(2)}) collective-permute-start(bf16[4,1,96,768]{3,2,1,0:T(8,128)(2,1)S(1)} %pad_maximum_fusion.8), channel_id=1, source_target_pairs={{0,2},{1,3},{2,0},{3,1},{4,6},{5,7},{6,4},{7,5},{8,10},{9,11},{10,... | collective-permute-start | bytes 1769480 | tf_op jit(solution)/shard_map/ppermute | solution.py:775
  373.9 20.3 %collective-permute-start.60 = (bf16[1,96,768]{2,1,0:T(8,128)(2,1)}, bf16[1,96,768]{2,1,0:T(8,128)(2,1)}, u32[]{:S(2)}, u32[]{:S(2)}) collective-permute-start(bf16[1,96,768]{2,1,0:T(8,128)(2,1)} %get-tuple-element.533), channel_id=1, source_target_pairs={{0,8},{4,12},{8,0},{12,4},{16,24},{20,28},{24,16},{28,20},{1,9},{5... | collective-permute-start | bytes 442376 | tf_op jit(solution)/shard_map/ppermute | solution.py:775
  375.0 19.3 %collective-permute-start.61 = (bf16[1,96,768]{2,1,0:T(8,128)(2,1)}, bf16[1,96,768]{2,1,0:T(8,128)(2,1)}, u32[]{:S(2)}, u32[]{:S(2)}) collective-permute-start(bf16[1,96,768]{2,1,0:T(8,128)(2,1)} %get-tuple-element.535), channel_id=1, source_target_pairs={{0,16},{4,20},{8,24},{12,28},{16,0},{20,4},{24,8},{28,12},{1,17},{... | collective-permute-start | bytes 442376 | tf_op jit(solution)/shard_map/ppermute | solution.py:775
  376.9 17.4 %collective-permute-start.62 = (bf16[1,96,768]{2,1,0:T(8,128)(2,1)}, bf16[1,96,768]{2,1,0:T(8,128)(2,1)}, u32[]{:S(2)}, u32[]{:S(2)}) collective-permute-start(bf16[1,96,768]{2,1,0:T(8,128)(2,1)} %get-tuple-element.534), channel_id=1, source_target_pairs={{0,24},{4,28},{8,16},{12,20},{16,8},{20,12},{24,0},{28,4},{1,25},{... | collective-permute-start | bytes 442376 | tf_op jit(solution)/shard_map/ppermute | solution.py:775
  378.3 26.7 %all-to-all-start.3 = ((bf16[4,240,768]{2,1,0:T(8,128)(2,1)}), bf16[4,240,768]{2,1,0:T(8,128)(2,1)S(1)}, u32[]{:S(2)}, u32[]{:S(2)}) async-start(bf16[4,240,768]{2,1,0:T(8,128)(2,1)} %bitcast.220), calls=%async_computation.3 | async-start | bytes 2949120 | tf_op jit(solution)/shard_map/all_to_all | solution.py:781
  (79 other events, 632.8 us)
